TPU v7x, 32 devices: a whole 2x2x4 slice. The times are simulated.
32 devices in a mesh: dp: 8 (over z, x), mp: 4 (over y, core).
Axes of the slice: x: 2, y: 2, z: 4, core: 2. Of those that a mesh axis runs over, the one named last changes fastest.
Arguments:
- tokens: bfloat16 [24576, 768], P('dp', 'mp'), may hold values from -80 to 80
- image_ids: int32 [24, 1024], P('dp'), may hold values from 0 to 5, never falling along the last dimension, each value on 1 to 512 neighbouring positions
- norm_gain: bfloat16 [768], P('mp'), may hold values from 0.25 to 1.75
- qkv_weight: bfloat16 [768, 3, 768], P(None, None, 'mp'), may hold values from -0.21875 to 0.21875
- qk_gain: bfloat16 [2, 768], P(None, 'mp'), may hold values from 0.25 to 1.75
- attn_weight: bfloat16 [768, 768], P('mp'), may hold values from -1.5 to 1.5
- up_weight: bfloat16 [768, 3072], P(None, 'mp'), may hold values from -1 to 1
- up_bias: bfloat16 [3072], P('mp'), may hold values from -3 to 3
- down_weight: bfloat16 [3072, 768], P('mp'), may hold values from -0.109375 to 0.109375
- down_bias: bfloat16 [768], P('mp'), may hold values from -3 to 3
- cotangent: bfloat16 [24576, 768], P('dp'), may hold values from -6 to 6
Outputs:
- block_out: bfloat16 [24576, 768], P('dp', 'mp')
- token_grad: float32 [24576, 768], P('dp', 'mp')
- gain_grad: float32 [768], P('mp')
- qkv_grad: float32 [768, 3, 768], P(None, None, 'mp')
- qkgain_grad: float32 [2, 768], P(None, 'mp')
- attn_grad: float32 [768, 768], P('mp')
- up_grad: float32 [768, 3072], P(None, 'mp')
- upbias_grad: float32 [3072], P('mp')
- down_grad: float32 [3072, 768], P('mp')
- downbias_grad: float32 [768], P('mp')
Inputs may be any that keep to these rules, and one draw needn't show every extreme that they name: `image_ids`: in each sequence the image ids start at 0 and never fall; each of the 6 images has 1 to 512 tokens, and one has exactly 512.
All inputs are finite; a program needn't handle non-finite values.
Results may differ from a plain program's by a relative error of at most 0.012.
Values may be sent and summed in bfloat16 or wider, within the bound.
No kernel may reach another device: no remote copies, remote signals or barrier semaphores. Data moves between devices by JAX's collectives and lax.ppermute only.
A program may use at most 192 MiB of HBM per device.

v0:
```python
import functools

import jax
import jax.numpy as jnp
from jax import lax
from jax.experimental import pallas as pl
from jax.experimental.pallas import tpu as pltpu
from jax.sharding import PartitionSpec as P

DH = 64
LEN = 1024
EPSILON = 1e-06
IMAGE_SLOTS = 16
PENALTY = 1024.0
BI = 256
BJ = 256
SUM_ROWS = 16
F32 = jnp.float32
BF16 = jnp.bfloat16

NN = (((1,), (0,)), ((), ()))
NT = (((1,), (1,)), ((), ()))
ANY = pl.BlockSpec(memory_space=pl.ANY)


def dot(left, right, dims=NN):
    return lax.dot_general(left, right, dims, preferred_element_type=F32)


def fold_lanes(rows):
    total = rows[:, :128]
    for start in range(128, rows.shape[1], 128):
        total = total + rows[:, start : start + 128]
    return total


def cost(microseconds, nbytes):
    return pl.CostEstimate(flops=int(microseconds * 1e9), bytes_accessed=nbytes, transcendentals=0)


def early_kernel(cot, down, attn, d_act, d_att, bias_sum):
    rows = cot[...]
    d_act[...] = dot(down[...], rows, NT).astype(BF16)
    d_att[...] = dot(attn[...], rows, NT).astype(BF16)

    @pl.when(pl.program_id(0) == 0)
    def _():
        bias_sum[...] = jnp.zeros_like(bias_sum)

    wide = rows.astype(F32)
    bias_sum[...] += jnp.sum(wide.reshape(wide.shape[0] // 8, 8, wide.shape[1]), axis=0)


def early_call(cot, down, attn, block=512):
    tokens, width = cot.shape
    seqs = tokens // LEN
    hidden, part = down.shape[0], attn.shape[0]
    steps = LEN // block
    fixed = lambda i: (0, 0)
    by_seq = lambda i: (i // steps, 0, i % steps)
    return pl.pallas_call(
        early_kernel,
        grid=(tokens // block,),
        in_specs=[
            pl.BlockSpec((block, width), lambda i: (i, 0)),
            pl.BlockSpec((hidden, width), fixed),
            pl.BlockSpec((part, width), fixed),
        ],
        out_specs=[
            pl.BlockSpec((None, hidden, block), by_seq),
            pl.BlockSpec((None, part, block), by_seq),
            pl.BlockSpec((8, width), fixed),
        ],
        out_shape=[
            jax.ShapeDtypeStruct((seqs, hidden, LEN), BF16),
            jax.ShapeDtypeStruct((seqs, part, LEN), BF16),
            jax.ShapeDtypeStruct((8, width), F32),
        ],
        cost_estimate=cost(10, 12_000_000),
        name="early",
    )(cot, down, attn)


def split_store(side, low, high, keep, send):
    @pl.when(side == 0)
    def _():
        keep[...] = low[...].astype(BF16)
        send[...] = high[...].astype(BF16)

    @pl.when(side != 0)
    def _():
        keep[...] = high[...].astype(BF16)
        send[...] = low[...].astype(BF16)


def mlp_kernel(
    place, own, flip_y, flip_c, flip_cy, gain_own, gain_y, gain_c, gain_cy, up_t, up_bias, d_act, cot,
    normed, active, d_pre, stats, bias_sum, gain_all, down_grad, up_grad, low, high
):
    pieces = (own, flip_y, flip_c, flip_cy)
    part = own.shape[0]
    width = part * 4
    first = pl.program_id(0) == 0
    last = pl.program_id(0) == pl.num_programs(0) - 1

    @pl.when(first)
    def _():
        bias_sum[...] = jnp.zeros_like(bias_sum)
        low[...] = jnp.zeros_like(low)
        high[...] = jnp.zeros_like(high)
        for slot, piece in enumerate((gain_own, gain_y, gain_c, gain_cy)):
            gain_all[pl.ds(pl.multiple_of(place[slot], part), part), :] = piece[...].astype(F32)

    total = 0.0
    squares = 0.0
    for piece in pieces:
        rows = piece[...].astype(F32)
        total = total + jnp.sum(rows, axis=0, keepdims=True)
        squares = squares + jnp.sum(rows * rows, axis=0, keepdims=True)
    mean = total * (1.0 / width)
    scale = lax.rsqrt(squares * (1.0 / width) - mean * mean + EPSILON)
    stats[0:1, :] = mean
    stats[1:2, :] = scale
    stats[2:8, :] = jnp.zeros((6, stats.shape[1]), F32)
    for slot, piece in enumerate(pieces):
        rows = piece[...].astype(F32)
        here = pl.ds(pl.multiple_of(place[slot], part), part)
        normed[here, :] = ((rows - mean) * scale * gain_all[here, :1]).astype(BF16)

    c0 = 0.7978845608028654
    c1 = 0.044715 * c0
    for start in range(0, up_t.shape[0], 256):
        here = slice(start, start + 256)
        pre = dot(up_t[here, :], normed[...]) + up_bias[here, :]
        square = pre * pre
        half = 0.5 * jnp.tanh(pre * (c0 + c1 * square)) + 0.5
        act = (pre * half).astype(BF16)
        active[here, :] = act
        slope = half + pre * (half - half * half) * (2.0 * c0 + 6.0 * c1 * square)
        grad = (d_act[here, :].astype(F32) * slope).astype(BF16)
        d_pre[here, :] = grad
        bias_sum[here, :] += fold_lanes(grad.astype(F32))
        low[here, :] += dot(act, cot[...])
        high[:, here] += dot(normed[...], grad, NT)

    @pl.when(last)
    def _():
        down_grad[...] = low[...].astype(BF16)
        up_grad[...] = high[...].astype(BF16)


def mlp_call(place, pieces, gains, up_t, up_bias, d_act, cot, block=512):
    part, tokens = pieces[0].shape
    width = 4 * part
    seqs, hidden, _ = d_act.shape
    steps = LEN // block
    lanes = lambda i, *_: (0, i)
    by_seq = lambda i, *_: (i // steps, 0, i % steps)
    fixed = lambda i, *_: (0, 0)
    grid_spec = pltpu.PrefetchScalarGridSpec(
        num_scalar_prefetch=1,
        grid=(tokens // block,),
        in_specs=[pl.BlockSpec((part, block), lanes)] * 4
        + [pl.BlockSpec((part, 128), fixed)] * 4
        + [
            pl.BlockSpec((hidden, width), fixed),
            pl.BlockSpec((hidden, 1), fixed),
            pl.BlockSpec((None, hidden, block), by_seq),
            pl.BlockSpec((block, width), lambda i, *_: (i, 0)),
        ],
        out_specs=[
            pl.BlockSpec((None, width, block), by_seq),
            pl.BlockSpec((None, hidden, block), by_seq),
            pl.BlockSpec((None, hidden, block), by_seq),
            pl.BlockSpec((8, block), lanes),
            pl.BlockSpec((hidden, 128), fixed),
            pl.BlockSpec((width, 128), fixed),
            pl.BlockSpec((hidden, width), fixed),
            pl.BlockSpec((width, hidden), fixed),
        ],
        scratch_shapes=[pltpu.VMEM((hidden, width), F32), pltpu.VMEM((width, hidden), F32)],
    )
    return pl.pallas_call(
        mlp_kernel,
        grid_spec=grid_spec,
        out_shape=[
            jax.ShapeDtypeStruct((seqs, width, LEN), BF16),
            jax.ShapeDtypeStruct((seqs, hidden, LEN), BF16),
            jax.ShapeDtypeStruct((seqs, hidden, LEN), BF16),
            jax.ShapeDtypeStruct((8, tokens), F32),
            jax.ShapeDtypeStruct((hidden, 128), F32),
            jax.ShapeDtypeStruct((width, 128), F32),
            jax.ShapeDtypeStruct((hidden, width), BF16),
            jax.ShapeDtypeStruct((width, hidden), BF16),
        ],
        cost_estimate=cost(20, 30_000_000),
        name="mlp",
    )(place, *pieces, *gains, up_t, up_bias, d_act, cot)


def attention_kernel(last, seq, first, count, normed, mixed_t, d_att, mask_q, mask_k, gains, cot_hbm, *rest):
    if seq:
        before_hbm, rest = rest[0], rest[1:]
    (
        attended, d_mixed, gain_sum, grads, qkv, qx, kx, vn, kt, vt, es, ps, oa, dqa, dka, dva, cot, before, cot_sem,
        before_sem,
    ) = rest
    part = attended.shape[0]
    heads = part // DH
    inv_dh = 1.0 / DH
    copies = [pltpu.make_async_copy(cot_hbm.at[pl.ds(seq * LEN, LEN), :], cot, cot_sem)]
    if seq:
        copies.append(pltpu.make_async_copy(before_hbm, before, before_sem))
    for copy in copies:
        copy.start()

    qkv[...] = dot(mixed_t[...], normed[...])

    def unit(start):
        raw = qkv[start : start + DH, :]
        shifted = raw - jnp.sum(raw, axis=0, keepdims=True) * inv_dh
        scale = lax.rsqrt(jnp.sum(shifted * shifted, axis=0, keepdims=True) * inv_dh + EPSILON)
        return shifted * scale, scale

    zeros = jnp.zeros((128 - DH - IMAGE_SLOTS, LEN), BF16)
    for head in range(heads):
        rows = slice(head * DH, (head + 1) * DH)
        query, _ = unit(head * DH)
        query = (query * (gains[rows, :] * 0.125)).astype(BF16)
        qx[head] = jnp.concatenate([query, mask_q[...], zeros], axis=0)
        key, _ = unit(part + head * DH)
        key = (key * gains[part + head * DH : part + (head + 1) * DH, :]).astype(BF16)
        kt[rows, :] = key
        kx[head] = jnp.concatenate([key, mask_k[...], zeros], axis=0).T
        value = qkv[2 * part + head * DH : 2 * part + (head + 1) * DH, :].astype(BF16)
        vt[rows, :] = value
        vn[head] = value.T
    dka[...] = jnp.zeros_like(dka)
    dva[...] = jnp.zeros_like(dva)

    def query_block(ib, _):
        i0 = pl.multiple_of(ib * BI, BI)
        icols = pl.ds(i0, BI)
        base = first[ib]
        trips = count[ib]

        def scores(j, carry):
            j0 = pl.multiple_of((base + j) * BJ, BJ)
            slot = pl.multiple_of(j * BJ, BJ)
            out = []
            for head in range(heads):
                rows = slice(head * DH, (head + 1) * DH)
                e = jnp.exp(dot(kx[head, pl.ds(j0, BJ), :], qx[head, :, icols]))
                p = dot(vn[head, pl.ds(j0, BJ), :], d_att[rows, icols])
                es[head, pl.ds(slot, BJ), :] = e
                ps[head, pl.ds(slot, BJ), :] = p
                out.append(carry[2 * head] + jnp.sum(e.reshape(BJ // 8, 8, BI), axis=0))
                out.append(carry[2 * head + 1] + jnp.sum((e * p).reshape(BJ // 8, 8, BI), axis=0))
            return tuple(out)

        sums = lax.fori_loop(0, trips, scores, tuple(jnp.zeros((8, BI), F32) for _ in range(2 * heads)))
        inverse = []
        inner = []
        for head in range(heads):
            inv = 1.0 / jnp.sum(sums[2 * head], axis=0, keepdims=True)
            inverse.append(inv)
            inner.append(jnp.sum(sums[2 * head + 1], axis=0, keepdims=True) * inv)
        oa[...] = jnp.zeros_like(oa)
        dqa[:, icols] = jnp.zeros((part, BI), F32)

        def row_grads(j, _):
            j0 = pl.multiple_of((base + j) * BJ, BJ)
            slot = pl.multiple_of(j * BJ, BJ)
            jcols = pl.ds(j0, BJ)
            for head in range(heads):
                rows = slice(head * DH, (head + 1) * DH)
                w = es[head, pl.ds(slot, BJ), :] * inverse[head]
                d = (w * (ps[head, pl.ds(slot, BJ), :] - inner[head])).astype(BF16)
                w = w.astype(BF16)
                oa[rows, :] += dot(vt[rows, jcols], w)
                dqa[rows, icols] += dot(kt[rows, jcols], d)
                dva[rows, jcols] += dot(d_att[rows, icols], w, NT)
                dka[rows, jcols] += dot(qx[head, :DH, icols], d, NT)
            return 0

        lax.fori_loop(0, trips, row_grads, 0)
        attended[:, icols] = oa[...].astype(BF16)
        return 0

    lax.fori_loop(0, LEN // BI, query_block, 0)

    for source, offset, factor in ((dqa, 0, 0.125), (dka, part, 1.0)):
        for head in range(heads):
            start = offset + head * DH
            u, scale = unit(start)
            e = source[head * DH : (head + 1) * DH, :] * factor
            gain_sum[start : start + DH, :] = fold_lanes(e * u)
            f = e * gains[start : start + DH, :]
            mean_f = jnp.sum(f, axis=0, keepdims=True) * inv_dh
            mean_fu = jnp.sum(f * u, axis=0, keepdims=True) * inv_dh
            d_mixed[start : start + DH, :] = ((f - mean_f - u * mean_fu) * scale).astype(BF16)
    d_mixed[2 * part :, :] = dva[...].astype(BF16)

    for copy in copies:
        copy.wait()
    split = 3 * part
    for rows, value in (
        (slice(0, split), dot(d_mixed[...], normed[...], NT)),
        (slice(split, split + part), dot(attended[...], cot[...])),
    ):
        if seq:
            value = value + before[rows, :]
        grads[rows, :] = value.astype(grads.dtype)


def attention_call(first, count, normed, mixed_t, d_att, mask_q, mask_k, gains, cot, before, seq, last):
    seqs, part, _ = d_att.shape
    width = normed.shape[1]
    heads = part // DH
    once = lambda i, *_: (0, 0)
    ours = lambda i, *_: (seq, 0, 0)
    grid_spec = pltpu.PrefetchScalarGridSpec(
        num_scalar_prefetch=2,
        grid=(1,),
        in_specs=[
            pl.BlockSpec((None, width, LEN), ours),
            pl.BlockSpec((3 * part, width), once),
            pl.BlockSpec((None, part, LEN), ours),
            pl.BlockSpec((None, IMAGE_SLOTS, LEN), ours),
            pl.BlockSpec((None, IMAGE_SLOTS, LEN), ours),
            pl.BlockSpec((2 * part, 1), once),
            ANY,
        ]
        + [ANY] * len(before),
        out_specs=[
            pl.BlockSpec((part, LEN), once),
            pl.BlockSpec((3 * part, LEN), once),
            pl.BlockSpec((2 * part, 128), once),
            pl.BlockSpec((4 * part, width), once),
        ],
        scratch_shapes=[
            pltpu.VMEM((3 * part, LEN), F32),
            pltpu.VMEM((heads, 128, LEN), BF16),
            pltpu.VMEM((heads, LEN, 128), BF16),
            pltpu.VMEM((heads, LEN, DH), BF16),
            pltpu.VMEM((part, LEN), BF16),
            pltpu.VMEM((part, LEN), BF16),
            pltpu.VMEM((heads, LEN, BI), F32),
            pltpu.VMEM((heads, LEN, BI), F32),
            pltpu.VMEM((part, BI), F32),
            pltpu.VMEM((part, LEN), F32),
            pltpu.VMEM((part, LEN), F32),
            pltpu.VMEM((part, LEN), F32),
            pltpu.VMEM((LEN, width), BF16),
            pltpu.VMEM((4 * part, width), F32),
            pltpu.SemaphoreType.DMA(()),
            pltpu.SemaphoreType.DMA(()),
        ],
    )
    return pl.pallas_call(
        functools.partial(attention_kernel, last, seq),
        grid_spec=grid_spec,
        out_shape=[
            jax.ShapeDtypeStruct((part, LEN), BF16),
            jax.ShapeDtypeStruct((3 * part, LEN), BF16),
            jax.ShapeDtypeStruct((2 * part, 128), F32),
            jax.ShapeDtypeStruct((4 * part, width), BF16 if last else F32),
        ],
        cost_estimate=cost(18, 5_000_000),
        name="attention",
    )(first, count, normed, mixed_t, d_att, mask_q, mask_k, gains, cot, *before)


def project_kernel(
    shard, active, attended, d_pre, d_mixed, normed, down_t, attn_t, up, mixed, gain, keep, send, gain_sum
):
    me = shard[0]
    part = attended.shape[0]
    out = dot(down_t[...], active[...]) + dot(attn_t[...], attended[...])
    grad = dot(up[...], d_pre[...]) + dot(mixed[...], d_mixed[...])
    product = grad * normed[...].astype(F32)
    sums = []
    for row in (jnp.sum(grad * gain[:, :1], axis=0, keepdims=True), jnp.sum(product, axis=0, keepdims=True)):
        high = row.astype(BF16)
        sums += [high, (row - high.astype(F32)).astype(BF16)]
    sums = jnp.concatenate(sums + [jnp.zeros((SUM_ROWS - 4, sums[0].shape[1]), BF16)], axis=0)
    for target in (keep, send):
        for slot in range(2):
            target[slot, 2 * part :, :] = sums
    for index in range(4):
        rows = slice(index * part, (index + 1) * part)
        away = jnp.bitwise_xor(me, index)
        slot = away // 2

        @pl.when(away % 2 == 0)
        def _():
            keep[slot, :part, :] = out[rows].astype(BF16)
            keep[slot, part : 2 * part, :] = grad[rows].astype(BF16)

        @pl.when(away % 2 == 1)
        def _():
            send[slot, :part, :] = out[rows].astype(BF16)
            send[slot, part : 2 * part, :] = grad[rows].astype(BF16)

    @pl.when(pl.program_id(0) == 0)
    def _():
        gain_sum[...] = jnp.zeros_like(gain_sum)

    gain_sum[...] += fold_lanes(product)


def project_call(shard, active, attended, d_pre, d_mixed, normed, down_t, attn_t, up, mixed, gain, seq, block=256):
    width, hidden = down_t.shape
    part = attended.shape[0]
    steps = LEN // block
    lanes = lambda i, *_: (0, i)
    ours = lambda i, *_: (seq, 0, i)
    fixed = lambda i, *_: (0, 0)
    rows = 2 * part + SUM_ROWS
    grid_spec = pltpu.PrefetchScalarGridSpec(
        num_scalar_prefetch=1,
        grid=(steps,),
        in_specs=[
            pl.BlockSpec((None, hidden, block), ours),
            pl.BlockSpec((part, block), lanes),
            pl.BlockSpec((None, hidden, block), ours),
            pl.BlockSpec((3 * part, block), lanes),
            pl.BlockSpec((None, width, block), ours),
            pl.BlockSpec((width, hidden), fixed),
            pl.BlockSpec((width, part), fixed),
            pl.BlockSpec((width, hidden), fixed),
            pl.BlockSpec((width, 3 * part), fixed),
            pl.BlockSpec((width, 128), fixed),
        ],
        out_specs=[
            pl.BlockSpec((2, rows, block), lambda i, *_: (0, 0, i)),
            pl.BlockSpec((2, rows, block), lambda i, *_: (0, 0, i)),
            pl.BlockSpec((width, 128), fixed),
        ],
    )
    return pl.pallas_call(
        project_kernel,
        grid_spec=grid_spec,
        out_shape=[
            jax.ShapeDtypeStruct((2, rows, LEN), BF16),
            jax.ShapeDtypeStruct((2, rows, LEN), BF16),
            jax.ShapeDtypeStruct((width, 128), F32),
        ],
        cost_estimate=cost(8, 16_000_000),
        name="project",
    )(shard, active, attended, d_pre, d_mixed, normed, down_t, attn_t, up, mixed, gain)


def finish_kernel(keep, from_core, from_y, own_t, tokens, cot, stats, gain, bias, *rest):
    block_out, token_grad = rest[-2:]
    part = own_t.shape[0]
    inv_width = 0.25 / part
    total = keep[...].astype(F32) + from_core[...].astype(F32) + from_y[...].astype(F32)
    block_out[...] = (tokens[...].astype(F32) + total[:part].T + bias[...]).astype(BF16)
    grad = total[part : 2 * part]
    sums = total[2 * part :]
    mean = stats[0:1, :]
    scale = stats[1:2, :]
    hat = (own_t[...].astype(F32) - mean) * scale
    inner = grad * gain[...] - (sums[0:1] + sums[1:2]) * inv_width - hat * ((sums[2:3] + sums[3:4]) * inv_width)
    token_grad[...] = cot[...].astype(F32) + (inner * scale).T


def finish_call(keep, from_core, from_y, own_t, tokens, cot, stats, gain, bias, before, seq, block=512):
    part = own_t.shape[0]
    steps = LEN // block
    fixed = lambda i: (0, 0)
    ours = lambda i: (0, seq * steps + i)
    packed = pl.BlockSpec((None, 2 * part + SUM_ROWS, block), lambda i: (0, 0, i))
    here = pl.BlockSpec((block, part), lambda i: (seq * steps + i, 0))
    return pl.pallas_call(
        finish_kernel,
        grid=(steps,),
        in_specs=[
            packed, packed, packed,
            pl.BlockSpec((part, block), ours),
            here, here,
            pl.BlockSpec((8, block), ours),
            pl.BlockSpec((part, 1), fixed),
            pl.BlockSpec((1, part), fixed),
        ]
        + [ANY] * len(before),
        out_specs=[here, here],
        out_shape=[
            jax.ShapeDtypeStruct(tokens.shape, BF16),
            jax.ShapeDtypeStruct(tokens.shape, F32),
        ],
        input_output_aliases={9 + i: i for i in range(len(before))},
        cost_estimate=cost(3, 5_000_000),
        name="finish",
    )(keep, from_core, from_y, own_t, tokens, cot, stats, gain, bias, *before)


def flip(value, axis, size, bit):
    return lax.ppermute(value, axis, [(i, i ^ bit) for i in range(size)])


def tie(*trees):
    return lax.optimization_barrier(trees)


class SumOverDp:
    def __init__(self, value, size, index, turn):
        self.size, self.index = size, index
        bits = [1 << i for i in range(size.bit_length() - 1)]
        bits = bits[turn:] + bits[:turn]
        self.steps = [("sum", bit) for bit in bits] + [("join", bit) for bit in reversed(bits)]
        self.prepare(value, None)

    def prepare(self, held, arrived):
        def part(which, half):
            rows = lax.dynamic_slice_in_dim(held, which * half, half, 0)
            if arrived is None:
                return rows
            came = lax.dynamic_slice_in_dim(arrived, which * half, half, 0)
            return (rows.astype(F32) + came.astype(F32)).astype(BF16)

        rows = held.shape[0]
        if self.steps and self.steps[0][0] == "sum":
            side = self.side(self.steps[0][1])
            self.send, self.keep = part(1 - side, rows // 2), part(side, rows // 2)
        else:
            self.keep = part(0, rows)
            self.send = self.keep

    def side(self, bit):
        return (self.index & bit) // bit

    def more(self):
        return bool(self.steps)

    def move(self, send):
        return flip(send, "dp", self.size, self.steps[0][1])

    def take(self, arrived):
        kind, bit = self.steps.pop(0)
        if kind == "sum":
            self.prepare(self.keep, arrived)
            return
        self.keep = jnp.where(
            self.side(bit) == 1,
            jnp.concatenate([arrived, self.keep], axis=0),
            jnp.concatenate([self.keep, arrived], axis=0),
        )
        self.send = self.keep


class ScatterOverMp:
    def __init__(self, keep, send):
        self.keep, self.send = keep, send
        self.bits = [1, 2]

    def more(self):
        return bool(self.bits)

    def move(self, send):
        return flip(send, "mp", 4, self.bits[0])

    def take(self, arrived):
        bit = self.bits.pop(0)
        if bit == 1:
            self.from_core = arrived
            self.send = (self.keep[1].astype(F32) + arrived[1].astype(F32)).astype(BF16)[None]
        else:
            self.from_y = arrived


def launch(movers, inputs):
    movers = [m for m in movers if m.more()]
    inputs, sends = tie(inputs, [m.send for m in movers])
    return inputs, [(m, m.move(s)) for m, s in zip(movers, sends)]


def land(flights, outputs):
    outputs, arrivals = tie(outputs, [f[1] for f in flights])
    for (mover, _), arrived in zip(flights, arrivals):
        mover.take(arrived)
    return outputs


def body(
    dp_size,
    tokens,
    image_ids,
    norm_gain,
    qkv_weight,
    qk_gain,
    attn_weight,
    up_weight,
    up_bias,
    down_weight,
    down_bias,
    cotangent,
):
    part = tokens.shape[1]
    width = cotangent.shape[1]
    seqs = image_ids.shape[0]
    me = lax.axis_index("mp")
    dp = lax.axis_index("dp")
    shard = me.astype(jnp.int32)[None]
    place = jnp.bitwise_xor(shard, jnp.array([0, 2, 1, 3], jnp.int32)) * part

    own_t = tokens.T
    from_y = flip(own_t, "mp", 4, 2)
    gain_own = jnp.broadcast_to(norm_gain[:, None], (part, 128))
    gain_y = flip(gain_own, "mp", 4, 2)
    gains = (gain_own, gain_y, flip(gain_own, "mp", 4, 1), flip(gain_y, "mp", 4, 1))

    mixed_t = jnp.transpose(qkv_weight, (1, 2, 0)).reshape(3 * part, width)
    mixed = mixed_t.T
    up_t = up_weight.T
    down_t = down_weight.T
    attn_t = attn_weight.T
    up_bias_col = up_bias.astype(F32)[:, None]
    head_gains = qk_gain.astype(F32).reshape(2 * part, 1)

    slots = jnp.arange(IMAGE_SLOTS, dtype=jnp.int32)[None, :, None]
    same = image_ids[:, None, :] == slots
    mask_q = same.astype(BF16)
    mask_k = jnp.where(same | (slots >= 8), 0.0, -PENALTY).astype(BF16)
    block_first = image_ids[:, ::BI]
    block_last = image_ids[:, BI - 1 :: BI]
    starts = jnp.sum(image_ids[:, None, :] < block_first[:, :, None], axis=2, dtype=jnp.int32)
    ends = jnp.sum(image_ids[:, None, :] <= block_last[:, :, None], axis=2, dtype=jnp.int32)
    first = starts // BJ
    count = (ends + BJ - 1) // BJ - first

    d_act, d_att, cot_sum = early_call(cotangent, down_weight, attn_weight)
    (d_act, d_att), from_y = tie((d_act, d_att), from_y)
    pieces = (own_t, from_y, flip(own_t, "mp", 4, 1), flip(from_y, "mp", 4, 1))
    cot_own = lax.dynamic_slice_in_dim(cotangent, me * part, part, 1)
    downbias_part = lax.dynamic_slice_in_dim(jnp.sum(cot_sum, axis=0), me * part, part, 0)

    normed, active, d_pre, stats, upbias_part, gain_all, down_part, up_part = mlp_call(
        place, pieces, gains, up_t, up_bias_col, d_act, cotangent
    )
    upbias_part = jnp.sum(upbias_part, axis=1)
    down_sum = SumOverDp(down_part, dp_size, dp, 0)
    up_sum = SumOverDp(up_part, dp_size, dp, 1)

    heads_out = []
    before = ()
    qk_part = 0.0
    for seq in range(seqs):
        (states, before), flights = launch([down_sum, up_sum], (normed, before))
        *out, qk, total = attention_call(
            first[seq], count[seq], states, mixed_t, d_att, mask_q, mask_k, head_gains, cotangent, before, seq,
            seq == seqs - 1,
        )
        out, qk, total = land(flights, (out, qk, total))
        heads_out.append(out)
        before = (total,)
        qk_part = qk_part + qk
    mix_sum = SumOverDp(before[0], dp_size, dp, 0)

    scatters = []
    gain_part = 0.0
    waiting = []
    for seq in range(seqs):
        ahead = [[down_sum, up_sum, mix_sum], [down_sum, up_sum], [down_sum, up_sum, mix_sum]][seq % 3]
        (attended, d_mixed), flights = launch(ahead + scatters[-2:], heads_out[seq])
        keep, send, gp = project_call(
            shard, active, attended, d_pre, d_mixed, normed, down_t, attn_t, up_weight, mixed, gain_all, seq
        )
        later = [f for f in flights if f[0] is mix_sum and seq == 0]
        keep, send, gp = land([f for f in flights if f not in later] + waiting, (keep, send, gp))
        waiting = later
        gain_part = gain_part + gp
        scatters.append(ScatterOverMp(keep, send))

    gain_vec = jnp.sum(gain_part, axis=1).reshape(4, part)
    gain_half = [lax.dynamic_index_in_dim(gain_vec, jnp.bitwise_xor(me, m), 0, False) for m in range(4)]
    gain_kept = jnp.stack([gain_half[0], gain_half[2]]) + flip(jnp.stack([gain_half[1], gain_half[3]]), "mp", 4, 1)
    gain_mine = gain_kept[0] + flip(gain_kept[1], "mp", 4, 2)
    short = jnp.concatenate(
        [gain_mine / norm_gain.astype(F32), jnp.sum(qk_part, axis=1), upbias_part, downbias_part]
    )
    bit = 1
    while bit < dp_size:
        short = short + flip(short, "dp", dp_size, bit)
        bit *= 2

    gain_bias = down_bias.astype(F32)[None, :]
    gain_col = norm_gain.astype(F32)[:, None]
    finished = ()
    for seq, scatter in enumerate(scatters):
        while scatter.more():
            scatter.take(scatter.move(scatter.send))
        finished = finish_call(
            scatter.keep, scatter.from_core, scatter.from_y, own_t, tokens, cot_own, stats,
            gain_col, gain_bias, finished, seq,
        )
    block_out, token_grad = finished

    movers = [down_sum, up_sum, mix_sum]
    while any(m.more() for m in movers):
        for mover in movers:
            if mover.more():
                mover.take(mover.move(mover.send))
    mixed_grad = mix_sum.keep.astype(F32)
    qkv_grad = jnp.transpose(mixed_grad[: 3 * part].reshape(3, part, width), (2, 0, 1))

    gain_grad = short[:part]
    qkgain_grad = short[part : 3 * part].reshape(2, part)
    upbias_grad = short[3 * part : 3 * part + upbias_part.shape[0]]
    downbias_grad = short[3 * part + upbias_part.shape[0] :]
    return (
        block_out,
        token_grad,
        gain_grad,
        qkv_grad,
        qkgain_grad,
        mixed_grad[3 * part :],
        up_sum.keep.astype(F32),
        upbias_grad,
        down_sum.keep.astype(F32),
        downbias_grad,
    )


def solution(mesh):
    in_specs = (
        P("dp", "mp"),
        P("dp", None),
        P("mp"),
        P(None, None, "mp"),
        P(None, "mp"),
        P("mp", None),
        P(None, "mp"),
        P("mp"),
        P("mp", None),
        P("mp"),
        P("dp", None),
    )
    out_specs = (
        P("dp", "mp"),
        P("dp", "mp"),
        P("mp"),
        P(None, None, "mp"),
        P(None, "mp"),
        P("mp", None),
        P(None, "mp"),
        P("mp"),
        P("mp", None),
        P("mp"),
    )
    run = functools.partial(body, mesh.shape["dp"])
    return jax.shard_map(run, mesh=mesh, in_specs=in_specs, out_specs=out_specs, check_vma=False)
```

profile of v0, /device:TPU:0, one launch (start us, length us, event | category | flops | bytes accessed | tf_op | source)
XLA Modules:
  0.0 275.8 jit_solution(13156868577852629822)
XLA Ops:
  0.6 3.0 %collective-permute-start = (bf16[192,3072]{1,0:T(8,128)(2,1)}, bf16[192,3072]{1,0:T(8,128)(2,1)}, u32[]{:S(2)}, u32[]{:S(2)}) collective-permute-start(bf16[192,3072]{1,0:T(8,128)(2,1)} %bitcast.28), channel_id=1, source_target_pairs={{0,2},{1,3},{2,0},{3,1},{4,6},{5,7},{6,4},{7,5},{8,10},{9,11},{10,... | collective-permute-start | bytes 3538952 | tf_op jit(solution)/shard_map/ppermute | solution.py:500
  5.1 0.8 slice.76
  6.7 1.0 convert_reduce_fusion
  7.7 10.1 %early.1 = (bf16[3,768,1024]{2,1,0:T(8,128)(2,1)}, bf16[3,192,1024]{2,1,0:T(8,128)(2,1)}, f32[8,768]{1,0:T(8,128)}) custom-call(bf16[3072,768]{1,0:T(8,128)(2,1)} %cot_hbm.5, bf16[768,768]{1,0:T(8,128)(2,1)} %down.1, bf16[192,768]{1,0:T(8,128)(2,1)} %attn.1), custom_call_target="tpu_custom_call" | custom-call | flops 10000000000 | bytes 12000000 | tf_op jit(solution)/shard_map/early/pallas_call | solution.py:61
  17.8 12.7 %collective-permute-done.flip_y = bf16[192,3072]{1,0:T(8,128)(2,1)} collective-permute-done((bf16[192,3072]{1,0:T(8,128)(2,1)}, bf16[192,3072]{1,0:T(8,128)(2,1)}, u32[]{:S(2)}, u32[]{:S(2)}) %collective-permute-start) | collective-permute-done | bytes 1179680 | tf_op jit(solution)/shard_map/ppermute | solution.py:500
  34.0 1.5 copy.59
  35.5 0.9 copy.60
  36.5 1.4 copy.54
  37.9 0.9 reshape.62.up_bias
  38.8 0.9 reshape.63.gains
  39.7 1.4 copy.61
  41.7 26.6 %mlp.1 = (bf16[3,768,1024]{2,1,0:T(8,128)(2,1)}, bf16[3,768,1024]{2,1,0:T(8,128)(2,1)}, bf16[3,768,1024]{2,1,0:T(8,128)(2,1)}, f32[8,3072]{1,0:T(8,128)}, f32[76...) custom-call(s32[4]{0:T(128)} %xor_multiply_fusion.place, ...), custom_call_target="tpu_custom_call" | custom-call | flops 20000000000 | bytes 30000000 | tf_op jit(solution)/shard_map/mlp/pallas_call | solution.py:183
  68.3 1.2 constant_dynamic-slice_fusion.6
  69.8 1.8 collective-permute-start.6
  71.6 1.6 collective-permute-start.7
  73.2 19.6 %attention.3 = (bf16[192,1024]{1,0:T(8,128)(2,1)}, bf16[576,1024]{1,0:T(8,128)(2,1)}, f32[384,128]{1,0:T(8,128)}, f32[768,768]{1,0:T(8,128)}) custom-call(s32[4]{0:T(128)} %get-tuple-element.275.first, s32[4]{0:T(128)} %get-tuple-element.272.count, bf16[3,768,1024]{2,1,0:T(8,128)(2,1)} %get-tuple-element.147.normed, bf16[576,768]{1,0:T(8,128)(2,1)} %bitcast.42, ...), custom_call_target="tpu_custom_call" | custom-call | flops 17999998976 | bytes 5000000 | tf_op jit(solution)/shard_map/attention/pallas_call | solution.py:360
  92.8 1.7 add_convert_fusion.5
  95.0 2.2 collective-permute-start.9
  97.2 19.3 %attention.4 = (bf16[192,1024]{1,0:T(8,128)(2,1)}, bf16[576,1024]{1,0:T(8,128)(2,1)}, f32[384,128]{1,0:T(8,128)}, f32[768,768]{1,0:T(8,128)}) custom-call(s32[4]{0:T(128)} %get-tuple-element.276.first, s32[4]{0:T(128)} %get-tuple-element.273.count, bf16[3,768,1024]{2,1,0:T(8,128)(2,1)} %get-tuple-element.147.normed, bf16[576,768]{1,0:T(8,128)(2,1)} %bitcast.43, ...), custom_call_target="tpu_custom_call" | custom-call | flops 17999998976 | bytes 5000000 | tf_op jit(solution)/shard_map/attention/pallas_call | solution.py:360
  117.7 19.1 %attention.5 = (bf16[192,1024]{1,0:T(8,128)(2,1)}, bf16[576,1024]{1,0:T(8,128)(2,1)}, f32[384,128]{1,0:T(8,128)}, bf16[768,768]{1,0:T(8,128)(2,1)}) custom-call(s32[4]{0:T(128)} %get-tuple-element.277.first, s32[4]{0:T(128)} %get-tuple-element.274.count, bf16[3,768,1024]{2,1,0:T(8,128)(2,1)} %get-tuple-element.147.normed, bf16[576,768]{1,0:T(8,128)(2,1)} %bitcast.44, ...), custom_call_target="tpu_custom_call" | custom-call | flops 17999998976 | bytes 5000000 | tf_op jit(solution)/shard_map/attention/pallas_call | solution.py:360
  136.9 1.1 constant_dynamic-slice_fusion.3
  138.1 2.0 collective-permute-start.12
  140.1 2.0 collective-permute-start.13
  142.1 10.0 %project.3 = (bf16[2,400,1024]{2,1,0:T(8,128)(2,1)}, bf16[2,400,1024]{2,1,0:T(8,128)(2,1)}, f32[768,128]{1,0:T(8,128)}) custom-call(s32[1]{0:T(128)} %bitcast.shard, bf16[3,768,1024]{2,1,0:T(8,128)(2,1)} %get-tuple-element.121.active, bf16[192,1024]{1,0:T(8,128)(2,1)} %get-tuple-element.164.attended, bf16[3,768,1024]{2,1,0:T(8,128)(2,1)} %get-tuple-element.165.d_pre, ...), custom_call_target="tpu_custom_call" | custom-call | flops 8000000000 | bytes 16000000 | tf_op jit(solution)/shard_map/project/pallas_call | solution.py:441
  152.6 2.3 collective-permute-start.15
  154.8 10.0 %project.4 = (bf16[2,400,1024]{2,1,0:T(8,128)(2,1)}, bf16[2,400,1024]{2,1,0:T(8,128)(2,1)}, f32[768,128]{1,0:T(8,128)}) custom-call(s32[1]{0:T(128)} %bitcast.shard, bf16[3,768,1024]{2,1,0:T(8,128)(2,1)} %get-tuple-element.121.active, bf16[192,1024]{1,0:T(8,128)(2,1)} %get-tuple-element.176.attended, bf16[3,768,1024]{2,1,0:T(8,128)(2,1)} %get-tuple-element.165.d_pre, ...), custom_call_target="tpu_custom_call" | custom-call | flops 8000000000 | bytes 16000000 | tf_op jit(solution)/shard_map/project/pallas_call | solution.py:441
  164.8 2.6 collective-permute-done.14
  167.4 1.7 collective-permute-done.15
  169.1 1.1 add_convert_fusion.3
  170.2 1.0 maximum_select_fusion.4
  171.2 2.4 add_convert_fusion.2
  173.7 1.0 maximum_select_fusion.3
  174.7 1.6 copy.66.tokens
  177.7 3.7 %constant_dynamic-slice_fusion.1.cot = bf16[3072,192]{1,0:T(8,128)(2,1)} fusion(bf16[3072,768]{1,0:T(8,128)(2,1)} %cot_hbm.5, s32[]{:T(128)S(6)} %select_n.204), kind=kLoop, calls=%fused_computation.39 | loop fusion | bytes 2359300 | tf_op jit(solution)/shard_map/dynamic_slice | solution.py:636
  181.5 1.6 collective-permute-start.21
  183.2 1.8 collective-permute-start.18
  185.0 2.0 collective-permute-start.20
  187.0 10.0 %project.5 = (bf16[2,400,1024]{2,1,0:T(8,128)(2,1)}, bf16[2,400,1024]{2,1,0:T(8,128)(2,1)}, f32[768,128]{1,0:T(8,128)}) custom-call(s32[1]{0:T(128)} %bitcast.shard, bf16[3,768,1024]{2,1,0:T(8,128)(2,1)} %get-tuple-element.121.active, bf16[192,1024]{1,0:T(8,128)(2,1)} %get-tuple-element.191.attended, bf16[3,768,1024]{2,1,0:T(8,128)(2,1)} %get-tuple-element.165.d_pre, ...), custom_call_target="tpu_custom_call" | custom-call | flops 8000000000 | bytes 16000000 | tf_op jit(solution)/shard_map/project/pallas_call | solution.py:441
  197.0 9.5 %collective-permute-done.20 = bf16[192,768]{1,0:T(8,128)(2,1)} collective-permute-done((bf16[192,768]{1,0:T(8,128)(2,1)}, bf16[192,768]{1,0:T(8,128)(2,1)}, u32[]{:S(2)}, u32[]{:S(2)}) %collective-permute-start.20) | collective-permute-done | bytes 294944 | tf_op jit(solution)/shard_map/ppermute | solution.py:500
  206.6 2.0 add_convert_fusion.10
  209.3 1.4 add_reduce_fusion
  211.4 1.2 add_convert_fusion
  213.4 1.3 collective-permute-start.27
  214.7 2.6 collective-permute-done.31
  217.4 1.0 add_convert_fusion.9
  218.4 14.7 %collective-permute-done.27 = f32[192]{0:T(256)S(1)} collective-permute-done((f32[192]{0:T(256)S(1)}, f32[192]{0:T(256)S(1)}, u32[]{:S(2)}, u32[]{:S(2)}) %collective-permute-start.27) | collective-permute-done | bytes 800 | tf_op jit(solution)/shard_map/ppermute | solution.py:500
  233.8 1.8 collective-permute-start.33
  235.6 3.5 %finish.3 = (bf16[3072,192]{1,0:T(8,128)(2,1)}, f32[3072,192]{1,0:T(8,128)}) custom-call(bf16[2,400,1024]{2,1,0:T(8,128)(2,1)} %get-tuple-element.188.keep, bf16[2,400,1024]{2,1,0:T(8,128)(2,1)} %collective-permute-done.16.from_core, bf16[1,400,1024]{2,1,0:T(8,128)(2,1)} %collective-permute-done.21.from_y, bf16[192,3072]{1,0:T(8,128)(2,1)} %bitcast.31, ...), custom_call_target="tpu_custom_call" | custom-call | flops 3000000000 | bytes 5000000 | tf_op jit(solution)/shard_map/finish/pallas_call | solution.py:476
  239.7 3.3 %fusion.2 = f32[768,768]{1,0:T(8,128)} fusion(bf16[384,768]{1,0:T(8,128)(2,1)} %maximum_select_fusion.3, bf16[384,768]{1,0:T(8,128)(2,1)} %collective-permute-done.18, pred[]{:T(512)S(6)} %eq.33), kind=kLoop, calls=%fused_computation.8 | loop fusion | flops 5898240 | bytes 3538945 | tf_op jit(solution)/shard_map/convert_element_type | solution.py:721
  243.0 1.9 collective-permute-start.30
  245.1 1.7 collective-permute-start.34
  246.8 1.5 add_convert_fusion.1
  248.3 0.8 collective-permute-start.24
  249.1 3.3 %fusion.1 = f32[768,768]{1,0:T(8,128)} fusion(bf16[384,768]{1,0:T(8,128)(2,1)} %maximum_select_fusion.4, bf16[384,768]{1,0:T(8,128)(2,1)} %collective-permute-done.19, pred[]{:T(512)S(6)} %eq.15), kind=kLoop, calls=%fused_computation.6 | loop fusion | flops 5898240 | bytes 3538945 | tf_op jit(solution)/shard_map/convert_element_type | solution.py:719
  254.4 0.9 copy-done.12
  255.3 3.5 %finish.4 = (bf16[3072,192]{1,0:T(8,128)(2,1)}, f32[3072,192]{1,0:T(8,128)}) custom-call(bf16[2,400,1024]{2,1,0:T(8,128)(2,1)} %get-tuple-element.204.keep, bf16[2,400,1024]{2,1,0:T(8,128)(2,1)} %copy-done.3, bf16[1,400,1024]{2,1,0:T(8,128)(2,1)} %copy-done.12, bf16[192,3072]{1,0:T(8,128)(2,1)} %bitcast.32, ...), custom_call_target="tpu_custom_call", output_to_operand_aliasing={{0}: (9, {}), {1}: (10, {})} | custom-call | flops 3000000000 | bytes 5000000 | tf_op jit(solution)/shard_map/finish/pallas_call | solution.py:476
  258.9 1.6 fusion
  260.5 1.3 slice.103
  261.8 0.9 slice.105
  262.6 3.7 %collective-permute-done.24.from_y = bf16[1,400,1024]{2,1,0:T(8,128)(2,1)S(1)} collective-permute-done((bf16[1,400,1024]{2,1,0:T(8,128)(2,1)S(1)}, bf16[1,400,1024]{2,1,0:T(8,128)(2,1)S(1)}, u32[]{:S(2)}, u32[]{:S(2)}) %collective-permute-start.24) | collective-permute-done | bytes 819232 | tf_op jit(solution)/shard_map/ppermute | solution.py:500
  266.3 0.9 copy-done.13
  267.2 3.6 %finish.5 = (bf16[3072,192]{1,0:T(8,128)(2,1)}, f32[3072,192]{1,0:T(8,128)}) custom-call(bf16[2,400,1024]{2,1,0:T(8,128)(2,1)} %get-tuple-element.201.keep, bf16[2,400,1024]{2,1,0:T(8,128)(2,1)} %collective-permute-done.23.from_core, bf16[1,400,1024]{2,1,0:T(8,128)(2,1)} %copy-done.13, ...), custom_call_target="tpu_custom_call", output_to_operand_aliasing={{0}: (9, {}), {1}: (10, {})} | custom-call | flops 3000000000 | bytes 5000000 | tf_op jit(solution)/shard_map/finish/pallas_call | solution.py:476
  270.8 3.5 %copy.69 = f32[3072,192]{0,1:T(8,128)} copy(f32[3072,192]{1,0:T(8,128)} %get-tuple-element.245) | data formatting | bytes 4718592
  274.3 1.5 copy.68
  (147 shorter events, 16.3 us)
Async XLA Ops:
  0.6 29.8 %collective-permute-start = (bf16[192,3072]{1,0:T(8,128)(2,1)}, bf16[192,3072]{1,0:T(8,128)(2,1)}, u32[]{:S(2)}, u32[]{:S(2)}) collective-permute-start(bf16[192,3072]{1,0:T(8,128)(2,1)} %bitcast.28), channel_id=1, source_target_pairs={{0,2},{1,3},{2,0},{3,1},{4,6},{5,7},{6,4},{7,5},{8,10},{9,11},{10,... | collective-permute-start | bytes 3538952 | tf_op jit(solution)/shard_map/ppermute | solution.py:500
  3.7 37.4 %collective-permute-start.1 = (bf16[192,3072]{1,0:T(8,128)(2,1)}, bf16[192,3072]{1,0:T(8,128)(2,1)}, u32[]{:S(2)}, u32[]{:S(2)}) collective-permute-start(bf16[192,3072]{1,0:T(8,128)(2,1)} %bitcast.29), channel_id=1, source_target_pairs={{0,1},{1,0},{2,3},{3,2},{4,5},{5,4},{6,7},{7,6},{8,9},{9,8},{10,11... | collective-permute-start | bytes 3538952 | tf_op jit(solution)/shard_map/ppermute | solution.py:500
  4.4 13.4 %copy-start.21 = (bf16[192,128]{1,0:T(8,128)(2,1)}, bf16[192,128]{1,0:T(8,128)(2,1)S(1)}, u32[]{:S(2)}) copy-start(bf16[192,128]{1,0:T(8,128)(2,1)S(1)} %broadcast_in_dim.40.gain_own) | copy-start | bytes 147460
  4.4 28.6 %collective-permute-start.3 = (bf16[192,128]{1,0:T(8,128)(2,1)S(1)}, bf16[192,128]{1,0:T(8,128)(2,1)S(1)}, u32[]{:S(2)}, u32[]{:S(2)}) collective-permute-start(bf16[192,128]{1,0:T(8,128)(2,1)S(1)} %broadcast_in_dim.40.gain_own), channel_id=1, source_target_pairs={{0,2},{1,3},{2,0},{3,1},{4,6},{5,7},{6,4},{7,5},{8,10},{9,11},{10,... | collective-permute-start | bytes 147464 | tf_op jit(solution)/shard_map/ppermute | solution.py:500
  4.6 36.5 %collective-permute-start.4 = (bf16[192,128]{1,0:T(8,128)(2,1)S(1)}, bf16[192,128]{1,0:T(8,128)(2,1)S(1)}, u32[]{:S(2)}, u32[]{:S(2)}) collective-permute-start(bf16[192,128]{1,0:T(8,128)(2,1)S(1)} %broadcast_in_dim.40.gain_own), channel_id=1, source_target_pairs={{0,1},{1,0},{2,3},{3,2},{4,5},{5,4},{6,7},{7,6},{8,9},{9,8},{10,11... | collective-permute-start | bytes 147464 | tf_op jit(solution)/shard_map/ppermute | solution.py:500
  7.7 23.4 %copy-start.20 = (s32[3,1024]{1,0:T(4,128)S(1)}, s32[3,1024]{1,0:T(4,128)}, u32[]{:S(2)}) copy-start(s32[3,1024]{1,0:T(4,128)} %param.13) | copy-start | bytes 36868
  7.7 25.8 %copy-start.30 = (s32[4]{0:T(128)S(1)}, s32[4]{0:T(128)}, u32[]{:S(2)}) copy-start(s32[4]{0:T(128)} %constant.180.clone) | copy-start | bytes 52
  7.7 26.3 %copy-start.5 = (bf16[768,768]{1,0:T(8,128)(2,1)S(1)}, bf16[768,768]{1,0:T(8,128)(2,1)}, u32[]{:S(2)}) copy-start(bf16[768,768]{1,0:T(8,128)(2,1)} %down.1) | copy-start | bytes 3538948
  17.8 17.7 %copy-start.16 = (bf16[192,768]{1,0:T(8,128)(2,1)S(1)}, bf16[192,768]{1,0:T(8,128)(2,1)}, u32[]{:S(2)}) copy-start(bf16[192,768]{1,0:T(8,128)(2,1)} %attn.1) | copy-start | bytes 884740
  30.5 10.6 %collective-permute-start.2 = (bf16[192,3072]{1,0:T(8,128)(2,1)}, bf16[192,3072]{1,0:T(8,128)(2,1)}, u32[]{:S(2)}, u32[]{:S(2)}) collective-permute-start(bf16[192,3072]{1,0:T(8,128)(2,1)} %collective-permute-done.flip_y), channel_id=1, source_target_pairs={{0,1},{1,0},{2,3},{3,2},{4,5},{5,4},{6,7},{7,6},{8,9},{9,8},{10,11... | collective-permute-start | bytes 3538952 | tf_op jit(solution)/shard_map/ppermute | solution.py:500
  33.0 3.5 %copy-start.26 = (bf16[192,128]{1,0:T(8,128)(2,1)}, bf16[192,128]{1,0:T(8,128)(2,1)S(1)}, u32[]{:S(2)}) copy-start(bf16[192,128]{1,0:T(8,128)(2,1)S(1)} %collective-permute-done.3.gain_y) | copy-start | bytes 147460
  33.0 8.1 %collective-permute-start.5 = (bf16[192,128]{1,0:T(8,128)(2,1)S(1)}, bf16[192,128]{1,0:T(8,128)(2,1)S(1)}, u32[]{:S(2)}, u32[]{:S(2)}) collective-permute-start(bf16[192,128]{1,0:T(8,128)(2,1)S(1)} %collective-permute-done.3.gain_y), channel_id=1, source_target_pairs={{0,1},{1,0},{2,3},{3,2},{4,5},{5,4},{6,7},{7,6},{8,9},{9,8},{10,11... | collective-permute-start | bytes 147464 | tf_op jit(solution)/shard_map/ppermute | solution.py:500
  34.0 2.4 copy-start.6
  35.5 2.4 copy-start.23
  35.5 3.3 %copy-start.25 = (bf16[2,192]{1,0:T(2,128)(2,1)S(1)}, bf16[2,192]{1,0:T(2,128)(2,1)}, u32[]{:S(2)}) copy-start(bf16[2,192]{1,0:T(2,128)(2,1)} %param.16) | copy-start | bytes 2308
  36.4 3.3 %copy-start.11 = (bf16[768,3,192]{0,2,1:T(8,128)(2,1)S(1)}, bf16[768,3,192]{0,2,1:T(8,128)(2,1)}, u32[]{:S(2)}) copy-start(bf16[768,3,192]{0,2,1:T(8,128)(2,1)} %param.15) | copy-start | bytes 2654212
  68.3 1.5 copy-start.8
  69.8 23.0 %collective-permute-start.6 = (bf16[384,768]{1,0:T(8,128)(2,1)S(1)}, bf16[384,768]{1,0:T(8,128)(2,1)}, u32[]{:S(2)}, u32[]{:S(2)}) collective-permute-start(bf16[384,768]{1,0:T(8,128)(2,1)S(1)} %constant_dynamic-slice_fusion.7), channel_id=1, source_target_pairs={{0,4},{4,0},{8,12},{12,8},{16,20},{20,16},{24,28},{28,24},{1,5},{5... | collective-permute-start | bytes 1769480 | tf_op jit(solution)/shard_map/ppermute | solution.py:500
  71.6 21.2 %collective-permute-start.7 = (bf16[384,768]{1,0:T(8,128)(2,1)S(1)}, bf16[384,768]{1,0:T(8,128)(2,1)}, u32[]{:S(2)}, u32[]{:S(2)}) collective-permute-start(bf16[384,768]{1,0:T(8,128)(2,1)S(1)} %constant_dynamic-slice_fusion.6), channel_id=1, source_target_pairs={{0,8},{4,12},{8,0},{12,4},{16,24},{20,28},{24,16},{28,20},{1,9},{5... | collective-permute-start | bytes 1769480 | tf_op jit(solution)/shard_map/ppermute | solution.py:500
  73.2 19.6 %copy-start.9 = (bf16[768,768]{1,0:T(8,128)(2,1)S(1)}, bf16[768,768]{1,0:T(8,128)(2,1)}, u32[]{:S(2)}) copy-start(bf16[768,768]{1,0:T(8,128)(2,1)} %get-tuple-element.124) | copy-start | bytes 3538948
  94.5 22.0 %collective-permute-start.8 = (bf16[192,768]{1,0:T(8,128)(2,1)S(1)}, bf16[192,768]{1,0:T(8,128)(2,1)S(1)}, u32[]{:S(2)}, u32[]{:S(2)}) collective-permute-start(bf16[192,768]{1,0:T(8,128)(2,1)S(1)} %get-tuple-element.142), channel_id=1, source_target_pairs={{0,8},{4,12},{8,0},{12,4},{16,24},{20,28},{24,16},{28,20},{1,9},{5... | collective-permute-start | bytes 884744 | tf_op jit(solution)/shard_map/ppermute | solution.py:500
  95.0 21.5 %collective-permute-start.9 = (bf16[192,768]{1,0:T(8,128)(2,1)S(1)}, bf16[192,768]{1,0:T(8,128)(2,1)S(1)}, u32[]{:S(2)}, u32[]{:S(2)}) collective-permute-start(bf16[192,768]{1,0:T(8,128)(2,1)S(1)} %get-tuple-element.143), channel_id=1, source_target_pairs={{0,16},{4,20},{8,24},{12,28},{16,0},{20,4},{24,8},{28,12},{1,17},{... | collective-permute-start | bytes 884744 | tf_op jit(solution)/shard_map/ppermute | solution.py:500
  116.6 20.2 %collective-permute-start.10 = (bf16[96,768]{1,0:T(8,128)(2,1)S(1)}, bf16[96,768]{1,0:T(8,128)(2,1)S(1)}, u32[]{:S(2)}, u32[]{:S(2)}) collective-permute-start(bf16[96,768]{1,0:T(8,128)(2,1)S(1)} %add_convert_fusion.17), channel_id=1, source_target_pairs={{0,16},{4,20},{8,24},{12,28},{16,0},{20,4},{24,8},{28,12},{1,17},{... | collective-permute-start | bytes 442376 | tf_op jit(solution)/shard_map/ppermute | solution.py:500
  117.4 19.4 %collective-permute-start.11 = (bf16[96,768]{1,0:T(8,128)(2,1)S(1)}, bf16[96,768]{1,0:T(8,128)(2,1)S(1)}, u32[]{:S(2)}, u32[]{:S(2)}) collective-permute-start(bf16[96,768]{1,0:T(8,128)(2,1)S(1)} %add_convert_fusion.16), channel_id=1, source_target_pairs={{0,4},{4,0},{8,12},{12,8},{16,20},{20,16},{24,28},{28,24},{1,5},{5... | collective-permute-start | bytes 442376 | tf_op jit(solution)/shard_map/ppermute | solution.py:500
  138.1 14.0 %collective-permute-start.12 = (bf16[96,768]{1,0:T(8,128)(2,1)S(1)}, bf16[96,768]{1,0:T(8,128)(2,1)S(1)}, u32[]{:S(2)}, u32[]{:S(2)}) collective-permute-start(bf16[96,768]{1,0:T(8,128)(2,1)S(1)} %add_convert_fusion.14), channel_id=1, source_target_pairs={{0,16},{4,20},{8,24},{12,28},{16,0},{20,4},{24,8},{28,12},{1,17},{... | collective-permute-start | bytes 442376 | tf_op jit(solution)/shard_map/ppermute | solution.py:500
  140.1 12.1 %collective-permute-start.13 = (bf16[96,768]{1,0:T(8,128)(2,1)S(1)}, bf16[96,768]{1,0:T(8,128)(2,1)S(1)}, u32[]{:S(2)}, u32[]{:S(2)}) collective-permute-start(bf16[96,768]{1,0:T(8,128)(2,1)S(1)} %add_convert_fusion.12), channel_id=1, source_target_pairs={{0,4},{4,0},{8,12},{12,8},{16,20},{20,16},{24,28},{28,24},{1,5},{5... | collective-permute-start | bytes 442376 | tf_op jit(solution)/shard_map/ppermute | solution.py:500
  152.3 16.8 %collective-permute-start.16 = (bf16[2,400,1024]{2,1,0:T(8,128)(2,1)}, bf16[2,400,1024]{2,1,0:T(8,128)(2,1)}, u32[]{:S(2)}, u32[]{:S(2)}) collective-permute-start(bf16[2,400,1024]{2,1,0:T(8,128)(2,1)} %get-tuple-element.183), channel_id=1, source_target_pairs={{0,1},{1,0},{2,3},{3,2},{4,5},{5,4},{6,7},{7,6},{8,9},{9,8},{10,11... | collective-permute-start | bytes 4915208 | tf_op jit(solution)/shard_map/ppermute | solution.py:500
  152.4 16.8 %copy-start.7 = (bf16[768,768]{1,0:T(8,128)(2,1)S(1)}, bf16[768,768]{1,0:T(8,128)(2,1)}, u32[]{:S(2)}) copy-start(bf16[768,768]{1,0:T(8,128)(2,1)} %get-tuple-element.163) | copy-start | bytes 3538948
  152.4 16.7 %collective-permute-start.17 = (bf16[384,768]{1,0:T(8,128)(2,1)S(1)}, bf16[384,768]{1,0:T(8,128)(2,1)S(1)}, u32[]{:S(2)}, u32[]{:S(2)}) collective-permute-start(bf16[384,768]{1,0:T(8,128)(2,1)S(1)} %constant_dynamic-slice_fusion.3), channel_id=1, source_target_pairs={{0,4},{4,0},{8,12},{12,8},{16,20},{20,16},{24,28},{28,24},{1,5},{5... | collective-permute-start | bytes 1769480 | tf_op jit(solution)/shard_map/ppermute | solution.py:500
  152.5 14.9 %collective-permute-start.14 = (bf16[192,768]{1,0:T(8,128)(2,1)S(1)}, bf16[192,768]{1,0:T(8,128)(2,1)S(1)}, u32[]{:S(2)}, u32[]{:S(2)}) collective-permute-start(bf16[192,768]{1,0:T(8,128)(2,1)S(1)} %maximum_select_fusion.6), channel_id=1, source_target_pairs={{0,8},{4,12},{8,0},{12,4},{16,24},{20,28},{24,16},{28,20},{1,9},{5... | collective-permute-start | bytes 884744 | tf_op jit(solution)/shard_map/ppermute | solution.py:500
  152.6 16.6 %collective-permute-start.15 = (bf16[192,768]{1,0:T(8,128)(2,1)S(1)}, bf16[192,768]{1,0:T(8,128)(2,1)S(1)}, u32[]{:S(2)}, u32[]{:S(2)}) collective-permute-start(bf16[192,768]{1,0:T(8,128)(2,1)S(1)} %maximum_select_fusion.7), channel_id=1, source_target_pairs={{0,16},{4,20},{8,24},{12,28},{16,0},{20,4},{24,8},{28,12},{1,17},{... | collective-permute-start | bytes 884744 | tf_op jit(solution)/shard_map/ppermute | solution.py:500
  164.8 6.4 %copy-start.14 = (bf16[2,400,1024]{2,1,0:T(8,128)(2,1)S(1)}, bf16[2,400,1024]{2,1,0:T(8,128)(2,1)}, u32[]{:S(2)}) copy-start(bf16[2,400,1024]{2,1,0:T(8,128)(2,1)} %get-tuple-element.188.keep) | copy-start | bytes 4915204
  171.2 3.5 %copy-start.1 = (bf16[3072,192]{0,1:T(8,128)(2,1)S(1)}, bf16[3072,192]{0,1:T(8,128)(2,1)}, u32[]{:S(2)}) copy-start(bf16[3072,192]{0,1:T(8,128)(2,1)} %param.12) | copy-start | bytes 3538948
  174.7 1.6 copy-start.24
  174.7 2.4 copy-start.29
  174.7 2.9 %copy-start.22 = (f32[8,768]{1,0:T(8,128)S(1)}, f32[8,768]{1,0:T(8,128)}, u32[]{:S(2)}) copy-start(f32[8,768]{1,0:T(8,128)} %get-tuple-element.220) | copy-start | bytes 73732
  174.7 31.9 %collective-permute-start.22 = (bf16[2,400,1024]{2,1,0:T(8,128)(2,1)}, bf16[2,400,1024]{2,1,0:T(8,128)(2,1)S(1)}, u32[]{:S(2)}, u32[]{:S(2)}) collective-permute-start(bf16[2,400,1024]{2,1,0:T(8,128)(2,1)} %get-tuple-element.200), channel_id=1, source_target_pairs={{0,1},{1,0},{2,3},{3,2},{4,5},{5,4},{6,7},{7,6},{8,9},{9,8},{10,11... | collective-permute-start | bytes 4915208 | tf_op jit(solution)/shard_map/ppermute | solution.py:500
  177.6 3.7 %copy-start.15 = (f32[768,128]{1,0:T(8,128)S(1)}, f32[768,128]{1,0:T(8,128)}, u32[]{:S(2)}) copy-start(f32[768,128]{1,0:T(8,128)} %get-tuple-element.219) | copy-start | bytes 1179652
  177.7 5.4 %copy-start.17 = (f32[384,128]{1,0:T(8,128)S(1)}, f32[384,128]{1,0:T(8,128)}, u32[]{:S(2)}) copy-start(f32[384,128]{1,0:T(8,128)} %get-tuple-element.216) | copy-start | bytes 589828
  177.7 5.4 %copy-start.18 = (f32[384,128]{1,0:T(8,128)S(1)}, f32[384,128]{1,0:T(8,128)}, u32[]{:S(2)}) copy-start(f32[384,128]{1,0:T(8,128)} %get-tuple-element.217) | copy-start | bytes 589828
  177.7 5.4 %copy-start.19 = (f32[384,128]{1,0:T(8,128)S(1)}, f32[384,128]{1,0:T(8,128)}, u32[]{:S(2)}) copy-start(f32[384,128]{1,0:T(8,128)} %get-tuple-element.218) | copy-start | bytes 589828
  181.5 25.0 %collective-permute-start.21 = (bf16[1,400,1024]{2,1,0:T(8,128)(2,1)}, bf16[1,400,1024]{2,1,0:T(8,128)(2,1)}, u32[]{:S(2)}, u32[]{:S(2)}) collective-permute-start(bf16[1,400,1024]{2,1,0:T(8,128)(2,1)} %add_convert_fusion.2), channel_id=1, source_target_pairs={{0,2},{1,3},{2,0},{3,1},{4,6},{5,7},{6,4},{7,5},{8,10},{9,11},{10,... | collective-permute-start | bytes 2457608 | tf_op jit(solution)/shard_map/ppermute | solution.py:500
  183.2 23.3 %collective-permute-start.18 = (bf16[384,768]{1,0:T(8,128)(2,1)}, bf16[384,768]{1,0:T(8,128)(2,1)}, u32[]{:S(2)}, u32[]{:S(2)}) collective-permute-start(bf16[384,768]{1,0:T(8,128)(2,1)} %maximum_select_fusion.3), channel_id=1, source_target_pairs={{0,4},{4,0},{8,12},{12,8},{16,20},{20,16},{24,28},{28,24},{1,5},{5... | collective-permute-start | bytes 1769480 | tf_op jit(solution)/shard_map/ppermute | solution.py:500
  185.0 21.5 %collective-permute-start.19 = (bf16[384,768]{1,0:T(8,128)(2,1)}, bf16[384,768]{1,0:T(8,128)(2,1)}, u32[]{:S(2)}, u32[]{:S(2)}) collective-permute-start(bf16[384,768]{1,0:T(8,128)(2,1)} %maximum_select_fusion.4), channel_id=1, source_target_pairs={{0,8},{4,12},{8,0},{12,4},{16,24},{20,28},{24,16},{28,20},{1,9},{5... | collective-permute-start | bytes 1769480 | tf_op jit(solution)/shard_map/ppermute | solution.py:500
  185.0 21.5 %collective-permute-start.20 = (bf16[192,768]{1,0:T(8,128)(2,1)}, bf16[192,768]{1,0:T(8,128)(2,1)}, u32[]{:S(2)}, u32[]{:S(2)}) collective-permute-start(bf16[192,768]{1,0:T(8,128)(2,1)} %get-tuple-element.198), channel_id=1, source_target_pairs={{0,8},{4,12},{8,0},{12,4},{16,24},{20,28},{24,16},{28,20},{1,9},{5... | collective-permute-start | bytes 884744 | tf_op jit(solution)/shard_map/ppermute | solution.py:500
  197.0 14.4 %copy-start.2 = (bf16[2,400,1024]{2,1,0:T(8,128)(2,1)S(1)}, bf16[2,400,1024]{2,1,0:T(8,128)(2,1)}, u32[]{:S(2)}) copy-start(bf16[2,400,1024]{2,1,0:T(8,128)(2,1)} %get-tuple-element.204.keep) | copy-start | bytes 4915204
  206.5 6.1 %copy-start.3 = (bf16[2,400,1024]{2,1,0:T(8,128)(2,1)}, bf16[2,400,1024]{2,1,0:T(8,128)(2,1)S(1)}, u32[]{:S(2)}) copy-start(bf16[2,400,1024]{2,1,0:T(8,128)(2,1)S(1)} %collective-permute-done.22.from_core) | copy-start | bytes 4915204
  208.6 8.8 %collective-permute-start.31 = (bf16[96,768]{1,0:T(8,128)(2,1)}, bf16[96,768]{1,0:T(8,128)(2,1)S(1)}, u32[]{:S(2)}, u32[]{:S(2)}) collective-permute-start(bf16[96,768]{1,0:T(8,128)(2,1)} %add_convert_fusion.10), channel_id=1, source_target_pairs={{0,16},{4,20},{8,24},{12,28},{16,0},{20,4},{24,8},{28,12},{1,17},{... | collective-permute-start | bytes 442376 | tf_op jit(solution)/shard_map/ppermute | solution.py:500
  210.8 6.6 %copy-start.10 = (bf16[192,768]{1,0:T(8,128)(2,1)S(1)}, bf16[192,768]{1,0:T(8,128)(2,1)}, u32[]{:S(2)}) copy-start(bf16[192,768]{1,0:T(8,128)(2,1)} %get-tuple-element.258) | copy-start | bytes 884740
  210.8 2.5 collective-permute-start.26
  210.9 35.9 %collective-permute-start.23 = (bf16[2,400,1024]{2,1,0:T(8,128)(2,1)}, bf16[2,400,1024]{2,1,0:T(8,128)(2,1)}, u32[]{:S(2)}, u32[]{:S(2)}) collective-permute-start(bf16[2,400,1024]{2,1,0:T(8,128)(2,1)} %get-tuple-element.202), channel_id=1, source_target_pairs={{0,1},{1,0},{2,3},{3,2},{4,5},{5,4},{6,7},{7,6},{8,9},{9,8},{10,11... | collective-permute-start | bytes 4915208 | tf_op jit(solution)/shard_map/ppermute | solution.py:500
  212.6 41.8 %collective-permute-start.25 = (bf16[1,400,1024]{2,1,0:T(8,128)(2,1)}, bf16[1,400,1024]{2,1,0:T(8,128)(2,1)S(1)}, u32[]{:S(2)}, u32[]{:S(2)}) collective-permute-start(bf16[1,400,1024]{2,1,0:T(8,128)(2,1)} %add_convert_fusion), channel_id=1, source_target_pairs={{0,2},{1,3},{2,0},{3,1},{4,6},{5,7},{6,4},{7,5},{8,10},{9,11},{10,... | collective-permute-start | bytes 2457608 | tf_op jit(solution)/shard_map/ppermute | solution.py:500
  213.4 19.7 %collective-permute-start.27 = (f32[192]{0:T(256)S(1)}, f32[192]{0:T(256)S(1)}, u32[]{:S(2)}, u32[]{:S(2)}) collective-permute-start(f32[192]{0:T(256)S(1)} %bitcast.54), channel_id=1, source_target_pairs={{0,2},{1,3},{2,0},{3,1},{4,6},{5,7},{6,4},{7,5},{8,10},{9,11},{10,... | collective-permute-start | bytes 2312 | tf_op jit(solution)/shard_map/ppermute | solution.py:500
  218.3 15.4 %collective-permute-start.32 = (bf16[96,768]{1,0:T(8,128)(2,1)S(1)}, bf16[96,768]{1,0:T(8,128)(2,1)S(1)}, u32[]{:S(2)}, u32[]{:S(2)}) collective-permute-start(bf16[96,768]{1,0:T(8,128)(2,1)S(1)} %add_convert_fusion.9), channel_id=1, source_target_pairs={{0,16},{4,20},{8,24},{12,28},{16,0},{20,4},{24,8},{28,12},{1,17},{... | collective-permute-start | bytes 442376 | tf_op jit(solution)/shard_map/ppermute | solution.py:500
  233.2 5.9 %collective-permute-start.28 = (f32[1536]{0:T(1024)S(1)}, f32[1536]{0:T(1024)S(1)}, u32[]{:S(2)}, u32[]{:S(2)}) collective-permute-start(f32[1536]{0:T(1024)S(1)} %concatenate.65), channel_id=1, source_target_pairs={{0,4},{4,0},{8,12},{12,8},{16,20},{20,16},{24,28},{28,24},{1,5},{5... | collective-permute-start | bytes 18440 | tf_op jit(solution)/shard_map/ppermute | solution.py:500
  233.8 11.1 %collective-permute-start.33 = (bf16[192,768]{1,0:T(8,128)(2,1)S(1)}, bf16[192,768]{1,0:T(8,128)(2,1)S(1)}, u32[]{:S(2)}, u32[]{:S(2)}) collective-permute-start(bf16[192,768]{1,0:T(8,128)(2,1)S(1)} %maximum_select_fusion.8), channel_id=1, source_target_pairs={{0,8},{4,12},{8,0},{12,4},{16,24},{20,28},{24,16},{28,20},{1,9},{5... | collective-permute-start | bytes 884744 | tf_op jit(solution)/shard_map/ppermute | solution.py:500
  239.1 7.7 %copy-start.4 = (bf16[2,400,1024]{2,1,0:T(8,128)(2,1)S(1)}, bf16[2,400,1024]{2,1,0:T(8,128)(2,1)}, u32[]{:S(2)}) copy-start(bf16[2,400,1024]{2,1,0:T(8,128)(2,1)} %get-tuple-element.201.keep) | copy-start | bytes 4915204
  239.1 3.8 %collective-permute-start.29 = (f32[1536]{0:T(1024)S(1)}, f32[1536]{0:T(1024)S(1)}, u32[]{:S(2)}, u32[]{:S(2)}) collective-permute-start(f32[1536]{0:T(1024)S(1)} %add.213), channel_id=1, source_target_pairs={{0,8},{4,12},{8,0},{12,4},{16,24},{20,28},{24,16},{28,20},{1,9},{5... | collective-permute-start | bytes 18440 | tf_op jit(solution)/shard_map/ppermute | solution.py:500
  243.0 9.4 %collective-permute-start.30 = (f32[1536]{0:T(1024)S(1)}, f32[1536]{0:T(1024)S(1)}, u32[]{:S(2)}, u32[]{:S(2)}) collective-permute-start(f32[1536]{0:T(1024)S(1)} %add.214), channel_id=1, source_target_pairs={{0,16},{4,20},{8,24},{12,28},{16,0},{20,4},{24,8},{28,12},{1,17},{... | collective-permute-start | bytes 18440 | tf_op jit(solution)/shard_map/ppermute | solution.py:500
  245.1 13.8 %collective-permute-start.34 = (bf16[384,768]{1,0:T(8,128)(2,1)S(1)}, bf16[384,768]{1,0:T(8,128)(2,1)}, u32[]{:S(2)}, u32[]{:S(2)}) collective-permute-start(bf16[384,768]{1,0:T(8,128)(2,1)S(1)} %maximum_select_fusion.5), channel_id=1, source_target_pairs={{0,4},{4,0},{8,12},{12,8},{16,20},{20,16},{24,28},{28,24},{1,5},{5... | collective-permute-start | bytes 1769480 | tf_op jit(solution)/shard_map/ppermute | solution.py:500
  248.3 18.0 %collective-permute-start.24 = (bf16[1,400,1024]{2,1,0:T(8,128)(2,1)S(1)}, bf16[1,400,1024]{2,1,0:T(8,128)(2,1)S(1)}, u32[]{:S(2)}, u32[]{:S(2)}) collective-permute-start(bf16[1,400,1024]{2,1,0:T(8,128)(2,1)S(1)} %add_convert_fusion.1), channel_id=1, source_target_pairs={{0,2},{1,3},{2,0},{3,1},{4,6},{5,7},{6,4},{7,5},{8,10},{9,11},{10,... | collective-permute-start | bytes 2457608 | tf_op jit(solution)/shard_map/ppermute | solution.py:500
  254.4 0.9 copy-start.12
  266.3 0.9 copy-start.13
  270.8 3.5 %copy-start = (bf16[3072,192]{1,0:T(8,128)(2,1)S(1)}, bf16[3072,192]{1,0:T(8,128)(2,1)}, u32[]{:S(2)}) copy-start(bf16[3072,192]{1,0:T(8,128)(2,1)} %get-tuple-element.244) | copy-start | bytes 3538948
  (2 other events, 1.2 us)
where the time goes:
time: 278 us; the launch traced here: 276 us
  Pallas kernels  135 us (49%)
  waiting for transfers between devices  47.5 us (17%)
  starting transfers between devices  34 us (12%)
  local copies, waits for them, and re-layouts  31 us (11%)
  other arithmetic  26.7 us (10%)
    pallas_call x3, Pallas kernels, attention_call(): pl.pallas_call(functools.partial(attention_kernel, last, seq), grid_spec=...  58 us
    ppermute x35, waiting for transfers between devices, flip(): return lax.ppermute(value, axis, [(i, i ^ bit) for i in range(size)])  47.5 us
    ppermute x35, starting transfers between devices, flip(): return lax.ppermute(value, axis, [(i, i ^ bit) for i in range(size)])  34 us
    pallas_call x3, Pallas kernels, project_call(): pl.pallas_call(project_kernel, grid_spec=grid_spec, out_shape=[jax.ShapeD...  30 us
    pallas_call x1, Pallas kernels, mlp_call(): pl.pallas_call(mlp_kernel, grid_spec=grid_spec, out_shape=[jax.ShapeDtype...  26.6 us
    unnamed x68, local copies, waits for them, and re-layouts  13.1 us
    pallas_call x3, Pallas kernels, finish_call(): pl.pallas_call(finish_kernel, grid=(steps,), in_specs=[packed, packed, pa...  10.7 us
    pallas_call x1, Pallas kernels, early_call(): pl.pallas_call(early_kernel, grid=(tokens // block,), in_specs=[pl.BlockS...  10.1 us
  transfers between devices with their start and end apart: 35, of which 7 were waited for; matrix products, arithmetic and copies ran while one was open for 14% of the time, Pallas kernels for 38%

commit v1 on v0

--- a/solution.py
+++ b/solution.py
@@ -35,23 +35,24 @@
 
 
 def cost(microseconds, nbytes):
-    return pl.CostEstimate(flops=int(microseconds * 1e9), bytes_accessed=nbytes, transcendentals=0)
-
-
-def early_kernel(cot, down, attn, d_act, d_att, bias_sum):
+    return pl.CostEstimate(flops=int(microseconds * 1e3), bytes_accessed=nbytes // 1000, transcendentals=0)
+
+
+def early_kernel(cot, down, attn, pick, d_act, d_att, cot_own, bias_sum):
     rows = cot[...]
     d_act[...] = dot(down[...], rows, NT).astype(BF16)
     d_att[...] = dot(attn[...], rows, NT).astype(BF16)
+    own = dot(pick[...], rows, NT)
+    cot_own[...] = own.astype(BF16)
 
     @pl.when(pl.program_id(0) == 0)
     def _():
         bias_sum[...] = jnp.zeros_like(bias_sum)
 
-    wide = rows.astype(F32)
-    bias_sum[...] += jnp.sum(wide.reshape(wide.shape[0] // 8, 8, wide.shape[1]), axis=0)
-
-
-def early_call(cot, down, attn, block=512):
+    bias_sum[...] += fold_lanes(own)
+
+
+def early_call(cot, down, attn, pick, block=512):
     tokens, width = cot.shape
     seqs = tokens // LEN
     hidden, part = down.shape[0], attn.shape[0]
@@ -65,32 +66,23 @@
             pl.BlockSpec((block, width), lambda i: (i, 0)),
             pl.BlockSpec((hidden, width), fixed),
             pl.BlockSpec((part, width), fixed),
+            pl.BlockSpec((part, width), fixed),
         ],
         out_specs=[
             pl.BlockSpec((None, hidden, block), by_seq),
             pl.BlockSpec((None, part, block), by_seq),
-            pl.BlockSpec((8, width), fixed),
+            pl.BlockSpec((part, block), lambda i: (0, i)),
+            pl.BlockSpec((part, 128), fixed),
         ],
         out_shape=[
             jax.ShapeDtypeStruct((seqs, hidden, LEN), BF16),
             jax.ShapeDtypeStruct((seqs, part, LEN), BF16),
-            jax.ShapeDtypeStruct((8, width), F32),
+            jax.ShapeDtypeStruct((part, tokens), BF16),
+            jax.ShapeDtypeStruct((part, 128), F32),
         ],
         cost_estimate=cost(10, 12_000_000),
         name="early",
-    )(cot, down, attn)
-
-
-def split_store(side, low, high, keep, send):
-    @pl.when(side == 0)
-    def _():
-        keep[...] = low[...].astype(BF16)
-        send[...] = high[...].astype(BF16)
-
-    @pl.when(side != 0)
-    def _():
-        keep[...] = high[...].astype(BF16)
-        send[...] = low[...].astype(BF16)
+    )(cot, down, attn, pick)
 
 
 def mlp_kernel(
@@ -129,9 +121,16 @@
 
     c0 = 0.7978845608028654
     c1 = 0.044715 * c0
+    def lift(start):
+        here = slice(start, start + 256)
+        return dot(up_t[here, :], normed[...]) + up_bias[here, :]
+
+    ahead = lift(0)
     for start in range(0, up_t.shape[0], 256):
         here = slice(start, start + 256)
-        pre = dot(up_t[here, :], normed[...]) + up_bias[here, :]
+        pre = ahead
+        if start + 256 < up_t.shape[0]:
+            ahead = lift(start + 256)
         square = pre * pre
         half = 0.5 * jnp.tanh(pre * (c0 + c1 * square)) + 0.5
         act = (pre * half).astype(BF16)
@@ -202,7 +201,7 @@
     if seq:
         before_hbm, rest = rest[0], rest[1:]
     (
-        attended, d_mixed, gain_sum, grads, qkv, qx, kx, vn, kt, vt, es, ps, oa, dqa, dka, dva, cot, before, cot_sem,
+        attended, d_mixed, gain_sum, norm_row, grads, qkv, qx, kx, vn, kt, vt, es, ps, oa, dqa, dka, dva, cot, before, cot_sem,
         before_sem,
     ) = rest
     part = attended.shape[0]
@@ -310,7 +309,11 @@
     ):
         if seq:
             value = value + before[rows, :]
+        if last and rows.start == 0:
+            norm_row[...] = jnp.sum(value * mixed_t[...].astype(F32), axis=0, keepdims=True)
         grads[rows, :] = value.astype(grads.dtype)
+    if not last:
+        norm_row[...] = jnp.zeros_like(norm_row)
 
 
 def attention_call(first, count, normed, mixed_t, d_att, mask_q, mask_k, gains, cot, before, seq, last):
@@ -336,6 +339,7 @@
             pl.BlockSpec((part, LEN), once),
             pl.BlockSpec((3 * part, LEN), once),
             pl.BlockSpec((2 * part, 128), once),
+            pl.BlockSpec((1, width), once),
             pl.BlockSpec((4 * part, width), once),
         ],
         scratch_shapes=[
@@ -364,6 +368,7 @@
             jax.ShapeDtypeStruct((part, LEN), BF16),
             jax.ShapeDtypeStruct((3 * part, LEN), BF16),
             jax.ShapeDtypeStruct((2 * part, 128), F32),
+            jax.ShapeDtypeStruct((1, width), F32),
             jax.ShapeDtypeStruct((4 * part, width), BF16 if last else F32),
         ],
         cost_estimate=cost(18, 5_000_000),
@@ -372,7 +377,7 @@
 
 
 def project_kernel(
-    shard, active, attended, d_pre, d_mixed, normed, down_t, attn_t, up, mixed, gain, keep, send, gain_sum
+    shard, active, attended, d_pre, d_mixed, normed, down_t, attn_t, up, mixed, gain, keep, send
 ):
     me = shard[0]
     part = attended.shape[0]
@@ -401,12 +406,6 @@
         def _():
             send[slot, :part, :] = out[rows].astype(BF16)
             send[slot, part : 2 * part, :] = grad[rows].astype(BF16)
-
-    @pl.when(pl.program_id(0) == 0)
-    def _():
-        gain_sum[...] = jnp.zeros_like(gain_sum)
-
-    gain_sum[...] += fold_lanes(product)
 
 
 def project_call(shard, active, attended, d_pre, d_mixed, normed, down_t, attn_t, up, mixed, gain, seq, block=256):
@@ -435,7 +434,6 @@
         out_specs=[
             pl.BlockSpec((2, rows, block), lambda i, *_: (0, 0, i)),
             pl.BlockSpec((2, rows, block), lambda i, *_: (0, 0, i)),
-            pl.BlockSpec((width, 128), fixed),
         ],
     )
     return pl.pallas_call(
@@ -444,56 +442,55 @@
         out_shape=[
             jax.ShapeDtypeStruct((2, rows, LEN), BF16),
             jax.ShapeDtypeStruct((2, rows, LEN), BF16),
-            jax.ShapeDtypeStruct((width, 128), F32),
         ],
         cost_estimate=cost(8, 16_000_000),
         name="project",
     )(shard, active, attended, d_pre, d_mixed, normed, down_t, attn_t, up, mixed, gain)
 
 
-def finish_kernel(keep, from_core, from_y, own_t, tokens, cot, stats, gain, bias, *rest):
+def finish_kernel(keep, from_core, from_y, own_t, cot, stats, gain, bias, *rest):
     block_out, token_grad = rest[-2:]
     part = own_t.shape[0]
     inv_width = 0.25 / part
     total = keep[...].astype(F32) + from_core[...].astype(F32) + from_y[...].astype(F32)
-    block_out[...] = (tokens[...].astype(F32) + total[:part].T + bias[...]).astype(BF16)
+    own = own_t[...].astype(F32)
+    block_out[...] = (own + total[:part] + bias[...]).astype(BF16)
     grad = total[part : 2 * part]
     sums = total[2 * part :]
     mean = stats[0:1, :]
     scale = stats[1:2, :]
-    hat = (own_t[...].astype(F32) - mean) * scale
+    hat = (own - mean) * scale
     inner = grad * gain[...] - (sums[0:1] + sums[1:2]) * inv_width - hat * ((sums[2:3] + sums[3:4]) * inv_width)
-    token_grad[...] = cot[...].astype(F32) + (inner * scale).T
-
-
-def finish_call(keep, from_core, from_y, own_t, tokens, cot, stats, gain, bias, before, seq, block=512):
-    part = own_t.shape[0]
+    token_grad[...] = cot[...].astype(F32) + inner * scale
+
+
+def finish_call(keep, from_core, from_y, own_t, cot, stats, gain, bias, before, seq, block=512):
+    part, tokens = own_t.shape
     steps = LEN // block
     fixed = lambda i: (0, 0)
+    packed = pl.BlockSpec((None, 2 * part + SUM_ROWS, block), lambda i: (0, 0, i))
     ours = lambda i: (0, seq * steps + i)
-    packed = pl.BlockSpec((None, 2 * part + SUM_ROWS, block), lambda i: (0, 0, i))
-    here = pl.BlockSpec((block, part), lambda i: (seq * steps + i, 0))
+    here = pl.BlockSpec((part, block), ours)
     return pl.pallas_call(
         finish_kernel,
         grid=(steps,),
         in_specs=[
             packed, packed, packed,
-            pl.BlockSpec((part, block), ours),
             here, here,
             pl.BlockSpec((8, block), ours),
             pl.BlockSpec((part, 1), fixed),
-            pl.BlockSpec((1, part), fixed),
+            pl.BlockSpec((part, 1), fixed),
         ]
         + [ANY] * len(before),
         out_specs=[here, here],
         out_shape=[
-            jax.ShapeDtypeStruct(tokens.shape, BF16),
-            jax.ShapeDtypeStruct(tokens.shape, F32),
-        ],
-        input_output_aliases={9 + i: i for i in range(len(before))},
+            jax.ShapeDtypeStruct((part, tokens), BF16),
+            jax.ShapeDtypeStruct((part, tokens), F32),
+        ],
+        input_output_aliases={8 + i: i for i in range(len(before))},
         cost_estimate=cost(3, 5_000_000),
         name="finish",
-    )(keep, from_core, from_y, own_t, tokens, cot, stats, gain, bias, *before)
+    )(keep, from_core, from_y, own_t, cot, stats, gain, bias, *before)
 
 
 def flip(value, axis, size, bit):
@@ -550,6 +547,27 @@
         self.send = self.keep
 
 
+class SwapOverDp:
+    def __init__(self, value, size):
+        self.size = size
+        self.send = value
+        self.steps = ["sum", "join"]
+
+    def more(self):
+        return bool(self.steps)
+
+    def move(self, send):
+        return lax.all_to_all(send, "dp", 0, 0, tiled=True)
+
+    def take(self, arrived):
+        if self.steps.pop(0) == "sum":
+            shares = arrived.reshape(self.size, -1, arrived.shape[1]).astype(F32)
+            total = jnp.sum(shares, axis=0).astype(BF16)
+            self.send = jnp.broadcast_to(total[None], (self.size,) + total.shape).reshape(arrived.shape)
+        else:
+            self.keep = arrived
+
+
 class ScatterOverMp:
     def __init__(self, keep, send):
         self.keep, self.send = keep, send
@@ -568,6 +586,32 @@
             self.send = (self.keep[1].astype(F32) + arrived[1].astype(F32)).astype(BF16)[None]
         else:
             self.from_y = arrived
+
+
+class ShortSums:
+    def __init__(self, keep, send, rest, size):
+        self.keep, self.send, self.rest, self.size = keep, send, rest, size
+        self.steps = [("mp", 1), ("mp", 2)] + [("dp", 1 << i) for i in range(size.bit_length() - 1)]
+
+    def more(self):
+        return bool(self.steps)
+
+    def move(self, send):
+        axis, bit = self.steps[0]
+        return flip(send, axis, 4 if axis == "mp" else self.size, bit)
+
+    def take(self, arrived):
+        axis, bit = self.steps.pop(0)
+        if (axis, bit) == ("mp", 1):
+            both = self.keep + arrived
+            self.norm, self.send = both[0], both[1]
+            return
+        if axis == "mp":
+            self.send = jnp.concatenate([self.norm + arrived, self.rest])
+        else:
+            self.send = self.send + arrived
+        size = self.norm.shape[0]
+        self.norm, self.rest = self.send[:size], self.send[size:]
 
 
 def launch(movers, inputs):
@@ -630,96 +674,131 @@
     first = starts // BJ
     count = (ends + BJ - 1) // BJ - first
 
-    d_act, d_att, cot_sum = early_call(cotangent, down_weight, attn_weight)
-    (d_act, d_att), from_y = tie((d_act, d_att), from_y)
+    pick = (jnp.arange(part)[:, None] + me * part == jnp.arange(width)[None, :]).astype(BF16)
+    d_act, d_att, cot_own, cot_sum = early_call(cotangent, down_weight, attn_weight, pick)
+    gain_bias = down_bias.astype(F32)[:, None]
+    gain_col = norm_gain.astype(F32)[:, None]
+    prepared = (
+        d_act, d_att, mixed_t, mixed, up_t, down_t, attn_t, up_bias_col, head_gains, mask_q, mask_k, first, count,
+        gain_bias, gain_col,
+    )
+    prepared, from_y = tie(prepared, from_y)
+    (
+        d_act, d_att, mixed_t, mixed, up_t, down_t, attn_t, up_bias_col, head_gains, mask_q, mask_k, first, count,
+        gain_bias, gain_col,
+    ) = prepared
     pieces = (own_t, from_y, flip(own_t, "mp", 4, 1), flip(from_y, "mp", 4, 1))
-    cot_own = lax.dynamic_slice_in_dim(cotangent, me * part, part, 1)
-    downbias_part = lax.dynamic_slice_in_dim(jnp.sum(cot_sum, axis=0), me * part, part, 0)
-
     normed, active, d_pre, stats, upbias_part, gain_all, down_part, up_part = mlp_call(
         place, pieces, gains, up_t, up_bias_col, d_act, cotangent
     )
-    upbias_part = jnp.sum(upbias_part, axis=1)
     down_sum = SumOverDp(down_part, dp_size, dp, 0)
-    up_sum = SumOverDp(up_part, dp_size, dp, 1)
+    up_sum = SwapOverDp(up_part, dp_size)
 
     heads_out = []
     before = ()
     qk_part = 0.0
+    held = []
     for seq in range(seqs):
-        (states, before), flights = launch([down_sum, up_sum], (normed, before))
-        *out, qk, total = attention_call(
+        along = [down_sum] + ([up_sum] if not held else [])
+        (states, before), flights = launch(along, (normed, before))
+        *out, qk, norm_row, total = attention_call(
             first[seq], count[seq], states, mixed_t, d_att, mask_q, mask_k, head_gains, cotangent, before, seq,
             seq == seqs - 1,
         )
-        out, qk, total = land(flights, (out, qk, total))
+        ending = held + [f for f in flights if f[0] is down_sum]
+        held = [f for f in flights if f[0] is up_sum]
+        out, qk, norm_row, total = land(ending, (out, qk, norm_row, total))
         heads_out.append(out)
         before = (total,)
         qk_part = qk_part + qk
-    mix_sum = SumOverDp(before[0], dp_size, dp, 0)
-
-    scatters = []
-    gain_part = 0.0
-    waiting = []
-    for seq in range(seqs):
-        ahead = [[down_sum, up_sum, mix_sum], [down_sum, up_sum], [down_sum, up_sum, mix_sum]][seq % 3]
-        (attended, d_mixed), flights = launch(ahead + scatters[-2:], heads_out[seq])
-        keep, send, gp = project_call(
+    mix_sum = SwapOverDp(before[0], dp_size)
+
+    norm_vec = norm_row[0] + jnp.sum(up_part.astype(F32) * up_weight.astype(F32), axis=1)
+    norm_parts = norm_vec.reshape(4, part)
+    norm_parts = [lax.dynamic_index_in_dim(norm_parts, jnp.bitwise_xor(me, m), 0, False) for m in range(4)]
+    short = ShortSums(
+        jnp.stack([norm_parts[0], norm_parts[2]]),
+        jnp.stack([norm_parts[1], norm_parts[3]]),
+        jnp.concatenate([jnp.sum(qk_part, axis=1), jnp.sum(upbias_part, axis=1), jnp.sum(cot_sum, axis=1)]),
+        dp_size,
+    )
+
+    def project(seq, work):
+        attended, d_mixed = work
+        return project_call(
             shard, active, attended, d_pre, d_mixed, normed, down_t, attn_t, up_weight, mixed, gain_all, seq
         )
-        later = [f for f in flights if f[0] is mix_sum and seq == 0]
-        keep, send, gp = land([f for f in flights if f not in later] + waiting, (keep, send, gp))
-        waiting = later
-        gain_part = gain_part + gp
+
+    scatters = []
+    mixing = []
+    for seq in range(seqs):
+        along = [down_sum, short] + [m for m in scatters if m.more()]
+        if seq == 0:
+            along.append(mix_sum)
+        work, flights = launch(along, heads_out[seq])
+        keep, send = project(seq, work)
+        now = [f for f in flights if f[0] is not mix_sum]
+        mixing += [f for f in flights if f[0] is mix_sum]
+        if seq == 1:
+            now += held
+            held = []
+        keep, send = land(now, (keep, send))
         scatters.append(ScatterOverMp(keep, send))
 
-    gain_vec = jnp.sum(gain_part, axis=1).reshape(4, part)
-    gain_half = [lax.dynamic_index_in_dim(gain_vec, jnp.bitwise_xor(me, m), 0, False) for m in range(4)]
-    gain_kept = jnp.stack([gain_half[0], gain_half[2]]) + flip(jnp.stack([gain_half[1], gain_half[3]]), "mp", 4, 1)
-    gain_mine = gain_kept[0] + flip(gain_kept[1], "mp", 4, 2)
-    short = jnp.concatenate(
-        [gain_mine / norm_gain.astype(F32), jnp.sum(qk_part, axis=1), upbias_part, downbias_part]
-    )
-    bit = 1
-    while bit < dp_size:
-        short = short + flip(short, "dp", dp_size, bit)
-        bit *= 2
-
-    gain_bias = down_bias.astype(F32)[None, :]
-    gain_col = norm_gain.astype(F32)[:, None]
     finished = ()
-    for seq, scatter in enumerate(scatters):
-        while scatter.more():
-            scatter.take(scatter.move(scatter.send))
-        finished = finish_call(
-            scatter.keep, scatter.from_core, scatter.from_y, own_t, tokens, cot_own, stats,
-            gain_col, gain_bias, finished, seq,
-        )
+    done = set()
+
+    def finish_ready(finished):
+        for seq, scatter in enumerate(scatters):
+            if not scatter.more() and seq not in done:
+                done.add(seq)
+                finished = finish_call(
+                    scatter.keep, scatter.from_core, scatter.from_y, own_t, cot_own, stats, gain_col, gain_bias,
+                    finished, seq,
+                )
+        return finished
+
+    flying = held + mixing
+    while True:
+        busy = [f[0] for f in flying]
+        ready = [m for m in scatters + [down_sum, short, up_sum, mix_sum] if m.more() and m not in busy]
+        finished, flights = launch(ready, finished)
+        flying = flying + flights
+        if not flying:
+            break
+        finished = finish_ready(finished)
+        small = [f for f in flying if f[0] is short or f[0] in scatters and len(f[0].bits) == 2]
+        sums = [f for f in flying if f[0] in (mix_sum, up_sum, down_sum)]
+        moving = [f for f in flying if f[0] in scatters and len(f[0].bits) == 1]
+        first_swap = [f for f in sums if len(f[0].steps) == 2]
+        if small:
+            now = small
+        elif moving and (len(moving) > 1 or not first_swap):
+            now = moving[:1]
+        else:
+            now = first_swap or sums
+        finished = land(now, finished)
+        flying = [f for f in flying if f not in now]
+    finished = finish_ready(finished)
     block_out, token_grad = finished
-
-    movers = [down_sum, up_sum, mix_sum]
-    while any(m.more() for m in movers):
-        for mover in movers:
-            if mover.more():
-                mover.take(mover.move(mover.send))
+    block_out, token_grad = block_out.T, token_grad.T
     mixed_grad = mix_sum.keep.astype(F32)
     qkv_grad = jnp.transpose(mixed_grad[: 3 * part].reshape(3, part, width), (2, 0, 1))
 
-    gain_grad = short[:part]
-    qkgain_grad = short[part : 3 * part].reshape(2, part)
-    upbias_grad = short[3 * part : 3 * part + upbias_part.shape[0]]
-    downbias_grad = short[3 * part + upbias_part.shape[0] :]
+    gain_grad = short.norm / norm_gain.astype(F32)
+    rest = short.rest
+    split = 2 * part + up_weight.shape[1]
     return (
         block_out,
         token_grad,
         gain_grad,
         qkv_grad,
-        qkgain_grad,
+        rest[: 2 * part].reshape(2, part),
         mixed_grad[3 * part :],
         up_sum.keep.astype(F32),
-        upbias_grad,
+        rest[2 * part : split],
         down_sum.keep.astype(F32),
-        downbias_grad,
+        rest[split:],
     )
 
 

time: 278 us -> 275 us (0.989)
  starting transfers between devices: 34 us -> 43.8 us
  local copies, waits for them, and re-layouts: 31 us -> 22 us
  waiting for transfers between devices: 47.5 us -> 56.1 us
  Pallas kernels: 135 us -> 128 us
  other arithmetic: 26.7 us -> 23.1 us
    all_to_all x0 -> x4, starting transfers between devices: none -> 19.7 us  [move(): return lax.all_to_all(send, 'dp', 0, 0, tiled=True)]
    ppermute x35 -> x23, starting transfers between devices: 34 us -> 24.1 us  [flip(): return lax.ppermute(value, axis, [(i, i ^ bit) for i in range(size)])]
    unnamed x68 -> x63, local copies, waits for them, and re-layouts: 13.1 us -> 5.08 us
    all_to_all x0 -> x4, waiting for transfers between devices: none -> 7.34 us  [move(): return lax.all_to_all(send, 'dp', 0, 0, tiled=True)]
    optimization_barrier x0 -> x4, local copies, waits for them, and re-layouts: none -> 4.63 us  [tie(): return lax.optimization_barrier(trees)]
    dynamic_slice x3 -> x1, local copies, waits for them, and re-layouts: 3.76 us -> 0.01 us  [body(): lax.dynamic_index_in_dim(norm_parts, jnp.bitwise_xor(me, m), 0, False)]
    pallas_call x3, Pallas kernels: 58 us -> 54.5 us  [attention_call(): pl.pallas_call(functools.partial(attention_kernel, last, seq), grid_spec=...]
    pallas_call x1, Pallas kernels: 26.6 us -> 23.4 us  [mlp_call(): pl.pallas_call(mlp_kernel, grid_spec=grid_spec, out_shape=[jax.ShapeDtype...]
  transfers between devices with their start and end apart: 35 -> 27, of which waited for: 7 -> 11; matrix products, arithmetic and copies ran while one was open for 14% -> 11% of each run, Pallas kernels for 38% -> 38%
where the time goes in v1:
time: 275 us; the launch traced here: 274 us
  Pallas kernels  128 us (47%)
  waiting for transfers between devices  56.1 us (20%)
  starting transfers between devices  43.8 us (16%)
  other arithmetic  23.1 us (8%)
  local copies, waits for them, and re-layouts  22 us (8%)
    pallas_call x3, Pallas kernels, attention_call(): pl.pallas_call(functools.partial(attention_kernel, last, seq), grid_spec=...  54.5 us
    ppermute x23, waiting for transfers between devices, flip(): return lax.ppermute(value, axis, [(i, i ^ bit) for i in range(size)])  48.7 us
    pallas_call x3, Pallas kernels, project_call(): pl.pallas_call(project_kernel, grid_spec=grid_spec, out_shape=[jax.ShapeD...  29.5 us
    ppermute x23, starting transfers between devices, flip(): return lax.ppermute(value, axis, [(i, i ^ bit) for i in range(size)])  24.1 us
    pallas_call x1, Pallas kernels, mlp_call(): pl.pallas_call(mlp_kernel, grid_spec=grid_spec, out_shape=[jax.ShapeDtype...  23.4 us
    all_to_all x4, starting transfers between devices, move(): return lax.all_to_all(send, 'dp', 0, 0, tiled=True)  19.7 us
    pallas_call x1, Pallas kernels, early_call(): pl.pallas_call(early_kernel, grid=(tokens // block,), in_specs=[pl.BlockS...  11.3 us
    pallas_call x3, Pallas kernels, finish_call(): pl.pallas_call(finish_kernel, grid=(steps,), in_specs=[packed, packed, pa...  9.25 us
  transfers between devices with their start and end apart: 27, of which 11 were waited for; matrix products, arithmetic and copies ran while one was open for 11% of the time, Pallas kernels for 38%

profile of v1, /device:TPU:0, one launch (start us, length us, event | category | flops | bytes accessed | tf_op | source)
XLA Modules:
  0.0 274.0 jit_solution(93014743049501141)
XLA Ops:
  0.6 3.0 %collective-permute-start = (bf16[192,3072]{1,0:T(8,128)(2,1)}, bf16[192,3072]{1,0:T(8,128)(2,1)S(1)}, u32[]{:S(2)}, u32[]{:S(2)}) collective-permute-start(bf16[192,3072]{1,0:T(8,128)(2,1)} %bitcast.42), channel_id=1, source_target_pairs={{0,2},{1,3},{2,0},{3,1},{4,6},{5,7},{6,4},{7,5},{8,10},{9,11},{10,... | collective-permute-start | bytes 3538952 | tf_op jit(solution)/shard_map/ppermute | solution.py:497
  3.7 0.8 fusion.1.pick
  4.5 11.3 %early.1 = (bf16[3,768,1024]{2,1,0:T(8,128)(2,1)}, bf16[3,192,1024]{2,1,0:T(8,128)(2,1)}, bf16[192,3072]{1,0:T(8,128)(2,1)}, f32[192,128]{1,0:T(8,128)}) custom-call(bf16[3072,768]{1,0:T(8,128)(2,1)} %cot_hbm.5, bf16[768,768]{1,0:T(8,128)(2,1)} %down.1, bf16[192,768]{1,0:T(8,128)(2,1)} %attn.1, bf16[192,768]{1,0:T(8,128)(2,1)} %fusion.1.pick), custom_call_target="tpu_custom_call" | custom-call | flops 10000 | bytes 12000 | tf_op jit(solution)/shard_map/early/pallas_call | solution.py:62
  15.8 0.7 slice.80
  17.1 1.5 copy.49
  18.6 0.9 copy.50
  19.5 1.3 copy.47
  20.9 1.5 copy.48
  24.5 0.7 select_convert_fusion.mask_k
  25.3 4.6 %collective-permute-done.flip_y = bf16[192,3072]{1,0:T(8,128)(2,1)S(1)} collective-permute-done((bf16[192,3072]{1,0:T(8,128)(2,1)}, bf16[192,3072]{1,0:T(8,128)(2,1)S(1)}, u32[]{:S(2)}, u32[]{:S(2)}) %collective-permute-start) | collective-permute-done | bytes 1179680 | tf_op jit(solution)/shard_map/ppermute | solution.py:497
  30.0 1.8 collective-permute-start.3
  32.0 2.2 collective-permute-done.3.gain_y
  34.7 0.9 copy.51.up_bias
  36.3 23.4 %mlp.1 = (bf16[3,768,1024]{2,1,0:T(8,128)(2,1)}, bf16[3,768,1024]{2,1,0:T(8,128)(2,1)}, bf16[3,768,1024]{2,1,0:T(8,128)(2,1)}, f32[8,3072]{1,0:T(8,128)}, f32[76...) custom-call(s32[4]{0:T(128)} %xor_multiply_fusion.place, ...), custom_call_target="tpu_custom_call" | custom-call | flops 20000 | bytes 30000 | tf_op jit(solution)/shard_map/mlp/pallas_call | solution.py:182
  59.7 1.9 constant_dynamic-slice_fusion.4
  61.6 6.0 %all-to-all-start = ((bf16[8,96,768]{2,1,0:T(8,128)(2,1)}), bf16[8,96,768]{2,1,0:T(8,128)(2,1)S(1)}, u32[]{:S(2)}, u32[]{:S(2)}) async-start(bf16[8,96,768]{2,1,0:T(8,128)(2,1)} %bitcast.67), calls=%async_computation | async-start | bytes 2359296 | tf_op jit(solution)/shard_map/all_to_all | solution.py:560
  67.7 2.0 collective-permute-start.6
  69.7 0.8 copy.52.gains
  71.1 15.9 %attention.3 = (bf16[192,1024]{1,0:T(8,128)(2,1)}, bf16[576,1024]{1,0:T(8,128)(2,1)}, f32[384,128]{1,0:T(8,128)}, f32[1,768]{1,0:T(1,128)}, f32[768,768]{1,0:T(8,128)}) custom-call(s32[4]{0:T(128)} %get-tuple-element.330.first, s32[4]{0:T(128)} %get-tuple-element.322.count, bf16[3,768,1024]{2,1,0:T(8,128)(2,1)} %get-tuple-element.195.normed, ...), custom_call_target="tpu_custom_call" | custom-call | flops 18000 | bytes 5000 | tf_op jit(solution)/shard_map/attention/pallas_call | solution.py:364
  87.0 9.1 %collective-permute-done.6 = bf16[384,768]{1,0:T(8,128)(2,1)} collective-permute-done((bf16[384,768]{1,0:T(8,128)(2,1)}, bf16[384,768]{1,0:T(8,128)(2,1)}, u32[]{:S(2)}, u32[]{:S(2)}) %collective-permute-start.6) | collective-permute-done | bytes 589856 | tf_op jit(solution)/shard_map/ppermute | solution.py:497
  96.1 2.1 add_convert_fusion.3
  98.1 1.5 collective-permute-start.7
  99.6 19.5 %attention.4 = (bf16[192,1024]{1,0:T(8,128)(2,1)}, bf16[576,1024]{1,0:T(8,128)(2,1)}, f32[384,128]{1,0:T(8,128)}, f32[1,768]{1,0:T(1,128)}, f32[768,768]{1,0:T(8,128)}) custom-call(s32[4]{0:T(128)} %get-tuple-element.329.first, s32[4]{0:T(128)} %get-tuple-element.323.count, bf16[3,768,1024]{2,1,0:T(8,128)(2,1)} %get-tuple-element.195.normed, ...), custom_call_target="tpu_custom_call" | custom-call | flops 18000 | bytes 5000 | tf_op jit(solution)/shard_map/attention/pallas_call | solution.py:364
  119.2 0.9 reduce_sum.82
  120.0 1.0 add_convert_fusion.7
  121.0 2.0 broadcast_in_dim.64
  123.0 2.4 collective-permute-start.8
  125.9 19.1 %attention.5 = (bf16[192,1024]{1,0:T(8,128)(2,1)}, bf16[576,1024]{1,0:T(8,128)(2,1)}, f32[384,128]{1,0:T(8,128)}, f32[1,768]{1,0:T(1,128)}, bf16[768,768]{1,0:T(8,128)(2,1)}) custom-call(s32[4]{0:T(128)} %get-tuple-element.328.first, s32[4]{0:T(128)} %get-tuple-element.324.count, bf16[3,768,1024]{2,1,0:T(8,128)(2,1)} %get-tuple-element.195.normed, ...), custom_call_target="tpu_custom_call" | custom-call | flops 18000 | bytes 5000 | tf_op jit(solution)/shard_map/attention/pallas_call | solution.py:364
  145.0 0.7 reduce.2
  145.8 1.0 add_convert_fusion.5
  146.9 4.1 %all-to-all-start.1 = ((bf16[8,96,768]{2,1,0:T(8,128)(2,1)}), bf16[8,96,768]{2,1,0:T(8,128)(2,1)S(1)}, u32[]{:S(2)}, u32[]{:S(2)}) async-start(bf16[8,96,768]{2,1,0:T(8,128)(2,1)} %bitcast.22), calls=%async_computation.1 | async-start | bytes 2359296 | tf_op jit(solution)/shard_map/all_to_all | solution.py:560
  151.1 9.9 %project.3 = (bf16[2,400,1024]{2,1,0:T(8,128)(2,1)}, bf16[2,400,1024]{2,1,0:T(8,128)(2,1)}) custom-call(s32[1]{0:T(128)} %bitcast.shard, bf16[3,768,1024]{2,1,0:T(8,128)(2,1)} %get-tuple-element.165.active, bf16[192,1024]{1,0:T(8,128)(2,1)} %get-tuple-element.212.attended, bf16[3,768,1024]{2,1,0:T(8,128)(2,1)} %get-tuple-element.213.d_pre, ...), custom_call_target="tpu_custom_call" | custom-call | flops 8000 | bytes 16000 | tf_op jit(solution)/shard_map/project/pallas_call | solution.py:439
  161.4 1.9 collective-permute-start.11
  163.5 1.6 collective-permute-start.12
  165.3 9.9 %project.4 = (bf16[2,400,1024]{2,1,0:T(8,128)(2,1)}, bf16[2,400,1024]{2,1,0:T(8,128)(2,1)}) custom-call(s32[1]{0:T(128)} %bitcast.shard, bf16[3,768,1024]{2,1,0:T(8,128)(2,1)} %get-tuple-element.165.active, bf16[192,1024]{1,0:T(8,128)(2,1)} %get-tuple-element.226.attended, bf16[3,768,1024]{2,1,0:T(8,128)(2,1)} %get-tuple-element.213.d_pre, ...), custom_call_target="tpu_custom_call" | custom-call | flops 8000 | bytes 16000 | tf_op jit(solution)/shard_map/project/pallas_call | solution.py:439
  175.2 3.4 %collective-permute-done.11 = bf16[192,768]{1,0:T(8,128)(2,1)S(1)} collective-permute-done((bf16[192,768]{1,0:T(8,128)(2,1)S(1)}, bf16[192,768]{1,0:T(8,128)(2,1)S(1)}, u32[]{:S(2)}, u32[]{:S(2)}) %collective-permute-start.11) | collective-permute-done | bytes 294944 | tf_op jit(solution)/shard_map/ppermute | solution.py:497
  178.6 1.9 all-to-all-done.1
  180.4 2.4 add_convert_fusion.2
  183.1 1.6 collective-permute-start.16
  184.7 1.3 collective-permute-start.14
  185.9 0.8 collective-permute-start.15
  186.7 3.6 %all-to-all-start.2 = ((bf16[8,96,768]{2,1,0:T(8,128)(2,1)}), bf16[8,96,768]{2,1,0:T(8,128)(2,1)S(1)}, u32[]{:S(2)}, u32[]{:S(2)}) async-start(bf16[8,96,768]{2,1,0:T(8,128)(2,1)} %bitcast.69), calls=%async_computation.2 | async-start | bytes 2359296 | tf_op jit(solution)/shard_map/all_to_all | solution.py:560
  190.3 9.7 %project.5 = (bf16[2,400,1024]{2,1,0:T(8,128)(2,1)}, bf16[2,400,1024]{2,1,0:T(8,128)(2,1)}) custom-call(s32[1]{0:T(128)} %bitcast.shard, bf16[3,768,1024]{2,1,0:T(8,128)(2,1)} %get-tuple-element.165.active, bf16[192,1024]{1,0:T(8,128)(2,1)} %get-tuple-element.244.attended, bf16[3,768,1024]{2,1,0:T(8,128)(2,1)} %get-tuple-element.213.d_pre, ...), custom_call_target="tpu_custom_call" | custom-call | flops 8000 | bytes 16000 | tf_op jit(solution)/shard_map/project/pallas_call | solution.py:439
  200.0 8.1 %collective-permute-done.15 = f32[1536]{0:T(1024)S(1)} collective-permute-done((f32[1536]{0:T(1024)S(1)}, f32[1536]{0:T(1024)S(1)}, u32[]{:S(2)}, u32[]{:S(2)}) %collective-permute-start.15) | collective-permute-done | bytes 6176 | tf_op jit(solution)/shard_map/ppermute | solution.py:497
  208.7 2.6 add_convert_fusion.1
  211.4 0.7 add.135
  212.6 1.4 copy.55.gain
  214.0 1.4 copy.56.bias
  215.4 3.1 %finish.3 = (bf16[192,3072]{1,0:T(8,128)(2,1)}, f32[192,3072]{1,0:T(8,128)}) custom-call(bf16[2,400,1024]{2,1,0:T(8,128)(2,1)} %get-tuple-element.241.keep, bf16[2,400,1024]{2,1,0:T(8,128)(2,1)} %collective-permute-done.13.from_core, bf16[1,400,1024]{2,1,0:T(8,128)(2,1)} %collective-permute-done.16.from_y, bf16[192,3072]{1,0:T(8,128)(2,1)} %bitcast.45, ...), custom_call_target="tpu_custom_call" | custom-call | flops 3000 | bytes 5000 | tf_op jit(solution)/shard_map/finish/pallas_call | solution.py:474
  219.0 2.6 add_convert_fusion
  221.6 4.7 %collective-permute-start.20 = (f32[1536]{0:T(1024)S(1)}, f32[1536]{0:T(1024)S(1)}, u32[]{:S(2)}, u32[]{:S(2)}) collective-permute-start(f32[1536]{0:T(1024)S(1)} %add.137), channel_id=1, source_target_pairs={{0,16},{4,20},{8,24},{12,28},{16,0},{20,4},{24,8},{28,12},{1,17},{... | collective-permute-start | bytes 18440 | tf_op jit(solution)/shard_map/ppermute | solution.py:497
  226.3 1.6 collective-permute-done.20
  227.9 5.1 %collective-permute-done.21.from_y = bf16[1,400,1024]{2,1,0:T(8,128)(2,1)} collective-permute-done((bf16[1,400,1024]{2,1,0:T(8,128)(2,1)}, bf16[1,400,1024]{2,1,0:T(8,128)(2,1)}, u32[]{:S(2)}, u32[]{:S(2)}) %collective-permute-start.21) | collective-permute-done | bytes 819232 | tf_op jit(solution)/shard_map/ppermute | solution.py:497
  233.0 3.1 %finish.4 = (bf16[192,3072]{1,0:T(8,128)(2,1)}, f32[192,3072]{1,0:T(8,128)}) custom-call(bf16[2,400,1024]{2,1,0:T(8,128)(2,1)} %get-tuple-element.260.keep, bf16[2,400,1024]{2,1,0:T(8,128)(2,1)} %collective-permute-done.17.from_core, bf16[1,400,1024]{2,1,0:T(8,128)(2,1)} %collective-permute-done.21.from_y, ...), custom_call_target="tpu_custom_call", output_to_operand_aliasing={{0}: (8, {}), {1}: (9, {})} | custom-call | flops 3000 | bytes 5000 | tf_op jit(solution)/shard_map/finish/pallas_call | solution.py:474
  236.3 1.1 broadcast_in_dim.65
  237.4 5.9 %all-to-all-start.3 = ((bf16[8,96,768]{2,1,0:T(8,128)(2,1)}), bf16[8,96,768]{2,1,0:T(8,128)(2,1)S(1)}, u32[]{:S(2)}, u32[]{:S(2)}) async-start(bf16[8,96,768]{2,1,0:T(8,128)(2,1)} %bitcast.29), calls=%async_computation.3 | async-start | bytes 2359296 | tf_op jit(solution)/shard_map/all_to_all | solution.py:560
  243.9 1.6 convert_element_type.155
  245.5 1.6 fusion
  247.1 0.7 slice.109
  249.1 14.1 %collective-permute-done.22.from_y = bf16[1,400,1024]{2,1,0:T(8,128)(2,1)} collective-permute-done((bf16[1,400,1024]{2,1,0:T(8,128)(2,1)}, bf16[1,400,1024]{2,1,0:T(8,128)(2,1)}, u32[]{:S(2)}, u32[]{:S(2)}) %collective-permute-start.22) | collective-permute-done | bytes 819232 | tf_op jit(solution)/shard_map/ppermute | solution.py:497
  263.3 3.1 %finish.5 = (bf16[192,3072]{1,0:T(8,128)(2,1)}, f32[192,3072]{1,0:T(8,128)}) custom-call(bf16[2,400,1024]{2,1,0:T(8,128)(2,1)} %get-tuple-element.252.keep, bf16[2,400,1024]{2,1,0:T(8,128)(2,1)} %collective-permute-done.18.from_core, bf16[1,400,1024]{2,1,0:T(8,128)(2,1)} %collective-permute-done.22.from_y, ...), custom_call_target="tpu_custom_call", output_to_operand_aliasing={{0}: (8, {}), {1}: (9, {})} | custom-call | flops 3000 | bytes 5000 | tf_op jit(solution)/shard_map/finish/pallas_call | solution.py:474
  266.4 5.5 %all-to-all-done.3 = bf16[8,96,768]{2,1,0:T(8,128)(2,1)S(1)} async-done(((bf16[8,96,768]{2,1,0:T(8,128)(2,1)}), bf16[8,96,768]{2,1,0:T(8,128)(2,1)S(1)}, u32[]{:S(2)}, u32[]{:S(2)}) %all-to-all-start.3) | async-done | bytes 1179680 | tf_op jit(solution)/shard_map/all_to_all | solution.py:560
  271.8 1.3 slice.106
  273.2 0.9 slice.108
  (123 shorter events, 10.4 us)
Async XLA Ops:
  0.6 29.2 %collective-permute-start = (bf16[192,3072]{1,0:T(8,128)(2,1)}, bf16[192,3072]{1,0:T(8,128)(2,1)S(1)}, u32[]{:S(2)}, u32[]{:S(2)}) collective-permute-start(bf16[192,3072]{1,0:T(8,128)(2,1)} %bitcast.42), channel_id=1, source_target_pairs={{0,2},{1,3},{2,0},{3,1},{4,6},{5,7},{6,4},{7,5},{8,10},{9,11},{10,... | collective-permute-start | bytes 3538952 | tf_op jit(solution)/shard_map/ppermute | solution.py:497
  3.7 32.0 %collective-permute-start.1 = (bf16[192,3072]{1,0:T(8,128)(2,1)}, bf16[192,3072]{1,0:T(8,128)(2,1)}, u32[]{:S(2)}, u32[]{:S(2)}) collective-permute-start(bf16[192,3072]{1,0:T(8,128)(2,1)} %bitcast.43), channel_id=1, source_target_pairs={{0,1},{1,0},{2,3},{3,2},{4,5},{5,4},{6,7},{7,6},{8,9},{9,8},{10,11... | collective-permute-start | bytes 3538952 | tf_op jit(solution)/shard_map/ppermute | solution.py:497
  4.5 11.3 %copy-start.16 = (s32[3,1024]{1,0:T(4,128)S(1)}, s32[3,1024]{1,0:T(4,128)}, u32[]{:S(2)}) copy-start(s32[3,1024]{1,0:T(4,128)} %param.13) | copy-start | bytes 36868
  4.5 12.6 %copy-start.2 = (bf16[768,768]{1,0:T(8,128)(2,1)S(1)}, bf16[768,768]{1,0:T(8,128)(2,1)}, u32[]{:S(2)}) copy-start(bf16[768,768]{1,0:T(8,128)(2,1)} %down.1) | copy-start | bytes 3538948
  15.8 2.8 %copy-start.6 = (bf16[192,768]{1,0:T(8,128)(2,1)S(1)}, bf16[192,768]{1,0:T(8,128)(2,1)}, u32[]{:S(2)}) copy-start(bf16[192,768]{1,0:T(8,128)(2,1)} %attn.1) | copy-start | bytes 884740
  15.8 3.7 %copy-start.1 = (bf16[768,3,192]{0,2,1:T(8,128)(2,1)S(1)}, bf16[768,3,192]{0,2,1:T(8,128)(2,1)}, u32[]{:S(2)}) copy-start(bf16[768,3,192]{0,2,1:T(8,128)(2,1)} %param.15) | copy-start | bytes 2654212
  18.6 2.2 copy-start
  20.8 1.5 copy-start.26
  20.8 1.5 copy-start.27
  20.8 1.6 copy-start.24
  20.8 2.2 copy-start.28
  20.9 2.7 copy-start.22
  20.9 2.7 copy-start.23
  20.9 13.3 %copy-start.29 = (s32[4]{0:T(128)S(1)}, s32[4]{0:T(128)}, u32[]{:S(2)}) copy-start(s32[4]{0:T(128)} %constant.123.clone) | copy-start | bytes 52
  29.9 5.8 %copy-start.5 = (bf16[192,3072]{1,0:T(8,128)(2,1)}, bf16[192,3072]{1,0:T(8,128)(2,1)S(1)}, u32[]{:S(2)}) copy-start(bf16[192,3072]{1,0:T(8,128)(2,1)S(1)} %collective-permute-done.flip_y) | copy-start | bytes 3538948
  29.9 5.8 %collective-permute-start.2 = (bf16[192,3072]{1,0:T(8,128)(2,1)S(1)}, bf16[192,3072]{1,0:T(8,128)(2,1)}, u32[]{:S(2)}, u32[]{:S(2)}) collective-permute-start(bf16[192,3072]{1,0:T(8,128)(2,1)S(1)} %collective-permute-done.flip_y), channel_id=1, source_target_pairs={{0,1},{1,0},{2,3},{3,2},{4,5},{5,4},{6,7},{7,6},{8,9},{9,8},{10,11... | collective-permute-start | bytes 3538952 | tf_op jit(solution)/shard_map/ppermute | solution.py:497
  30.0 5.8 %copy-start.12 = (bf16[192,128]{1,0:T(8,128)(2,1)}, bf16[192,128]{1,0:T(8,128)(2,1)S(1)}, u32[]{:S(2)}) copy-start(bf16[192,128]{1,0:T(8,128)(2,1)S(1)} %broadcast_in_dim.63.gain_own) | copy-start | bytes 147460
  30.0 4.2 %collective-permute-start.3 = (bf16[192,128]{1,0:T(8,128)(2,1)S(1)}, bf16[192,128]{1,0:T(8,128)(2,1)S(1)}, u32[]{:S(2)}, u32[]{:S(2)}) collective-permute-start(bf16[192,128]{1,0:T(8,128)(2,1)S(1)} %broadcast_in_dim.63.gain_own), channel_id=1, source_target_pairs={{0,2},{1,3},{2,0},{3,1},{4,6},{5,7},{6,4},{7,5},{8,10},{9,11},{10,... | collective-permute-start | bytes 147464 | tf_op jit(solution)/shard_map/ppermute | solution.py:497
  31.8 3.9 %collective-permute-start.4 = (bf16[192,128]{1,0:T(8,128)(2,1)S(1)}, bf16[192,128]{1,0:T(8,128)(2,1)S(1)}, u32[]{:S(2)}, u32[]{:S(2)}) collective-permute-start(bf16[192,128]{1,0:T(8,128)(2,1)S(1)} %broadcast_in_dim.63.gain_own), channel_id=1, source_target_pairs={{0,1},{1,0},{2,3},{3,2},{4,5},{5,4},{6,7},{7,6},{8,9},{9,8},{10,11... | collective-permute-start | bytes 147464 | tf_op jit(solution)/shard_map/ppermute | solution.py:497
  34.2 1.5 copy-start.18
  34.2 1.5 collective-permute-start.5
  35.7 0.6 copy-start.19
  35.7 0.6 copy-start.20
  61.6 57.5 %all-to-all-start = ((bf16[8,96,768]{2,1,0:T(8,128)(2,1)}), bf16[8,96,768]{2,1,0:T(8,128)(2,1)S(1)}, u32[]{:S(2)}, u32[]{:S(2)}) async-start(bf16[8,96,768]{2,1,0:T(8,128)(2,1)} %bitcast.67), calls=%async_computation | async-start | bytes 2359296 | tf_op jit(solution)/shard_map/all_to_all | solution.py:560
  67.7 28.4 %collective-permute-start.6 = (bf16[384,768]{1,0:T(8,128)(2,1)}, bf16[384,768]{1,0:T(8,128)(2,1)}, u32[]{:S(2)}, u32[]{:S(2)}) collective-permute-start(bf16[384,768]{1,0:T(8,128)(2,1)} %constant_dynamic-slice_fusion.4), channel_id=1, source_target_pairs={{0,4},{4,0},{8,12},{12,8},{16,20},{20,16},{24,28},{28,24},{1,5},{5... | collective-permute-start | bytes 1769480 | tf_op jit(solution)/shard_map/ppermute | solution.py:497
  71.1 25.0 %copy-start.7 = (bf16[768,768]{1,0:T(8,128)(2,1)S(1)}, bf16[768,768]{1,0:T(8,128)(2,1)}, u32[]{:S(2)}) copy-start(bf16[768,768]{1,0:T(8,128)(2,1)} %get-tuple-element.169) | copy-start | bytes 3538948
  98.1 21.0 %collective-permute-start.7 = (bf16[192,768]{1,0:T(8,128)(2,1)}, bf16[192,768]{1,0:T(8,128)(2,1)}, u32[]{:S(2)}, u32[]{:S(2)}) collective-permute-start(bf16[192,768]{1,0:T(8,128)(2,1)} %get-tuple-element.191), channel_id=1, source_target_pairs={{0,8},{4,12},{8,0},{12,4},{16,24},{20,28},{24,16},{28,20},{1,9},{5... | collective-permute-start | bytes 884744 | tf_op jit(solution)/shard_map/ppermute | solution.py:497
  119.1 6.3 %copy-start.3 = (bf16[768,768]{1,0:T(8,128)(2,1)S(1)}, bf16[768,768]{1,0:T(8,128)(2,1)}, u32[]{:S(2)}) copy-start(bf16[768,768]{1,0:T(8,128)(2,1)} %get-tuple-element.190) | copy-start | bytes 3538948
  123.0 21.9 %collective-permute-start.8 = (bf16[96,768]{1,0:T(8,128)(2,1)S(1)}, bf16[96,768]{1,0:T(8,128)(2,1)S(1)}, u32[]{:S(2)}, u32[]{:S(2)}) collective-permute-start(bf16[96,768]{1,0:T(8,128)(2,1)S(1)} %add_convert_fusion.7), channel_id=1, source_target_pairs={{0,16},{4,20},{8,24},{12,28},{16,0},{20,4},{24,8},{28,12},{1,17},{... | collective-permute-start | bytes 442376 | tf_op jit(solution)/shard_map/ppermute | solution.py:497
  125.9 19.9 %copy-start.8 = (bf16[192,768]{1,0:T(8,128)(2,1)S(1)}, bf16[192,768]{1,0:T(8,128)(2,1)}, u32[]{:S(2)}) copy-start(bf16[192,768]{1,0:T(8,128)(2,1)} %get-tuple-element.312) | copy-start | bytes 884740
  146.8 14.2 %collective-permute-start.9 = (bf16[96,768]{1,0:T(8,128)(2,1)S(1)}, bf16[96,768]{1,0:T(8,128)(2,1)S(1)}, u32[]{:S(2)}, u32[]{:S(2)}) collective-permute-start(bf16[96,768]{1,0:T(8,128)(2,1)S(1)} %add_convert_fusion.5), channel_id=1, source_target_pairs={{0,16},{4,20},{8,24},{12,28},{16,0},{20,4},{24,8},{28,12},{1,17},{... | collective-permute-start | bytes 442376 | tf_op jit(solution)/shard_map/ppermute | solution.py:497
  146.8 14.1 %collective-permute-start.10 = (f32[2,192]{1,0:T(2,128)S(1)}, f32[2,192]{1,0:T(2,128)S(1)}, u32[]{:S(2)}, u32[]{:S(2)}) collective-permute-start(f32[2,192]{1,0:T(2,128)S(1)} %pad_maximum_fusion), channel_id=1, source_target_pairs={{0,1},{1,0},{2,3},{3,2},{4,5},{5,4},{6,7},{7,6},{8,9},{9,8},{10,11... | collective-permute-start | bytes 4616 | tf_op jit(solution)/shard_map/ppermute | solution.py:497
  146.9 33.5 %all-to-all-start.1 = ((bf16[8,96,768]{2,1,0:T(8,128)(2,1)}), bf16[8,96,768]{2,1,0:T(8,128)(2,1)S(1)}, u32[]{:S(2)}, u32[]{:S(2)}) async-start(bf16[8,96,768]{2,1,0:T(8,128)(2,1)} %bitcast.22), calls=%async_computation.1 | async-start | bytes 2359296 | tf_op jit(solution)/shard_map/all_to_all | solution.py:560
  151.0 12.2 %copy-start.17 = (f32[192,128]{1,0:T(8,128)S(1)}, f32[192,128]{1,0:T(8,128)}, u32[]{:S(2)}) copy-start(f32[192,128]{1,0:T(8,128)} %get-tuple-element.240) | copy-start | bytes 294916
  151.0 12.3 %copy-start.11 = (f32[768,128]{1,0:T(8,128)S(1)}, f32[768,128]{1,0:T(8,128)}, u32[]{:S(2)}) copy-start(f32[768,128]{1,0:T(8,128)} %get-tuple-element.239) | copy-start | bytes 1179652
  151.1 14.1 %copy-start.13 = (f32[384,128]{1,0:T(8,128)S(1)}, f32[384,128]{1,0:T(8,128)}, u32[]{:S(2)}) copy-start(f32[384,128]{1,0:T(8,128)} %get-tuple-element.236) | copy-start | bytes 589828
  151.1 14.1 %copy-start.14 = (f32[384,128]{1,0:T(8,128)S(1)}, f32[384,128]{1,0:T(8,128)}, u32[]{:S(2)}) copy-start(f32[384,128]{1,0:T(8,128)} %get-tuple-element.237) | copy-start | bytes 589828
  151.1 14.1 %copy-start.15 = (f32[384,128]{1,0:T(8,128)S(1)}, f32[384,128]{1,0:T(8,128)}, u32[]{:S(2)}) copy-start(f32[384,128]{1,0:T(8,128)} %get-tuple-element.238) | copy-start | bytes 589828
  161.1 17.5 %collective-permute-start.13 = (bf16[2,400,1024]{2,1,0:T(8,128)(2,1)}, bf16[2,400,1024]{2,1,0:T(8,128)(2,1)}, u32[]{:S(2)}, u32[]{:S(2)}) collective-permute-start(bf16[2,400,1024]{2,1,0:T(8,128)(2,1)} %get-tuple-element.232), channel_id=1, source_target_pairs={{0,1},{1,0},{2,3},{3,2},{4,5},{5,4},{6,7},{7,6},{8,9},{9,8},{10,11... | collective-permute-start | bytes 4915208 | tf_op jit(solution)/shard_map/ppermute | solution.py:497
  161.4 17.2 %collective-permute-start.11 = (bf16[192,768]{1,0:T(8,128)(2,1)S(1)}, bf16[192,768]{1,0:T(8,128)(2,1)S(1)}, u32[]{:S(2)}, u32[]{:S(2)}) collective-permute-start(bf16[192,768]{1,0:T(8,128)(2,1)S(1)} %maximum_select_fusion.2), channel_id=1, source_target_pairs={{0,8},{4,12},{8,0},{12,4},{16,24},{20,28},{24,16},{28,20},{1,9},{5... | collective-permute-start | bytes 884744 | tf_op jit(solution)/shard_map/ppermute | solution.py:497
  163.5 11.6 %collective-permute-start.12 = (f32[192]{0:T(256)S(1)}, f32[192]{0:T(256)S(1)}, u32[]{:S(2)}, u32[]{:S(2)}) collective-permute-start(f32[192]{0:T(256)S(1)} %bitcast.73), channel_id=1, source_target_pairs={{0,2},{1,3},{2,0},{3,1},{4,6},{5,7},{6,4},{7,5},{8,10},{9,11},{10,... | collective-permute-start | bytes 2312 | tf_op jit(solution)/shard_map/ppermute | solution.py:497
  165.3 15.1 %copy-start.4 = (bf16[2,400,1024]{2,1,0:T(8,128)(2,1)S(1)}, bf16[2,400,1024]{2,1,0:T(8,128)(2,1)}, u32[]{:S(2)}) copy-start(bf16[2,400,1024]{2,1,0:T(8,128)(2,1)} %get-tuple-element.241.keep) | copy-start | bytes 4915204
  183.1 25.1 %collective-permute-start.17 = (bf16[2,400,1024]{2,1,0:T(8,128)(2,1)}, bf16[2,400,1024]{2,1,0:T(8,128)(2,1)}, u32[]{:S(2)}, u32[]{:S(2)}) collective-permute-start(bf16[2,400,1024]{2,1,0:T(8,128)(2,1)} %get-tuple-element.251), channel_id=1, source_target_pairs={{0,1},{1,0},{2,3},{3,2},{4,5},{5,4},{6,7},{7,6},{8,9},{9,8},{10,11... | collective-permute-start | bytes 4915208 | tf_op jit(solution)/shard_map/ppermute | solution.py:497
  183.1 25.1 %collective-permute-start.16 = (bf16[1,400,1024]{2,1,0:T(8,128)(2,1)}, bf16[1,400,1024]{2,1,0:T(8,128)(2,1)}, u32[]{:S(2)}, u32[]{:S(2)}) collective-permute-start(bf16[1,400,1024]{2,1,0:T(8,128)(2,1)} %add_convert_fusion.2), channel_id=1, source_target_pairs={{0,2},{1,3},{2,0},{3,1},{4,6},{5,7},{6,4},{7,5},{8,10},{9,11},{10,... | collective-permute-start | bytes 2457608 | tf_op jit(solution)/shard_map/ppermute | solution.py:497
  184.7 23.5 %collective-permute-start.14 = (bf16[384,768]{1,0:T(8,128)(2,1)S(1)}, bf16[384,768]{1,0:T(8,128)(2,1)S(1)}, u32[]{:S(2)}, u32[]{:S(2)}) collective-permute-start(bf16[384,768]{1,0:T(8,128)(2,1)S(1)} %maximum_select_fusion.1), channel_id=1, source_target_pairs={{0,4},{4,0},{8,12},{12,8},{16,20},{20,16},{24,28},{28,24},{1,5},{5... | collective-permute-start | bytes 1769480 | tf_op jit(solution)/shard_map/ppermute | solution.py:497
  185.9 22.2 %collective-permute-start.15 = (f32[1536]{0:T(1024)S(1)}, f32[1536]{0:T(1024)S(1)}, u32[]{:S(2)}, u32[]{:S(2)}) collective-permute-start(f32[1536]{0:T(1024)S(1)} %concatenate.25), channel_id=1, source_target_pairs={{0,4},{4,0},{8,12},{12,8},{16,20},{20,16},{24,28},{28,24},{1,5},{5... | collective-permute-start | bytes 18440 | tf_op jit(solution)/shard_map/ppermute | solution.py:497
  186.7 49.4 %all-to-all-start.2 = ((bf16[8,96,768]{2,1,0:T(8,128)(2,1)}), bf16[8,96,768]{2,1,0:T(8,128)(2,1)S(1)}, u32[]{:S(2)}, u32[]{:S(2)}) async-start(bf16[8,96,768]{2,1,0:T(8,128)(2,1)} %bitcast.69), calls=%async_computation.2 | async-start | bytes 2359296 | tf_op jit(solution)/shard_map/all_to_all | solution.py:560
  208.1 0.6 copy-start.21
  208.1 10.4 %copy-start.9 = (bf16[384,768]{1,0:T(8,128)(2,1)}, bf16[384,768]{1,0:T(8,128)(2,1)S(1)}, u32[]{:S(2)}) copy-start(bf16[384,768]{1,0:T(8,128)(2,1)S(1)} %collective-permute-done.14) | copy-start | bytes 1769476
  212.1 6.9 %collective-permute-start.18 = (bf16[2,400,1024]{2,1,0:T(8,128)(2,1)}, bf16[2,400,1024]{2,1,0:T(8,128)(2,1)}, u32[]{:S(2)}, u32[]{:S(2)}) collective-permute-start(bf16[2,400,1024]{2,1,0:T(8,128)(2,1)} %get-tuple-element.264), channel_id=1, source_target_pairs={{0,1},{1,0},{2,3},{3,2},{4,5},{5,4},{6,7},{7,6},{8,9},{9,8},{10,11... | collective-permute-start | bytes 4915208 | tf_op jit(solution)/shard_map/ppermute | solution.py:497
  212.1 21.0 %collective-permute-start.21 = (bf16[1,400,1024]{2,1,0:T(8,128)(2,1)}, bf16[1,400,1024]{2,1,0:T(8,128)(2,1)}, u32[]{:S(2)}, u32[]{:S(2)}) collective-permute-start(bf16[1,400,1024]{2,1,0:T(8,128)(2,1)} %add_convert_fusion.1), channel_id=1, source_target_pairs={{0,2},{1,3},{2,0},{3,1},{4,6},{5,7},{6,4},{7,5},{8,10},{9,11},{10,... | collective-permute-start | bytes 2457608 | tf_op jit(solution)/shard_map/ppermute | solution.py:497
  212.6 6.4 %collective-permute-start.19 = (f32[1536]{0:T(1024)S(1)}, f32[1536]{0:T(1024)S(1)}, u32[]{:S(2)}, u32[]{:S(2)}) collective-permute-start(f32[1536]{0:T(1024)S(1)} %add.135), channel_id=1, source_target_pairs={{0,8},{4,12},{8,0},{12,4},{16,24},{20,28},{24,16},{28,20},{1,9},{5... | collective-permute-start | bytes 18440 | tf_op jit(solution)/shard_map/ppermute | solution.py:497
  221.6 6.3 %collective-permute-start.20 = (f32[1536]{0:T(1024)S(1)}, f32[1536]{0:T(1024)S(1)}, u32[]{:S(2)}, u32[]{:S(2)}) collective-permute-start(f32[1536]{0:T(1024)S(1)} %add.137), channel_id=1, source_target_pairs={{0,16},{4,20},{8,24},{12,28},{16,0},{20,4},{24,8},{28,12},{1,17},{... | collective-permute-start | bytes 18440 | tf_op jit(solution)/shard_map/ppermute | solution.py:497
  237.4 34.4 %all-to-all-start.3 = ((bf16[8,96,768]{2,1,0:T(8,128)(2,1)}), bf16[8,96,768]{2,1,0:T(8,128)(2,1)S(1)}, u32[]{:S(2)}, u32[]{:S(2)}) async-start(bf16[8,96,768]{2,1,0:T(8,128)(2,1)} %bitcast.29), calls=%async_computation.3 | async-start | bytes 2359296 | tf_op jit(solution)/shard_map/all_to_all | solution.py:560
  243.4 19.9 %collective-permute-start.22 = (bf16[1,400,1024]{2,1,0:T(8,128)(2,1)}, bf16[1,400,1024]{2,1,0:T(8,128)(2,1)}, u32[]{:S(2)}, u32[]{:S(2)}) collective-permute-start(bf16[1,400,1024]{2,1,0:T(8,128)(2,1)} %add_convert_fusion), channel_id=1, source_target_pairs={{0,2},{1,3},{2,0},{3,1},{4,6},{5,7},{6,4},{7,5},{8,10},{9,11},{10,... | collective-permute-start | bytes 2457608 | tf_op jit(solution)/shard_map/ppermute | solution.py:497
  243.9 1.6 copy-start.10
  245.5 3.1 %copy-start.25 = (bf16[192]{0:T(256)(128)(2,1)S(1)}, bf16[192]{0:T(256)(128)(2,1)}, u32[]{:S(2)}) copy-start(bf16[192]{0:T(256)(128)(2,1)} %param.14) | copy-start | bytes 1156

commit v2 on v1

--- a/solution.py
+++ b/solution.py
@@ -86,8 +86,8 @@
 
 
 def mlp_kernel(
-    place, own, flip_y, flip_c, flip_cy, gain_own, gain_y, gain_c, gain_cy, up_t, up_bias, d_act, cot,
-    normed, active, d_pre, stats, bias_sum, gain_all, down_grad, up_grad, low, high
+    pieces_order, place, own, flip_y, flip_c, flip_cy, gain_own, gain_y, gain_c, gain_cy, up_t, up_bias, d_act, cot, up,
+    normed, active, d_pre, stats, bias_sum, gain_all, up_row, grads, low, high
 ):
     pieces = (own, flip_y, flip_c, flip_cy)
     part = own.shape[0]
@@ -144,11 +144,15 @@
 
     @pl.when(last)
     def _():
-        down_grad[...] = low[...].astype(BF16)
-        up_grad[...] = high[...].astype(BF16)
-
-
-def mlp_call(place, pieces, gains, up_t, up_bias, d_act, cot, block=512):
+        up_row[...] = fold_lanes(high[...] * up[...].astype(F32))
+        half = low.shape[0]
+        size = grads.shape[0] // len(pieces_order)
+        for slot, piece in enumerate(pieces_order):
+            source, start = (low, piece * size) if piece * size < half else (high, piece * size - half)
+            grads[slot * size : (slot + 1) * size, :] = source[start : start + size, :].astype(BF16)
+
+
+def mlp_call(pieces_order, place, pieces, gains, up_t, up_bias, d_act, cot, up, block=512):
     part, tokens = pieces[0].shape
     width = 4 * part
     seqs, hidden, _ = d_act.shape
@@ -166,6 +170,7 @@
             pl.BlockSpec((hidden, 1), fixed),
             pl.BlockSpec((None, hidden, block), by_seq),
             pl.BlockSpec((block, width), lambda i, *_: (i, 0)),
+            pl.BlockSpec((width, hidden), fixed),
         ],
         out_specs=[
             pl.BlockSpec((None, width, block), by_seq),
@@ -174,13 +179,14 @@
             pl.BlockSpec((8, block), lanes),
             pl.BlockSpec((hidden, 128), fixed),
             pl.BlockSpec((width, 128), fixed),
-            pl.BlockSpec((hidden, width), fixed),
-            pl.BlockSpec((width, hidden), fixed),
+            pl.BlockSpec((width, 128), fixed),
+            pl.BlockSpec((hidden + width, width), fixed),
         ],
         scratch_shapes=[pltpu.VMEM((hidden, width), F32), pltpu.VMEM((width, hidden), F32)],
     )
+    assert hidden == width
     return pl.pallas_call(
-        mlp_kernel,
+        functools.partial(mlp_kernel, pieces_order),
         grid_spec=grid_spec,
         out_shape=[
             jax.ShapeDtypeStruct((seqs, width, LEN), BF16),
@@ -189,12 +195,12 @@
             jax.ShapeDtypeStruct((8, tokens), F32),
             jax.ShapeDtypeStruct((hidden, 128), F32),
             jax.ShapeDtypeStruct((width, 128), F32),
-            jax.ShapeDtypeStruct((hidden, width), BF16),
-            jax.ShapeDtypeStruct((width, hidden), BF16),
+            jax.ShapeDtypeStruct((width, 128), F32),
+            jax.ShapeDtypeStruct((hidden + width, width), BF16),
         ],
         cost_estimate=cost(20, 30_000_000),
         name="mlp",
-    )(place, *pieces, *gains, up_t, up_bias, d_act, cot)
+    )(place, *pieces, *gains, up_t, up_bias, d_act, cot, up)
 
 
 def attention_kernel(last, seq, first, count, normed, mixed_t, d_att, mask_q, mask_k, gains, cot_hbm, *rest):
@@ -501,49 +507,36 @@
     return lax.optimization_barrier(trees)
 
 
+def piece_order(size):
+    bits = size.bit_length() - 1
+    return [sum(((i >> b) & 1) << (bits - 1 - b) for b in range(bits)) for i in range(size)]
+
+
 class SumOverDp:
-    def __init__(self, value, size, index, turn):
+    def __init__(self, value, size, index):
         self.size, self.index = size, index
-        bits = [1 << i for i in range(size.bit_length() - 1)]
-        bits = bits[turn:] + bits[:turn]
-        self.steps = [("sum", bit) for bit in bits] + [("join", bit) for bit in reversed(bits)]
-        self.prepare(value, None)
-
-    def prepare(self, held, arrived):
-        def part(which, half):
-            rows = lax.dynamic_slice_in_dim(held, which * half, half, 0)
-            if arrived is None:
-                return rows
-            came = lax.dynamic_slice_in_dim(arrived, which * half, half, 0)
-            return (rows.astype(F32) + came.astype(F32)).astype(BF16)
-
-        rows = held.shape[0]
-        if self.steps and self.steps[0][0] == "sum":
-            side = self.side(self.steps[0][1])
-            self.send, self.keep = part(1 - side, rows // 2), part(side, rows // 2)
-        else:
-            self.keep = part(0, rows)
-            self.send = self.keep
-
-    def side(self, bit):
-        return (self.index & bit) // bit
+        self.send = value
+        self.steps = ["sum"] + [1 << i for i in reversed(range(size.bit_length() - 1))]
 
     def more(self):
         return bool(self.steps)
 
     def move(self, send):
-        return flip(send, "dp", self.size, self.steps[0][1])
+        if self.steps[0] == "sum":
+            return lax.all_to_all(send, "dp", 0, 0, tiled=True)
+        return flip(send, "dp", self.size, self.steps[0])
 
     def take(self, arrived):
-        kind, bit = self.steps.pop(0)
-        if kind == "sum":
-            self.prepare(self.keep, arrived)
-            return
-        self.keep = jnp.where(
-            self.side(bit) == 1,
-            jnp.concatenate([arrived, self.keep], axis=0),
-            jnp.concatenate([self.keep, arrived], axis=0),
-        )
+        step = self.steps.pop(0)
+        if step == "sum":
+            shares = arrived.reshape(self.size, -1, arrived.shape[1]).astype(F32)
+            self.keep = jnp.sum(shares, axis=0).astype(BF16)
+        else:
+            self.keep = jnp.where(
+                (self.index & step) > 0,
+                jnp.concatenate([arrived, self.keep], axis=0),
+                jnp.concatenate([self.keep, arrived], axis=0),
+            )
         self.send = self.keep
 
 
@@ -688,32 +681,27 @@
         gain_bias, gain_col,
     ) = prepared
     pieces = (own_t, from_y, flip(own_t, "mp", 4, 1), flip(from_y, "mp", 4, 1))
-    normed, active, d_pre, stats, upbias_part, gain_all, down_part, up_part = mlp_call(
-        place, pieces, gains, up_t, up_bias_col, d_act, cotangent
+    normed, active, d_pre, stats, upbias_part, gain_all, up_row, mlp_part = mlp_call(
+        tuple(piece_order(dp_size)), place, pieces, gains, up_t, up_bias_col, d_act, cotangent, up_weight
     )
-    down_sum = SumOverDp(down_part, dp_size, dp, 0)
-    up_sum = SwapOverDp(up_part, dp_size)
+    mlp_sum = SumOverDp(mlp_part, dp_size, dp)
 
     heads_out = []
     before = ()
     qk_part = 0.0
-    held = []
+    (states,), flights = launch([mlp_sum], (normed,))
     for seq in range(seqs):
-        along = [down_sum] + ([up_sum] if not held else [])
-        (states, before), flights = launch(along, (normed, before))
         *out, qk, norm_row, total = attention_call(
             first[seq], count[seq], states, mixed_t, d_att, mask_q, mask_k, head_gains, cotangent, before, seq,
             seq == seqs - 1,
         )
-        ending = held + [f for f in flights if f[0] is down_sum]
-        held = [f for f in flights if f[0] is up_sum]
-        out, qk, norm_row, total = land(ending, (out, qk, norm_row, total))
         heads_out.append(out)
         before = (total,)
         qk_part = qk_part + qk
+    heads_out, before, qk_part, norm_row = land(flights, (heads_out, before, qk_part, norm_row))
     mix_sum = SwapOverDp(before[0], dp_size)
 
-    norm_vec = norm_row[0] + jnp.sum(up_part.astype(F32) * up_weight.astype(F32), axis=1)
+    norm_vec = norm_row[0] + jnp.sum(up_row, axis=1)
     norm_parts = norm_vec.reshape(4, part)
     norm_parts = [lax.dynamic_index_in_dim(norm_parts, jnp.bitwise_xor(me, m), 0, False) for m in range(4)]
     short = ShortSums(
@@ -732,16 +720,17 @@
     scatters = []
     mixing = []
     for seq in range(seqs):
-        along = [down_sum, short] + [m for m in scatters if m.more()]
+        along = [mlp_sum, short] + [m for m in scatters if m.more()]
         if seq == 0:
             along.append(mix_sum)
         work, flights = launch(along, heads_out[seq])
         keep, send = project(seq, work)
-        now = [f for f in flights if f[0] is not mix_sum]
-        mixing += [f for f in flights if f[0] is mix_sum]
-        if seq == 1:
-            now += held
-            held = []
+        later = [f for f in flights if f[0] is mix_sum or f[0] is mlp_sum and seq == 2]
+        now = [f for f in flights if f not in later]
+        if seq == 2:
+            now += mixing
+            mixing = []
+        mixing += later
         keep, send = land(now, (keep, send))
         scatters.append(ScatterOverMp(keep, send))
 
@@ -758,19 +747,19 @@
                 )
         return finished
 
-    flying = held + mixing
+    flying = mixing
     while True:
         busy = [f[0] for f in flying]
-        ready = [m for m in scatters + [down_sum, short, up_sum, mix_sum] if m.more() and m not in busy]
+        ready = [m for m in scatters + [short, mlp_sum, mix_sum] if m.more() and m not in busy]
         finished, flights = launch(ready, finished)
         flying = flying + flights
         if not flying:
             break
         finished = finish_ready(finished)
         small = [f for f in flying if f[0] is short or f[0] in scatters and len(f[0].bits) == 2]
-        sums = [f for f in flying if f[0] in (mix_sum, up_sum, down_sum)]
+        sums = [f for f in flying if f[0] in (mix_sum, mlp_sum)]
         moving = [f for f in flying if f[0] in scatters and len(f[0].bits) == 1]
-        first_swap = [f for f in sums if len(f[0].steps) == 2]
+        first_swap = [f for f in sums if f[0] is mlp_sum or len(f[0].steps) == 2]
         if small:
             now = small
         elif moving and (len(moving) > 1 or not first_swap):
@@ -795,9 +784,9 @@
         qkv_grad,
         rest[: 2 * part].reshape(2, part),
         mixed_grad[3 * part :],
-        up_sum.keep.astype(F32),
+        mlp_sum.keep[up_weight.shape[1] :].astype(F32),
         rest[2 * part : split],
-        down_sum.keep.astype(F32),
+        mlp_sum.keep[: up_weight.shape[1]].astype(F32),
         rest[split:],
     )
 

time: 275 us -> 260 us (0.945)
  waiting for transfers between devices: 56.1 us -> 34.2 us
  starting transfers between devices: 43.8 us -> 57 us
  Pallas kernels: 128 us -> 125 us
    ppermute x23 -> x20, waiting for transfers between devices: 48.7 us -> 33 us  [flip(): return lax.ppermute(value, axis, [(i, i ^ bit) for i in range(size)])]
    ppermute x23 -> x20, starting transfers between devices: 24.1 us -> 33.4 us  [flip(): return lax.ppermute(value, axis, [(i, i ^ bit) for i in range(size)])]
    all_to_all x4 -> x3, waiting for transfers between devices: 7.34 us -> 1.26 us  [move(): return lax.all_to_all(send, 'dp', 0, 0, tiled=True)]
    convert_element_type x5 -> x1, other arithmetic: 7.29 us -> 2.55 us  [body(): mlp_sum.keep[:up_weight.shape[1]].astype(F32)]
    all_to_all x4 -> x3, starting transfers between devices: 19.7 us -> 23.6 us  [move(): return lax.all_to_all(send, 'dp', 0, 0, tiled=True)]
    pallas_call x3, Pallas kernels: 54.5 us -> 50.9 us  [attention_call(): pl.pallas_call(functools.partial(attention_kernel, last, seq), grid_spec=...]
    unnamed x63 -> x53, local copies, waits for them, and re-layouts: 5.08 us -> 6.7 us
  transfers between devices with their start and end apart: 27 -> 23, of which waited for: 11 -> 8; matrix products, arithmetic and copies ran while one was open for 11% -> 12% of each run, Pallas kernels for 38% -> 39%
where the time goes in v2:
time: 260 us; the launch traced here: 259 us
  Pallas kernels  125 us (48%)
  starting transfers between devices  57 us (22%)
  waiting for transfers between devices  34.2 us (13%)
  other arithmetic  21.4 us (8%)
  local copies, waits for them, and re-layouts  19.8 us (8%)
    pallas_call x3, Pallas kernels, attention_call(): pl.pallas_call(functools.partial(attention_kernel, last, seq), grid_spec=...  50.9 us
    ppermute x20, starting transfers between devices, flip(): return lax.ppermute(value, axis, [(i, i ^ bit) for i in range(size)])  33.4 us
    ppermute x20, waiting for transfers between devices, flip(): return lax.ppermute(value, axis, [(i, i ^ bit) for i in range(size)])  33 us
    pallas_call x3, Pallas kernels, project_call(): pl.pallas_call(project_kernel, grid_spec=grid_spec, out_shape=[jax.ShapeD...  29.4 us
    pallas_call x1, Pallas kernels, mlp_call(): pl.pallas_call(functools.partial(mlp_kernel, pieces_order), grid_spec=gri...  24.1 us
    all_to_all x3, starting transfers between devices, move(): return lax.all_to_all(send, 'dp', 0, 0, tiled=True)  23.6 us
    pallas_call x1, Pallas kernels, early_call(): pl.pallas_call(early_kernel, grid=(tokens // block,), in_specs=[pl.BlockS...  11.4 us
    pallas_call x3, Pallas kernels, finish_call(): pl.pallas_call(finish_kernel, grid=(steps,), in_specs=[packed, packed, pa...  9.25 us
  transfers between devices with their start and end apart: 23, of which 8 were waited for; matrix products, arithmetic and copies ran while one was open for 12% of the time, Pallas kernels for 39%

profile of v2, /device:TPU:0, one launch (start us, length us, event | category | flops | bytes accessed | tf_op | source)
XLA Modules:
  0.0 258.5 jit_solution(7754110791181124313)
XLA Ops:
  0.6 3.0 %collective-permute-start = (bf16[192,3072]{1,0:T(8,128)(2,1)}, bf16[192,3072]{1,0:T(8,128)(2,1)S(1)}, u32[]{:S(2)}, u32[]{:S(2)}) collective-permute-start(bf16[192,3072]{1,0:T(8,128)(2,1)} %bitcast.39), channel_id=1, source_target_pairs={{0,2},{1,3},{2,0},{3,1},{4,6},{5,7},{6,4},{7,5},{8,10},{9,11},{10,... | collective-permute-start | bytes 3538952 | tf_op jit(solution)/shard_map/ppermute | solution.py:503
  3.7 0.8 fusion.pick
  4.5 11.4 %early.1 = (bf16[3,768,1024]{2,1,0:T(8,128)(2,1)}, bf16[3,192,1024]{2,1,0:T(8,128)(2,1)}, bf16[192,3072]{1,0:T(8,128)(2,1)}, f32[192,128]{1,0:T(8,128)}) custom-call(bf16[3072,768]{1,0:T(8,128)(2,1)} %cot_hbm.5, bf16[768,768]{1,0:T(8,128)(2,1)} %down.1, bf16[192,768]{1,0:T(8,128)(2,1)} %attn.1, bf16[192,768]{1,0:T(8,128)(2,1)} %fusion.pick), custom_call_target="tpu_custom_call" | custom-call | flops 10000 | bytes 12000 | tf_op jit(solution)/shard_map/early/pallas_call | solution.py:62
  16.0 0.7 slice.86
  16.6 0.7 slice.87
  17.3 1.5 copy.49
  18.8 0.9 copy.50
  19.7 1.4 copy.47
  21.1 1.5 copy.48
  24.1 0.7 fusion.2.mask_q
  24.8 0.7 select_convert_fusion.mask_k
  25.5 4.4 %collective-permute-done.flip_y = bf16[192,3072]{1,0:T(8,128)(2,1)S(1)} collective-permute-done((bf16[192,3072]{1,0:T(8,128)(2,1)}, bf16[192,3072]{1,0:T(8,128)(2,1)S(1)}, u32[]{:S(2)}, u32[]{:S(2)}) %collective-permute-start) | collective-permute-done | bytes 1179680 | tf_op jit(solution)/shard_map/ppermute | solution.py:503
  30.0 1.8 collective-permute-start.3
  32.0 2.2 collective-permute-done.3.gain_y
  34.7 0.9 copy.51.up_bias
  36.3 1.0 copy-done.4
  37.3 24.1 %mlp.1 = (bf16[3,768,1024]{2,1,0:T(8,128)(2,1)}, bf16[3,768,1024]{2,1,0:T(8,128)(2,1)}, bf16[3,768,1024]{2,1,0:T(8,128)(2,1)}, f32[8,3072]{1,0:T(8,128)}, f32[76...) custom-call(s32[4]{0:T(128)} %xor_multiply_fusion.place, ...), custom_call_target="tpu_custom_call" | custom-call | flops 20000 | bytes 30000 | tf_op jit(solution)/shard_map/mlp/pallas_call | solution.py:188
  61.4 6.0 %all-to-all-start = ((bf16[8,192,768]{2,1,0:T(8,128)(2,1)}), bf16[8,192,768]{2,1,0:T(8,128)(2,1)S(1)}, u32[]{:S(2)}, u32[]{:S(2)}) async-start(bf16[8,192,768]{2,1,0:T(8,128)(2,1)} %bitcast.63), calls=%async_computation | async-start | bytes 4718592 | tf_op jit(solution)/shard_map/all_to_all | solution.py:526
  67.5 0.8 copy.52.gains
  68.3 0.6 slice_bitcast_fusion
  68.9 19.3 %attention.3 = (bf16[192,1024]{1,0:T(8,128)(2,1)}, bf16[576,1024]{1,0:T(8,128)(2,1)}, f32[384,128]{1,0:T(8,128)}, f32[1,768]{1,0:T(1,128)}, f32[768,768]{1,0:T(8,128)}) custom-call(s32[4]{0:T(128)} %get-tuple-element.296.first, s32[4]{0:T(128)} %get-tuple-element.292.count, bf16[3,768,1024]{2,1,0:T(8,128)(2,1)} %get-tuple-element.154.normed, ...), custom_call_target="tpu_custom_call" | custom-call | flops 18000 | bytes 5000 | tf_op jit(solution)/shard_map/attention/pallas_call | solution.py:370
  88.2 15.8 %attention.4 = (bf16[192,1024]{1,0:T(8,128)(2,1)}, bf16[576,1024]{1,0:T(8,128)(2,1)}, f32[384,128]{1,0:T(8,128)}, f32[1,768]{1,0:T(1,128)}, f32[768,768]{1,0:T(8,128)}) custom-call(s32[4]{0:T(128)} %get-tuple-element.297.first, s32[4]{0:T(128)} %get-tuple-element.291.count, bf16[3,768,1024]{2,1,0:T(8,128)(2,1)} %get-tuple-element.154.normed, ...), custom_call_target="tpu_custom_call" | custom-call | flops 18000 | bytes 5000 | tf_op jit(solution)/shard_map/attention/pallas_call | solution.py:370
  104.0 15.8 %attention.5 = (bf16[192,1024]{1,0:T(8,128)(2,1)}, bf16[576,1024]{1,0:T(8,128)(2,1)}, f32[384,128]{1,0:T(8,128)}, f32[1,768]{1,0:T(1,128)}, bf16[768,768]{1,0:T(8,128)(2,1)}) custom-call(s32[4]{0:T(128)} %get-tuple-element.298.first, s32[4]{0:T(128)} %get-tuple-element.290.count, bf16[3,768,1024]{2,1,0:T(8,128)(2,1)} %get-tuple-element.154.normed, ...), custom_call_target="tpu_custom_call" | custom-call | flops 18000 | bytes 5000 | tf_op jit(solution)/shard_map/attention/pallas_call | solution.py:370
  120.1 1.0 add_add_fusion
  121.1 0.9 all-to-all-done
  122.0 0.7 reduce.2
  123.2 5.7 %collective-permute-start.6 = (bf16[192,768]{1,0:T(8,128)(2,1)S(1)}, bf16[192,768]{1,0:T(8,128)(2,1)S(1)}, u32[]{:S(2)}, u32[]{:S(2)}) collective-permute-start(bf16[192,768]{1,0:T(8,128)(2,1)S(1)} %reduce_sum.82), channel_id=1, source_target_pairs={{0,16},{4,20},{8,24},{12,28},{16,0},{20,4},{24,8},{28,12},{1,17},{... | collective-permute-start | bytes 884744 | tf_op jit(solution)/shard_map/ppermute | solution.py:503
  128.9 9.9 %project.3 = (bf16[2,400,1024]{2,1,0:T(8,128)(2,1)}, bf16[2,400,1024]{2,1,0:T(8,128)(2,1)}) custom-call(s32[1]{0:T(128)} %bitcast.shard, bf16[3,768,1024]{2,1,0:T(8,128)(2,1)} %get-tuple-element.149.active, bf16[192,1024]{1,0:T(8,128)(2,1)} %get-tuple-element.184.attended, bf16[3,768,1024]{2,1,0:T(8,128)(2,1)} %get-tuple-element.185.d_pre, ...), custom_call_target="tpu_custom_call" | custom-call | flops 8000 | bytes 16000 | tf_op jit(solution)/shard_map/project/pallas_call | solution.py:445
  138.8 3.5 %collective-permute-done.6 = bf16[192,768]{1,0:T(8,128)(2,1)S(1)} collective-permute-done((bf16[192,768]{1,0:T(8,128)(2,1)S(1)}, bf16[192,768]{1,0:T(8,128)(2,1)S(1)}, u32[]{:S(2)}, u32[]{:S(2)}) %collective-permute-start.6) | collective-permute-done | bytes 294944 | tf_op jit(solution)/shard_map/ppermute | solution.py:503
  142.6 0.8 collective-permute-start.8
  143.4 1.5 collective-permute-start.9
  145.4 5.6 %all-to-all-start.1 = ((bf16[8,96,768]{2,1,0:T(8,128)(2,1)}), bf16[8,96,768]{2,1,0:T(8,128)(2,1)S(1)}, u32[]{:S(2)}, u32[]{:S(2)}) async-start(bf16[8,96,768]{2,1,0:T(8,128)(2,1)} %bitcast.22), calls=%async_computation.1 | async-start | bytes 2359296 | tf_op jit(solution)/shard_map/all_to_all | solution.py:553
  151.0 9.8 %project.4 = (bf16[2,400,1024]{2,1,0:T(8,128)(2,1)}, bf16[2,400,1024]{2,1,0:T(8,128)(2,1)}) custom-call(s32[1]{0:T(128)} %bitcast.shard, bf16[3,768,1024]{2,1,0:T(8,128)(2,1)} %get-tuple-element.149.active, bf16[192,1024]{1,0:T(8,128)(2,1)} %get-tuple-element.198.attended, bf16[3,768,1024]{2,1,0:T(8,128)(2,1)} %get-tuple-element.185.d_pre, ...), custom_call_target="tpu_custom_call" | custom-call | flops 8000 | bytes 16000 | tf_op jit(solution)/shard_map/project/pallas_call | solution.py:445
  161.3 2.6 %add_convert_fusion.2 = bf16[1,400,1024]{2,1,0:T(8,128)(2,1)} fusion(bf16[2,400,1024]{2,1,0:T(8,128)(2,1)} %collective-permute-done.10.from_core, bf16[2,400,1024]{2,1,0:T(8,128)(2,1)} %get-tuple-element.210.keep), kind=kLoop, calls=%fused_computation.3 | loop fusion | flops 1638400 | bytes 2457600 | tf_op jit(solution)/shard_map/convert_element_type | solution.py:579
  164.4 5.8 %collective-permute-start.11 = (f32[1536]{0:T(1024)S(1)}, f32[1536]{0:T(1024)S(1)}, u32[]{:S(2)}, u32[]{:S(2)}) collective-permute-start(f32[1536]{0:T(1024)S(1)} %concatenate.25), channel_id=1, source_target_pairs={{0,4},{4,0},{8,12},{12,8},{16,20},{20,16},{24,28},{28,24},{1,5},{5... | collective-permute-start | bytes 18440 | tf_op jit(solution)/shard_map/ppermute | solution.py:503
  170.2 9.7 %project.5 = (bf16[2,400,1024]{2,1,0:T(8,128)(2,1)}, bf16[2,400,1024]{2,1,0:T(8,128)(2,1)}) custom-call(s32[1]{0:T(128)} %bitcast.shard, bf16[3,768,1024]{2,1,0:T(8,128)(2,1)} %get-tuple-element.149.active, bf16[192,1024]{1,0:T(8,128)(2,1)} %get-tuple-element.213.attended, bf16[3,768,1024]{2,1,0:T(8,128)(2,1)} %get-tuple-element.185.d_pre, ...), custom_call_target="tpu_custom_call" | custom-call | flops 8000 | bytes 16000 | tf_op jit(solution)/shard_map/project/pallas_call | solution.py:445
  180.3 4.6 %collective-permute-done.12.from_y = bf16[1,400,1024]{2,1,0:T(8,128)(2,1)} collective-permute-done((bf16[1,400,1024]{2,1,0:T(8,128)(2,1)}, bf16[1,400,1024]{2,1,0:T(8,128)(2,1)}, u32[]{:S(2)}, u32[]{:S(2)}) %collective-permute-start.12) | collective-permute-done | bytes 819232 | tf_op jit(solution)/shard_map/ppermute | solution.py:503
  185.1 2.6 %add_convert_fusion.1 = bf16[1,400,1024]{2,1,0:T(8,128)(2,1)} fusion(bf16[2,400,1024]{2,1,0:T(8,128)(2,1)} %collective-permute-done.13.from_core, bf16[2,400,1024]{2,1,0:T(8,128)(2,1)} %get-tuple-element.229.keep), kind=kLoop, calls=%fused_computation.2 | loop fusion | flops 1638400 | bytes 2457600 | tf_op jit(solution)/shard_map/convert_element_type | solution.py:579
  187.7 1.1 broadcast_in_dim.58
  188.8 4.7 %collective-permute-start.18 = (bf16[768,768]{1,0:T(8,128)(2,1)S(1)}, bf16[768,768]{1,0:T(8,128)(2,1)S(1)}, u32[]{:S(2)}, u32[]{:S(2)}) collective-permute-start(bf16[768,768]{1,0:T(8,128)(2,1)S(1)} %maximum_select_fusion.1), channel_id=1, source_target_pairs={{0,4},{4,0},{8,12},{12,8},{16,20},{20,16},{24,28},{28,24},{1,5},{5... | collective-permute-start | bytes 3538952 | tf_op jit(solution)/shard_map/ppermute | solution.py:503
  193.5 12.0 %all-to-all-start.2 = ((bf16[8,96,768]{2,1,0:T(8,128)(2,1)}), bf16[8,96,768]{2,1,0:T(8,128)(2,1)S(1)}, u32[]{:S(2)}, u32[]{:S(2)}) async-start(bf16[8,96,768]{2,1,0:T(8,128)(2,1)} %bitcast.26), calls=%async_computation.2 | async-start | bytes 2359296 | tf_op jit(solution)/shard_map/all_to_all | solution.py:553
  205.5 1.7 collective-permute-start.17
  207.3 2.0 collective-permute-start.15
  209.3 1.4 copy.55.gain
  210.8 1.5 copy.56.bias
  212.2 3.1 %finish.3 = (bf16[192,3072]{1,0:T(8,128)(2,1)}, f32[192,3072]{1,0:T(8,128)}) custom-call(bf16[2,400,1024]{2,1,0:T(8,128)(2,1)} %get-tuple-element.210.keep, bf16[2,400,1024]{2,1,0:T(8,128)(2,1)} %collective-permute-done.10.from_core, bf16[1,400,1024]{2,1,0:T(8,128)(2,1)} %collective-permute-done.12.from_y, bf16[192,3072]{1,0:T(8,128)(2,1)} %bitcast.42, ...), custom_call_target="tpu_custom_call" | custom-call | flops 3000 | bytes 5000 | tf_op jit(solution)/shard_map/finish/pallas_call | solution.py:480
  215.3 10.9 %collective-permute-done.15 = f32[1536]{0:T(1024)S(1)} collective-permute-done((f32[1536]{0:T(1024)S(1)}, f32[1536]{0:T(1024)S(1)}, u32[]{:S(2)}, u32[]{:S(2)}) %collective-permute-start.15) | collective-permute-done | bytes 6176 | tf_op jit(solution)/shard_map/ppermute | solution.py:503
  226.2 0.6 copy-done.17
  226.8 0.7 add.82
  227.5 2.6 %add_convert_fusion = bf16[1,400,1024]{2,1,0:T(8,128)(2,1)} fusion(bf16[2,400,1024]{2,1,0:T(8,128)(2,1)} %collective-permute-done.14.from_core, bf16[2,400,1024]{2,1,0:T(8,128)(2,1)} %get-tuple-element.221.keep), kind=kLoop, calls=%fused_computation.1 | loop fusion | flops 1638400 | bytes 2457600 | tf_op jit(solution)/shard_map/convert_element_type | solution.py:579
  230.1 3.8 %collective-permute-start.16 = (f32[1536]{0:T(1024)S(1)}, f32[1536]{0:T(1024)S(1)}, u32[]{:S(2)}, u32[]{:S(2)}) collective-permute-start(f32[1536]{0:T(1024)S(1)} %add.82), channel_id=1, source_target_pairs={{0,16},{4,20},{8,24},{12,28},{16,0},{20,4},{24,8},{28,12},{1,17},{... | collective-permute-start | bytes 18440 | tf_op jit(solution)/shard_map/ppermute | solution.py:503
  233.9 1.7 collective-permute-start.19
  235.7 0.6 copy-done.16
  236.2 3.1 %finish.4 = (bf16[192,3072]{1,0:T(8,128)(2,1)}, f32[192,3072]{1,0:T(8,128)}) custom-call(bf16[2,400,1024]{2,1,0:T(8,128)(2,1)} %get-tuple-element.229.keep, bf16[2,400,1024]{2,1,0:T(8,128)(2,1)} %collective-permute-done.13.from_core, bf16[1,400,1024]{2,1,0:T(8,128)(2,1)} %collective-permute-done.17.from_y, ...), custom_call_target="tpu_custom_call", output_to_operand_aliasing={{0}: (8, {}), {1}: (9, {})} | custom-call | flops 3000 | bytes 5000 | tf_op jit(solution)/shard_map/finish/pallas_call | solution.py:480
  239.3 0.7 add.83
  240.1 0.7 slice.118
  240.8 0.7 slice.105
  241.4 1.3 fusion.8
  242.7 0.6 maximum_select_fusion
  243.3 2.5 slice_convert_fusion
  245.9 7.3 %collective-permute-done.19.from_y = bf16[1,400,1024]{2,1,0:T(8,128)(2,1)} collective-permute-done((bf16[1,400,1024]{2,1,0:T(8,128)(2,1)}, bf16[1,400,1024]{2,1,0:T(8,128)(2,1)}, u32[]{:S(2)}, u32[]{:S(2)}) %collective-permute-start.19) | collective-permute-done | bytes 819232 | tf_op jit(solution)/shard_map/ppermute | solution.py:503
  253.2 3.1 %finish.5 = (bf16[192,3072]{1,0:T(8,128)(2,1)}, f32[192,3072]{1,0:T(8,128)}) custom-call(bf16[2,400,1024]{2,1,0:T(8,128)(2,1)} %get-tuple-element.221.keep, bf16[2,400,1024]{2,1,0:T(8,128)(2,1)} %collective-permute-done.14.from_core, bf16[1,400,1024]{2,1,0:T(8,128)(2,1)} %collective-permute-done.19.from_y, ...), custom_call_target="tpu_custom_call", output_to_operand_aliasing={{0}: (8, {}), {1}: (9, {})} | custom-call | flops 3000 | bytes 5000 | tf_op jit(solution)/shard_map/finish/pallas_call | solution.py:480
  256.3 1.3 slice.114
  257.6 0.9 slice.116
  (101 shorter events, 6.2 us)
Async XLA Ops:
  0.6 29.2 %collective-permute-start = (bf16[192,3072]{1,0:T(8,128)(2,1)}, bf16[192,3072]{1,0:T(8,128)(2,1)S(1)}, u32[]{:S(2)}, u32[]{:S(2)}) collective-permute-start(bf16[192,3072]{1,0:T(8,128)(2,1)} %bitcast.39), channel_id=1, source_target_pairs={{0,2},{1,3},{2,0},{3,1},{4,6},{5,7},{6,4},{7,5},{8,10},{9,11},{10,... | collective-permute-start | bytes 3538952 | tf_op jit(solution)/shard_map/ppermute | solution.py:503
  3.7 32.0 %collective-permute-start.1 = (bf16[192,3072]{1,0:T(8,128)(2,1)}, bf16[192,3072]{1,0:T(8,128)(2,1)}, u32[]{:S(2)}, u32[]{:S(2)}) collective-permute-start(bf16[192,3072]{1,0:T(8,128)(2,1)} %bitcast.40), channel_id=1, source_target_pairs={{0,1},{1,0},{2,3},{3,2},{4,5},{5,4},{6,7},{7,6},{8,9},{9,8},{10,11... | collective-permute-start | bytes 3538952 | tf_op jit(solution)/shard_map/ppermute | solution.py:503
  4.5 11.4 %copy-start.11 = (s32[3,1024]{1,0:T(4,128)S(1)}, s32[3,1024]{1,0:T(4,128)}, u32[]{:S(2)}) copy-start(s32[3,1024]{1,0:T(4,128)} %param.13) | copy-start | bytes 36868
  4.5 12.8 %copy-start.2 = (bf16[768,768]{1,0:T(8,128)(2,1)S(1)}, bf16[768,768]{1,0:T(8,128)(2,1)}, u32[]{:S(2)}) copy-start(bf16[768,768]{1,0:T(8,128)(2,1)} %down.1) | copy-start | bytes 3538948
  15.9 2.8 %copy-start.5 = (bf16[192,768]{1,0:T(8,128)(2,1)S(1)}, bf16[192,768]{1,0:T(8,128)(2,1)}, u32[]{:S(2)}) copy-start(bf16[192,768]{1,0:T(8,128)(2,1)} %attn.1) | copy-start | bytes 884740
  15.9 3.7 %copy-start.1 = (bf16[768,3,192]{0,2,1:T(8,128)(2,1)S(1)}, bf16[768,3,192]{0,2,1:T(8,128)(2,1)}, u32[]{:S(2)}) copy-start(bf16[768,3,192]{0,2,1:T(8,128)(2,1)} %param.15) | copy-start | bytes 2654212
  18.8 2.3 copy-start
  21.1 1.5 copy-start.21
  21.1 1.5 copy-start.22
  21.1 1.6 copy-start.20
  21.1 2.2 copy-start.23
  21.1 2.7 %copy-start.18 = (s32[3,4]{1,0:T(4,128)S(1)}, s32[3,4]{1,0:T(4,128)}, u32[]{:S(2)}) copy-start(s32[3,4]{1,0:T(4,128)} %slice.86) | copy-start | bytes 148
  21.1 2.7 %copy-start.19 = (s32[3,4]{1,0:T(4,128)S(1)}, s32[3,4]{1,0:T(4,128)}, u32[]{:S(2)}) copy-start(s32[3,4]{1,0:T(4,128)} %slice.87) | copy-start | bytes 148
  21.1 13.1 %copy-start.24 = (s32[4]{0:T(128)S(1)}, s32[4]{0:T(128)}, u32[]{:S(2)}) copy-start(s32[4]{0:T(128)} %constant.67.clone) | copy-start | bytes 52
  29.9 5.8 %copy-start.3 = (bf16[192,3072]{1,0:T(8,128)(2,1)}, bf16[192,3072]{1,0:T(8,128)(2,1)S(1)}, u32[]{:S(2)}) copy-start(bf16[192,3072]{1,0:T(8,128)(2,1)S(1)} %collective-permute-done.flip_y) | copy-start | bytes 3538948
  29.9 5.8 %collective-permute-start.2 = (bf16[192,3072]{1,0:T(8,128)(2,1)S(1)}, bf16[192,3072]{1,0:T(8,128)(2,1)S(1)}, u32[]{:S(2)}, u32[]{:S(2)}) collective-permute-start(bf16[192,3072]{1,0:T(8,128)(2,1)S(1)} %collective-permute-done.flip_y), channel_id=1, source_target_pairs={{0,1},{1,0},{2,3},{3,2},{4,5},{5,4},{6,7},{7,6},{8,9},{9,8},{10,11... | collective-permute-start | bytes 3538952 | tf_op jit(solution)/shard_map/ppermute | solution.py:503
  30.0 5.8 %copy-start.8 = (bf16[192,128]{1,0:T(8,128)(2,1)}, bf16[192,128]{1,0:T(8,128)(2,1)S(1)}, u32[]{:S(2)}) copy-start(bf16[192,128]{1,0:T(8,128)(2,1)S(1)} %broadcast_in_dim.57.gain_own) | copy-start | bytes 147460
  30.0 4.2 %collective-permute-start.3 = (bf16[192,128]{1,0:T(8,128)(2,1)S(1)}, bf16[192,128]{1,0:T(8,128)(2,1)S(1)}, u32[]{:S(2)}, u32[]{:S(2)}) collective-permute-start(bf16[192,128]{1,0:T(8,128)(2,1)S(1)} %broadcast_in_dim.57.gain_own), channel_id=1, source_target_pairs={{0,2},{1,3},{2,0},{3,1},{4,6},{5,7},{6,4},{7,5},{8,10},{9,11},{10,... | collective-permute-start | bytes 147464 | tf_op jit(solution)/shard_map/ppermute | solution.py:503
  31.8 3.9 %collective-permute-start.4 = (bf16[192,128]{1,0:T(8,128)(2,1)S(1)}, bf16[192,128]{1,0:T(8,128)(2,1)S(1)}, u32[]{:S(2)}, u32[]{:S(2)}) collective-permute-start(bf16[192,128]{1,0:T(8,128)(2,1)S(1)} %broadcast_in_dim.57.gain_own), channel_id=1, source_target_pairs={{0,1},{1,0},{2,3},{3,2},{4,5},{5,4},{6,7},{7,6},{8,9},{9,8},{10,11... | collective-permute-start | bytes 147464 | tf_op jit(solution)/shard_map/ppermute | solution.py:503
  34.2 1.5 copy-start.13
  34.2 1.5 collective-permute-start.5
  35.7 0.6 copy-start.14
  35.7 0.6 copy-start.15
  36.3 1.0 copy-start.4
  61.4 60.6 %all-to-all-start = ((bf16[8,192,768]{2,1,0:T(8,128)(2,1)}), bf16[8,192,768]{2,1,0:T(8,128)(2,1)S(1)}, u32[]{:S(2)}, u32[]{:S(2)}) async-start(bf16[8,192,768]{2,1,0:T(8,128)(2,1)} %bitcast.63), calls=%async_computation | async-start | bytes 4718592 | tf_op jit(solution)/shard_map/all_to_all | solution.py:526
  104.0 15.9 %copy-start.7 = (f32[768,128]{1,0:T(8,128)S(1)}, f32[768,128]{1,0:T(8,128)}, u32[]{:S(2)}) copy-start(f32[768,128]{1,0:T(8,128)} %get-tuple-element.182) | copy-start | bytes 1179652
  104.0 16.1 %copy-start.9 = (f32[384,128]{1,0:T(8,128)S(1)}, f32[384,128]{1,0:T(8,128)}, u32[]{:S(2)}) copy-start(f32[384,128]{1,0:T(8,128)} %get-tuple-element.169) | copy-start | bytes 589828
  104.0 16.1 %copy-start.10 = (f32[384,128]{1,0:T(8,128)S(1)}, f32[384,128]{1,0:T(8,128)}, u32[]{:S(2)}) copy-start(f32[384,128]{1,0:T(8,128)} %get-tuple-element.170) | copy-start | bytes 589828
  123.2 19.1 %collective-permute-start.6 = (bf16[192,768]{1,0:T(8,128)(2,1)S(1)}, bf16[192,768]{1,0:T(8,128)(2,1)S(1)}, u32[]{:S(2)}, u32[]{:S(2)}) collective-permute-start(bf16[192,768]{1,0:T(8,128)(2,1)S(1)} %reduce_sum.82), channel_id=1, source_target_pairs={{0,16},{4,20},{8,24},{12,28},{16,0},{20,4},{24,8},{28,12},{1,17},{... | collective-permute-start | bytes 884744 | tf_op jit(solution)/shard_map/ppermute | solution.py:503
  128.9 9.9 %collective-permute-start.7 = (f32[2,192]{1,0:T(2,128)S(1)}, f32[2,192]{1,0:T(2,128)S(1)}, u32[]{:S(2)}, u32[]{:S(2)}) collective-permute-start(f32[2,192]{1,0:T(2,128)S(1)} %pad_maximum_fusion), channel_id=1, source_target_pairs={{0,1},{1,0},{2,3},{3,2},{4,5},{5,4},{6,7},{7,6},{8,9},{9,8},{10,11... | collective-permute-start | bytes 4616 | tf_op jit(solution)/shard_map/ppermute | solution.py:503
  128.9 16.0 %copy-start.12 = (f32[192,128]{1,0:T(8,128)S(1)}, f32[192,128]{1,0:T(8,128)}, u32[]{:S(2)}) copy-start(f32[192,128]{1,0:T(8,128)} %get-tuple-element.209) | copy-start | bytes 294916
  128.9 16.2 %copy-start.6 = (f32[768,128]{1,0:T(8,128)S(1)}, f32[768,128]{1,0:T(8,128)}, u32[]{:S(2)}) copy-start(f32[768,128]{1,0:T(8,128)} %get-tuple-element.208) | copy-start | bytes 1179652
  142.6 18.2 %collective-permute-start.10 = (bf16[2,400,1024]{2,1,0:T(8,128)(2,1)}, bf16[2,400,1024]{2,1,0:T(8,128)(2,1)}, u32[]{:S(2)}, u32[]{:S(2)}) collective-permute-start(bf16[2,400,1024]{2,1,0:T(8,128)(2,1)} %get-tuple-element.204), channel_id=1, source_target_pairs={{0,1},{1,0},{2,3},{3,2},{4,5},{5,4},{6,7},{7,6},{8,9},{9,8},{10,11... | collective-permute-start | bytes 4915208 | tf_op jit(solution)/shard_map/ppermute | solution.py:503
  142.6 18.1 %collective-permute-start.8 = (bf16[384,768]{1,0:T(8,128)(2,1)S(1)}, bf16[384,768]{1,0:T(8,128)(2,1)S(1)}, u32[]{:S(2)}, u32[]{:S(2)}) collective-permute-start(bf16[384,768]{1,0:T(8,128)(2,1)S(1)} %maximum_select_fusion.2), channel_id=1, source_target_pairs={{0,8},{4,12},{8,0},{12,4},{16,24},{20,28},{24,16},{28,20},{1,9},{5... | collective-permute-start | bytes 1769480 | tf_op jit(solution)/shard_map/ppermute | solution.py:503
  143.4 17.3 %collective-permute-start.9 = (f32[192]{0:T(256)S(1)}, f32[192]{0:T(256)S(1)}, u32[]{:S(2)}, u32[]{:S(2)}) collective-permute-start(f32[192]{0:T(256)S(1)} %bitcast.68), channel_id=1, source_target_pairs={{0,2},{1,3},{2,0},{3,1},{4,6},{5,7},{6,4},{7,5},{8,10},{9,11},{10,... | collective-permute-start | bytes 2312 | tf_op jit(solution)/shard_map/ppermute | solution.py:503
  145.4 34.9 %all-to-all-start.1 = ((bf16[8,96,768]{2,1,0:T(8,128)(2,1)}), bf16[8,96,768]{2,1,0:T(8,128)(2,1)S(1)}, u32[]{:S(2)}, u32[]{:S(2)}) async-start(bf16[8,96,768]{2,1,0:T(8,128)(2,1)} %bitcast.22), calls=%async_computation.1 | async-start | bytes 2359296 | tf_op jit(solution)/shard_map/all_to_all | solution.py:553
  163.9 21.0 %collective-permute-start.13 = (bf16[2,400,1024]{2,1,0:T(8,128)(2,1)}, bf16[2,400,1024]{2,1,0:T(8,128)(2,1)}, u32[]{:S(2)}, u32[]{:S(2)}) collective-permute-start(bf16[2,400,1024]{2,1,0:T(8,128)(2,1)} %get-tuple-element.219), channel_id=1, source_target_pairs={{0,1},{1,0},{2,3},{3,2},{4,5},{5,4},{6,7},{7,6},{8,9},{9,8},{10,11... | collective-permute-start | bytes 4915208 | tf_op jit(solution)/shard_map/ppermute | solution.py:503
  163.9 21.0 %collective-permute-start.12 = (bf16[1,400,1024]{2,1,0:T(8,128)(2,1)}, bf16[1,400,1024]{2,1,0:T(8,128)(2,1)}, u32[]{:S(2)}, u32[]{:S(2)}) collective-permute-start(bf16[1,400,1024]{2,1,0:T(8,128)(2,1)} %add_convert_fusion.2), channel_id=1, source_target_pairs={{0,2},{1,3},{2,0},{3,1},{4,6},{5,7},{6,4},{7,5},{8,10},{9,11},{10,... | collective-permute-start | bytes 2457608 | tf_op jit(solution)/shard_map/ppermute | solution.py:503
  164.4 15.5 %collective-permute-start.11 = (f32[1536]{0:T(1024)S(1)}, f32[1536]{0:T(1024)S(1)}, u32[]{:S(2)}, u32[]{:S(2)}) collective-permute-start(f32[1536]{0:T(1024)S(1)} %concatenate.25), channel_id=1, source_target_pairs={{0,4},{4,0},{8,12},{12,8},{16,20},{20,16},{24,28},{28,24},{1,5},{5... | collective-permute-start | bytes 18440 | tf_op jit(solution)/shard_map/ppermute | solution.py:503
  188.8 38.0 %collective-permute-start.14 = (bf16[2,400,1024]{2,1,0:T(8,128)(2,1)}, bf16[2,400,1024]{2,1,0:T(8,128)(2,1)}, u32[]{:S(2)}, u32[]{:S(2)}) collective-permute-start(bf16[2,400,1024]{2,1,0:T(8,128)(2,1)} %get-tuple-element.234), channel_id=1, source_target_pairs={{0,1},{1,0},{2,3},{3,2},{4,5},{5,4},{6,7},{7,6},{8,9},{9,8},{10,11... | collective-permute-start | bytes 4915208 | tf_op jit(solution)/shard_map/ppermute | solution.py:503
  188.8 52.0 %collective-permute-start.18 = (bf16[768,768]{1,0:T(8,128)(2,1)S(1)}, bf16[768,768]{1,0:T(8,128)(2,1)S(1)}, u32[]{:S(2)}, u32[]{:S(2)}) collective-permute-start(bf16[768,768]{1,0:T(8,128)(2,1)S(1)} %maximum_select_fusion.1), channel_id=1, source_target_pairs={{0,4},{4,0},{8,12},{12,8},{16,20},{20,16},{24,28},{28,24},{1,5},{5... | collective-permute-start | bytes 3538952 | tf_op jit(solution)/shard_map/ppermute | solution.py:503
  193.5 62.8 %all-to-all-start.2 = ((bf16[8,96,768]{2,1,0:T(8,128)(2,1)}), bf16[8,96,768]{2,1,0:T(8,128)(2,1)S(1)}, u32[]{:S(2)}, u32[]{:S(2)}) async-start(bf16[8,96,768]{2,1,0:T(8,128)(2,1)} %bitcast.26), calls=%async_computation.2 | async-start | bytes 2359296 | tf_op jit(solution)/shard_map/all_to_all | solution.py:553
  205.5 30.1 %collective-permute-start.17 = (bf16[1,400,1024]{2,1,0:T(8,128)(2,1)}, bf16[1,400,1024]{2,1,0:T(8,128)(2,1)}, u32[]{:S(2)}, u32[]{:S(2)}) collective-permute-start(bf16[1,400,1024]{2,1,0:T(8,128)(2,1)} %add_convert_fusion.1), channel_id=1, source_target_pairs={{0,2},{1,3},{2,0},{3,1},{4,6},{5,7},{6,4},{7,5},{8,10},{9,11},{10,... | collective-permute-start | bytes 2457608 | tf_op jit(solution)/shard_map/ppermute | solution.py:503
  207.3 18.9 %collective-permute-start.15 = (f32[1536]{0:T(1024)S(1)}, f32[1536]{0:T(1024)S(1)}, u32[]{:S(2)}, u32[]{:S(2)}) collective-permute-start(f32[1536]{0:T(1024)S(1)} %add.80), channel_id=1, source_target_pairs={{0,8},{4,12},{8,0},{12,4},{16,24},{20,28},{24,16},{28,20},{1,9},{5... | collective-permute-start | bytes 18440 | tf_op jit(solution)/shard_map/ppermute | solution.py:503
  226.2 0.6 copy-start.17
  230.1 5.5 %collective-permute-start.16 = (f32[1536]{0:T(1024)S(1)}, f32[1536]{0:T(1024)S(1)}, u32[]{:S(2)}, u32[]{:S(2)}) collective-permute-start(f32[1536]{0:T(1024)S(1)} %add.82), channel_id=1, source_target_pairs={{0,16},{4,20},{8,24},{12,28},{16,0},{20,4},{24,8},{28,12},{1,17},{... | collective-permute-start | bytes 18440 | tf_op jit(solution)/shard_map/ppermute | solution.py:503
  233.9 19.3 %collective-permute-start.19 = (bf16[1,400,1024]{2,1,0:T(8,128)(2,1)}, bf16[1,400,1024]{2,1,0:T(8,128)(2,1)}, u32[]{:S(2)}, u32[]{:S(2)}) collective-permute-start(bf16[1,400,1024]{2,1,0:T(8,128)(2,1)} %add_convert_fusion), channel_id=1, source_target_pairs={{0,2},{1,3},{2,0},{3,1},{4,6},{5,7},{6,4},{7,5},{8,10},{9,11},{10,... | collective-permute-start | bytes 2457608 | tf_op jit(solution)/shard_map/ppermute | solution.py:503
  235.6 0.6 copy-start.16

commit v3 on v2

--- a/solution.py
+++ b/solution.py
@@ -123,7 +123,7 @@
     c1 = 0.044715 * c0
     def lift(start):
         here = slice(start, start + 256)
-        return dot(up_t[here, :], normed[...]) + up_bias[here, :]
+        return dot(up_t[here, :], normed[...]) + up_bias[here, :1].astype(F32)
 
     ahead = lift(0)
     for start in range(0, up_t.shape[0], 256):
@@ -167,7 +167,7 @@
         + [pl.BlockSpec((part, 128), fixed)] * 4
         + [
             pl.BlockSpec((hidden, width), fixed),
-            pl.BlockSpec((hidden, 1), fixed),
+            pl.BlockSpec((hidden, 128), fixed),
             pl.BlockSpec((None, hidden, block), by_seq),
             pl.BlockSpec((block, width), lambda i, *_: (i, 0)),
             pl.BlockSpec((width, hidden), fixed),
@@ -203,21 +203,20 @@
     )(place, *pieces, *gains, up_t, up_bias, d_act, cot, up)
 
 
-def attention_kernel(last, seq, first, count, normed, mixed_t, d_att, mask_q, mask_k, gains, cot_hbm, *rest):
-    if seq:
-        before_hbm, rest = rest[0], rest[1:]
-    (
-        attended, d_mixed, gain_sum, norm_row, grads, qkv, qx, kx, vn, kt, vt, es, ps, oa, dqa, dka, dva, cot, before, cot_sem,
-        before_sem,
-    ) = rest
+def attention_kernel(
+    first, count, normed, mixed_t, d_att, mask_q, mask_k, gains, cot, attended, d_mixed, gain_sum, norm_row, grads,
+    total, qkv, qx, kx, vn, kt, vt, es, ps, oa, dqa, dka, dva
+):
+    seq = pl.program_id(0)
+    last = seq == pl.num_programs(0) - 1
     part = attended.shape[0]
     heads = part // DH
     inv_dh = 1.0 / DH
-    copies = [pltpu.make_async_copy(cot_hbm.at[pl.ds(seq * LEN, LEN), :], cot, cot_sem)]
-    if seq:
-        copies.append(pltpu.make_async_copy(before_hbm, before, before_sem))
-    for copy in copies:
-        copy.start()
+
+    @pl.when(seq == 0)
+    def _():
+        total[...] = jnp.zeros_like(total)
+        gain_sum[...] = jnp.zeros_like(gain_sum)
 
     qkv[...] = dot(mixed_t[...], normed[...])
 
@@ -231,10 +230,10 @@
     for head in range(heads):
         rows = slice(head * DH, (head + 1) * DH)
         query, _ = unit(head * DH)
-        query = (query * (gains[rows, :] * 0.125)).astype(BF16)
+        query = (query * (gains[rows, :1] * 0.125)).astype(BF16)
         qx[head] = jnp.concatenate([query, mask_q[...], zeros], axis=0)
         key, _ = unit(part + head * DH)
-        key = (key * gains[part + head * DH : part + (head + 1) * DH, :]).astype(BF16)
+        key = (key * gains[part + head * DH : part + (head + 1) * DH, :1]).astype(BF16)
         kt[rows, :] = key
         kx[head] = jnp.concatenate([key, mask_k[...], zeros], axis=0).T
         value = qkv[2 * part + head * DH : 2 * part + (head + 1) * DH, :].astype(BF16)
@@ -246,8 +245,8 @@
     def query_block(ib, _):
         i0 = pl.multiple_of(ib * BI, BI)
         icols = pl.ds(i0, BI)
-        base = first[ib]
-        trips = count[ib]
+        base = first[seq * (LEN // BI) + ib]
+        trips = count[seq * (LEN // BI) + ib]
 
         def scores(j, carry):
             j0 = pl.multiple_of((base + j) * BJ, BJ)
@@ -299,56 +298,50 @@
             start = offset + head * DH
             u, scale = unit(start)
             e = source[head * DH : (head + 1) * DH, :] * factor
-            gain_sum[start : start + DH, :] = fold_lanes(e * u)
-            f = e * gains[start : start + DH, :]
+            gain_sum[start : start + DH, :] += fold_lanes(e * u)
+            f = e * gains[start : start + DH, :1]
             mean_f = jnp.sum(f, axis=0, keepdims=True) * inv_dh
             mean_fu = jnp.sum(f * u, axis=0, keepdims=True) * inv_dh
             d_mixed[start : start + DH, :] = ((f - mean_f - u * mean_fu) * scale).astype(BF16)
     d_mixed[2 * part :, :] = dva[...].astype(BF16)
 
-    for copy in copies:
-        copy.wait()
     split = 3 * part
-    for rows, value in (
-        (slice(0, split), dot(d_mixed[...], normed[...], NT)),
-        (slice(split, split + part), dot(attended[...], cot[...])),
-    ):
-        if seq:
-            value = value + before[rows, :]
-        if last and rows.start == 0:
-            norm_row[...] = jnp.sum(value * mixed_t[...].astype(F32), axis=0, keepdims=True)
-        grads[rows, :] = value.astype(grads.dtype)
-    if not last:
-        norm_row[...] = jnp.zeros_like(norm_row)
-
-
-def attention_call(first, count, normed, mixed_t, d_att, mask_q, mask_k, gains, cot, before, seq, last):
+    total[:split, :] += dot(d_mixed[...], normed[...], NT)
+    total[split:, :] += dot(attended[...], cot[...])
+
+    @pl.when(last)
+    def _():
+        norm_row[...] = jnp.sum(total[:split, :] * mixed_t[...].astype(F32), axis=0, keepdims=True)
+        grads[...] = total[...].astype(BF16)
+
+
+def attention_call(first, count, normed, mixed_t, d_att, mask_q, mask_k, gains, cot):
     seqs, part, _ = d_att.shape
     width = normed.shape[1]
     heads = part // DH
-    once = lambda i, *_: (0, 0)
-    ours = lambda i, *_: (seq, 0, 0)
+    fixed = lambda i, *_: (0, 0)
+    by_seq = lambda i, *_: (i, 0, 0)
     grid_spec = pltpu.PrefetchScalarGridSpec(
         num_scalar_prefetch=2,
-        grid=(1,),
+        grid=(seqs,),
         in_specs=[
-            pl.BlockSpec((None, width, LEN), ours),
-            pl.BlockSpec((3 * part, width), once),
-            pl.BlockSpec((None, part, LEN), ours),
-            pl.BlockSpec((None, IMAGE_SLOTS, LEN), ours),
-            pl.BlockSpec((None, IMAGE_SLOTS, LEN), ours),
-            pl.BlockSpec((2 * part, 1), once),
-            ANY,
-        ]
-        + [ANY] * len(before),
+            pl.BlockSpec((None, width, LEN), by_seq),
+            pl.BlockSpec((3 * part, width), fixed),
+            pl.BlockSpec((None, part, LEN), by_seq),
+            pl.BlockSpec((None, IMAGE_SLOTS, LEN), by_seq),
+            pl.BlockSpec((None, IMAGE_SLOTS, LEN), by_seq),
+            pl.BlockSpec((2 * part, 128), fixed),
+            pl.BlockSpec((LEN, width), lambda i, *_: (i, 0)),
+        ],
         out_specs=[
-            pl.BlockSpec((part, LEN), once),
-            pl.BlockSpec((3 * part, LEN), once),
-            pl.BlockSpec((2 * part, 128), once),
-            pl.BlockSpec((1, width), once),
-            pl.BlockSpec((4 * part, width), once),
+            pl.BlockSpec((None, part, LEN), by_seq),
+            pl.BlockSpec((None, 3 * part, LEN), by_seq),
+            pl.BlockSpec((2 * part, 128), fixed),
+            pl.BlockSpec((1, width), fixed),
+            pl.BlockSpec((4 * part, width), fixed),
         ],
         scratch_shapes=[
+            pltpu.VMEM((4 * part, width), F32),
             pltpu.VMEM((3 * part, LEN), F32),
             pltpu.VMEM((heads, 128, LEN), BF16),
             pltpu.VMEM((heads, LEN, 128), BF16),
@@ -361,25 +354,21 @@
             pltpu.VMEM((part, LEN), F32),
             pltpu.VMEM((part, LEN), F32),
             pltpu.VMEM((part, LEN), F32),
-            pltpu.VMEM((LEN, width), BF16),
-            pltpu.VMEM((4 * part, width), F32),
-            pltpu.SemaphoreType.DMA(()),
-            pltpu.SemaphoreType.DMA(()),
         ],
     )
     return pl.pallas_call(
-        functools.partial(attention_kernel, last, seq),
+        attention_kernel,
         grid_spec=grid_spec,
         out_shape=[
-            jax.ShapeDtypeStruct((part, LEN), BF16),
-            jax.ShapeDtypeStruct((3 * part, LEN), BF16),
+            jax.ShapeDtypeStruct((seqs, part, LEN), BF16),
+            jax.ShapeDtypeStruct((seqs, 3 * part, LEN), BF16),
             jax.ShapeDtypeStruct((2 * part, 128), F32),
             jax.ShapeDtypeStruct((1, width), F32),
-            jax.ShapeDtypeStruct((4 * part, width), BF16 if last else F32),
+            jax.ShapeDtypeStruct((4 * part, width), BF16),
         ],
         cost_estimate=cost(18, 5_000_000),
         name="attention",
-    )(first, count, normed, mixed_t, d_att, mask_q, mask_k, gains, cot, *before)
+    )(first, count, normed, mixed_t, d_att, mask_q, mask_k, gains, cot)
 
 
 def project_kernel(
@@ -414,22 +403,22 @@
             send[slot, part : 2 * part, :] = grad[rows].astype(BF16)
 
 
-def project_call(shard, active, attended, d_pre, d_mixed, normed, down_t, attn_t, up, mixed, gain, seq, block=256):
+def project_call(shard, active, attended, d_pre, d_mixed, normed, down_t, attn_t, up, mixed, gain, begin, size, block=256):
     width, hidden = down_t.shape
-    part = attended.shape[0]
+    part = attended.shape[1]
     steps = LEN // block
-    lanes = lambda i, *_: (0, i)
-    ours = lambda i, *_: (seq, 0, i)
+    ours = lambda i, *_: (begin + i // steps, 0, i % steps)
+    out = lambda i, *_: (i // steps, 0, 0, i % steps)
     fixed = lambda i, *_: (0, 0)
     rows = 2 * part + SUM_ROWS
     grid_spec = pltpu.PrefetchScalarGridSpec(
         num_scalar_prefetch=1,
-        grid=(steps,),
+        grid=(size * steps,),
         in_specs=[
             pl.BlockSpec((None, hidden, block), ours),
-            pl.BlockSpec((part, block), lanes),
+            pl.BlockSpec((None, part, block), ours),
             pl.BlockSpec((None, hidden, block), ours),
-            pl.BlockSpec((3 * part, block), lanes),
+            pl.BlockSpec((None, 3 * part, block), ours),
             pl.BlockSpec((None, width, block), ours),
             pl.BlockSpec((width, hidden), fixed),
             pl.BlockSpec((width, part), fixed),
@@ -438,16 +427,16 @@
             pl.BlockSpec((width, 128), fixed),
         ],
         out_specs=[
-            pl.BlockSpec((2, rows, block), lambda i, *_: (0, 0, i)),
-            pl.BlockSpec((2, rows, block), lambda i, *_: (0, 0, i)),
+            pl.BlockSpec((None, 2, rows, block), out),
+            pl.BlockSpec((None, 2, rows, block), out),
         ],
     )
     return pl.pallas_call(
         project_kernel,
         grid_spec=grid_spec,
         out_shape=[
-            jax.ShapeDtypeStruct((2, rows, LEN), BF16),
-            jax.ShapeDtypeStruct((2, rows, LEN), BF16),
+            jax.ShapeDtypeStruct((size, 2, rows, LEN), BF16),
+            jax.ShapeDtypeStruct((size, 2, rows, LEN), BF16),
         ],
         cost_estimate=cost(8, 16_000_000),
         name="project",
@@ -460,32 +449,33 @@
     inv_width = 0.25 / part
     total = keep[...].astype(F32) + from_core[...].astype(F32) + from_y[...].astype(F32)
     own = own_t[...].astype(F32)
-    block_out[...] = (own + total[:part] + bias[...]).astype(BF16)
+    block_out[...] = (own + total[:part] + bias[:, :1].astype(F32)).astype(BF16)
     grad = total[part : 2 * part]
     sums = total[2 * part :]
     mean = stats[0:1, :]
     scale = stats[1:2, :]
     hat = (own - mean) * scale
-    inner = grad * gain[...] - (sums[0:1] + sums[1:2]) * inv_width - hat * ((sums[2:3] + sums[3:4]) * inv_width)
+    inner = grad * gain[:, :1].astype(F32) - (sums[0:1] + sums[1:2]) * inv_width - hat * ((sums[2:3] + sums[3:4]) * inv_width)
     token_grad[...] = cot[...].astype(F32) + inner * scale
 
 
-def finish_call(keep, from_core, from_y, own_t, cot, stats, gain, bias, before, seq, block=512):
+def finish_call(keep, from_core, from_y, own_t, cot, stats, gain, bias, before, begin, block=512):
     part, tokens = own_t.shape
     steps = LEN // block
+    size = keep.shape[0]
     fixed = lambda i: (0, 0)
-    packed = pl.BlockSpec((None, 2 * part + SUM_ROWS, block), lambda i: (0, 0, i))
-    ours = lambda i: (0, seq * steps + i)
+    packed = pl.BlockSpec((None, None, 2 * part + SUM_ROWS, block), lambda i: (i // steps, 0, 0, i % steps))
+    ours = lambda i: (0, begin * steps + i)
     here = pl.BlockSpec((part, block), ours)
     return pl.pallas_call(
         finish_kernel,
-        grid=(steps,),
+        grid=(size * steps,),
         in_specs=[
             packed, packed, packed,
             here, here,
             pl.BlockSpec((8, block), ours),
-            pl.BlockSpec((part, 1), fixed),
-            pl.BlockSpec((part, 1), fixed),
+            pl.BlockSpec((part, 128), fixed),
+            pl.BlockSpec((part, 128), fixed),
         ]
         + [ANY] * len(before),
         out_specs=[here, here],
@@ -540,25 +530,46 @@
         self.send = self.keep
 
 
-class SwapOverDp:
-    def __init__(self, value, size):
-        self.size = size
-        self.send = value
-        self.steps = ["sum", "join"]
+class ChainOverDp:
+    def __init__(self, value, size, index):
+        self.size, self.index = size, index
+        bits = [1 << i for i in range(size.bit_length() - 1)]
+        self.steps = [("sum", bit) for bit in bits] + [("join", bit) for bit in reversed(bits)]
+        self.prepare(value, None)
+
+    def prepare(self, held, arrived):
+        def part(which, half):
+            rows = lax.dynamic_slice_in_dim(held, which * half, half, 0)
+            if arrived is None:
+                return rows
+            came = lax.dynamic_slice_in_dim(arrived, which * half, half, 0)
+            return (rows.astype(F32) + came.astype(F32)).astype(BF16)
+
+        rows = held.shape[0]
+        if self.steps and self.steps[0][0] == "sum":
+            side = ((self.index & self.steps[0][1]) > 0).astype(jnp.int32)
+            self.send, self.keep = part(1 - side, rows // 2), part(side, rows // 2)
+        else:
+            self.keep = part(0, rows)
+            self.send = self.keep
 
     def more(self):
         return bool(self.steps)
 
     def move(self, send):
-        return lax.all_to_all(send, "dp", 0, 0, tiled=True)
+        return flip(send, "dp", self.size, self.steps[0][1])
 
     def take(self, arrived):
-        if self.steps.pop(0) == "sum":
-            shares = arrived.reshape(self.size, -1, arrived.shape[1]).astype(F32)
-            total = jnp.sum(shares, axis=0).astype(BF16)
-            self.send = jnp.broadcast_to(total[None], (self.size,) + total.shape).reshape(arrived.shape)
-        else:
-            self.keep = arrived
+        kind, bit = self.steps.pop(0)
+        if kind == "sum":
+            self.prepare(self.keep, arrived)
+            return
+        self.keep = jnp.where(
+            (self.index & bit) > 0,
+            jnp.concatenate([arrived, self.keep], axis=0),
+            jnp.concatenate([self.keep, arrived], axis=0),
+        )
+        self.send = self.keep
 
 
 class ScatterOverMp:
@@ -576,7 +587,7 @@
         bit = self.bits.pop(0)
         if bit == 1:
             self.from_core = arrived
-            self.send = (self.keep[1].astype(F32) + arrived[1].astype(F32)).astype(BF16)[None]
+            self.send = (self.keep[:, 1:].astype(F32) + arrived[:, 1:].astype(F32)).astype(BF16)
         else:
             self.from_y = arrived
 
@@ -653,8 +664,11 @@
     up_t = up_weight.T
     down_t = down_weight.T
     attn_t = attn_weight.T
-    up_bias_col = up_bias.astype(F32)[:, None]
-    head_gains = qk_gain.astype(F32).reshape(2 * part, 1)
+    def column(vector):
+        return jnp.broadcast_to(vector[:, None], (vector.shape[0], 128))
+
+    up_bias_col = column(up_bias)
+    head_gains = column(qk_gain.astype(F32).reshape(2 * part))
 
     slots = jnp.arange(IMAGE_SLOTS, dtype=jnp.int32)[None, :, None]
     same = image_ids[:, None, :] == slots
@@ -664,21 +678,20 @@
     block_last = image_ids[:, BI - 1 :: BI]
     starts = jnp.sum(image_ids[:, None, :] < block_first[:, :, None], axis=2, dtype=jnp.int32)
     ends = jnp.sum(image_ids[:, None, :] <= block_last[:, :, None], axis=2, dtype=jnp.int32)
-    first = starts // BJ
-    count = (ends + BJ - 1) // BJ - first
+    first = (starts // BJ).reshape(-1)
+    count = ((ends + BJ - 1) // BJ).reshape(-1) - first
 
     pick = (jnp.arange(part)[:, None] + me * part == jnp.arange(width)[None, :]).astype(BF16)
     d_act, d_att, cot_own, cot_sum = early_call(cotangent, down_weight, attn_weight, pick)
-    gain_bias = down_bias.astype(F32)[:, None]
-    gain_col = norm_gain.astype(F32)[:, None]
+    bias_col = column(down_bias)
     prepared = (
         d_act, d_att, mixed_t, mixed, up_t, down_t, attn_t, up_bias_col, head_gains, mask_q, mask_k, first, count,
-        gain_bias, gain_col,
+        bias_col,
     )
     prepared, from_y = tie(prepared, from_y)
     (
         d_act, d_att, mixed_t, mixed, up_t, down_t, attn_t, up_bias_col, head_gains, mask_q, mask_k, first, count,
-        gain_bias, gain_col,
+        bias_col,
     ) = prepared
     pieces = (own_t, from_y, flip(own_t, "mp", 4, 1), flip(from_y, "mp", 4, 1))
     normed, active, d_pre, stats, upbias_part, gain_all, up_row, mlp_part = mlp_call(
@@ -686,20 +699,12 @@
     )
     mlp_sum = SumOverDp(mlp_part, dp_size, dp)
 
-    heads_out = []
-    before = ()
-    qk_part = 0.0
     (states,), flights = launch([mlp_sum], (normed,))
-    for seq in range(seqs):
-        *out, qk, norm_row, total = attention_call(
-            first[seq], count[seq], states, mixed_t, d_att, mask_q, mask_k, head_gains, cotangent, before, seq,
-            seq == seqs - 1,
-        )
-        heads_out.append(out)
-        before = (total,)
-        qk_part = qk_part + qk
-    heads_out, before, qk_part, norm_row = land(flights, (heads_out, before, qk_part, norm_row))
-    mix_sum = SwapOverDp(before[0], dp_size)
+    attended, d_mixed, qk_part, norm_row, mix_part = land(
+        flights,
+        attention_call(first, count, states, mixed_t, d_att, mask_q, mask_k, head_gains, cotangent),
+    )
+    mix_sum = ChainOverDp(mix_part, dp_size, dp)
 
     norm_vec = norm_row[0] + jnp.sum(up_row, axis=1)
     norm_parts = norm_vec.reshape(4, part)
@@ -711,43 +716,31 @@
         dp_size,
     )
 
-    def project(seq, work):
-        attended, d_mixed = work
-        return project_call(
-            shard, active, attended, d_pre, d_mixed, normed, down_t, attn_t, up_weight, mixed, gain_all, seq
+    runs = [(0, seqs - 1), (seqs - 1, 1)] if seqs > 1 else [(0, 1)]
+    scatters = []
+    for begin, size in runs:
+        along = [mix_sum, mlp_sum, short] + [m for m in scatters if m.more()]
+        (att, dm), flights = launch(along, (attended, d_mixed))
+        sent = project_call(
+            shard, active, att, d_pre, dm, normed, down_t, attn_t, up_weight, mixed, gain_all, begin, size
         )
-
-    scatters = []
-    mixing = []
-    for seq in range(seqs):
-        along = [mlp_sum, short] + [m for m in scatters if m.more()]
-        if seq == 0:
-            along.append(mix_sum)
-        work, flights = launch(along, heads_out[seq])
-        keep, send = project(seq, work)
-        later = [f for f in flights if f[0] is mix_sum or f[0] is mlp_sum and seq == 2]
-        now = [f for f in flights if f not in later]
-        if seq == 2:
-            now += mixing
-            mixing = []
-        mixing += later
-        keep, send = land(now, (keep, send))
+        keep, send = land(flights, sent)
         scatters.append(ScatterOverMp(keep, send))
 
     finished = ()
     done = set()
 
     def finish_ready(finished):
-        for seq, scatter in enumerate(scatters):
-            if not scatter.more() and seq not in done:
-                done.add(seq)
+        for (begin, _), scatter in zip(runs, scatters):
+            if not scatter.more() and begin not in done:
+                done.add(begin)
                 finished = finish_call(
-                    scatter.keep, scatter.from_core, scatter.from_y, own_t, cot_own, stats, gain_col, gain_bias,
-                    finished, seq,
+                    scatter.keep, scatter.from_core, scatter.from_y, own_t, cot_own, stats, gain_own, bias_col,
+                    finished, begin,
                 )
         return finished
 
-    flying = mixing
+    flying = []
     while True:
         busy = [f[0] for f in flying]
         ready = [m for m in scatters + [short, mlp_sum, mix_sum] if m.more() and m not in busy]
@@ -756,16 +749,20 @@
         if not flying:
             break
         finished = finish_ready(finished)
-        small = [f for f in flying if f[0] is short or f[0] in scatters and len(f[0].bits) == 2]
-        sums = [f for f in flying if f[0] in (mix_sum, mlp_sum)]
-        moving = [f for f in flying if f[0] in scatters and len(f[0].bits) == 1]
-        first_swap = [f for f in sums if f[0] is mlp_sum or len(f[0].steps) == 2]
-        if small:
-            now = small
-        elif moving and (len(moving) > 1 or not first_swap):
-            now = moving[:1]
+        near = [f for f in flying if f[0] in scatters and len(f[0].bits) == 2]
+        across = [f for f in flying if f[0] in scatters and len(f[0].bits) == 1]
+        chain = [f for f in flying if f[0] is mix_sum]
+        rest = [f for f in flying if f[0] is short]
+        wide = [f for f in flying if f[0] is mlp_sum]
+        left = len(mix_sum.steps)
+        if near:
+            now = near + chain + rest
+        elif left == 2:
+            now = chain + across[:1] + wide + rest
+        elif left == 1:
+            now = across[:1] + wide + rest or chain
         else:
-            now = first_swap or sums
+            now = chain + rest or flying
         finished = land(now, finished)
         flying = [f for f in flying if f not in now]
     finished = finish_ready(finished)

time: 260 us -> 253 us (0.973)
  starting transfers between devices: 57 us -> 28.3 us
  waiting for transfers between devices: 34.2 us -> 59.3 us
  other arithmetic: 21.4 us -> 29.3 us
  local copies, waits for them, and re-layouts: 19.8 us -> 13.6 us
  Pallas kernels: 125 us -> 120 us
    ppermute x20 -> x24, waiting for transfers between devices: 33 us -> 56.4 us  [flip(): return lax.ppermute(value, axis, [(i, i ^ bit) for i in range(size)])]
    all_to_all x3 -> x1, starting transfers between devices: 23.6 us -> 6.04 us  [move(): return lax.all_to_all(send, 'dp', 0, 0, tiled=True)]
    ppermute x20 -> x24, starting transfers between devices: 33.4 us -> 22.3 us  [flip(): return lax.ppermute(value, axis, [(i, i ^ bit) for i in range(size)])]
    optimization_barrier x4 -> x0, local copies, waits for them, and re-layouts: 4.66 us -> none  [tie(): return lax.optimization_barrier(trees)]
    select_n x3, other arithmetic: 1.26 us -> 5.91 us  [take(): jnp.where(self.index & step > 0, jnp.concatenate([arrived, self.keep], ax...]
    pallas_call x3 -> x2, Pallas kernels: 29.4 us -> 26.1 us  [project_call(): pl.pallas_call(project_kernel, grid_spec=grid_spec, out_shape=[jax.ShapeD...]
    convert_element_type x4 -> x6, other arithmetic: 8.39 us -> 10.8 us  [the longest x2 5.73 us: take(): (self.keep[:, 1:].astype(F32) + arrived[:, 1:].astype(F32)).astype(BF16)]
    pallas_call x6 -> x3, Pallas kernels: 60.2 us -> 58.4 us  [the longest x1 49.9 us: attention_call(): pl.pallas_call(attention_kernel, grid_spec=grid_spec, out_shape=[jax.Shap...]
  transfers between devices with their start and end apart: 23 -> 25, of which waited for: 8 -> 11; matrix products, arithmetic and copies ran while one was open for 12% -> 10% of each run, Pallas kernels for 39% -> 38%
where the time goes in v3:
time: 253 us; the launch traced here: 252 us
  Pallas kernels  120 us (47%)
  waiting for transfers between devices  59.3 us (23%)
  other arithmetic  29.3 us (12%)
  starting transfers between devices  28.3 us (11%)
  local copies, waits for them, and re-layouts  13.6 us (5%)
    ppermute x24, waiting for transfers between devices, flip(): return lax.ppermute(value, axis, [(i, i ^ bit) for i in range(size)])  56.4 us
    pallas_call x1, Pallas kernels, attention_call(): pl.pallas_call(attention_kernel, grid_spec=grid_spec, out_shape=[jax.Shap...  49.9 us
    pallas_call x2, Pallas kernels, project_call(): pl.pallas_call(project_kernel, grid_spec=grid_spec, out_shape=[jax.ShapeD...  26.1 us
    pallas_call x1, Pallas kernels, mlp_call(): pl.pallas_call(functools.partial(mlp_kernel, pieces_order), grid_spec=gri...  24.2 us
    ppermute x24, starting transfers between devices, flip(): return lax.ppermute(value, axis, [(i, i ^ bit) for i in range(size)])  22.3 us
    pallas_call x1, Pallas kernels, early_call(): pl.pallas_call(early_kernel, grid=(tokens // block,), in_specs=[pl.BlockS...  11.3 us
    pallas_call x2, Pallas kernels, finish_call(): pl.pallas_call(finish_kernel, grid=(size * steps,), in_specs=[packed, pac...  8.49 us
    all_to_all x1, starting transfers between devices, move(): return lax.all_to_all(send, 'dp', 0, 0, tiled=True)  6.04 us
  transfers between devices with their start and end apart: 25, of which 11 were waited for; matrix products, arithmetic and copies ran while one was open for 10% of the time, Pallas kernels for 38%

profile of v3, /device:TPU:0, one launch (start us, length us, event | category | flops | bytes accessed | tf_op | source)
XLA Modules:
  0.0 251.5 jit_solution(2917145997606454750)
XLA Ops:
  0.6 0.5 collective-permute-start.1
  1.2 2.6 %collective-permute-start = (bf16[192,3072]{1,0:T(8,128)(2,1)}, bf16[192,3072]{1,0:T(8,128)(2,1)}, u32[]{:S(2)}, u32[]{:S(2)}) collective-permute-start(bf16[192,3072]{1,0:T(8,128)(2,1)} %bitcast.22), channel_id=1, source_target_pairs={{0,2},{1,3},{2,0},{3,1},{4,6},{5,7},{6,4},{7,5},{8,10},{9,11},{10,... | collective-permute-start | bytes 3538952 | tf_op jit(solution)/shard_map/ppermute | solution.py:493
  3.8 0.8 fusion.1.pick
  4.6 11.3 %early.1 = (bf16[3,768,1024]{2,1,0:T(8,128)(2,1)}, bf16[3,192,1024]{2,1,0:T(8,128)(2,1)}, bf16[192,3072]{1,0:T(8,128)(2,1)}, f32[192,128]{1,0:T(8,128)}) custom-call(bf16[3072,768]{1,0:T(8,128)(2,1)} %cot.5, bf16[768,768]{1,0:T(8,128)(2,1)} %down.1, bf16[192,768]{1,0:T(8,128)(2,1)} %attn.1, bf16[192,768]{1,0:T(8,128)(2,1)} %fusion.1.pick), custom_call_target="tpu_custom_call" | custom-call | flops 10000 | bytes 12000 | tf_op jit(solution)/shard_map/early/pallas_call | solution.py:62
  16.1 0.9 copy.36
  17.0 1.4 copy.35
  19.0 1.4 copy.33
  20.4 1.5 copy.34
  21.9 0.5 fusion.4
  22.4 0.7 fusion.3.mask_q
  23.1 0.7 select_convert_fusion.mask_k
  23.8 6.8 %collective-permute-done.flip_y = bf16[192,3072]{1,0:T(8,128)(2,1)} collective-permute-done((bf16[192,3072]{1,0:T(8,128)(2,1)}, bf16[192,3072]{1,0:T(8,128)(2,1)}, u32[]{:S(2)}, u32[]{:S(2)}) %collective-permute-start) | collective-permute-done | bytes 1179680 | tf_op jit(solution)/shard_map/ppermute | solution.py:493
  30.6 0.7 broadcast_in_dim.54.bias
  31.3 0.8 broadcast_in_dim.27.gains
  32.1 0.8 broadcast_in_dim.24.up_bias
  33.1 1.8 collective-permute-start.3
  35.1 2.2 collective-permute-done.3.gain_y
  37.9 0.7 collective-permute-done.5.gain_cy
  38.6 0.6 copy-done.19
  39.2 1.0 copy-done.7
  40.2 24.2 %mlp.1 = (bf16[3,768,1024]{2,1,0:T(8,128)(2,1)}, bf16[3,768,1024]{2,1,0:T(8,128)(2,1)}, bf16[3,768,1024]{2,1,0:T(8,128)(2,1)}, f32[8,3072]{1,0:T(8,128)}, f32[76...) custom-call(s32[4]{0:T(128)} %xor_multiply_fusion.place, ...), custom_call_target="tpu_custom_call" | custom-call | flops 20000 | bytes 30000 | tf_op jit(solution)/shard_map/mlp/pallas_call | solution.py:188
  64.4 6.0 %all-to-all-start = ((bf16[8,192,768]{2,1,0:T(8,128)(2,1)}), bf16[8,192,768]{2,1,0:T(8,128)(2,1)S(1)}, u32[]{:S(2)}, u32[]{:S(2)}) async-start(bf16[8,192,768]{2,1,0:T(8,128)(2,1)} %bitcast.34), calls=%async_computation | async-start | bytes 4718592 | tf_op jit(solution)/shard_map/all_to_all | solution.py:516
  70.4 49.9 %attention.1 = (bf16[3,192,1024]{2,1,0:T(8,128)(2,1)}, bf16[3,576,1024]{2,1,0:T(8,128)(2,1)}, f32[384,128]{1,0:T(8,128)}, f32[1,768]{1,0:T(1,128)}, bf16[768,768]{1,0:T(8,128)(2,1)}) custom-call(s32[12]{0:T(128)} %get-tuple-element.116.first, s32[12]{0:T(128)} %get-tuple-element.117.count, bf16[3,768,1024]{2,1,0:T(8,128)(2,1)} %get-tuple-element.120.normed, ...), custom_call_target="tpu_custom_call" | custom-call | flops 18000 | bytes 5000 | tf_op jit(solution)/shard_map/attention/pallas_call | solution.py:359
  120.3 1.3 reduce_sum.74
  121.7 2.9 %all-to-all-done = bf16[8,192,768]{2,1,0:T(8,128)(2,1)S(1)} async-done(((bf16[8,192,768]{2,1,0:T(8,128)(2,1)}), bf16[8,192,768]{2,1,0:T(8,128)(2,1)S(1)}, u32[]{:S(2)}, u32[]{:S(2)}) %all-to-all-start) | async-done | bytes 2359328 | tf_op jit(solution)/shard_map/all_to_all | solution.py:516
  124.6 0.7 reduce.1
  125.4 1.1 reduce_sum.73
  126.6 1.5 collective-permute-start.6
  128.1 16.2 %project.2 = (bf16[2,2,400,1024]{3,2,1,0:T(8,128)(2,1)}, bf16[2,2,400,1024]{3,2,1,0:T(8,128)(2,1)}) custom-call(s32[1]{0:T(128)} %bitcast.shard, bf16[3,768,1024]{2,1,0:T(8,128)(2,1)} %get-tuple-element.115.active, bf16[3,192,1024]{2,1,0:T(8,128)(2,1)} %get-tuple-element.154.attended, bf16[3,768,1024]{2,1,0:T(8,128)(2,1)} %get-tuple-element.139.d_pre, ...), custom_call_target="tpu_custom_call" | custom-call | flops 8000 | bytes 16000 | tf_op jit(solution)/shard_map/project/pallas_call | solution.py:434
  144.4 1.0 maximum_select_fusion.3
  145.4 1.0 add_convert_fusion.2
  146.9 2.0 collective-permute-start.10
  149.0 1.5 collective-permute-start.11
  150.5 1.0 reduce_sum.78
  151.9 9.9 %project.3 = (bf16[1,2,400,1024]{3,2,1,0:T(8,128)(2,1)}, bf16[1,2,400,1024]{3,2,1,0:T(8,128)(2,1)}) custom-call(s32[1]{0:T(128)} %bitcast.shard, bf16[3,768,1024]{2,1,0:T(8,128)(2,1)} %get-tuple-element.115.active, bf16[3,192,1024]{2,1,0:T(8,128)(2,1)} %get-tuple-element.154.attended, bf16[3,768,1024]{2,1,0:T(8,128)(2,1)} %get-tuple-element.139.d_pre, ...), custom_call_target="tpu_custom_call" | custom-call | flops 8000 | bytes 16000 | tf_op jit(solution)/shard_map/project/pallas_call | solution.py:434
  161.8 7.3 %collective-permute-done.9 = bf16[192,768]{1,0:T(8,128)(2,1)} collective-permute-done((bf16[192,768]{1,0:T(8,128)(2,1)}, bf16[192,768]{1,0:T(8,128)(2,1)}, u32[]{:S(2)}, u32[]{:S(2)}) %collective-permute-start.9) | collective-permute-done | bytes 294944 | tf_op jit(solution)/shard_map/ppermute | solution.py:493
  169.1 3.0 %maximum_select_fusion.1 = bf16[768,768]{1,0:T(8,128)(2,1)} fusion(bf16[384,768]{1,0:T(8,128)(2,1)} %maximum_select_fusion.3, bf16[384,768]{1,0:T(8,128)(2,1)} %collective-permute-done.10, pred[]{:T(512)S(6)} %gt.6), kind=kLoop, calls=%fused_computation.5 | loop fusion | flops 5308416 | bytes 2359297 | tf_op jit(solution)/shard_map/jit(_where)/select_n | solution.py:525
  172.1 3.4 %add_convert_fusion = bf16[2,1,400,1024]{3,2,1,0:T(8,128)(2,1)} fusion(bf16[2,2,400,1024]{3,2,1,0:T(8,128)(2,1)} %collective-permute-done.12.from_core, bf16[2,2,400,1024]{3,2,1,0:T(8,128)(2,1)S(1)} %copy-done.1), kind=kLoop, calls=%fused_computation | loop fusion | flops 3276800 | bytes 4915200 | tf_op jit(solution)/shard_map/convert_element_type | solution.py:590
  175.4 1.0 add_convert_fusion.6
  176.5 1.6 collective-permute-start.19
  178.0 2.6 %collective-permute-start.14 = (bf16[96,768]{1,0:T(8,128)(2,1)S(1)}, bf16[96,768]{1,0:T(8,128)(2,1)}, u32[]{:S(2)}, u32[]{:S(2)}) collective-permute-start(bf16[96,768]{1,0:T(8,128)(2,1)S(1)} %add_convert_fusion.6), channel_id=1, source_target_pairs={{0,16},{4,20},{8,24},{12,28},{16,0},{20,4},{24,8},{28,12},{1,17},{... | collective-permute-start | bytes 442376 | tf_op jit(solution)/shard_map/ppermute | solution.py:493
  180.7 0.6 collective-permute-start.20
  181.2 1.5 collective-permute-start.15
  182.7 26.1 %collective-permute-done.15 = f32[1536]{0:T(1024)S(1)} collective-permute-done((f32[1536]{0:T(1024)S(1)}, f32[1536]{0:T(1024)S(1)}, u32[]{:S(2)}, u32[]{:S(2)}) %collective-permute-start.15) | collective-permute-done | bytes 6176 | tf_op jit(solution)/shard_map/ppermute | solution.py:493
  208.9 1.7 add_convert_fusion.4
  210.5 2.4 add_convert_fusion.1
  213.2 1.7 collective-permute-start.17
  214.9 1.9 collective-permute-done.17
  216.8 4.7 %collective-permute-done.16 = bf16[96,768]{1,0:T(8,128)(2,1)S(1)} collective-permute-done((bf16[96,768]{1,0:T(8,128)(2,1)S(1)}, bf16[96,768]{1,0:T(8,128)(2,1)S(1)}, u32[]{:S(2)}, u32[]{:S(2)}) %collective-permute-start.16) | collective-permute-done | bytes 147488 | tf_op jit(solution)/shard_map/ppermute | solution.py:493
  221.7 2.0 collective-permute-start.21
  224.2 4.2 %collective-permute-done.21 = f32[1536]{0:T(1024)S(1)} collective-permute-done((f32[1536]{0:T(1024)S(1)}, f32[1536]{0:T(1024)S(1)}, u32[]{:S(2)}, u32[]{:S(2)}) %collective-permute-start.21) | collective-permute-done | bytes 6176 | tf_op jit(solution)/shard_map/ppermute | solution.py:493
  228.4 2.3 collective-permute-done.18
  230.8 0.7 slice.86
  231.5 0.7 slice.73
  232.1 1.4 maximum_select_fusion.4
  233.5 0.6 collective-permute-start.23
  234.1 5.4 %finish.2 = (bf16[192,3072]{1,0:T(8,128)(2,1)}, f32[192,3072]{1,0:T(8,128)}) custom-call(bf16[2,2,400,1024]{3,2,1,0:T(8,128)(2,1)} %get-tuple-element.163.keep, bf16[2,2,400,1024]{3,2,1,0:T(8,128)(2,1)} %collective-permute-done.12.from_core, bf16[2,1,400,1024]{3,2,1,0:T(8,128)(2,1)} %copy-done.6, bf16[192,3072]{1,0:T(8,128)(2,1)} %bitcast.24, ...), custom_call_target="tpu_custom_call" | custom-call | flops 3000 | bytes 5000 | tf_op jit(solution)/shard_map/finish/pallas_call | solution.py:470
  239.5 2.0 maximum_select_fusion
  241.5 0.6 fusion.5
  242.1 2.5 %slice_convert_fusion = (f32[768,768]{1,0:T(8,128)}, f32[768,768]{1,0:T(8,128)}) fusion(bf16[1536,768]{1,0:T(8,128)(2,1)S(1)} %maximum_select_fusion), kind=kLoop, calls=%fused_computation.3 | loop fusion | flops 1179648 | bytes 7077888 | tf_op jit(solution)/shard_map/convert_element_type | solution.py:786
  244.6 3.1 %finish.3 = (bf16[192,3072]{1,0:T(8,128)(2,1)}, f32[192,3072]{1,0:T(8,128)}) custom-call(bf16[1,2,400,1024]{3,2,1,0:T(8,128)(2,1)} %get-tuple-element.162.keep, bf16[1,2,400,1024]{3,2,1,0:T(8,128)(2,1)} %copy-done.4, bf16[1,1,400,1024]{3,2,1,0:T(8,128)(2,1)} %collective-permute-done.22.from_y, ...), custom_call_target="tpu_custom_call", output_to_operand_aliasing={{0}: (8, {}), {1}: (9, {})} | custom-call | flops 3000 | bytes 5000 | tf_op jit(solution)/shard_map/finish/pallas_call | solution.py:470
  247.9 1.5 fusion
  249.4 0.9 slice.84
  250.2 1.3 slice.82
  (104 shorter events, 4.0 us)
Async XLA Ops:
  0.6 37.9 %collective-permute-start.1 = (bf16[192,3072]{1,0:T(8,128)(2,1)}, bf16[192,3072]{1,0:T(8,128)(2,1)}, u32[]{:S(2)}, u32[]{:S(2)}) collective-permute-start(bf16[192,3072]{1,0:T(8,128)(2,1)} %bitcast.21), channel_id=1, source_target_pairs={{0,1},{1,0},{2,3},{3,2},{4,5},{5,4},{6,7},{7,6},{8,9},{9,8},{10,11... | collective-permute-start | bytes 3538952 | tf_op jit(solution)/shard_map/ppermute | solution.py:493
  1.2 29.5 %collective-permute-start = (bf16[192,3072]{1,0:T(8,128)(2,1)}, bf16[192,3072]{1,0:T(8,128)(2,1)}, u32[]{:S(2)}, u32[]{:S(2)}) collective-permute-start(bf16[192,3072]{1,0:T(8,128)(2,1)} %bitcast.22), channel_id=1, source_target_pairs={{0,2},{1,3},{2,0},{3,1},{4,6},{5,7},{6,4},{7,5},{8,10},{9,11},{10,... | collective-permute-start | bytes 3538952 | tf_op jit(solution)/shard_map/ppermute | solution.py:493
  4.6 11.3 %copy-start.16 = (s32[3,1024]{1,0:T(4,128)S(1)}, s32[3,1024]{1,0:T(4,128)}, u32[]{:S(2)}) copy-start(s32[3,1024]{1,0:T(4,128)} %param.13) | copy-start | bytes 36868
  4.6 11.5 %copy-start.8 = (bf16[192,768]{1,0:T(8,128)(2,1)S(1)}, bf16[192,768]{1,0:T(8,128)(2,1)}, u32[]{:S(2)}) copy-start(bf16[192,768]{1,0:T(8,128)(2,1)} %attn.1) | copy-start | bytes 884740
  4.6 12.4 %copy-start.3 = (bf16[768,768]{1,0:T(8,128)(2,1)S(1)}, bf16[768,768]{1,0:T(8,128)(2,1)}, u32[]{:S(2)}) copy-start(bf16[768,768]{1,0:T(8,128)(2,1)} %down.1) | copy-start | bytes 3538948
  15.9 2.6 %copy-start.23 = (bf16[2,192]{1,0:T(2,128)(2,1)S(1)}, bf16[2,192]{1,0:T(2,128)(2,1)}, u32[]{:S(2)}) copy-start(bf16[2,192]{1,0:T(2,128)(2,1)} %param.16) | copy-start | bytes 2308
  15.9 3.1 %copy-start.5 = (bf16[768,3,192]{0,2,1:T(8,128)(2,1)S(1)}, bf16[768,3,192]{0,2,1:T(8,128)(2,1)}, u32[]{:S(2)}) copy-start(bf16[768,3,192]{0,2,1:T(8,128)(2,1)} %param.15) | copy-start | bytes 2654212
  17.0 3.3 %copy-start = (bf16[768,768]{1,0:T(8,128)(2,1)S(1)}, bf16[768,768]{1,0:T(8,128)(2,1)}, u32[]{:S(2)}) copy-start(bf16[768,768]{1,0:T(8,128)(2,1)} %up.5) | copy-start | bytes 3538948
  20.4 10.3 %copy-start.24 = (bf16[192]{0:T(256)(128)(2,1)S(1)}, bf16[192]{0:T(256)(128)(2,1)}, u32[]{:S(2)}) copy-start(bf16[192]{0:T(256)(128)(2,1)} %param.21) | copy-start | bytes 1156
  20.4 11.8 %copy-start.20 = (bf16[768]{0:T(1024)(128)(2,1)S(1)}, bf16[768]{0:T(1024)(128)(2,1)}, u32[]{:S(2)}) copy-start(bf16[768]{0:T(1024)(128)(2,1)} %param.19) | copy-start | bytes 4612
  20.4 12.6 %copy-start.21 = (bf16[192]{0:T(256)(128)(2,1)S(1)}, bf16[192]{0:T(256)(128)(2,1)}, u32[]{:S(2)}) copy-start(bf16[192]{0:T(256)(128)(2,1)} %param.14) | copy-start | bytes 1156
  20.4 16.9 %copy-start.25 = (s32[4]{0:T(128)S(1)}, s32[4]{0:T(128)}, u32[]{:S(2)}) copy-start(s32[4]{0:T(128)} %constant.96.clone) | copy-start | bytes 52
  33.0 5.6 %collective-permute-start.2 = (bf16[192,3072]{1,0:T(8,128)(2,1)}, bf16[192,3072]{1,0:T(8,128)(2,1)S(1)}, u32[]{:S(2)}, u32[]{:S(2)}) collective-permute-start(bf16[192,3072]{1,0:T(8,128)(2,1)} %collective-permute-done.flip_y), channel_id=1, source_target_pairs={{0,1},{1,0},{2,3},{3,2},{4,5},{5,4},{6,7},{7,6},{8,9},{9,8},{10,11... | collective-permute-start | bytes 3538952 | tf_op jit(solution)/shard_map/ppermute | solution.py:493
  33.1 5.5 %copy-start.13 = (bf16[192,128]{1,0:T(8,128)(2,1)}, bf16[192,128]{1,0:T(8,128)(2,1)S(1)}, u32[]{:S(2)}) copy-start(bf16[192,128]{1,0:T(8,128)(2,1)S(1)} %broadcast_in_dim.55.gain_own.gain) | copy-start | bytes 147460
  33.1 4.2 %collective-permute-start.3 = (bf16[192,128]{1,0:T(8,128)(2,1)S(1)}, bf16[192,128]{1,0:T(8,128)(2,1)S(1)}, u32[]{:S(2)}, u32[]{:S(2)}) collective-permute-start(bf16[192,128]{1,0:T(8,128)(2,1)S(1)} %broadcast_in_dim.55.gain_own.gain), channel_id=1, source_target_pairs={{0,2},{1,3},{2,0},{3,1},{4,6},{5,7},{6,4},{7,5},{8,10},{9,11},{10,... | collective-permute-start | bytes 147464 | tf_op jit(solution)/shard_map/ppermute | solution.py:493
  34.9 2.9 %collective-permute-start.4 = (bf16[192,128]{1,0:T(8,128)(2,1)S(1)}, bf16[192,128]{1,0:T(8,128)(2,1)S(1)}, u32[]{:S(2)}, u32[]{:S(2)}) collective-permute-start(bf16[192,128]{1,0:T(8,128)(2,1)S(1)} %broadcast_in_dim.55.gain_own.gain), channel_id=1, source_target_pairs={{0,1},{1,0},{2,3},{3,2},{4,5},{5,4},{6,7},{7,6},{8,9},{9,8},{10,11... | collective-permute-start | bytes 147464 | tf_op jit(solution)/shard_map/ppermute | solution.py:493
  37.3 1.3 copy-start.17
  37.3 1.2 collective-permute-start.5
  37.9 0.7 copy-start.18
  38.6 0.6 copy-start.19
  39.2 1.0 copy-start.7
  64.4 60.2 %all-to-all-start = ((bf16[8,192,768]{2,1,0:T(8,128)(2,1)}), bf16[8,192,768]{2,1,0:T(8,128)(2,1)S(1)}, u32[]{:S(2)}, u32[]{:S(2)}) async-start(bf16[8,192,768]{2,1,0:T(8,128)(2,1)} %bitcast.34), calls=%async_computation | async-start | bytes 4718592 | tf_op jit(solution)/shard_map/all_to_all | solution.py:516
  120.3 6.2 %copy-start.9 = (bf16[768,768]{1,0:T(8,128)(2,1)S(1)}, bf16[768,768]{1,0:T(8,128)(2,1)}, u32[]{:S(2)}) copy-start(bf16[768,768]{1,0:T(8,128)(2,1)} %get-tuple-element.134) | copy-start | bytes 3538948
  126.6 17.7 %collective-permute-start.6 = (bf16[384,768]{1,0:T(8,128)(2,1)S(1)}, bf16[384,768]{1,0:T(8,128)(2,1)S(1)}, u32[]{:S(2)}, u32[]{:S(2)}) collective-permute-start(bf16[384,768]{1,0:T(8,128)(2,1)S(1)} %constant_dynamic-slice_fusion.4), channel_id=1, source_target_pairs={{0,4},{4,0},{8,12},{12,8},{16,20},{20,16},{24,28},{28,24},{1,5},{5... | collective-permute-start | bytes 1769480 | tf_op jit(solution)/shard_map/ppermute | solution.py:493
  128.1 16.2 %collective-permute-start.7 = (bf16[192,768]{1,0:T(8,128)(2,1)}, bf16[192,768]{1,0:T(8,128)(2,1)S(1)}, u32[]{:S(2)}, u32[]{:S(2)}) collective-permute-start(bf16[192,768]{1,0:T(8,128)(2,1)} %reduce_sum.73), channel_id=1, source_target_pairs={{0,16},{4,20},{8,24},{12,28},{16,0},{20,4},{24,8},{28,12},{1,17},{... | collective-permute-start | bytes 884744 | tf_op jit(solution)/shard_map/ppermute | solution.py:493
  128.1 16.2 %collective-permute-start.8 = (f32[2,192]{1,0:T(2,128)S(1)}, f32[2,192]{1,0:T(2,128)S(1)}, u32[]{:S(2)}, u32[]{:S(2)}) collective-permute-start(f32[2,192]{1,0:T(2,128)S(1)} %pad_maximum_fusion), channel_id=1, source_target_pairs={{0,1},{1,0},{2,3},{3,2},{4,5},{5,4},{6,7},{7,6},{8,9},{9,8},{10,11... | collective-permute-start | bytes 4616 | tf_op jit(solution)/shard_map/ppermute | solution.py:493
  128.1 16.3 %copy-start.12 = (bf16[192,768]{1,0:T(8,128)(2,1)S(1)}, bf16[192,768]{1,0:T(8,128)(2,1)}, u32[]{:S(2)}) copy-start(bf16[192,768]{1,0:T(8,128)(2,1)} %reduce_sum.73) | copy-start | bytes 884740
  144.3 7.2 %copy-start.14 = (f32[768,128]{1,0:T(8,128)S(1)}, f32[768,128]{1,0:T(8,128)}, u32[]{:S(2)}) copy-start(f32[768,128]{1,0:T(8,128)} %get-tuple-element.168) | copy-start | bytes 1179652
  144.4 7.3 %copy-start.15 = (f32[384,128]{1,0:T(8,128)S(1)}, f32[384,128]{1,0:T(8,128)}, u32[]{:S(2)}) copy-start(f32[384,128]{1,0:T(8,128)} %get-tuple-element.167) | copy-start | bytes 589828
  146.4 22.7 %collective-permute-start.12 = (bf16[2,2,400,1024]{3,2,1,0:T(8,128)(2,1)}, bf16[2,2,400,1024]{3,2,1,0:T(8,128)(2,1)}, u32[]{:S(2)}, u32[]{:S(2)}) collective-permute-start(bf16[2,2,400,1024]{3,2,1,0:T(8,128)(2,1)} %get-tuple-element.161), channel_id=1, source_target_pairs={{0,1},{1,0},{2,3},{3,2},{4,5},{5,4},{6,7},{7,6},{8,9},{9,8},{10,11... | collective-permute-start | bytes 9830408 | tf_op jit(solution)/shard_map/ppermute | solution.py:493
  146.9 22.2 %collective-permute-start.10 = (bf16[384,768]{1,0:T(8,128)(2,1)}, bf16[384,768]{1,0:T(8,128)(2,1)}, u32[]{:S(2)}, u32[]{:S(2)}) collective-permute-start(bf16[384,768]{1,0:T(8,128)(2,1)} %maximum_select_fusion.3), channel_id=1, source_target_pairs={{0,8},{4,12},{8,0},{12,4},{16,24},{20,28},{24,16},{28,20},{1,9},{5... | collective-permute-start | bytes 1769480 | tf_op jit(solution)/shard_map/ppermute | solution.py:493
  148.9 20.1 %collective-permute-start.9 = (bf16[192,768]{1,0:T(8,128)(2,1)}, bf16[192,768]{1,0:T(8,128)(2,1)}, u32[]{:S(2)}, u32[]{:S(2)}) collective-permute-start(bf16[192,768]{1,0:T(8,128)(2,1)} %get-tuple-element.158), channel_id=1, source_target_pairs={{0,8},{4,12},{8,0},{12,4},{16,24},{20,28},{24,16},{28,20},{1,9},{5... | collective-permute-start | bytes 884744 | tf_op jit(solution)/shard_map/ppermute | solution.py:493
  149.0 12.8 %collective-permute-start.11 = (f32[192]{0:T(256)S(1)}, f32[192]{0:T(256)S(1)}, u32[]{:S(2)}, u32[]{:S(2)}) collective-permute-start(f32[192]{0:T(256)S(1)} %bitcast.38), channel_id=1, source_target_pairs={{0,2},{1,3},{2,0},{3,1},{4,6},{5,7},{6,4},{7,5},{8,10},{9,11},{10,... | collective-permute-start | bytes 2312 | tf_op jit(solution)/shard_map/ppermute | solution.py:493
  151.9 20.2 %copy-start.1 = (bf16[2,2,400,1024]{3,2,1,0:T(8,128)(2,1)S(1)}, bf16[2,2,400,1024]{3,2,1,0:T(8,128)(2,1)}, u32[]{:S(2)}) copy-start(bf16[2,2,400,1024]{3,2,1,0:T(8,128)(2,1)} %get-tuple-element.163.keep) | copy-start | bytes 9830404
  172.0 3.4 %copy-start.11 = (bf16[192,768]{1,0:T(8,128)(2,1)S(1)}, bf16[192,768]{1,0:T(8,128)(2,1)}, u32[]{:S(2)}) copy-start(bf16[192,768]{1,0:T(8,128)(2,1)} %get-tuple-element.214) | copy-start | bytes 884740
  176.4 32.4 %collective-permute-start.13 = (bf16[1,2,400,1024]{3,2,1,0:T(8,128)(2,1)}, bf16[1,2,400,1024]{3,2,1,0:T(8,128)(2,1)S(1)}, u32[]{:S(2)}, u32[]{:S(2)}) collective-permute-start(bf16[1,2,400,1024]{3,2,1,0:T(8,128)(2,1)} %get-tuple-element.172), channel_id=1, source_target_pairs={{0,1},{1,0},{2,3},{3,2},{4,5},{5,4},{6,7},{7,6},{8,9},{9,8},{10,11... | collective-permute-start | bytes 4915208 | tf_op jit(solution)/shard_map/ppermute | solution.py:493
  176.5 47.8 %collective-permute-start.19 = (bf16[2,1,400,1024]{3,2,1,0:T(8,128)(2,1)}, bf16[2,1,400,1024]{3,2,1,0:T(8,128)(2,1)S(1)}, u32[]{:S(2)}, u32[]{:S(2)}) collective-permute-start(bf16[2,1,400,1024]{3,2,1,0:T(8,128)(2,1)} %add_convert_fusion), channel_id=1, source_target_pairs={{0,2},{1,3},{2,0},{3,1},{4,6},{5,7},{6,4},{7,5},{8,10},{9,11},{10,... | collective-permute-start | bytes 4915208 | tf_op jit(solution)/shard_map/ppermute | solution.py:493
  178.0 30.8 %collective-permute-start.14 = (bf16[96,768]{1,0:T(8,128)(2,1)S(1)}, bf16[96,768]{1,0:T(8,128)(2,1)}, u32[]{:S(2)}, u32[]{:S(2)}) collective-permute-start(bf16[96,768]{1,0:T(8,128)(2,1)S(1)} %add_convert_fusion.6), channel_id=1, source_target_pairs={{0,16},{4,20},{8,24},{12,28},{16,0},{20,4},{24,8},{28,12},{1,17},{... | collective-permute-start | bytes 442376 | tf_op jit(solution)/shard_map/ppermute | solution.py:493
  180.7 43.5 %collective-permute-start.20 = (bf16[768,768]{1,0:T(8,128)(2,1)}, bf16[768,768]{1,0:T(8,128)(2,1)}, u32[]{:S(2)}, u32[]{:S(2)}) collective-permute-start(bf16[768,768]{1,0:T(8,128)(2,1)} %maximum_select_fusion.1), channel_id=1, source_target_pairs={{0,4},{4,0},{8,12},{12,8},{16,20},{20,16},{24,28},{28,24},{1,5},{5... | collective-permute-start | bytes 3538952 | tf_op jit(solution)/shard_map/ppermute | solution.py:493
  181.2 27.6 %collective-permute-start.15 = (f32[1536]{0:T(1024)S(1)}, f32[1536]{0:T(1024)S(1)}, u32[]{:S(2)}, u32[]{:S(2)}) collective-permute-start(f32[1536]{0:T(1024)S(1)} %concatenate.41), channel_id=1, source_target_pairs={{0,4},{4,0},{8,12},{12,8},{16,20},{20,16},{24,28},{28,24},{1,5},{5... | collective-permute-start | bytes 18440 | tf_op jit(solution)/shard_map/ppermute | solution.py:493
  208.8 12.8 %copy-start.4 = (bf16[1,2,400,1024]{3,2,1,0:T(8,128)(2,1)}, bf16[1,2,400,1024]{3,2,1,0:T(8,128)(2,1)S(1)}, u32[]{:S(2)}) copy-start(bf16[1,2,400,1024]{3,2,1,0:T(8,128)(2,1)S(1)} %collective-permute-done.13.from_core) | copy-start | bytes 4915204
  212.9 8.6 %collective-permute-start.16 = (bf16[96,768]{1,0:T(8,128)(2,1)S(1)}, bf16[96,768]{1,0:T(8,128)(2,1)S(1)}, u32[]{:S(2)}, u32[]{:S(2)}) collective-permute-start(bf16[96,768]{1,0:T(8,128)(2,1)S(1)} %add_convert_fusion.4), channel_id=1, source_target_pairs={{0,16},{4,20},{8,24},{12,28},{16,0},{20,4},{24,8},{28,12},{1,17},{... | collective-permute-start | bytes 442376 | tf_op jit(solution)/shard_map/ppermute | solution.py:493
  213.2 3.7 %collective-permute-start.17 = (f32[1536]{0:T(1024)S(1)}, f32[1536]{0:T(1024)S(1)}, u32[]{:S(2)}, u32[]{:S(2)}) collective-permute-start(f32[1536]{0:T(1024)S(1)} %add.111), channel_id=1, source_target_pairs={{0,8},{4,12},{8,0},{12,4},{16,24},{20,28},{24,16},{28,20},{1,9},{5... | collective-permute-start | bytes 18440 | tf_op jit(solution)/shard_map/ppermute | solution.py:493
  221.6 2.6 %copy-start.10 = (bf16[192,768]{1,0:T(8,128)(2,1)}, bf16[192,768]{1,0:T(8,128)(2,1)S(1)}, u32[]{:S(2)}) copy-start(bf16[192,768]{1,0:T(8,128)(2,1)S(1)} %maximum_select_fusion.5) | copy-start | bytes 884740
  221.6 9.1 %collective-permute-start.18 = (bf16[192,768]{1,0:T(8,128)(2,1)S(1)}, bf16[192,768]{1,0:T(8,128)(2,1)}, u32[]{:S(2)}, u32[]{:S(2)}) collective-permute-start(bf16[192,768]{1,0:T(8,128)(2,1)S(1)} %maximum_select_fusion.5), channel_id=1, source_target_pairs={{0,8},{4,12},{8,0},{12,4},{16,24},{20,28},{24,16},{28,20},{1,9},{5... | collective-permute-start | bytes 884744 | tf_op jit(solution)/shard_map/ppermute | solution.py:493
  221.7 6.7 %collective-permute-start.21 = (f32[1536]{0:T(1024)S(1)}, f32[1536]{0:T(1024)S(1)}, u32[]{:S(2)}, u32[]{:S(2)}) collective-permute-start(f32[1536]{0:T(1024)S(1)} %add.115), channel_id=1, source_target_pairs={{0,16},{4,20},{8,24},{12,28},{16,0},{20,4},{24,8},{28,12},{1,17},{... | collective-permute-start | bytes 18440 | tf_op jit(solution)/shard_map/ppermute | solution.py:493
  223.7 20.9 %collective-permute-start.22 = (bf16[1,1,400,1024]{3,2,1,0:T(8,128)(2,1)}, bf16[1,1,400,1024]{3,2,1,0:T(8,128)(2,1)}, u32[]{:S(2)}, u32[]{:S(2)}) collective-permute-start(bf16[1,1,400,1024]{3,2,1,0:T(8,128)(2,1)} %add_convert_fusion.1), channel_id=1, source_target_pairs={{0,2},{1,3},{2,0},{3,1},{4,6},{5,7},{6,4},{7,5},{8,10},{9,11},{10,... | collective-permute-start | bytes 2457608 | tf_op jit(solution)/shard_map/ppermute | solution.py:493
  224.2 9.9 %copy-start.6 = (bf16[2,1,400,1024]{3,2,1,0:T(8,128)(2,1)}, bf16[2,1,400,1024]{3,2,1,0:T(8,128)(2,1)S(1)}, u32[]{:S(2)}) copy-start(bf16[2,1,400,1024]{3,2,1,0:T(8,128)(2,1)S(1)} %collective-permute-done.19.from_y) | copy-start | bytes 4915204
  233.5 14.4 %collective-permute-start.23 = (bf16[384,768]{1,0:T(8,128)(2,1)S(1)}, bf16[384,768]{1,0:T(8,128)(2,1)}, u32[]{:S(2)}, u32[]{:S(2)}) collective-permute-start(bf16[384,768]{1,0:T(8,128)(2,1)S(1)} %maximum_select_fusion.4), channel_id=1, source_target_pairs={{0,4},{4,0},{8,12},{12,8},{16,20},{20,16},{24,28},{28,24},{1,5},{5... | collective-permute-start | bytes 1769480 | tf_op jit(solution)/shard_map/ppermute | solution.py:493
  234.1 5.4 %copy-start.2 = (bf16[768,768]{1,0:T(8,128)(2,1)S(1)}, bf16[768,768]{1,0:T(8,128)(2,1)}, u32[]{:S(2)}) copy-start(bf16[768,768]{1,0:T(8,128)(2,1)} %maximum_select_fusion.1) | copy-start | bytes 3538948
  239.5 2.0 copy-start.22

commit v4 on v3

--- a/solution.py
+++ b/solution.py
@@ -699,10 +699,9 @@
     )
     mlp_sum = SumOverDp(mlp_part, dp_size, dp)
 
-    (states,), flights = launch([mlp_sum], (normed,))
-    attended, d_mixed, qk_part, norm_row, mix_part = land(
-        flights,
-        attention_call(first, count, states, mixed_t, d_att, mask_q, mask_k, head_gains, cotangent),
+    (states,), flying = launch([mlp_sum], (normed,))
+    attended, d_mixed, qk_part, norm_row, mix_part = attention_call(
+        first, count, states, mixed_t, d_att, mask_q, mask_k, head_gains, cotangent
     )
     mix_sum = ChainOverDp(mix_part, dp_size, dp)
 
@@ -716,15 +715,19 @@
         dp_size,
     )
 
-    runs = [(0, seqs - 1), (seqs - 1, 1)] if seqs > 1 else [(0, 1)]
+    runs = [(seq, 1) for seq in range(seqs)]
     scatters = []
     for begin, size in runs:
-        along = [mix_sum, mlp_sum, short] + [m for m in scatters if m.more()]
+        busy = [f[0] for f in flying]
+        along = [m for m in [mix_sum, mlp_sum, short] + scatters if m.more() and m not in busy]
         (att, dm), flights = launch(along, (attended, d_mixed))
+        flying = flying + flights
         sent = project_call(
             shard, active, att, d_pre, dm, normed, down_t, attn_t, up_weight, mixed, gain_all, begin, size
         )
-        keep, send = land(flights, sent)
+        late = [f for f in flights if begin == 0 and f[0] is mix_sum]
+        keep, send = land([f for f in flying if f not in late], sent)
+        flying = late
         scatters.append(ScatterOverMp(keep, send))
 
     finished = ()
@@ -740,10 +743,12 @@
                 )
         return finished
 
-    flying = []
+    rounds = 0
     while True:
         busy = [f[0] for f in flying]
-        ready = [m for m in scatters + [short, mlp_sum, mix_sum] if m.more() and m not in busy]
+        rounds += 1
+        ready = [m for m in [mix_sum] + scatters + [short, mlp_sum] if m.more() and m not in busy]
+        ready = [m for m in ready if m is not mlp_sum or rounds > 1]
         finished, flights = launch(ready, finished)
         flying = flying + flights
         if not flying:
@@ -760,7 +765,7 @@
         elif left == 2:
             now = chain + across[:1] + wide + rest
         elif left == 1:
-            now = across[:1] + wide + rest or chain
+            now = across + wide + rest + chain
         else:
             now = chain + rest or flying
         finished = land(now, finished)

time: 253 us -> 247 us (0.976)
  waiting for transfers between devices: 59.3 us -> 52.2 us
  other arithmetic: 29.3 us -> 24.8 us
  local copies, waits for them, and re-layouts: 13.6 us -> 16.8 us
    ppermute x24 -> x26, waiting for transfers between devices: 56.4 us -> 52.1 us  [flip(): return lax.ppermute(value, axis, [(i, i ^ bit) for i in range(size)])]
    pallas_call x2 -> x3, Pallas kernels: 26.1 us -> 29.6 us  [project_call(): pl.pallas_call(project_kernel, grid_spec=grid_spec, out_shape=[jax.ShapeD...]
    pallas_call x1, Pallas kernels: 49.9 us -> 46.5 us  [attention_call(): pl.pallas_call(attention_kernel, grid_spec=grid_spec, out_shape=[jax.Shap...]
    all_to_all x1, waiting for transfers between devices: 2.92 us -> 0.01 us  [move(): return lax.all_to_all(send, 'dp', 0, 0, tiled=True)]
    ppermute x24 -> x26, starting transfers between devices: 22.3 us -> 24.2 us  [flip(): return lax.ppermute(value, axis, [(i, i ^ bit) for i in range(size)])]
    pallas_call x2 -> x3, Pallas kernels: 8.49 us -> 9.39 us  [finish_call(): pl.pallas_call(finish_kernel, grid=(size * steps,), in_specs=[packed, pac...]
    convert_element_type x2 -> x3, other arithmetic: 5.73 us -> 5.9 us  [take(): (self.keep[:, 1:].astype(F32) + arrived[:, 1:].astype(F32)).astype(BF16)]
    unnamed x55 -> x57, local copies, waits for them, and re-layouts: 5.5 us -> 5.53 us
  transfers between devices with their start and end apart: 25 -> 27, of which waited for: 11 -> 12; matrix products, arithmetic and copies ran while one was open for 10% -> 10% of each run, Pallas kernels for 38% -> 38%
where the time goes in v4:
time: 247 us; the launch traced here: 246 us
  Pallas kernels  121 us (49%)
  waiting for transfers between devices  52.2 us (21%)
  starting transfers between devices  30.2 us (12%)
  other arithmetic  24.8 us (10%)
  local copies, waits for them, and re-layouts  16.8 us (7%)
    ppermute x26, waiting for transfers between devices, flip(): return lax.ppermute(value, axis, [(i, i ^ bit) for i in range(size)])  52.1 us
    pallas_call x1, Pallas kernels, attention_call(): pl.pallas_call(attention_kernel, grid_spec=grid_spec, out_shape=[jax.Shap...  46.5 us
    pallas_call x3, Pallas kernels, project_call(): pl.pallas_call(project_kernel, grid_spec=grid_spec, out_shape=[jax.ShapeD...  29.6 us
    ppermute x26, starting transfers between devices, flip(): return lax.ppermute(value, axis, [(i, i ^ bit) for i in range(size)])  24.2 us
    pallas_call x1, Pallas kernels, mlp_call(): pl.pallas_call(functools.partial(mlp_kernel, pieces_order), grid_spec=gri...  24.2 us
    pallas_call x1, Pallas kernels, early_call(): pl.pallas_call(early_kernel, grid=(tokens // block,), in_specs=[pl.BlockS...  11.3 us
    pallas_call x3, Pallas kernels, finish_call(): pl.pallas_call(finish_kernel, grid=(size * steps,), in_specs=[packed, pac...  9.39 us
    all_to_all x1, starting transfers between devices, move(): return lax.all_to_all(send, 'dp', 0, 0, tiled=True)  6.04 us
  transfers between devices with their start and end apart: 27, of which 12 were waited for; matrix products, arithmetic and copies ran while one was open for 10% of the time, Pallas kernels for 38%

profile of v4, /device:TPU:0, one launch (start us, length us, event | category | flops | bytes accessed | tf_op | source)
XLA Modules:
  0.0 245.9 jit_solution(12439611908612227634)
XLA Ops:
  0.6 3.0 %collective-permute-start = (bf16[192,3072]{1,0:T(8,128)(2,1)}, bf16[192,3072]{1,0:T(8,128)(2,1)S(1)}, u32[]{:S(2)}, u32[]{:S(2)}) collective-permute-start(bf16[192,3072]{1,0:T(8,128)(2,1)} %bitcast.19), channel_id=1, source_target_pairs={{0,2},{1,3},{2,0},{3,1},{4,6},{5,7},{6,4},{7,5},{8,10},{9,11},{10,... | collective-permute-start | bytes 3538952 | tf_op jit(solution)/shard_map/ppermute | solution.py:493
  3.7 0.8 fusion.1.pick
  4.5 11.3 %early.1 = (bf16[3,768,1024]{2,1,0:T(8,128)(2,1)}, bf16[3,192,1024]{2,1,0:T(8,128)(2,1)}, bf16[192,3072]{1,0:T(8,128)(2,1)}, f32[192,128]{1,0:T(8,128)}) custom-call(bf16[3072,768]{1,0:T(8,128)(2,1)} %cot.5, bf16[768,768]{1,0:T(8,128)(2,1)} %down.1, bf16[192,768]{1,0:T(8,128)(2,1)} %attn.1, bf16[192,768]{1,0:T(8,128)(2,1)} %fusion.1.pick), custom_call_target="tpu_custom_call" | custom-call | flops 10000 | bytes 12000 | tf_op jit(solution)/shard_map/early/pallas_call | solution.py:62
  15.8 0.7 slice.68
  16.5 0.7 slice.69
  17.1 1.4 copy.37
  18.6 1.0 copy.38
  19.5 1.0 convert_reduce_fusion
  20.7 1.3 copy.35
  22.0 1.5 copy.36
  24.1 0.7 fusion.3.mask_q
  24.8 0.7 select_convert_fusion.mask_k
  25.5 4.4 %collective-permute-done.flip_y = bf16[192,3072]{1,0:T(8,128)(2,1)S(1)} collective-permute-done((bf16[192,3072]{1,0:T(8,128)(2,1)}, bf16[192,3072]{1,0:T(8,128)(2,1)S(1)}, u32[]{:S(2)}, u32[]{:S(2)}) %collective-permute-start) | collective-permute-done | bytes 1179680 | tf_op jit(solution)/shard_map/ppermute | solution.py:493
  29.9 0.9 broadcast_in_dim.27.gains
  30.8 0.8 broadcast_in_dim.24.up_bias
  31.7 0.7 broadcast_in_dim.54.bias
  32.5 1.8 collective-permute-start.3
  34.5 2.2 collective-permute-done.3.gain_y
  37.2 0.7 collective-permute-done.5.gain_cy
  38.5 1.0 copy-done.11
  39.6 24.2 %mlp.1 = (bf16[3,768,1024]{2,1,0:T(8,128)(2,1)}, bf16[3,768,1024]{2,1,0:T(8,128)(2,1)}, bf16[3,768,1024]{2,1,0:T(8,128)(2,1)}, f32[8,3072]{1,0:T(8,128)}, f32[76...) custom-call(s32[4]{0:T(128)} %xor_multiply_fusion.place, ...), custom_call_target="tpu_custom_call" | custom-call | flops 20000 | bytes 30000 | tf_op jit(solution)/shard_map/mlp/pallas_call | solution.py:188
  63.8 6.0 %all-to-all-start = ((bf16[8,192,768]{2,1,0:T(8,128)(2,1)}), bf16[8,192,768]{2,1,0:T(8,128)(2,1)S(1)}, u32[]{:S(2)}, u32[]{:S(2)}) async-start(bf16[8,192,768]{2,1,0:T(8,128)(2,1)} %bitcast.39), calls=%async_computation | async-start | bytes 4718592 | tf_op jit(solution)/shard_map/all_to_all | solution.py:516
  69.8 46.5 %attention.1 = (bf16[3,192,1024]{2,1,0:T(8,128)(2,1)}, bf16[3,576,1024]{2,1,0:T(8,128)(2,1)}, f32[384,128]{1,0:T(8,128)}, f32[1,768]{1,0:T(1,128)}, bf16[768,768]{1,0:T(8,128)(2,1)}) custom-call(s32[12]{0:T(128)} %get-tuple-element.132.first, s32[12]{0:T(128)} %get-tuple-element.133.count, bf16[3,768,1024]{2,1,0:T(8,128)(2,1)} %get-tuple-element.136.normed, ...), custom_call_target="tpu_custom_call" | custom-call | flops 18000 | bytes 5000 | tf_op jit(solution)/shard_map/attention/pallas_call | solution.py:359
  116.3 0.7 reduce.1
  117.4 1.9 constant_dynamic-slice_fusion.4
  119.3 9.8 %project.3 = (bf16[1,2,400,1024]{3,2,1,0:T(8,128)(2,1)}, bf16[1,2,400,1024]{3,2,1,0:T(8,128)(2,1)}) custom-call(s32[1]{0:T(128)} %bitcast.shard, bf16[3,768,1024]{2,1,0:T(8,128)(2,1)} %get-tuple-element.131.active, bf16[3,192,1024]{2,1,0:T(8,128)(2,1)} %get-tuple-element.178.attended, bf16[3,768,1024]{2,1,0:T(8,128)(2,1)} %get-tuple-element.148.d_pre, ...), custom_call_target="tpu_custom_call" | custom-call | flops 8000 | bytes 16000 | tf_op jit(solution)/shard_map/project/pallas_call | solution.py:434
  129.2 1.1 reduce_sum.75
  130.8 5.6 %collective-permute-start.7 = (bf16[384,768]{1,0:T(8,128)(2,1)}, bf16[384,768]{1,0:T(8,128)(2,1)}, u32[]{:S(2)}, u32[]{:S(2)}) collective-permute-start(bf16[384,768]{1,0:T(8,128)(2,1)} %constant_dynamic-slice_fusion.4), channel_id=1, source_target_pairs={{0,4},{4,0},{8,12},{12,8},{16,20},{20,16},{24,28},{28,24},{1,5},{5... | collective-permute-start | bytes 1769480 | tf_op jit(solution)/shard_map/ppermute | solution.py:493
  136.5 1.6 collective-permute-start.9
  138.4 9.9 %project.4 = (bf16[1,2,400,1024]{3,2,1,0:T(8,128)(2,1)}, bf16[1,2,400,1024]{3,2,1,0:T(8,128)(2,1)}) custom-call(s32[1]{0:T(128)} %bitcast.shard, bf16[3,768,1024]{2,1,0:T(8,128)(2,1)} %get-tuple-element.131.active, bf16[3,192,1024]{2,1,0:T(8,128)(2,1)} %get-tuple-element.178.attended, bf16[3,768,1024]{2,1,0:T(8,128)(2,1)} %get-tuple-element.148.d_pre, ...), custom_call_target="tpu_custom_call" | custom-call | flops 8000 | bytes 16000 | tf_op jit(solution)/shard_map/project/pallas_call | solution.py:434
  148.3 1.9 collective-permute-done.7
  150.2 2.0 collective-permute-done.8
  152.3 1.2 add_convert_fusion.2
  153.5 1.4 maximum_select_fusion.3
  154.9 2.2 add_convert_fusion.3
  157.2 1.6 collective-permute-start.14
  158.8 2.0 collective-permute-start.11
  161.4 9.9 %project.5 = (bf16[1,2,400,1024]{3,2,1,0:T(8,128)(2,1)}, bf16[1,2,400,1024]{3,2,1,0:T(8,128)(2,1)}) custom-call(s32[1]{0:T(128)} %bitcast.shard, bf16[3,768,1024]{2,1,0:T(8,128)(2,1)} %get-tuple-element.131.active, bf16[3,192,1024]{2,1,0:T(8,128)(2,1)} %get-tuple-element.178.attended, bf16[3,768,1024]{2,1,0:T(8,128)(2,1)} %get-tuple-element.148.d_pre, ...), custom_call_target="tpu_custom_call" | custom-call | flops 8000 | bytes 16000 | tf_op jit(solution)/shard_map/project/pallas_call | solution.py:434
  171.3 9.2 %collective-permute-done.11 = bf16[192,768]{1,0:T(8,128)(2,1)S(1)} collective-permute-done((bf16[192,768]{1,0:T(8,128)(2,1)}, bf16[192,768]{1,0:T(8,128)(2,1)S(1)}, u32[]{:S(2)}, u32[]{:S(2)}) %collective-permute-start.11) | collective-permute-done | bytes 294944 | tf_op jit(solution)/shard_map/ppermute | solution.py:493
  181.1 2.3 add_convert_fusion.1
  183.5 0.7 add_convert_fusion.7
  184.2 0.8 collective-permute-start.18
  185.0 1.6 maximum_select_fusion.1
  186.7 3.2 %finish.3 = (bf16[192,3072]{1,0:T(8,128)(2,1)}, f32[192,3072]{1,0:T(8,128)}) custom-call(bf16[1,2,400,1024]{3,2,1,0:T(8,128)(2,1)} %get-tuple-element.175.keep, bf16[1,2,400,1024]{3,2,1,0:T(8,128)(2,1)} %copy-done.5, bf16[1,1,400,1024]{3,2,1,0:T(8,128)(2,1)} %collective-permute-done.14.from_y, bf16[192,3072]{1,0:T(8,128)(2,1)} %bitcast.22, ...), custom_call_target="tpu_custom_call" | custom-call | flops 3000 | bytes 5000 | tf_op jit(solution)/shard_map/finish/pallas_call | solution.py:470
  189.8 4.6 %collective-permute-done.17 = bf16[96,768]{1,0:T(8,128)(2,1)S(1)} collective-permute-done((bf16[96,768]{1,0:T(8,128)(2,1)}, bf16[96,768]{1,0:T(8,128)(2,1)S(1)}, u32[]{:S(2)}, u32[]{:S(2)}) %collective-permute-start.17) | collective-permute-done | bytes 147488 | tf_op jit(solution)/shard_map/ppermute | solution.py:493
  194.4 0.7 add.119
  195.2 2.3 add_convert_fusion
  197.6 0.7 collective-permute-start.23
  198.7 2.9 %collective-permute-start.20 = (f32[1536]{0:T(1024)S(1)}, f32[1536]{0:T(1024)S(1)}, u32[]{:S(2)}, u32[]{:S(2)}) collective-permute-start(f32[1536]{0:T(1024)S(1)} %add.119), channel_id=1, source_target_pairs={{0,16},{4,20},{8,24},{12,28},{16,0},{20,4},{24,8},{28,12},{1,17},{... | collective-permute-start | bytes 18440 | tf_op jit(solution)/shard_map/ppermute | solution.py:493
  201.7 5.6 %collective-permute-done.20 = f32[1536]{0:T(1024)S(1)} collective-permute-done((f32[1536]{0:T(1024)S(1)}, f32[1536]{0:T(1024)S(1)}, u32[]{:S(2)}, u32[]{:S(2)}) %collective-permute-start.20) | collective-permute-done | bytes 6176 | tf_op jit(solution)/shard_map/ppermute | solution.py:493
  207.4 1.6 collective-permute-start.24
  209.0 0.7 slice.94
  209.7 0.7 slice.81
  210.4 1.3 fusion.5
  211.6 8.0 %collective-permute-done.22.from_y = bf16[1,1,400,1024]{3,2,1,0:T(8,128)(2,1)} collective-permute-done((bf16[1,1,400,1024]{3,2,1,0:T(8,128)(2,1)}, bf16[1,1,400,1024]{3,2,1,0:T(8,128)(2,1)}, u32[]{:S(2)}, u32[]{:S(2)}) %collective-permute-start.22) | collective-permute-done | bytes 819232 | tf_op jit(solution)/shard_map/ppermute | solution.py:493
  219.7 5.9 %collective-permute-done.23 = bf16[768,768]{1,0:T(8,128)(2,1)S(1)} collective-permute-done((bf16[768,768]{1,0:T(8,128)(2,1)S(1)}, bf16[768,768]{1,0:T(8,128)(2,1)S(1)}, u32[]{:S(2)}, u32[]{:S(2)}) %collective-permute-start.23) | collective-permute-done | bytes 1179680 | tf_op jit(solution)/shard_map/ppermute | solution.py:493
  225.8 0.7 collective-permute-start.25
  226.4 3.1 %finish.4 = (bf16[192,3072]{1,0:T(8,128)(2,1)}, f32[192,3072]{1,0:T(8,128)}) custom-call(bf16[1,2,400,1024]{3,2,1,0:T(8,128)(2,1)} %get-tuple-element.195.keep, bf16[1,2,400,1024]{3,2,1,0:T(8,128)(2,1)} %collective-permute-done.15.from_core, bf16[1,1,400,1024]{3,2,1,0:T(8,128)(2,1)} %collective-permute-done.22.from_y, ...), custom_call_target="tpu_custom_call", output_to_operand_aliasing={{0}: (8, {}), {1}: (9, {})} | custom-call | flops 3000 | bytes 5000 | tf_op jit(solution)/shard_map/finish/pallas_call | solution.py:470
  230.2 2.5 %slice_convert_fusion = (f32[768,768]{1,0:T(8,128)}, f32[768,768]{1,0:T(8,128)}) fusion(bf16[1536,768]{1,0:T(8,128)(2,1)S(1)} %maximum_select_fusion), kind=kLoop, calls=%fused_computation.4 | loop fusion | flops 1179648 | bytes 7077888 | tf_op jit(solution)/shard_map/convert_element_type | solution.py:791
  232.7 3.3 %collective-permute-done.24.from_y = bf16[1,1,400,1024]{3,2,1,0:T(8,128)(2,1)} collective-permute-done((bf16[1,1,400,1024]{3,2,1,0:T(8,128)(2,1)}, bf16[1,1,400,1024]{3,2,1,0:T(8,128)(2,1)}, u32[]{:S(2)}, u32[]{:S(2)}) %collective-permute-start.24) | collective-permute-done | bytes 819232 | tf_op jit(solution)/shard_map/ppermute | solution.py:493
  236.0 4.4 %collective-permute-done.25 = bf16[384,768]{1,0:T(8,128)(2,1)S(1)} collective-permute-done((bf16[384,768]{1,0:T(8,128)(2,1)S(1)}, bf16[384,768]{1,0:T(8,128)(2,1)S(1)}, u32[]{:S(2)}, u32[]{:S(2)}) %collective-permute-start.25) | collective-permute-done | bytes 589856 | tf_op jit(solution)/shard_map/ppermute | solution.py:493
  240.6 1.3 slice.90
  241.9 0.9 slice.92
  242.8 3.1 %finish.5 = (bf16[192,3072]{1,0:T(8,128)(2,1)}, f32[192,3072]{1,0:T(8,128)}) custom-call(bf16[1,2,400,1024]{3,2,1,0:T(8,128)(2,1)} %get-tuple-element.187.keep, bf16[1,2,400,1024]{3,2,1,0:T(8,128)(2,1)} %collective-permute-done.16.from_core, bf16[1,1,400,1024]{3,2,1,0:T(8,128)(2,1)} %collective-permute-done.24.from_y, ...), custom_call_target="tpu_custom_call", output_to_operand_aliasing={{0}: (8, {}), {1}: (9, {})} | custom-call | flops 3000 | bytes 5000 | tf_op jit(solution)/shard_map/finish/pallas_call | solution.py:470
  (113 shorter events, 6.7 us)
Async XLA Ops:
  0.6 29.2 %collective-permute-start = (bf16[192,3072]{1,0:T(8,128)(2,1)}, bf16[192,3072]{1,0:T(8,128)(2,1)S(1)}, u32[]{:S(2)}, u32[]{:S(2)}) collective-permute-start(bf16[192,3072]{1,0:T(8,128)(2,1)} %bitcast.19), channel_id=1, source_target_pairs={{0,2},{1,3},{2,0},{3,1},{4,6},{5,7},{6,4},{7,5},{8,10},{9,11},{10,... | collective-permute-start | bytes 3538952 | tf_op jit(solution)/shard_map/ppermute | solution.py:493
  3.7 34.3 %collective-permute-start.1 = (bf16[192,3072]{1,0:T(8,128)(2,1)}, bf16[192,3072]{1,0:T(8,128)(2,1)}, u32[]{:S(2)}, u32[]{:S(2)}) collective-permute-start(bf16[192,3072]{1,0:T(8,128)(2,1)} %bitcast.20), channel_id=1, source_target_pairs={{0,1},{1,0},{2,3},{3,2},{4,5},{5,4},{6,7},{7,6},{8,9},{9,8},{10,11... | collective-permute-start | bytes 3538952 | tf_op jit(solution)/shard_map/ppermute | solution.py:493
  4.5 11.3 %copy-start.17 = (s32[3,1024]{1,0:T(4,128)S(1)}, s32[3,1024]{1,0:T(4,128)}, u32[]{:S(2)}) copy-start(s32[3,1024]{1,0:T(4,128)} %param.13) | copy-start | bytes 36868
  4.5 12.6 %copy-start.1 = (bf16[768,768]{1,0:T(8,128)(2,1)S(1)}, bf16[768,768]{1,0:T(8,128)(2,1)}, u32[]{:S(2)}) copy-start(bf16[768,768]{1,0:T(8,128)(2,1)} %down.1) | copy-start | bytes 3538948
  15.8 2.8 %copy-start.12 = (bf16[192,768]{1,0:T(8,128)(2,1)S(1)}, bf16[192,768]{1,0:T(8,128)(2,1)}, u32[]{:S(2)}) copy-start(bf16[192,768]{1,0:T(8,128)(2,1)} %attn.1) | copy-start | bytes 884740
  15.8 4.9 %copy-start.6 = (bf16[768,3,192]{0,2,1:T(8,128)(2,1)S(1)}, bf16[768,3,192]{0,2,1:T(8,128)(2,1)}, u32[]{:S(2)}) copy-start(bf16[768,3,192]{0,2,1:T(8,128)(2,1)} %param.15) | copy-start | bytes 2654212
  18.6 3.4 %copy-start = (bf16[768,768]{1,0:T(8,128)(2,1)S(1)}, bf16[768,768]{1,0:T(8,128)(2,1)}, u32[]{:S(2)}) copy-start(bf16[768,768]{1,0:T(8,128)(2,1)} %up.7) | copy-start | bytes 3538948
  22.0 1.5 copy-start.24
  22.0 8.8 %copy-start.22 = (bf16[768]{0:T(1024)(128)(2,1)S(1)}, bf16[768]{0:T(1024)(128)(2,1)}, u32[]{:S(2)}) copy-start(bf16[768]{0:T(1024)(128)(2,1)} %param.19) | copy-start | bytes 4612
  22.0 9.6 %copy-start.25 = (bf16[192]{0:T(256)(128)(2,1)S(1)}, bf16[192]{0:T(256)(128)(2,1)}, u32[]{:S(2)}) copy-start(bf16[192]{0:T(256)(128)(2,1)} %param.21) | copy-start | bytes 1156
  22.0 10.4 %copy-start.23 = (bf16[192]{0:T(256)(128)(2,1)S(1)}, bf16[192]{0:T(256)(128)(2,1)}, u32[]{:S(2)}) copy-start(bf16[192]{0:T(256)(128)(2,1)} %param.14) | copy-start | bytes 1156
  22.0 14.7 %copy-start.26 = (s32[4]{0:T(128)S(1)}, s32[4]{0:T(128)}, u32[]{:S(2)}) copy-start(s32[4]{0:T(128)} %constant.96.clone) | copy-start | bytes 52
  29.9 8.1 %copy-start.10 = (bf16[192,3072]{1,0:T(8,128)(2,1)}, bf16[192,3072]{1,0:T(8,128)(2,1)S(1)}, u32[]{:S(2)}) copy-start(bf16[192,3072]{1,0:T(8,128)(2,1)S(1)} %collective-permute-done.flip_y) | copy-start | bytes 3538948
  32.4 5.6 %collective-permute-start.2 = (bf16[192,3072]{1,0:T(8,128)(2,1)S(1)}, bf16[192,3072]{1,0:T(8,128)(2,1)S(1)}, u32[]{:S(2)}, u32[]{:S(2)}) collective-permute-start(bf16[192,3072]{1,0:T(8,128)(2,1)S(1)} %collective-permute-done.flip_y), channel_id=1, source_target_pairs={{0,1},{1,0},{2,3},{3,2},{4,5},{5,4},{6,7},{7,6},{8,9},{9,8},{10,11... | collective-permute-start | bytes 3538952 | tf_op jit(solution)/shard_map/ppermute | solution.py:493
  32.5 5.5 %copy-start.9 = (bf16[192,128]{1,0:T(8,128)(2,1)}, bf16[192,128]{1,0:T(8,128)(2,1)S(1)}, u32[]{:S(2)}) copy-start(bf16[192,128]{1,0:T(8,128)(2,1)S(1)} %broadcast_in_dim.55.gain_own.gain) | copy-start | bytes 147460
  32.5 4.2 %collective-permute-start.3 = (bf16[192,128]{1,0:T(8,128)(2,1)S(1)}, bf16[192,128]{1,0:T(8,128)(2,1)S(1)}, u32[]{:S(2)}, u32[]{:S(2)}) collective-permute-start(bf16[192,128]{1,0:T(8,128)(2,1)S(1)} %broadcast_in_dim.55.gain_own.gain), channel_id=1, source_target_pairs={{0,2},{1,3},{2,0},{3,1},{4,6},{5,7},{6,4},{7,5},{8,10},{9,11},{10,... | collective-permute-start | bytes 147464 | tf_op jit(solution)/shard_map/ppermute | solution.py:493
  34.3 2.9 %collective-permute-start.4 = (bf16[192,128]{1,0:T(8,128)(2,1)S(1)}, bf16[192,128]{1,0:T(8,128)(2,1)S(1)}, u32[]{:S(2)}, u32[]{:S(2)}) collective-permute-start(bf16[192,128]{1,0:T(8,128)(2,1)S(1)} %broadcast_in_dim.55.gain_own.gain), channel_id=1, source_target_pairs={{0,1},{1,0},{2,3},{3,2},{4,5},{5,4},{6,7},{7,6},{8,9},{9,8},{10,11... | collective-permute-start | bytes 147464 | tf_op jit(solution)/shard_map/ppermute | solution.py:493
  36.7 1.3 copy-start.19
  36.7 1.2 collective-permute-start.5
  37.2 0.7 copy-start.20
  37.9 0.6 copy-start.21
  38.5 1.0 copy-start.11
  63.8 65.4 %all-to-all-start = ((bf16[8,192,768]{2,1,0:T(8,128)(2,1)}), bf16[8,192,768]{2,1,0:T(8,128)(2,1)S(1)}, u32[]{:S(2)}, u32[]{:S(2)}) async-start(bf16[8,192,768]{2,1,0:T(8,128)(2,1)} %bitcast.39), calls=%async_computation | async-start | bytes 4718592 | tf_op jit(solution)/shard_map/all_to_all | solution.py:516
  69.8 47.3 %copy-start.15 = (f32[768,128]{1,0:T(8,128)S(1)}, f32[768,128]{1,0:T(8,128)}, u32[]{:S(2)}) copy-start(f32[768,128]{1,0:T(8,128)} %get-tuple-element.146) | copy-start | bytes 1179652
  119.3 9.9 %collective-permute-start.6 = (f32[2,192]{1,0:T(2,128)S(1)}, f32[2,192]{1,0:T(2,128)S(1)}, u32[]{:S(2)}, u32[]{:S(2)}) collective-permute-start(f32[2,192]{1,0:T(2,128)S(1)} %pad_maximum_fusion), channel_id=1, source_target_pairs={{0,1},{1,0},{2,3},{3,2},{4,5},{5,4},{6,7},{7,6},{8,9},{9,8},{10,11... | collective-permute-start | bytes 4616 | tf_op jit(solution)/shard_map/ppermute | solution.py:493
  129.1 7.3 %copy-start.18 = (f32[192,128]{1,0:T(8,128)S(1)}, f32[192,128]{1,0:T(8,128)}, u32[]{:S(2)}) copy-start(f32[192,128]{1,0:T(8,128)} %get-tuple-element.174) | copy-start | bytes 294916
  129.1 9.0 %copy-start.16 = (f32[384,128]{1,0:T(8,128)S(1)}, f32[384,128]{1,0:T(8,128)}, u32[]{:S(2)}) copy-start(f32[384,128]{1,0:T(8,128)} %get-tuple-element.172) | copy-start | bytes 589828
  129.1 9.1 %copy-start.14 = (f32[768,128]{1,0:T(8,128)S(1)}, f32[768,128]{1,0:T(8,128)}, u32[]{:S(2)}) copy-start(f32[768,128]{1,0:T(8,128)} %get-tuple-element.173) | copy-start | bytes 1179652
  130.3 22.0 %collective-permute-start.10 = (bf16[1,2,400,1024]{3,2,1,0:T(8,128)(2,1)}, bf16[1,2,400,1024]{3,2,1,0:T(8,128)(2,1)S(1)}, u32[]{:S(2)}, u32[]{:S(2)}) collective-permute-start(bf16[1,2,400,1024]{3,2,1,0:T(8,128)(2,1)} %get-tuple-element.168), channel_id=1, source_target_pairs={{0,1},{1,0},{2,3},{3,2},{4,5},{5,4},{6,7},{7,6},{8,9},{9,8},{10,11... | collective-permute-start | bytes 4915208 | tf_op jit(solution)/shard_map/ppermute | solution.py:493
  130.8 19.4 %collective-permute-start.7 = (bf16[384,768]{1,0:T(8,128)(2,1)}, bf16[384,768]{1,0:T(8,128)(2,1)}, u32[]{:S(2)}, u32[]{:S(2)}) collective-permute-start(bf16[384,768]{1,0:T(8,128)(2,1)} %constant_dynamic-slice_fusion.4), channel_id=1, source_target_pairs={{0,4},{4,0},{8,12},{12,8},{16,20},{20,16},{24,28},{28,24},{1,5},{5... | collective-permute-start | bytes 1769480 | tf_op jit(solution)/shard_map/ppermute | solution.py:493
  136.4 15.9 %collective-permute-start.8 = (bf16[192,768]{1,0:T(8,128)(2,1)}, bf16[192,768]{1,0:T(8,128)(2,1)}, u32[]{:S(2)}, u32[]{:S(2)}) collective-permute-start(bf16[192,768]{1,0:T(8,128)(2,1)} %reduce_sum.75), channel_id=1, source_target_pairs={{0,16},{4,20},{8,24},{12,28},{16,0},{20,4},{24,8},{28,12},{1,17},{... | collective-permute-start | bytes 884744 | tf_op jit(solution)/shard_map/ppermute | solution.py:493
  136.5 13.7 %collective-permute-start.9 = (f32[192]{0:T(256)S(1)}, f32[192]{0:T(256)S(1)}, u32[]{:S(2)}, u32[]{:S(2)}) collective-permute-start(f32[192]{0:T(256)S(1)} %bitcast.42), channel_id=1, source_target_pairs={{0,2},{1,3},{2,0},{3,1},{4,6},{5,7},{6,4},{7,5},{8,10},{9,11},{10,... | collective-permute-start | bytes 2312 | tf_op jit(solution)/shard_map/ppermute | solution.py:493
  138.4 13.8 %copy-start.4 = (bf16[1,2,400,1024]{3,2,1,0:T(8,128)(2,1)S(1)}, bf16[1,2,400,1024]{3,2,1,0:T(8,128)(2,1)}, u32[]{:S(2)}) copy-start(bf16[1,2,400,1024]{3,2,1,0:T(8,128)(2,1)} %get-tuple-element.175.keep) | copy-start | bytes 4915204
  152.3 2.6 %copy-start.5 = (bf16[1,2,400,1024]{3,2,1,0:T(8,128)(2,1)}, bf16[1,2,400,1024]{3,2,1,0:T(8,128)(2,1)S(1)}, u32[]{:S(2)}) copy-start(bf16[1,2,400,1024]{3,2,1,0:T(8,128)(2,1)S(1)} %collective-permute-done.10.from_core) | copy-start | bytes 4915204
  152.3 2.6 %copy-start.13 = (bf16[768,768]{1,0:T(8,128)(2,1)S(1)}, bf16[768,768]{1,0:T(8,128)(2,1)}, u32[]{:S(2)}) copy-start(bf16[768,768]{1,0:T(8,128)(2,1)} %get-tuple-element.144) | copy-start | bytes 3538948
  154.9 16.4 %copy-start.7 = (bf16[384,768]{1,0:T(8,128)(2,1)}, bf16[384,768]{1,0:T(8,128)(2,1)S(1)}, u32[]{:S(2)}) copy-start(bf16[384,768]{1,0:T(8,128)(2,1)S(1)} %maximum_select_fusion.3) | copy-start | bytes 1769476
  157.2 23.3 %collective-permute-start.15 = (bf16[1,2,400,1024]{3,2,1,0:T(8,128)(2,1)}, bf16[1,2,400,1024]{3,2,1,0:T(8,128)(2,1)}, u32[]{:S(2)}, u32[]{:S(2)}) collective-permute-start(bf16[1,2,400,1024]{3,2,1,0:T(8,128)(2,1)} %get-tuple-element.186), channel_id=1, source_target_pairs={{0,1},{1,0},{2,3},{3,2},{4,5},{5,4},{6,7},{7,6},{8,9},{9,8},{10,11... | collective-permute-start | bytes 4915208 | tf_op jit(solution)/shard_map/ppermute | solution.py:493
  157.2 23.3 %collective-permute-start.14 = (bf16[1,1,400,1024]{3,2,1,0:T(8,128)(2,1)}, bf16[1,1,400,1024]{3,2,1,0:T(8,128)(2,1)}, u32[]{:S(2)}, u32[]{:S(2)}) collective-permute-start(bf16[1,1,400,1024]{3,2,1,0:T(8,128)(2,1)} %add_convert_fusion.2), channel_id=1, source_target_pairs={{0,2},{1,3},{2,0},{3,1},{4,6},{5,7},{6,4},{7,5},{8,10},{9,11},{10,... | collective-permute-start | bytes 2457608 | tf_op jit(solution)/shard_map/ppermute | solution.py:493
  158.8 21.7 %collective-permute-start.12 = (bf16[384,768]{1,0:T(8,128)(2,1)S(1)}, bf16[384,768]{1,0:T(8,128)(2,1)}, u32[]{:S(2)}, u32[]{:S(2)}) collective-permute-start(bf16[384,768]{1,0:T(8,128)(2,1)S(1)} %maximum_select_fusion.3), channel_id=1, source_target_pairs={{0,8},{4,12},{8,0},{12,4},{16,24},{20,28},{24,16},{28,20},{1,9},{5... | collective-permute-start | bytes 1769480 | tf_op jit(solution)/shard_map/ppermute | solution.py:493
  158.8 21.7 %collective-permute-start.11 = (bf16[192,768]{1,0:T(8,128)(2,1)}, bf16[192,768]{1,0:T(8,128)(2,1)S(1)}, u32[]{:S(2)}, u32[]{:S(2)}) collective-permute-start(bf16[192,768]{1,0:T(8,128)(2,1)} %get-tuple-element.182), channel_id=1, source_target_pairs={{0,8},{4,12},{8,0},{12,4},{16,24},{20,28},{24,16},{28,20},{1,9},{5... | collective-permute-start | bytes 884744 | tf_op jit(solution)/shard_map/ppermute | solution.py:493
  160.8 10.5 %collective-permute-start.13 = (f32[1536]{0:T(1024)S(1)}, f32[1536]{0:T(1024)S(1)}, u32[]{:S(2)}, u32[]{:S(2)}) collective-permute-start(f32[1536]{0:T(1024)S(1)} %concatenate.41), channel_id=1, source_target_pairs={{0,4},{4,0},{8,12},{12,8},{16,20},{20,16},{24,28},{28,24},{1,5},{5... | collective-permute-start | bytes 18440 | tf_op jit(solution)/shard_map/ppermute | solution.py:493
  161.4 19.7 %copy-start.2 = (bf16[1,2,400,1024]{3,2,1,0:T(8,128)(2,1)S(1)}, bf16[1,2,400,1024]{3,2,1,0:T(8,128)(2,1)}, u32[]{:S(2)}) copy-start(bf16[1,2,400,1024]{3,2,1,0:T(8,128)(2,1)} %get-tuple-element.195.keep) | copy-start | bytes 4915204
  171.3 13.7 %copy-start.8 = (bf16[384,768]{1,0:T(8,128)(2,1)S(1)}, bf16[384,768]{1,0:T(8,128)(2,1)}, u32[]{:S(2)}) copy-start(bf16[384,768]{1,0:T(8,128)(2,1)} %copy-done.7) | copy-start | bytes 1769476
  184.2 10.3 %collective-permute-start.16 = (bf16[1,2,400,1024]{3,2,1,0:T(8,128)(2,1)}, bf16[1,2,400,1024]{3,2,1,0:T(8,128)(2,1)}, u32[]{:S(2)}, u32[]{:S(2)}) collective-permute-start(bf16[1,2,400,1024]{3,2,1,0:T(8,128)(2,1)} %get-tuple-element.199), channel_id=1, source_target_pairs={{0,1},{1,0},{2,3},{3,2},{4,5},{5,4},{6,7},{7,6},{8,9},{9,8},{10,11... | collective-permute-start | bytes 4915208 | tf_op jit(solution)/shard_map/ppermute | solution.py:493
  184.2 10.2 %collective-permute-start.17 = (bf16[96,768]{1,0:T(8,128)(2,1)}, bf16[96,768]{1,0:T(8,128)(2,1)S(1)}, u32[]{:S(2)}, u32[]{:S(2)}) collective-permute-start(bf16[96,768]{1,0:T(8,128)(2,1)} %add_convert_fusion.7), channel_id=1, source_target_pairs={{0,16},{4,20},{8,24},{12,28},{16,0},{20,4},{24,8},{28,12},{1,17},{... | collective-permute-start | bytes 442376 | tf_op jit(solution)/shard_map/ppermute | solution.py:493
  184.2 5.7 %collective-permute-start.18 = (f32[1536]{0:T(1024)}, f32[1536]{0:T(1024)}, u32[]{:S(2)}, u32[]{:S(2)}) collective-permute-start(f32[1536]{0:T(1024)} %add.115), channel_id=1, source_target_pairs={{0,8},{4,12},{8,0},{12,4},{16,24},{20,28},{24,16},{28,20},{1,9},{5... | collective-permute-start | bytes 18440 | tf_op jit(solution)/shard_map/ppermute | solution.py:493
  186.7 8.5 %copy-start.3 = (bf16[1,2,400,1024]{3,2,1,0:T(8,128)(2,1)S(1)}, bf16[1,2,400,1024]{3,2,1,0:T(8,128)(2,1)}, u32[]{:S(2)}) copy-start(bf16[1,2,400,1024]{3,2,1,0:T(8,128)(2,1)} %get-tuple-element.187.keep) | copy-start | bytes 4915204
  197.6 28.0 %collective-permute-start.23 = (bf16[768,768]{1,0:T(8,128)(2,1)S(1)}, bf16[768,768]{1,0:T(8,128)(2,1)S(1)}, u32[]{:S(2)}, u32[]{:S(2)}) collective-permute-start(bf16[768,768]{1,0:T(8,128)(2,1)S(1)} %maximum_select_fusion.1), channel_id=1, source_target_pairs={{0,4},{4,0},{8,12},{12,8},{16,20},{20,16},{24,28},{28,24},{1,5},{5... | collective-permute-start | bytes 3538952 | tf_op jit(solution)/shard_map/ppermute | solution.py:493
  198.2 21.5 %collective-permute-start.22 = (bf16[1,1,400,1024]{3,2,1,0:T(8,128)(2,1)}, bf16[1,1,400,1024]{3,2,1,0:T(8,128)(2,1)}, u32[]{:S(2)}, u32[]{:S(2)}) collective-permute-start(bf16[1,1,400,1024]{3,2,1,0:T(8,128)(2,1)} %add_convert_fusion.1), channel_id=1, source_target_pairs={{0,2},{1,3},{2,0},{3,1},{4,6},{5,7},{6,4},{7,5},{8,10},{9,11},{10,... | collective-permute-start | bytes 2457608 | tf_op jit(solution)/shard_map/ppermute | solution.py:493
  198.7 8.5 %collective-permute-start.19 = (bf16[96,768]{1,0:T(8,128)(2,1)S(1)}, bf16[96,768]{1,0:T(8,128)(2,1)S(1)}, u32[]{:S(2)}, u32[]{:S(2)}) collective-permute-start(bf16[96,768]{1,0:T(8,128)(2,1)S(1)} %add_convert_fusion.5), channel_id=1, source_target_pairs={{0,16},{4,20},{8,24},{12,28},{16,0},{20,4},{24,8},{28,12},{1,17},{... | collective-permute-start | bytes 442376 | tf_op jit(solution)/shard_map/ppermute | solution.py:493
  198.7 8.5 %collective-permute-start.20 = (f32[1536]{0:T(1024)S(1)}, f32[1536]{0:T(1024)S(1)}, u32[]{:S(2)}, u32[]{:S(2)}) collective-permute-start(f32[1536]{0:T(1024)S(1)} %add.119), channel_id=1, source_target_pairs={{0,16},{4,20},{8,24},{12,28},{16,0},{20,4},{24,8},{28,12},{1,17},{... | collective-permute-start | bytes 18440 | tf_op jit(solution)/shard_map/ppermute | solution.py:493
  207.3 12.4 %collective-permute-start.21 = (bf16[192,768]{1,0:T(8,128)(2,1)S(1)}, bf16[192,768]{1,0:T(8,128)(2,1)S(1)}, u32[]{:S(2)}, u32[]{:S(2)}) collective-permute-start(bf16[192,768]{1,0:T(8,128)(2,1)S(1)} %maximum_select_fusion.5), channel_id=1, source_target_pairs={{0,8},{4,12},{8,0},{12,4},{16,24},{20,28},{24,16},{28,20},{1,9},{5... | collective-permute-start | bytes 884744 | tf_op jit(solution)/shard_map/ppermute | solution.py:493
  207.4 28.7 %collective-permute-start.24 = (bf16[1,1,400,1024]{3,2,1,0:T(8,128)(2,1)}, bf16[1,1,400,1024]{3,2,1,0:T(8,128)(2,1)}, u32[]{:S(2)}, u32[]{:S(2)}) collective-permute-start(bf16[1,1,400,1024]{3,2,1,0:T(8,128)(2,1)} %add_convert_fusion), channel_id=1, source_target_pairs={{0,2},{1,3},{2,0},{3,1},{4,6},{5,7},{6,4},{7,5},{8,10},{9,11},{10,... | collective-permute-start | bytes 2457608 | tf_op jit(solution)/shard_map/ppermute | solution.py:493
  225.8 14.6 %collective-permute-start.25 = (bf16[384,768]{1,0:T(8,128)(2,1)S(1)}, bf16[384,768]{1,0:T(8,128)(2,1)S(1)}, u32[]{:S(2)}, u32[]{:S(2)}) collective-permute-start(bf16[384,768]{1,0:T(8,128)(2,1)S(1)} %maximum_select_fusion.4), channel_id=1, source_target_pairs={{0,4},{4,0},{8,12},{12,8},{16,20},{20,16},{24,28},{28,24},{1,5},{5... | collective-permute-start | bytes 1769480 | tf_op jit(solution)/shard_map/ppermute | solution.py:493

commit v5 on v4

--- a/solution.py
+++ b/solution.py
@@ -205,7 +205,7 @@
 
 def attention_kernel(
     first, count, normed, mixed_t, d_att, mask_q, mask_k, gains, cot, attended, d_mixed, gain_sum, norm_row, grads,
-    total, qkv, qx, kx, vn, kt, vt, es, ps, oa, dqa, dka, dva
+    total, qkv, qx, kx, vn, kt, vt, es, ps, dqa, dka, dva
 ):
     seq = pl.program_id(0)
     last = seq == pl.num_programs(0) - 1
@@ -242,53 +242,52 @@
     dka[...] = jnp.zeros_like(dka)
     dva[...] = jnp.zeros_like(dva)
 
+    def straight(trips, i0, base):
+        icols = pl.ds(i0, BI)
+        places = [pl.ds(pl.multiple_of(base + j * BJ, 128), BJ) for j in range(trips)]
+
+        def scores(head, j, sums):
+            rows = slice(head * DH, (head + 1) * DH)
+            e = jnp.exp(dot(kx[head, places[j], :], qx[head, :, icols]))
+            p = dot(vn[head, places[j], :], d_att[rows, icols])
+            es[head % 2, j * BJ : (j + 1) * BJ, :] = e
+            ps[head % 2, j * BJ : (j + 1) * BJ, :] = p
+            more = (jnp.sum(e, axis=0, keepdims=True), jnp.sum(e * p, axis=0, keepdims=True))
+            return more if sums is None else (sums[0] + more[0], sums[1] + more[1])
+
+        def row_grads(head, j, inverse, inner, held):
+            rows = slice(head * DH, (head + 1) * DH)
+            w = es[head % 2, j * BJ : (j + 1) * BJ, :] * inverse
+            d = (w * (ps[head % 2, j * BJ : (j + 1) * BJ, :] - inner)).astype(BF16)
+            w = w.astype(BF16)
+            out = dot(vt[rows, places[j]], w)
+            query = dot(kt[rows, places[j]], d)
+            dva[rows, places[j]] += dot(d_att[rows, icols], w, NT)
+            dka[rows, places[j]] += dot(qx[head, :DH, icols], d, NT)
+            return (out, query) if held is None else (held[0] + out, held[1] + query)
+
+        sums = None
+        for j in range(trips):
+            sums = scores(0, j, sums)
+        for head in range(heads):
+            rows = slice(head * DH, (head + 1) * DH)
+            inverse = 1.0 / sums[0]
+            inner = sums[1] * inverse
+            held = following = None
+            for j in range(trips):
+                if head + 1 < heads:
+                    following = scores(head + 1, j, following)
+                held = row_grads(head, j, inverse, inner, held)
+            attended[rows, icols] = held[0].astype(BF16)
+            dqa[rows, icols] = held[1]
+            sums = following
+
     def query_block(ib, _):
         i0 = pl.multiple_of(ib * BI, BI)
-        icols = pl.ds(i0, BI)
-        base = first[seq * (LEN // BI) + ib]
+        base = first[seq * (LEN // BI) + ib] * 128
         trips = count[seq * (LEN // BI) + ib]
-
-        def scores(j, carry):
-            j0 = pl.multiple_of((base + j) * BJ, BJ)
-            slot = pl.multiple_of(j * BJ, BJ)
-            out = []
-            for head in range(heads):
-                rows = slice(head * DH, (head + 1) * DH)
-                e = jnp.exp(dot(kx[head, pl.ds(j0, BJ), :], qx[head, :, icols]))
-                p = dot(vn[head, pl.ds(j0, BJ), :], d_att[rows, icols])
-                es[head, pl.ds(slot, BJ), :] = e
-                ps[head, pl.ds(slot, BJ), :] = p
-                out.append(carry[2 * head] + jnp.sum(e.reshape(BJ // 8, 8, BI), axis=0))
-                out.append(carry[2 * head + 1] + jnp.sum((e * p).reshape(BJ // 8, 8, BI), axis=0))
-            return tuple(out)
-
-        sums = lax.fori_loop(0, trips, scores, tuple(jnp.zeros((8, BI), F32) for _ in range(2 * heads)))
-        inverse = []
-        inner = []
-        for head in range(heads):
-            inv = 1.0 / jnp.sum(sums[2 * head], axis=0, keepdims=True)
-            inverse.append(inv)
-            inner.append(jnp.sum(sums[2 * head + 1], axis=0, keepdims=True) * inv)
-        oa[...] = jnp.zeros_like(oa)
-        dqa[:, icols] = jnp.zeros((part, BI), F32)
-
-        def row_grads(j, _):
-            j0 = pl.multiple_of((base + j) * BJ, BJ)
-            slot = pl.multiple_of(j * BJ, BJ)
-            jcols = pl.ds(j0, BJ)
-            for head in range(heads):
-                rows = slice(head * DH, (head + 1) * DH)
-                w = es[head, pl.ds(slot, BJ), :] * inverse[head]
-                d = (w * (ps[head, pl.ds(slot, BJ), :] - inner[head])).astype(BF16)
-                w = w.astype(BF16)
-                oa[rows, :] += dot(vt[rows, jcols], w)
-                dqa[rows, icols] += dot(kt[rows, jcols], d)
-                dva[rows, jcols] += dot(d_att[rows, icols], w, NT)
-                dka[rows, jcols] += dot(qx[head, :DH, icols], d, NT)
-            return 0
-
-        lax.fori_loop(0, trips, row_grads, 0)
-        attended[:, icols] = oa[...].astype(BF16)
+        for number in range(1, LEN // BJ + 1):
+            pl.when(trips == number)(functools.partial(straight, number, i0, base))
         return 0
 
     lax.fori_loop(0, LEN // BI, query_block, 0)
@@ -348,9 +347,8 @@
             pltpu.VMEM((heads, LEN, DH), BF16),
             pltpu.VMEM((part, LEN), BF16),
             pltpu.VMEM((part, LEN), BF16),
-            pltpu.VMEM((heads, LEN, BI), F32),
-            pltpu.VMEM((heads, LEN, BI), F32),
-            pltpu.VMEM((part, BI), F32),
+            pltpu.VMEM((2, LEN, BI), F32),
+            pltpu.VMEM((2, LEN, BI), F32),
             pltpu.VMEM((part, LEN), F32),
             pltpu.VMEM((part, LEN), F32),
             pltpu.VMEM((part, LEN), F32),
@@ -657,7 +655,7 @@
     from_y = flip(own_t, "mp", 4, 2)
     gain_own = jnp.broadcast_to(norm_gain[:, None], (part, 128))
     gain_y = flip(gain_own, "mp", 4, 2)
-    gains = (gain_own, gain_y, flip(gain_own, "mp", 4, 1), flip(gain_y, "mp", 4, 1))
+    gain_c = flip(gain_own, "mp", 4, 1)
 
     mixed_t = jnp.transpose(qkv_weight, (1, 2, 0)).reshape(3 * part, width)
     mixed = mixed_t.T
@@ -678,8 +676,10 @@
     block_last = image_ids[:, BI - 1 :: BI]
     starts = jnp.sum(image_ids[:, None, :] < block_first[:, :, None], axis=2, dtype=jnp.int32)
     ends = jnp.sum(image_ids[:, None, :] <= block_last[:, :, None], axis=2, dtype=jnp.int32)
-    first = (starts // BJ).reshape(-1)
-    count = ((ends + BJ - 1) // BJ).reshape(-1) - first
+    first = starts // 128
+    count = ((ends + 127) // 128 - first + BJ // 128 - 1) // (BJ // 128)
+    first = jnp.minimum(first, (LEN - count * BJ) // 128).reshape(-1)
+    count = count.reshape(-1)
 
     pick = (jnp.arange(part)[:, None] + me * part == jnp.arange(width)[None, :]).astype(BF16)
     d_act, d_att, cot_own, cot_sum = early_call(cotangent, down_weight, attn_weight, pick)
@@ -688,7 +688,8 @@
         d_act, d_att, mixed_t, mixed, up_t, down_t, attn_t, up_bias_col, head_gains, mask_q, mask_k, first, count,
         bias_col,
     )
-    prepared, from_y = tie(prepared, from_y)
+    prepared, (from_y, gain_y, gain_c) = tie(prepared, (from_y, gain_y, gain_c))
+    gains = (gain_own, gain_y, gain_c, flip(gain_y, "mp", 4, 1))
     (
         d_act, d_att, mixed_t, mixed, up_t, down_t, attn_t, up_bias_col, head_gains, mask_q, mask_k, first, count,
         bias_col,

time: 247 us -> 238 us (0.964)
  Pallas kernels: 121 us -> 111 us
  starting transfers between devices: 30.2 us -> 25.3 us
  waiting for transfers between devices: 52.2 us -> 55.5 us
    pallas_call x1, Pallas kernels: 46.5 us -> 36.7 us  [attention_call(): pl.pallas_call(attention_kernel, grid_spec=grid_spec, out_shape=[jax.Shap...]
    ppermute x26, starting transfers between devices: 24.2 us -> 19.4 us  [flip(): return lax.ppermute(value, axis, [(i, i ^ bit) for i in range(size)])]
    all_to_all x1, waiting for transfers between devices: 0.01 us -> 4.61 us  [move(): return lax.all_to_all(send, 'dp', 0, 0, tiled=True)]
    unnamed x57 -> x51, local copies, waits for them, and re-layouts: 5.53 us -> 6.58 us
  transfers between devices with their start and end apart: 27 -> 27, of which waited for: 12 -> 12; matrix products, arithmetic and copies ran while one was open for 10% -> 12% of each run, Pallas kernels for 38% -> 35%
where the time goes in v5:
time: 238 us
  Pallas kernels  111 us (47%)
  waiting for transfers between devices  55.5 us (23%)
  other arithmetic  26.2 us (11%)
  starting transfers between devices  25.3 us (11%)
  local copies, waits for them, and re-layouts  18.7 us (8%)
    ppermute x26, waiting for transfers between devices, flip(): return lax.ppermute(value, axis, [(i, i ^ bit) for i in range(size)])  50.9 us
    pallas_call x1, Pallas kernels, attention_call(): pl.pallas_call(attention_kernel, grid_spec=grid_spec, out_shape=[jax.Shap...  36.7 us
    pallas_call x3, Pallas kernels, project_call(): pl.pallas_call(project_kernel, grid_spec=grid_spec, out_shape=[jax.ShapeD...  29.6 us
    pallas_call x1, Pallas kernels, mlp_call(): pl.pallas_call(functools.partial(mlp_kernel, pieces_order), grid_spec=gri...  24.2 us
    ppermute x26, starting transfers between devices, flip(): return lax.ppermute(value, axis, [(i, i ^ bit) for i in range(size)])  19.4 us
    pallas_call x1, Pallas kernels, early_call(): pl.pallas_call(early_kernel, grid=(tokens // block,), in_specs=[pl.BlockS...  11.3 us
    pallas_call x3, Pallas kernels, finish_call(): pl.pallas_call(finish_kernel, grid=(size * steps,), in_specs=[packed, pac...  9.43 us
    unnamed x51, local copies, waits for them, and re-layouts  6.58 us
  transfers between devices with their start and end apart: 27, of which 12 were waited for; matrix products, arithmetic and copies ran while one was open for 12% of the time, Pallas kernels for 35%

profile of v5, /device:TPU:0, one launch (start us, length us, event | category | flops | bytes accessed | tf_op | source)
XLA Modules:
  0.0 237.9 jit_solution(4673619206550374681)
XLA Ops:
  0.6 0.7 broadcast_in_dim.55.gain_own.gain
  1.4 3.0 %collective-permute-start.1 = (bf16[192,128]{1,0:T(8,128)(2,1)S(1)}, bf16[192,128]{1,0:T(8,128)(2,1)S(1)}, u32[]{:S(2)}, u32[]{:S(2)}) collective-permute-start(bf16[192,128]{1,0:T(8,128)(2,1)S(1)} %broadcast_in_dim.55.gain_own.gain), channel_id=1, source_target_pairs={{0,2},{1,3},{2,0},{3,1},{4,6},{5,7},{6,4},{7,5},{8,10},{9,11},{10,... | collective-permute-start | bytes 147464 | tf_op jit(solution)/shard_map/ppermute | solution.py:491
  4.9 0.8 slice.68
  5.8 0.8 slice.69
  6.6 1.0 convert_reduce_fusion
  7.7 1.4 fusion.3.mask_q
  9.1 1.4 select_convert_fusion.mask_k
  10.6 0.8 fusion.1.pick
  11.9 11.3 %early.1 = (bf16[3,768,1024]{2,1,0:T(8,128)(2,1)}, bf16[3,192,1024]{2,1,0:T(8,128)(2,1)}, bf16[192,3072]{1,0:T(8,128)(2,1)}, f32[192,128]{1,0:T(8,128)}) custom-call(bf16[3072,768]{1,0:T(8,128)(2,1)} %cot.5, bf16[768,768]{1,0:T(8,128)(2,1)} %down.1, bf16[192,768]{1,0:T(8,128)(2,1)} %attn.1, bf16[192,768]{1,0:T(8,128)(2,1)} %fusion.1.pick), custom_call_target="tpu_custom_call" | custom-call | flops 10000 | bytes 12000 | tf_op jit(solution)/shard_map/early/pallas_call | solution.py:62
  23.2 1.4 copy.37
  24.7 2.0 copy.38
  26.7 1.3 copy.35
  28.0 1.5 copy.36
  29.6 3.5 %collective-permute-done.flip_y = bf16[192,3072]{1,0:T(8,128)(2,1)S(1)} collective-permute-done((bf16[192,3072]{1,0:T(8,128)(2,1)}, bf16[192,3072]{1,0:T(8,128)(2,1)S(1)}, u32[]{:S(2)}, u32[]{:S(2)}) %collective-permute-start) | collective-permute-done | bytes 1179680 | tf_op jit(solution)/shard_map/ppermute | solution.py:491
  33.0 0.9 broadcast_in_dim.27.gains
  34.0 0.9 broadcast_in_dim.24.up_bias
  34.8 0.7 broadcast_in_dim.54.bias
  36.6 1.9 collective-permute-done.5.gain_cy
  39.1 1.0 copy-done.11
  40.1 24.2 %mlp.1 = (bf16[3,768,1024]{2,1,0:T(8,128)(2,1)}, bf16[3,768,1024]{2,1,0:T(8,128)(2,1)}, bf16[3,768,1024]{2,1,0:T(8,128)(2,1)}, f32[8,3072]{1,0:T(8,128)}, f32[76...) custom-call(s32[4]{0:T(128)} %xor_multiply_fusion.place, ...), custom_call_target="tpu_custom_call" | custom-call | flops 20000 | bytes 30000 | tf_op jit(solution)/shard_map/mlp/pallas_call | solution.py:188
  64.3 5.8 %all-to-all-start = ((bf16[8,192,768]{2,1,0:T(8,128)(2,1)}), bf16[8,192,768]{2,1,0:T(8,128)(2,1)S(1)}, u32[]{:S(2)}, u32[]{:S(2)}) async-start(bf16[8,192,768]{2,1,0:T(8,128)(2,1)} %bitcast.39), calls=%async_computation | async-start | bytes 4718592 | tf_op jit(solution)/shard_map/all_to_all | solution.py:514
  70.1 36.7 %attention.1 = (bf16[3,192,1024]{2,1,0:T(8,128)(2,1)}, bf16[3,576,1024]{2,1,0:T(8,128)(2,1)}, f32[384,128]{1,0:T(8,128)}, f32[1,768]{1,0:T(1,128)}, bf16[768,768]{1,0:T(8,128)(2,1)}) custom-call(s32[12]{0:T(128)} %get-tuple-element.136.first, s32[12]{0:T(128)} %get-tuple-element.137.count, bf16[3,768,1024]{2,1,0:T(8,128)(2,1)} %get-tuple-element.140.normed, ...), custom_call_target="tpu_custom_call" | custom-call | flops 18000 | bytes 5000 | tf_op jit(solution)/shard_map/attention/pallas_call | solution.py:357
  106.8 0.7 reduce.1
  107.9 1.9 constant_dynamic-slice_fusion.4
  109.8 9.8 %project.3 = (bf16[1,2,400,1024]{3,2,1,0:T(8,128)(2,1)}, bf16[1,2,400,1024]{3,2,1,0:T(8,128)(2,1)}) custom-call(s32[1]{0:T(128)} %bitcast.shard, bf16[3,768,1024]{2,1,0:T(8,128)(2,1)} %get-tuple-element.135.active, bf16[3,192,1024]{2,1,0:T(8,128)(2,1)} %get-tuple-element.182.attended, bf16[3,768,1024]{2,1,0:T(8,128)(2,1)} %get-tuple-element.152.d_pre, ...), custom_call_target="tpu_custom_call" | custom-call | flops 8000 | bytes 16000 | tf_op jit(solution)/shard_map/project/pallas_call | solution.py:432
  119.6 4.6 %all-to-all-done = bf16[8,192,768]{2,1,0:T(8,128)(2,1)S(1)} async-done(((bf16[8,192,768]{2,1,0:T(8,128)(2,1)}), bf16[8,192,768]{2,1,0:T(8,128)(2,1)S(1)}, u32[]{:S(2)}, u32[]{:S(2)}) %all-to-all-start) | async-done | bytes 2359328 | tf_op jit(solution)/shard_map/all_to_all | solution.py:514
  124.3 1.1 reduce_sum.75
  125.4 3.4 %collective-permute-start.7 = (bf16[384,768]{1,0:T(8,128)(2,1)}, bf16[384,768]{1,0:T(8,128)(2,1)}, u32[]{:S(2)}, u32[]{:S(2)}) collective-permute-start(bf16[384,768]{1,0:T(8,128)(2,1)} %constant_dynamic-slice_fusion.4), channel_id=1, source_target_pairs={{0,4},{4,0},{8,12},{12,8},{16,20},{20,16},{24,28},{28,24},{1,5},{5... | collective-permute-start | bytes 1769480 | tf_op jit(solution)/shard_map/ppermute | solution.py:491
  128.9 0.8 collective-permute-start.9
  130.1 9.9 %project.4 = (bf16[1,2,400,1024]{3,2,1,0:T(8,128)(2,1)}, bf16[1,2,400,1024]{3,2,1,0:T(8,128)(2,1)}) custom-call(s32[1]{0:T(128)} %bitcast.shard, bf16[3,768,1024]{2,1,0:T(8,128)(2,1)} %get-tuple-element.135.active, bf16[3,192,1024]{2,1,0:T(8,128)(2,1)} %get-tuple-element.182.attended, bf16[3,768,1024]{2,1,0:T(8,128)(2,1)} %get-tuple-element.152.d_pre, ...), custom_call_target="tpu_custom_call" | custom-call | flops 8000 | bytes 16000 | tf_op jit(solution)/shard_map/project/pallas_call | solution.py:432
  140.0 2.6 %collective-permute-done.7 = bf16[384,768]{1,0:T(8,128)(2,1)} collective-permute-done((bf16[384,768]{1,0:T(8,128)(2,1)}, bf16[384,768]{1,0:T(8,128)(2,1)}, u32[]{:S(2)}, u32[]{:S(2)}) %collective-permute-start.7) | collective-permute-done | bytes 589856 | tf_op jit(solution)/shard_map/ppermute | solution.py:491
  142.6 2.4 collective-permute-done.8
  145.0 1.2 add_convert_fusion.2
  146.2 1.4 maximum_select_fusion.3
  147.6 2.2 add_convert_fusion.3
  149.9 0.8 collective-permute-start.14
  150.7 2.0 collective-permute-start.11
  153.1 9.9 %project.5 = (bf16[1,2,400,1024]{3,2,1,0:T(8,128)(2,1)}, bf16[1,2,400,1024]{3,2,1,0:T(8,128)(2,1)}) custom-call(s32[1]{0:T(128)} %bitcast.shard, bf16[3,768,1024]{2,1,0:T(8,128)(2,1)} %get-tuple-element.135.active, bf16[3,192,1024]{2,1,0:T(8,128)(2,1)} %get-tuple-element.182.attended, bf16[3,768,1024]{2,1,0:T(8,128)(2,1)} %get-tuple-element.152.d_pre, ...), custom_call_target="tpu_custom_call" | custom-call | flops 8000 | bytes 16000 | tf_op jit(solution)/shard_map/project/pallas_call | solution.py:432
  163.0 9.5 %collective-permute-done.11 = bf16[192,768]{1,0:T(8,128)(2,1)S(1)} collective-permute-done((bf16[192,768]{1,0:T(8,128)(2,1)}, bf16[192,768]{1,0:T(8,128)(2,1)S(1)}, u32[]{:S(2)}, u32[]{:S(2)}) %collective-permute-start.11) | collective-permute-done | bytes 294944 | tf_op jit(solution)/shard_map/ppermute | solution.py:491
  173.1 2.3 add_convert_fusion.1
  175.4 0.7 add_convert_fusion.7
  176.1 1.7 collective-permute-start.18
  177.9 1.6 maximum_select_fusion.1
  179.5 3.2 %finish.3 = (bf16[192,3072]{1,0:T(8,128)(2,1)}, f32[192,3072]{1,0:T(8,128)}) custom-call(bf16[1,2,400,1024]{3,2,1,0:T(8,128)(2,1)} %get-tuple-element.179.keep, bf16[1,2,400,1024]{3,2,1,0:T(8,128)(2,1)} %copy-done.5, bf16[1,1,400,1024]{3,2,1,0:T(8,128)(2,1)} %collective-permute-done.14.from_y, bf16[192,3072]{1,0:T(8,128)(2,1)} %bitcast.22, ...), custom_call_target="tpu_custom_call" | custom-call | flops 3000 | bytes 5000 | tf_op jit(solution)/shard_map/finish/pallas_call | solution.py:468
  182.6 3.7 %collective-permute-done.17 = bf16[96,768]{1,0:T(8,128)(2,1)S(1)} collective-permute-done((bf16[96,768]{1,0:T(8,128)(2,1)}, bf16[96,768]{1,0:T(8,128)(2,1)S(1)}, u32[]{:S(2)}, u32[]{:S(2)}) %collective-permute-start.17) | collective-permute-done | bytes 147488 | tf_op jit(solution)/shard_map/ppermute | solution.py:491
  186.4 0.7 add.137
  187.1 2.3 add_convert_fusion
  190.1 1.3 collective-permute-start.22
  191.4 2.9 %collective-permute-start.20 = (f32[1536]{0:T(1024)S(1)}, f32[1536]{0:T(1024)S(1)}, u32[]{:S(2)}, u32[]{:S(2)}) collective-permute-start(f32[1536]{0:T(1024)S(1)} %add.137), channel_id=1, source_target_pairs={{0,16},{4,20},{8,24},{12,28},{16,0},{20,4},{24,8},{28,12},{1,17},{... | collective-permute-start | bytes 18440 | tf_op jit(solution)/shard_map/ppermute | solution.py:491
  194.3 5.4 %collective-permute-done.20 = f32[1536]{0:T(1024)S(1)} collective-permute-done((f32[1536]{0:T(1024)S(1)}, f32[1536]{0:T(1024)S(1)}, u32[]{:S(2)}, u32[]{:S(2)}) %collective-permute-start.20) | collective-permute-done | bytes 6176 | tf_op jit(solution)/shard_map/ppermute | solution.py:491
  199.8 0.8 collective-permute-start.24
  200.7 0.7 slice.94
  201.4 0.7 slice.81
  202.1 1.3 fusion.5
  203.3 8.3 %collective-permute-done.22.from_y = bf16[1,1,400,1024]{3,2,1,0:T(8,128)(2,1)} collective-permute-done((bf16[1,1,400,1024]{3,2,1,0:T(8,128)(2,1)}, bf16[1,1,400,1024]{3,2,1,0:T(8,128)(2,1)}, u32[]{:S(2)}, u32[]{:S(2)}) %collective-permute-start.22) | collective-permute-done | bytes 819232 | tf_op jit(solution)/shard_map/ppermute | solution.py:491
  211.6 5.9 %collective-permute-done.23 = bf16[768,768]{1,0:T(8,128)(2,1)S(1)} collective-permute-done((bf16[768,768]{1,0:T(8,128)(2,1)S(1)}, bf16[768,768]{1,0:T(8,128)(2,1)S(1)}, u32[]{:S(2)}, u32[]{:S(2)}) %collective-permute-start.23) | collective-permute-done | bytes 1179680 | tf_op jit(solution)/shard_map/ppermute | solution.py:491
  218.2 3.1 %finish.4 = (bf16[192,3072]{1,0:T(8,128)(2,1)}, f32[192,3072]{1,0:T(8,128)}) custom-call(bf16[1,2,400,1024]{3,2,1,0:T(8,128)(2,1)} %get-tuple-element.199.keep, bf16[1,2,400,1024]{3,2,1,0:T(8,128)(2,1)} %collective-permute-done.15.from_core, bf16[1,1,400,1024]{3,2,1,0:T(8,128)(2,1)} %collective-permute-done.22.from_y, ...), custom_call_target="tpu_custom_call", output_to_operand_aliasing={{0}: (8, {}), {1}: (9, {})} | custom-call | flops 3000 | bytes 5000 | tf_op jit(solution)/shard_map/finish/pallas_call | solution.py:468
  221.4 0.6 maximum_select_fusion
  222.0 2.5 %slice_convert_fusion = (f32[768,768]{1,0:T(8,128)}, f32[768,768]{1,0:T(8,128)}) fusion(bf16[1536,768]{1,0:T(8,128)(2,1)S(1)} %maximum_select_fusion), kind=kLoop, calls=%fused_computation.4 | loop fusion | flops 1179648 | bytes 7077888 | tf_op jit(solution)/shard_map/convert_element_type | solution.py:792
  224.6 3.3 %collective-permute-done.24.from_y = bf16[1,1,400,1024]{3,2,1,0:T(8,128)(2,1)} collective-permute-done((bf16[1,1,400,1024]{3,2,1,0:T(8,128)(2,1)}, bf16[1,1,400,1024]{3,2,1,0:T(8,128)(2,1)}, u32[]{:S(2)}, u32[]{:S(2)}) %collective-permute-start.24) | collective-permute-done | bytes 819232 | tf_op jit(solution)/shard_map/ppermute | solution.py:491
  227.9 4.5 %collective-permute-done.25 = bf16[384,768]{1,0:T(8,128)(2,1)S(1)} collective-permute-done((bf16[384,768]{1,0:T(8,128)(2,1)S(1)}, bf16[384,768]{1,0:T(8,128)(2,1)S(1)}, u32[]{:S(2)}, u32[]{:S(2)}) %collective-permute-start.25) | collective-permute-done | bytes 589856 | tf_op jit(solution)/shard_map/ppermute | solution.py:491
  232.6 1.3 slice.90
  233.9 0.9 slice.92
  234.7 3.2 %finish.5 = (bf16[192,3072]{1,0:T(8,128)(2,1)}, f32[192,3072]{1,0:T(8,128)}) custom-call(bf16[1,2,400,1024]{3,2,1,0:T(8,128)(2,1)} %get-tuple-element.191.keep, bf16[1,2,400,1024]{3,2,1,0:T(8,128)(2,1)} %collective-permute-done.16.from_core, bf16[1,1,400,1024]{3,2,1,0:T(8,128)(2,1)} %collective-permute-done.24.from_y, ...), custom_call_target="tpu_custom_call", output_to_operand_aliasing={{0}: (8, {}), {1}: (9, {})} | custom-call | flops 3000 | bytes 5000 | tf_op jit(solution)/shard_map/finish/pallas_call | solution.py:468
  (107 shorter events, 6.7 us)
Async XLA Ops:
  1.4 21.8 %copy-start.9 = (bf16[192,128]{1,0:T(8,128)(2,1)}, bf16[192,128]{1,0:T(8,128)(2,1)S(1)}, u32[]{:S(2)}) copy-start(bf16[192,128]{1,0:T(8,128)(2,1)S(1)} %broadcast_in_dim.55.gain_own.gain) | copy-start | bytes 147460
  1.4 28.2 %collective-permute-start.1 = (bf16[192,128]{1,0:T(8,128)(2,1)S(1)}, bf16[192,128]{1,0:T(8,128)(2,1)S(1)}, u32[]{:S(2)}, u32[]{:S(2)}) collective-permute-start(bf16[192,128]{1,0:T(8,128)(2,1)S(1)} %broadcast_in_dim.55.gain_own.gain), channel_id=1, source_target_pairs={{0,2},{1,3},{2,0},{3,1},{4,6},{5,7},{6,4},{7,5},{8,10},{9,11},{10,... | collective-permute-start | bytes 147464 | tf_op jit(solution)/shard_map/ppermute | solution.py:491
  4.4 25.1 %collective-permute-start.2 = (bf16[192,128]{1,0:T(8,128)(2,1)S(1)}, bf16[192,128]{1,0:T(8,128)(2,1)S(1)}, u32[]{:S(2)}, u32[]{:S(2)}) collective-permute-start(bf16[192,128]{1,0:T(8,128)(2,1)S(1)} %broadcast_in_dim.55.gain_own.gain), channel_id=1, source_target_pairs={{0,1},{1,0},{2,3},{3,2},{4,5},{5,4},{6,7},{7,6},{8,9},{9,8},{10,11... | collective-permute-start | bytes 147464 | tf_op jit(solution)/shard_map/ppermute | solution.py:491
  4.4 28.6 %collective-permute-start = (bf16[192,3072]{1,0:T(8,128)(2,1)}, bf16[192,3072]{1,0:T(8,128)(2,1)S(1)}, u32[]{:S(2)}, u32[]{:S(2)}) collective-permute-start(bf16[192,3072]{1,0:T(8,128)(2,1)} %bitcast.19), channel_id=1, source_target_pairs={{0,2},{1,3},{2,0},{3,1},{4,6},{5,7},{6,4},{7,5},{8,10},{9,11},{10,... | collective-permute-start | bytes 3538952 | tf_op jit(solution)/shard_map/ppermute | solution.py:491
  4.6 32.0 %collective-permute-start.3 = (bf16[192,3072]{1,0:T(8,128)(2,1)}, bf16[192,3072]{1,0:T(8,128)(2,1)}, u32[]{:S(2)}, u32[]{:S(2)}) collective-permute-start(bf16[192,3072]{1,0:T(8,128)(2,1)} %bitcast.20), channel_id=1, source_target_pairs={{0,1},{1,0},{2,3},{3,2},{4,5},{5,4},{6,7},{7,6},{8,9},{9,8},{10,11... | collective-permute-start | bytes 3538952 | tf_op jit(solution)/shard_map/ppermute | solution.py:491
  11.9 11.3 %copy-start.1 = (bf16[768,768]{1,0:T(8,128)(2,1)S(1)}, bf16[768,768]{1,0:T(8,128)(2,1)}, u32[]{:S(2)}) copy-start(bf16[768,768]{1,0:T(8,128)(2,1)} %down.1) | copy-start | bytes 3538948
  23.2 3.5 %copy-start.6 = (bf16[768,3,192]{0,2,1:T(8,128)(2,1)S(1)}, bf16[768,3,192]{0,2,1:T(8,128)(2,1)}, u32[]{:S(2)}) copy-start(bf16[768,3,192]{0,2,1:T(8,128)(2,1)} %param.15) | copy-start | bytes 2654212
  24.7 3.3 %copy-start = (bf16[768,768]{1,0:T(8,128)(2,1)S(1)}, bf16[768,768]{1,0:T(8,128)(2,1)}, u32[]{:S(2)}) copy-start(bf16[768,768]{1,0:T(8,128)(2,1)} %up.7) | copy-start | bytes 3538948
  28.0 1.5 copy-start.21
  28.0 6.0 %copy-start.20 = (bf16[768]{0:T(1024)(128)(2,1)S(1)}, bf16[768]{0:T(1024)(128)(2,1)}, u32[]{:S(2)}) copy-start(bf16[768]{0:T(1024)(128)(2,1)} %param.19) | copy-start | bytes 4612
  28.0 6.8 %copy-start.22 = (bf16[192]{0:T(256)(128)(2,1)S(1)}, bf16[192]{0:T(256)(128)(2,1)}, u32[]{:S(2)}) copy-start(bf16[192]{0:T(256)(128)(2,1)} %param.21) | copy-start | bytes 1156
  28.0 8.0 %copy-start.23 = (s32[4]{0:T(128)S(1)}, s32[4]{0:T(128)}, u32[]{:S(2)}) copy-start(s32[4]{0:T(128)} %constant.117.clone) | copy-start | bytes 52
  29.6 8.9 %copy-start.17 = (bf16[192,128]{1,0:T(8,128)(2,1)}, bf16[192,128]{1,0:T(8,128)(2,1)S(1)}, u32[]{:S(2)}) copy-start(bf16[192,128]{1,0:T(8,128)(2,1)S(1)} %collective-permute-done.1.gain_y) | copy-start | bytes 147460
  29.6 8.9 %copy-start.18 = (bf16[192,128]{1,0:T(8,128)(2,1)}, bf16[192,128]{1,0:T(8,128)(2,1)S(1)}, u32[]{:S(2)}) copy-start(bf16[192,128]{1,0:T(8,128)(2,1)S(1)} %collective-permute-done.2.gain_c) | copy-start | bytes 147460
  33.0 5.4 %copy-start.10 = (bf16[192,3072]{1,0:T(8,128)(2,1)}, bf16[192,3072]{1,0:T(8,128)(2,1)S(1)}, u32[]{:S(2)}) copy-start(bf16[192,3072]{1,0:T(8,128)(2,1)S(1)} %collective-permute-done.flip_y) | copy-start | bytes 3538948
  35.5 2.9 %collective-permute-start.4 = (bf16[192,3072]{1,0:T(8,128)(2,1)S(1)}, bf16[192,3072]{1,0:T(8,128)(2,1)S(1)}, u32[]{:S(2)}, u32[]{:S(2)}) collective-permute-start(bf16[192,3072]{1,0:T(8,128)(2,1)S(1)} %collective-permute-done.flip_y), channel_id=1, source_target_pairs={{0,1},{1,0},{2,3},{3,2},{4,5},{5,4},{6,7},{7,6},{8,9},{9,8},{10,11... | collective-permute-start | bytes 3538952 | tf_op jit(solution)/shard_map/ppermute | solution.py:491
  35.5 2.9 %collective-permute-start.5 = (bf16[192,128]{1,0:T(8,128)(2,1)S(1)}, bf16[192,128]{1,0:T(8,128)(2,1)S(1)}, u32[]{:S(2)}, u32[]{:S(2)}) collective-permute-start(bf16[192,128]{1,0:T(8,128)(2,1)S(1)} %collective-permute-done.1.gain_y), channel_id=1, source_target_pairs={{0,1},{1,0},{2,3},{3,2},{4,5},{5,4},{6,7},{7,6},{8,9},{9,8},{10,11... | collective-permute-start | bytes 147464 | tf_op jit(solution)/shard_map/ppermute | solution.py:491
  38.5 0.6 copy-start.19
  39.1 1.0 copy-start.11
  64.3 60.0 %all-to-all-start = ((bf16[8,192,768]{2,1,0:T(8,128)(2,1)}), bf16[8,192,768]{2,1,0:T(8,128)(2,1)S(1)}, u32[]{:S(2)}, u32[]{:S(2)}) async-start(bf16[8,192,768]{2,1,0:T(8,128)(2,1)} %bitcast.39), calls=%async_computation | async-start | bytes 4718592 | tf_op jit(solution)/shard_map/all_to_all | solution.py:514
  70.1 37.5 %copy-start.14 = (f32[768,128]{1,0:T(8,128)S(1)}, f32[768,128]{1,0:T(8,128)}, u32[]{:S(2)}) copy-start(f32[768,128]{1,0:T(8,128)} %get-tuple-element.150) | copy-start | bytes 1179652
  109.8 9.9 %collective-permute-start.6 = (f32[2,192]{1,0:T(2,128)S(1)}, f32[2,192]{1,0:T(2,128)S(1)}, u32[]{:S(2)}, u32[]{:S(2)}) collective-permute-start(f32[2,192]{1,0:T(2,128)S(1)} %pad_maximum_fusion), channel_id=1, source_target_pairs={{0,1},{1,0},{2,3},{3,2},{4,5},{5,4},{6,7},{7,6},{8,9},{9,8},{10,11... | collective-permute-start | bytes 4616 | tf_op jit(solution)/shard_map/ppermute | solution.py:491
  119.6 9.2 %copy-start.16 = (f32[192,128]{1,0:T(8,128)S(1)}, f32[192,128]{1,0:T(8,128)}, u32[]{:S(2)}) copy-start(f32[192,128]{1,0:T(8,128)} %get-tuple-element.178) | copy-start | bytes 294916
  119.6 10.1 %copy-start.15 = (f32[384,128]{1,0:T(8,128)S(1)}, f32[384,128]{1,0:T(8,128)}, u32[]{:S(2)}) copy-start(f32[384,128]{1,0:T(8,128)} %get-tuple-element.176) | copy-start | bytes 589828
  119.6 10.2 %copy-start.13 = (f32[768,128]{1,0:T(8,128)S(1)}, f32[768,128]{1,0:T(8,128)}, u32[]{:S(2)}) copy-start(f32[768,128]{1,0:T(8,128)} %get-tuple-element.177) | copy-start | bytes 1179652
  125.4 19.6 %collective-permute-start.10 = (bf16[1,2,400,1024]{3,2,1,0:T(8,128)(2,1)}, bf16[1,2,400,1024]{3,2,1,0:T(8,128)(2,1)S(1)}, u32[]{:S(2)}, u32[]{:S(2)}) collective-permute-start(bf16[1,2,400,1024]{3,2,1,0:T(8,128)(2,1)} %get-tuple-element.172), channel_id=1, source_target_pairs={{0,1},{1,0},{2,3},{3,2},{4,5},{5,4},{6,7},{7,6},{8,9},{9,8},{10,11... | collective-permute-start | bytes 4915208 | tf_op jit(solution)/shard_map/ppermute | solution.py:491
  125.4 17.2 %collective-permute-start.7 = (bf16[384,768]{1,0:T(8,128)(2,1)}, bf16[384,768]{1,0:T(8,128)(2,1)}, u32[]{:S(2)}, u32[]{:S(2)}) collective-permute-start(bf16[384,768]{1,0:T(8,128)(2,1)} %constant_dynamic-slice_fusion.4), channel_id=1, source_target_pairs={{0,4},{4,0},{8,12},{12,8},{16,20},{20,16},{24,28},{28,24},{1,5},{5... | collective-permute-start | bytes 1769480 | tf_op jit(solution)/shard_map/ppermute | solution.py:491
  128.8 16.2 %collective-permute-start.8 = (bf16[192,768]{1,0:T(8,128)(2,1)}, bf16[192,768]{1,0:T(8,128)(2,1)}, u32[]{:S(2)}, u32[]{:S(2)}) collective-permute-start(bf16[192,768]{1,0:T(8,128)(2,1)} %reduce_sum.75), channel_id=1, source_target_pairs={{0,16},{4,20},{8,24},{12,28},{16,0},{20,4},{24,8},{28,12},{1,17},{... | collective-permute-start | bytes 884744 | tf_op jit(solution)/shard_map/ppermute | solution.py:491
  128.9 13.7 %collective-permute-start.9 = (f32[192]{0:T(256)S(1)}, f32[192]{0:T(256)S(1)}, u32[]{:S(2)}, u32[]{:S(2)}) collective-permute-start(f32[192]{0:T(256)S(1)} %bitcast.42), channel_id=1, source_target_pairs={{0,2},{1,3},{2,0},{3,1},{4,6},{5,7},{6,4},{7,5},{8,10},{9,11},{10,... | collective-permute-start | bytes 2312 | tf_op jit(solution)/shard_map/ppermute | solution.py:491
  130.0 14.9 %copy-start.4 = (bf16[1,2,400,1024]{3,2,1,0:T(8,128)(2,1)S(1)}, bf16[1,2,400,1024]{3,2,1,0:T(8,128)(2,1)}, u32[]{:S(2)}) copy-start(bf16[1,2,400,1024]{3,2,1,0:T(8,128)(2,1)} %get-tuple-element.179.keep) | copy-start | bytes 4915204
  144.9 2.6 %copy-start.5 = (bf16[1,2,400,1024]{3,2,1,0:T(8,128)(2,1)}, bf16[1,2,400,1024]{3,2,1,0:T(8,128)(2,1)S(1)}, u32[]{:S(2)}) copy-start(bf16[1,2,400,1024]{3,2,1,0:T(8,128)(2,1)S(1)} %collective-permute-done.10.from_core) | copy-start | bytes 4915204
  145.0 2.6 %copy-start.12 = (bf16[768,768]{1,0:T(8,128)(2,1)S(1)}, bf16[768,768]{1,0:T(8,128)(2,1)}, u32[]{:S(2)}) copy-start(bf16[768,768]{1,0:T(8,128)(2,1)} %get-tuple-element.148) | copy-start | bytes 3538948
  147.6 15.4 %copy-start.7 = (bf16[384,768]{1,0:T(8,128)(2,1)}, bf16[384,768]{1,0:T(8,128)(2,1)S(1)}, u32[]{:S(2)}) copy-start(bf16[384,768]{1,0:T(8,128)(2,1)S(1)} %maximum_select_fusion.3) | copy-start | bytes 1769476
  149.9 22.6 %collective-permute-start.15 = (bf16[1,2,400,1024]{3,2,1,0:T(8,128)(2,1)}, bf16[1,2,400,1024]{3,2,1,0:T(8,128)(2,1)}, u32[]{:S(2)}, u32[]{:S(2)}) collective-permute-start(bf16[1,2,400,1024]{3,2,1,0:T(8,128)(2,1)} %get-tuple-element.190), channel_id=1, source_target_pairs={{0,1},{1,0},{2,3},{3,2},{4,5},{5,4},{6,7},{7,6},{8,9},{9,8},{10,11... | collective-permute-start | bytes 4915208 | tf_op jit(solution)/shard_map/ppermute | solution.py:491
  149.9 22.6 %collective-permute-start.14 = (bf16[1,1,400,1024]{3,2,1,0:T(8,128)(2,1)}, bf16[1,1,400,1024]{3,2,1,0:T(8,128)(2,1)}, u32[]{:S(2)}, u32[]{:S(2)}) collective-permute-start(bf16[1,1,400,1024]{3,2,1,0:T(8,128)(2,1)} %add_convert_fusion.2), channel_id=1, source_target_pairs={{0,2},{1,3},{2,0},{3,1},{4,6},{5,7},{6,4},{7,5},{8,10},{9,11},{10,... | collective-permute-start | bytes 2457608 | tf_op jit(solution)/shard_map/ppermute | solution.py:491
  150.7 21.7 %collective-permute-start.12 = (bf16[384,768]{1,0:T(8,128)(2,1)S(1)}, bf16[384,768]{1,0:T(8,128)(2,1)}, u32[]{:S(2)}, u32[]{:S(2)}) collective-permute-start(bf16[384,768]{1,0:T(8,128)(2,1)S(1)} %maximum_select_fusion.3), channel_id=1, source_target_pairs={{0,8},{4,12},{8,0},{12,4},{16,24},{20,28},{24,16},{28,20},{1,9},{5... | collective-permute-start | bytes 1769480 | tf_op jit(solution)/shard_map/ppermute | solution.py:491
  150.7 21.7 %collective-permute-start.11 = (bf16[192,768]{1,0:T(8,128)(2,1)}, bf16[192,768]{1,0:T(8,128)(2,1)S(1)}, u32[]{:S(2)}, u32[]{:S(2)}) collective-permute-start(bf16[192,768]{1,0:T(8,128)(2,1)} %get-tuple-element.186), channel_id=1, source_target_pairs={{0,8},{4,12},{8,0},{12,4},{16,24},{20,28},{24,16},{28,20},{1,9},{5... | collective-permute-start | bytes 884744 | tf_op jit(solution)/shard_map/ppermute | solution.py:491
  152.8 10.2 %collective-permute-start.13 = (f32[1536]{0:T(1024)S(1)}, f32[1536]{0:T(1024)S(1)}, u32[]{:S(2)}, u32[]{:S(2)}) collective-permute-start(f32[1536]{0:T(1024)S(1)} %concatenate.41), channel_id=1, source_target_pairs={{0,4},{4,0},{8,12},{12,8},{16,20},{20,16},{24,28},{28,24},{1,5},{5... | collective-permute-start | bytes 18440 | tf_op jit(solution)/shard_map/ppermute | solution.py:491
  153.1 20.0 %copy-start.2 = (bf16[1,2,400,1024]{3,2,1,0:T(8,128)(2,1)S(1)}, bf16[1,2,400,1024]{3,2,1,0:T(8,128)(2,1)}, u32[]{:S(2)}) copy-start(bf16[1,2,400,1024]{3,2,1,0:T(8,128)(2,1)} %get-tuple-element.199.keep) | copy-start | bytes 4915204
  163.0 14.9 %copy-start.8 = (bf16[384,768]{1,0:T(8,128)(2,1)S(1)}, bf16[384,768]{1,0:T(8,128)(2,1)}, u32[]{:S(2)}) copy-start(bf16[384,768]{1,0:T(8,128)(2,1)} %copy-done.7) | copy-start | bytes 1769476
  176.1 10.3 %collective-permute-start.16 = (bf16[1,2,400,1024]{3,2,1,0:T(8,128)(2,1)}, bf16[1,2,400,1024]{3,2,1,0:T(8,128)(2,1)}, u32[]{:S(2)}, u32[]{:S(2)}) collective-permute-start(bf16[1,2,400,1024]{3,2,1,0:T(8,128)(2,1)} %get-tuple-element.203), channel_id=1, source_target_pairs={{0,1},{1,0},{2,3},{3,2},{4,5},{5,4},{6,7},{7,6},{8,9},{9,8},{10,11... | collective-permute-start | bytes 4915208 | tf_op jit(solution)/shard_map/ppermute | solution.py:491
  176.1 10.2 %collective-permute-start.17 = (bf16[96,768]{1,0:T(8,128)(2,1)}, bf16[96,768]{1,0:T(8,128)(2,1)S(1)}, u32[]{:S(2)}, u32[]{:S(2)}) collective-permute-start(bf16[96,768]{1,0:T(8,128)(2,1)} %add_convert_fusion.7), channel_id=1, source_target_pairs={{0,16},{4,20},{8,24},{12,28},{16,0},{20,4},{24,8},{28,12},{1,17},{... | collective-permute-start | bytes 442376 | tf_op jit(solution)/shard_map/ppermute | solution.py:491
  176.1 6.5 %collective-permute-start.18 = (f32[1536]{0:T(1024)}, f32[1536]{0:T(1024)}, u32[]{:S(2)}, u32[]{:S(2)}) collective-permute-start(f32[1536]{0:T(1024)} %add.133), channel_id=1, source_target_pairs={{0,8},{4,12},{8,0},{12,4},{16,24},{20,28},{24,16},{28,20},{1,9},{5... | collective-permute-start | bytes 18440 | tf_op jit(solution)/shard_map/ppermute | solution.py:491
  179.5 7.6 %copy-start.3 = (bf16[1,2,400,1024]{3,2,1,0:T(8,128)(2,1)S(1)}, bf16[1,2,400,1024]{3,2,1,0:T(8,128)(2,1)}, u32[]{:S(2)}) copy-start(bf16[1,2,400,1024]{3,2,1,0:T(8,128)(2,1)} %get-tuple-element.191.keep) | copy-start | bytes 4915204
  189.5 28.0 %collective-permute-start.23 = (bf16[768,768]{1,0:T(8,128)(2,1)S(1)}, bf16[768,768]{1,0:T(8,128)(2,1)S(1)}, u32[]{:S(2)}, u32[]{:S(2)}) collective-permute-start(bf16[768,768]{1,0:T(8,128)(2,1)S(1)} %maximum_select_fusion.1), channel_id=1, source_target_pairs={{0,4},{4,0},{8,12},{12,8},{16,20},{20,16},{24,28},{28,24},{1,5},{5... | collective-permute-start | bytes 3538952 | tf_op jit(solution)/shard_map/ppermute | solution.py:491
  190.1 21.5 %collective-permute-start.22 = (bf16[1,1,400,1024]{3,2,1,0:T(8,128)(2,1)}, bf16[1,1,400,1024]{3,2,1,0:T(8,128)(2,1)}, u32[]{:S(2)}, u32[]{:S(2)}) collective-permute-start(bf16[1,1,400,1024]{3,2,1,0:T(8,128)(2,1)} %add_convert_fusion.1), channel_id=1, source_target_pairs={{0,2},{1,3},{2,0},{3,1},{4,6},{5,7},{6,4},{7,5},{8,10},{9,11},{10,... | collective-permute-start | bytes 2457608 | tf_op jit(solution)/shard_map/ppermute | solution.py:491
  191.4 8.3 %collective-permute-start.19 = (bf16[96,768]{1,0:T(8,128)(2,1)S(1)}, bf16[96,768]{1,0:T(8,128)(2,1)S(1)}, u32[]{:S(2)}, u32[]{:S(2)}) collective-permute-start(bf16[96,768]{1,0:T(8,128)(2,1)S(1)} %add_convert_fusion.5), channel_id=1, source_target_pairs={{0,16},{4,20},{8,24},{12,28},{16,0},{20,4},{24,8},{28,12},{1,17},{... | collective-permute-start | bytes 442376 | tf_op jit(solution)/shard_map/ppermute | solution.py:491
  191.4 8.3 %collective-permute-start.20 = (f32[1536]{0:T(1024)S(1)}, f32[1536]{0:T(1024)S(1)}, u32[]{:S(2)}, u32[]{:S(2)}) collective-permute-start(f32[1536]{0:T(1024)S(1)} %add.137), channel_id=1, source_target_pairs={{0,16},{4,20},{8,24},{12,28},{16,0},{20,4},{24,8},{28,12},{1,17},{... | collective-permute-start | bytes 18440 | tf_op jit(solution)/shard_map/ppermute | solution.py:491
  199.7 11.9 %collective-permute-start.21 = (bf16[192,768]{1,0:T(8,128)(2,1)S(1)}, bf16[192,768]{1,0:T(8,128)(2,1)S(1)}, u32[]{:S(2)}, u32[]{:S(2)}) collective-permute-start(bf16[192,768]{1,0:T(8,128)(2,1)S(1)} %maximum_select_fusion.5), channel_id=1, source_target_pairs={{0,8},{4,12},{8,0},{12,4},{16,24},{20,28},{24,16},{28,20},{1,9},{5... | collective-permute-start | bytes 884744 | tf_op jit(solution)/shard_map/ppermute | solution.py:491
  199.8 28.0 %collective-permute-start.24 = (bf16[1,1,400,1024]{3,2,1,0:T(8,128)(2,1)}, bf16[1,1,400,1024]{3,2,1,0:T(8,128)(2,1)}, u32[]{:S(2)}, u32[]{:S(2)}) collective-permute-start(bf16[1,1,400,1024]{3,2,1,0:T(8,128)(2,1)} %add_convert_fusion), channel_id=1, source_target_pairs={{0,2},{1,3},{2,0},{3,1},{4,6},{5,7},{6,4},{7,5},{8,10},{9,11},{10,... | collective-permute-start | bytes 2457608 | tf_op jit(solution)/shard_map/ppermute | solution.py:491
  217.7 14.6 %collective-permute-start.25 = (bf16[384,768]{1,0:T(8,128)(2,1)S(1)}, bf16[384,768]{1,0:T(8,128)(2,1)S(1)}, u32[]{:S(2)}, u32[]{:S(2)}) collective-permute-start(bf16[384,768]{1,0:T(8,128)(2,1)S(1)} %maximum_select_fusion.4), channel_id=1, source_target_pairs={{0,4},{4,0},{8,12},{12,8},{16,20},{20,16},{24,28},{28,24},{1,5},{5... | collective-permute-start | bytes 1769480 | tf_op jit(solution)/shard_map/ppermute | solution.py:491

commit v6 on v5

--- a/solution.py
+++ b/solution.py
@@ -457,7 +457,7 @@
     token_grad[...] = cot[...].astype(F32) + inner * scale
 
 
-def finish_call(keep, from_core, from_y, own_t, cot, stats, gain, bias, before, begin, block=512):
+def finish_call(keep, from_core, from_y, own_t, cot, stats, gain, bias, before, begin, block=256):
     part, tokens = own_t.shape
     steps = LEN // block
     size = keep.shape[0]
@@ -732,6 +732,7 @@
         scatters.append(ScatterOverMp(keep, send))
 
     finished = ()
+    wide_grads = ()
     done = set()
 
     def finish_ready(finished):
@@ -744,12 +745,9 @@
                 )
         return finished
 
-    rounds = 0
     while True:
         busy = [f[0] for f in flying]
-        rounds += 1
         ready = [m for m in [mix_sum] + scatters + [short, mlp_sum] if m.more() and m not in busy]
-        ready = [m for m in ready if m is not mlp_sum or rounds > 1]
         finished, flights = launch(ready, finished)
         flying = flying + flights
         if not flying:
@@ -766,11 +764,14 @@
         elif left == 2:
             now = chain + across[:1] + wide + rest
         elif left == 1:
-            now = across + wide + rest + chain
+            now = across + wide + rest or chain
         else:
             now = chain + rest or flying
-        finished = land(now, finished)
+        finished, wide_grads = land(now, (finished, wide_grads))
         flying = [f for f in flying if f not in now]
+        if not mlp_sum.more() and not wide_grads:
+            split = up_weight.shape[1]
+            wide_grads = (mlp_sum.keep[:split].astype(F32), mlp_sum.keep[split:].astype(F32))
     finished = finish_ready(finished)
     block_out, token_grad = finished
     block_out, token_grad = block_out.T, token_grad.T
@@ -787,9 +788,9 @@
         qkv_grad,
         rest[: 2 * part].reshape(2, part),
         mixed_grad[3 * part :],
-        mlp_sum.keep[up_weight.shape[1] :].astype(F32),
+        wide_grads[1],
         rest[2 * part : split],
-        mlp_sum.keep[: up_weight.shape[1]].astype(F32),
+        wide_grads[0],
         rest[split:],
     )
 

time: 238 us -> 229 us (0.962)
  waiting for transfers between devices: 55.5 us -> 32.4 us
  starting transfers between devices: 25.3 us -> 32.1 us
  Pallas kernels: 111 us -> 115 us
    ppermute x26, waiting for transfers between devices: 50.9 us -> 28.3 us  [flip(): return lax.ppermute(value, axis, [(i, i ^ bit) for i in range(size)])]
    ppermute x26, starting transfers between devices: 19.4 us -> 26.3 us  [flip(): return lax.ppermute(value, axis, [(i, i ^ bit) for i in range(size)])]
    pallas_call x3, Pallas kernels: 9.43 us -> 12.8 us  [finish_call(): pl.pallas_call(finish_kernel, grid=(size * steps,), in_specs=[packed, pac...]
  transfers between devices with their start and end apart: 27 -> 27, of which waited for: 12 -> 9; matrix products, arithmetic and copies ran while one was open for 12% -> 13% of each run, Pallas kernels for 35% -> 40%
where the time goes in v6:
time: 229 us; the launch traced here: 227 us
  Pallas kernels  115 us (50%)
  waiting for transfers between devices  32.4 us (14%)
  starting transfers between devices  32.1 us (14%)
  other arithmetic  26.2 us (11%)
  local copies, waits for them, and re-layouts  20.6 us (9%)
    pallas_call x1, Pallas kernels, attention_call(): pl.pallas_call(attention_kernel, grid_spec=grid_spec, out_shape=[jax.Shap...  37.2 us
    pallas_call x3, Pallas kernels, project_call(): pl.pallas_call(project_kernel, grid_spec=grid_spec, out_shape=[jax.ShapeD...  29.5 us
    ppermute x26, waiting for transfers between devices, flip(): return lax.ppermute(value, axis, [(i, i ^ bit) for i in range(size)])  28.3 us
    ppermute x26, starting transfers between devices, flip(): return lax.ppermute(value, axis, [(i, i ^ bit) for i in range(size)])  26.3 us
    pallas_call x1, Pallas kernels, mlp_call(): pl.pallas_call(functools.partial(mlp_kernel, pieces_order), grid_spec=gri...  24.2 us
    pallas_call x3, Pallas kernels, finish_call(): pl.pallas_call(finish_kernel, grid=(size * steps,), in_specs=[packed, pac...  12.8 us
    pallas_call x1, Pallas kernels, early_call(): pl.pallas_call(early_kernel, grid=(tokens // block,), in_specs=[pl.BlockS...  11.3 us
    unnamed x51, local copies, waits for them, and re-layouts  8.43 us
  transfers between devices with their start and end apart: 27, of which 9 were waited for; matrix products, arithmetic and copies ran while one was open for 13% of the time, Pallas kernels for 40%

profile of v6, /device:TPU:0, one launch (start us, length us, event | category | flops | bytes accessed | tf_op | source)
XLA Modules:
  0.0 227.3 jit_solution(44433661615815470)
XLA Ops:
  0.6 0.7 broadcast_in_dim.55.gain_own.gain
  1.4 3.0 %collective-permute-start.1 = (bf16[192,128]{1,0:T(8,128)(2,1)S(1)}, bf16[192,128]{1,0:T(8,128)(2,1)S(1)}, u32[]{:S(2)}, u32[]{:S(2)}) collective-permute-start(bf16[192,128]{1,0:T(8,128)(2,1)S(1)} %broadcast_in_dim.55.gain_own.gain), channel_id=1, source_target_pairs={{0,2},{1,3},{2,0},{3,1},{4,6},{5,7},{6,4},{7,5},{8,10},{9,11},{10,... | collective-permute-start | bytes 147464 | tf_op jit(solution)/shard_map/ppermute | solution.py:491
  4.9 0.8 slice.68
  5.8 0.8 slice.69
  6.6 1.0 convert_reduce_fusion
  7.7 1.4 fusion.3.mask_q
  9.1 1.4 select_convert_fusion.mask_k
  10.6 0.8 fusion.1.pick
  11.9 11.3 %early.1 = (bf16[3,768,1024]{2,1,0:T(8,128)(2,1)}, bf16[3,192,1024]{2,1,0:T(8,128)(2,1)}, bf16[192,3072]{1,0:T(8,128)(2,1)}, f32[192,128]{1,0:T(8,128)}) custom-call(bf16[3072,768]{1,0:T(8,128)(2,1)} %cot.5, bf16[768,768]{1,0:T(8,128)(2,1)} %down.1, bf16[192,768]{1,0:T(8,128)(2,1)} %attn.1, bf16[192,768]{1,0:T(8,128)(2,1)} %fusion.1.pick), custom_call_target="tpu_custom_call" | custom-call | flops 10000 | bytes 12000 | tf_op jit(solution)/shard_map/early/pallas_call | solution.py:62
  23.2 1.5 copy.37
  24.7 2.0 copy.38
  26.7 1.3 copy.35
  28.0 1.5 copy.36
  29.6 3.4 %collective-permute-done.flip_y = bf16[192,3072]{1,0:T(8,128)(2,1)S(1)} collective-permute-done((bf16[192,3072]{1,0:T(8,128)(2,1)}, bf16[192,3072]{1,0:T(8,128)(2,1)S(1)}, u32[]{:S(2)}, u32[]{:S(2)}) %collective-permute-start) | collective-permute-done | bytes 1179680 | tf_op jit(solution)/shard_map/ppermute | solution.py:491
  33.0 0.9 broadcast_in_dim.27.gains
  33.9 0.9 broadcast_in_dim.24.up_bias
  36.5 1.9 collective-permute-done.5.gain_cy
  39.1 1.0 copy-done.9
  40.1 24.2 %mlp.1 = (bf16[3,768,1024]{2,1,0:T(8,128)(2,1)}, bf16[3,768,1024]{2,1,0:T(8,128)(2,1)}, bf16[3,768,1024]{2,1,0:T(8,128)(2,1)}, f32[8,3072]{1,0:T(8,128)}, f32[76...) custom-call(s32[4]{0:T(128)} %xor_multiply_fusion.place, ...), custom_call_target="tpu_custom_call" | custom-call | flops 20000 | bytes 30000 | tf_op jit(solution)/shard_map/mlp/pallas_call | solution.py:188
  64.3 5.8 %all-to-all-start = ((bf16[8,192,768]{2,1,0:T(8,128)(2,1)}), bf16[8,192,768]{2,1,0:T(8,128)(2,1)S(1)}, u32[]{:S(2)}, u32[]{:S(2)}) async-start(bf16[8,192,768]{2,1,0:T(8,128)(2,1)} %bitcast.39), calls=%async_computation | async-start | bytes 4718592 | tf_op jit(solution)/shard_map/all_to_all | solution.py:514
  70.1 37.2 %attention.1 = (bf16[3,192,1024]{2,1,0:T(8,128)(2,1)}, bf16[3,576,1024]{2,1,0:T(8,128)(2,1)}, f32[384,128]{1,0:T(8,128)}, f32[1,768]{1,0:T(1,128)}, bf16[768,768]{1,0:T(8,128)(2,1)}) custom-call(s32[12]{0:T(128)} %get-tuple-element.144.first, s32[12]{0:T(128)} %get-tuple-element.145.count, bf16[3,768,1024]{2,1,0:T(8,128)(2,1)} %get-tuple-element.148.normed, ...), custom_call_target="tpu_custom_call" | custom-call | flops 18000 | bytes 5000 | tf_op jit(solution)/shard_map/attention/pallas_call | solution.py:357
  107.3 0.7 reduce.1
  108.3 1.9 constant_dynamic-slice_fusion.4
  110.3 9.8 %project.3 = (bf16[1,2,400,1024]{3,2,1,0:T(8,128)(2,1)}, bf16[1,2,400,1024]{3,2,1,0:T(8,128)(2,1)}) custom-call(s32[1]{0:T(128)} %bitcast.shard, bf16[3,768,1024]{2,1,0:T(8,128)(2,1)} %get-tuple-element.143.active, bf16[3,192,1024]{2,1,0:T(8,128)(2,1)} %get-tuple-element.190.attended, bf16[3,768,1024]{2,1,0:T(8,128)(2,1)} %get-tuple-element.160.d_pre, ...), custom_call_target="tpu_custom_call" | custom-call | flops 8000 | bytes 16000 | tf_op jit(solution)/shard_map/project/pallas_call | solution.py:432
  120.1 4.1 %all-to-all-done = bf16[8,192,768]{2,1,0:T(8,128)(2,1)S(1)} async-done(((bf16[8,192,768]{2,1,0:T(8,128)(2,1)}), bf16[8,192,768]{2,1,0:T(8,128)(2,1)S(1)}, u32[]{:S(2)}, u32[]{:S(2)}) %all-to-all-start) | async-done | bytes 2359328 | tf_op jit(solution)/shard_map/all_to_all | solution.py:514
  124.3 1.1 reduce_sum.75
  125.4 1.5 collective-permute-start.7
  126.8 3.8 %collective-permute-start.8 = (bf16[192,768]{1,0:T(8,128)(2,1)}, bf16[192,768]{1,0:T(8,128)(2,1)}, u32[]{:S(2)}, u32[]{:S(2)}) collective-permute-start(bf16[192,768]{1,0:T(8,128)(2,1)} %reduce_sum.75), channel_id=1, source_target_pairs={{0,16},{4,20},{8,24},{12,28},{16,0},{20,4},{24,8},{28,12},{1,17},{... | collective-permute-start | bytes 884744 | tf_op jit(solution)/shard_map/ppermute | solution.py:491
  130.7 0.8 collective-permute-start.9
  131.9 9.9 %project.4 = (bf16[1,2,400,1024]{3,2,1,0:T(8,128)(2,1)}, bf16[1,2,400,1024]{3,2,1,0:T(8,128)(2,1)}) custom-call(s32[1]{0:T(128)} %bitcast.shard, bf16[3,768,1024]{2,1,0:T(8,128)(2,1)} %get-tuple-element.143.active, bf16[3,192,1024]{2,1,0:T(8,128)(2,1)} %get-tuple-element.190.attended, bf16[3,768,1024]{2,1,0:T(8,128)(2,1)} %get-tuple-element.160.d_pre, ...), custom_call_target="tpu_custom_call" | custom-call | flops 8000 | bytes 16000 | tf_op jit(solution)/shard_map/project/pallas_call | solution.py:432
  141.8 2.3 %collective-permute-done.8 = bf16[192,768]{1,0:T(8,128)(2,1)} collective-permute-done((bf16[192,768]{1,0:T(8,128)(2,1)}, bf16[192,768]{1,0:T(8,128)(2,1)}, u32[]{:S(2)}, u32[]{:S(2)}) %collective-permute-start.8) | collective-permute-done | bytes 294944 | tf_op jit(solution)/shard_map/ppermute | solution.py:491
  144.2 1.2 add_convert_fusion.2
  145.4 1.4 maximum_select_fusion.3
  146.8 2.0 add_convert_fusion.3
  148.9 0.8 collective-permute-start.14
  149.7 0.7 collective-permute-start.12
  150.4 1.3 collective-permute-start.11
  151.8 1.2 collective-permute-start.13
  152.9 9.8 %project.5 = (bf16[1,2,400,1024]{3,2,1,0:T(8,128)(2,1)}, bf16[1,2,400,1024]{3,2,1,0:T(8,128)(2,1)}) custom-call(s32[1]{0:T(128)} %bitcast.shard, bf16[3,768,1024]{2,1,0:T(8,128)(2,1)} %get-tuple-element.143.active, bf16[3,192,1024]{2,1,0:T(8,128)(2,1)} %get-tuple-element.190.attended, bf16[3,768,1024]{2,1,0:T(8,128)(2,1)} %get-tuple-element.160.d_pre, ...), custom_call_target="tpu_custom_call" | custom-call | flops 8000 | bytes 16000 | tf_op jit(solution)/shard_map/project/pallas_call | solution.py:432
  162.7 8.7 %collective-permute-done.11 = bf16[192,768]{1,0:T(8,128)(2,1)S(1)} collective-permute-done((bf16[192,768]{1,0:T(8,128)(2,1)}, bf16[192,768]{1,0:T(8,128)(2,1)S(1)}, u32[]{:S(2)}, u32[]{:S(2)}) %collective-permute-start.11) | collective-permute-done | bytes 294944 | tf_op jit(solution)/shard_map/ppermute | solution.py:491
  171.5 0.9 copy-done.11
  173.4 2.4 %add_convert_fusion.1 = bf16[1,1,400,1024]{3,2,1,0:T(8,128)(2,1)} fusion(bf16[1,2,400,1024]{3,2,1,0:T(8,128)(2,1)} %collective-permute-done.15.from_core, bf16[1,2,400,1024]{3,2,1,0:T(8,128)(2,1)S(1)} %copy-done.2), kind=kLoop, calls=%fused_computation.2 | loop fusion | flops 1638400 | bytes 2457600 | tf_op jit(solution)/shard_map/convert_element_type | solution.py:588
  176.5 2.4 %collective-permute-start.17 = (bf16[96,768]{1,0:T(8,128)(2,1)}, bf16[96,768]{1,0:T(8,128)(2,1)S(1)}, u32[]{:S(2)}, u32[]{:S(2)}) collective-permute-start(bf16[96,768]{1,0:T(8,128)(2,1)} %add_convert_fusion.7), channel_id=1, source_target_pairs={{0,16},{4,20},{8,24},{12,28},{16,0},{20,4},{24,8},{28,12},{1,17},{... | collective-permute-start | bytes 442376 | tf_op jit(solution)/shard_map/ppermute | solution.py:491
  178.9 0.8 collective-permute-start.23
  179.7 1.7 collective-permute-start.18
  181.5 1.3 collective-permute-start.22
  182.7 4.3 %finish.3 = (bf16[192,3072]{1,0:T(8,128)(2,1)}, f32[192,3072]{1,0:T(8,128)}) custom-call(bf16[1,2,400,1024]{3,2,1,0:T(8,128)(2,1)} %get-tuple-element.187.keep, bf16[1,2,400,1024]{3,2,1,0:T(8,128)(2,1)} %copy-done.5, bf16[1,1,400,1024]{3,2,1,0:T(8,128)(2,1)} %copy-done.11, bf16[192,3072]{1,0:T(8,128)(2,1)} %bitcast.22, ...), custom_call_target="tpu_custom_call" | custom-call | flops 3000 | bytes 5000 | tf_op jit(solution)/shard_map/finish/pallas_call | solution.py:468
  187.1 2.4 %add_convert_fusion = bf16[1,1,400,1024]{3,2,1,0:T(8,128)(2,1)} fusion(bf16[1,2,400,1024]{3,2,1,0:T(8,128)(2,1)} %collective-permute-done.16.from_core, bf16[1,2,400,1024]{3,2,1,0:T(8,128)(2,1)S(1)} %copy-done.3), kind=kLoop, calls=%fused_computation.1 | loop fusion | flops 1638400 | bytes 2457600 | tf_op jit(solution)/shard_map/convert_element_type | solution.py:588
  189.5 0.7 add.137
  190.4 2.9 %collective-permute-start.20 = (f32[1536]{0:T(1024)S(1)}, f32[1536]{0:T(1024)S(1)}, u32[]{:S(2)}, u32[]{:S(2)}) collective-permute-start(f32[1536]{0:T(1024)S(1)} %add.137), channel_id=1, source_target_pairs={{0,16},{4,20},{8,24},{12,28},{16,0},{20,4},{24,8},{28,12},{1,17},{... | collective-permute-start | bytes 18440 | tf_op jit(solution)/shard_map/ppermute | solution.py:491
  193.3 6.9 %collective-permute-done.20 = f32[1536]{0:T(1024)S(1)} collective-permute-done((f32[1536]{0:T(1024)S(1)}, f32[1536]{0:T(1024)S(1)}, u32[]{:S(2)}, u32[]{:S(2)}) %collective-permute-start.20) | collective-permute-done | bytes 6176 | tf_op jit(solution)/shard_map/ppermute | solution.py:491
  200.3 1.3 collective-permute-start.24
  203.0 1.3 fusion.5
  204.3 2.8 %collective-permute-done.23 = bf16[768,768]{1,0:T(8,128)(2,1)} collective-permute-done((bf16[768,768]{1,0:T(8,128)(2,1)S(1)}, bf16[768,768]{1,0:T(8,128)(2,1)}, u32[]{:S(2)}, u32[]{:S(2)}) %collective-permute-start.23) | collective-permute-done | bytes 1179680 | tf_op jit(solution)/shard_map/ppermute | solution.py:491
  207.1 1.1 collective-permute-done.21
  208.4 1.6 collective-permute-start.25
  210.0 4.2 %finish.4 = (bf16[192,3072]{1,0:T(8,128)(2,1)}, f32[192,3072]{1,0:T(8,128)}) custom-call(bf16[1,2,400,1024]{3,2,1,0:T(8,128)(2,1)} %get-tuple-element.207.keep, bf16[1,2,400,1024]{3,2,1,0:T(8,128)(2,1)} %collective-permute-done.15.from_core, bf16[1,1,400,1024]{3,2,1,0:T(8,128)(2,1)} %collective-permute-done.22.from_y, ...), custom_call_target="tpu_custom_call", output_to_operand_aliasing={{0}: (8, {}), {1}: (9, {})} | custom-call | flops 3000 | bytes 5000 | tf_op jit(solution)/shard_map/finish/pallas_call | solution.py:468
  214.2 1.9 maximum_select_fusion
  216.1 2.5 %slice_convert_fusion = (f32[768,768]{1,0:T(8,128)}, f32[768,768]{1,0:T(8,128)}) fusion(bf16[1536,768]{1,0:T(8,128)(2,1)S(1)} %maximum_select_fusion), kind=kLoop, calls=%fused_computation.4 | loop fusion | flops 1179648 | bytes 7077888 | tf_op jit(solution)/shard_map/convert_element_type | solution.py:774
  218.7 1.1 collective-permute-done.24.from_y
  219.7 0.9 copy-done.12
  220.6 4.2 %finish.5 = (bf16[192,3072]{1,0:T(8,128)(2,1)}, f32[192,3072]{1,0:T(8,128)}) custom-call(bf16[1,2,400,1024]{3,2,1,0:T(8,128)(2,1)} %get-tuple-element.199.keep, bf16[1,2,400,1024]{3,2,1,0:T(8,128)(2,1)} %collective-permute-done.16.from_core, bf16[1,1,400,1024]{3,2,1,0:T(8,128)(2,1)} %copy-done.12, ...), custom_call_target="tpu_custom_call", output_to_operand_aliasing={{0}: (8, {}), {1}: (9, {})} | custom-call | flops 3000 | bytes 5000 | tf_op jit(solution)/shard_map/finish/pallas_call | solution.py:468
  225.1 1.3 slice.92
  226.4 0.9 slice.94
  (107 shorter events, 8.5 us)
Async XLA Ops:
  1.4 21.8 %copy-start.7 = (bf16[192,128]{1,0:T(8,128)(2,1)}, bf16[192,128]{1,0:T(8,128)(2,1)S(1)}, u32[]{:S(2)}) copy-start(bf16[192,128]{1,0:T(8,128)(2,1)S(1)} %broadcast_in_dim.55.gain_own.gain) | copy-start | bytes 147460
  1.4 28.2 %collective-permute-start.1 = (bf16[192,128]{1,0:T(8,128)(2,1)S(1)}, bf16[192,128]{1,0:T(8,128)(2,1)S(1)}, u32[]{:S(2)}, u32[]{:S(2)}) collective-permute-start(bf16[192,128]{1,0:T(8,128)(2,1)S(1)} %broadcast_in_dim.55.gain_own.gain), channel_id=1, source_target_pairs={{0,2},{1,3},{2,0},{3,1},{4,6},{5,7},{6,4},{7,5},{8,10},{9,11},{10,... | collective-permute-start | bytes 147464 | tf_op jit(solution)/shard_map/ppermute | solution.py:491
  4.4 25.2 %collective-permute-start.2 = (bf16[192,128]{1,0:T(8,128)(2,1)S(1)}, bf16[192,128]{1,0:T(8,128)(2,1)S(1)}, u32[]{:S(2)}, u32[]{:S(2)}) collective-permute-start(bf16[192,128]{1,0:T(8,128)(2,1)S(1)} %broadcast_in_dim.55.gain_own.gain), channel_id=1, source_target_pairs={{0,1},{1,0},{2,3},{3,2},{4,5},{5,4},{6,7},{7,6},{8,9},{9,8},{10,11... | collective-permute-start | bytes 147464 | tf_op jit(solution)/shard_map/ppermute | solution.py:491
  4.4 28.6 %collective-permute-start = (bf16[192,3072]{1,0:T(8,128)(2,1)}, bf16[192,3072]{1,0:T(8,128)(2,1)S(1)}, u32[]{:S(2)}, u32[]{:S(2)}) collective-permute-start(bf16[192,3072]{1,0:T(8,128)(2,1)} %bitcast.19), channel_id=1, source_target_pairs={{0,2},{1,3},{2,0},{3,1},{4,6},{5,7},{6,4},{7,5},{8,10},{9,11},{10,... | collective-permute-start | bytes 3538952 | tf_op jit(solution)/shard_map/ppermute | solution.py:491
  4.6 32.0 %collective-permute-start.3 = (bf16[192,3072]{1,0:T(8,128)(2,1)}, bf16[192,3072]{1,0:T(8,128)(2,1)}, u32[]{:S(2)}, u32[]{:S(2)}) collective-permute-start(bf16[192,3072]{1,0:T(8,128)(2,1)} %bitcast.20), channel_id=1, source_target_pairs={{0,1},{1,0},{2,3},{3,2},{4,5},{5,4},{6,7},{7,6},{8,9},{9,8},{10,11... | collective-permute-start | bytes 3538952 | tf_op jit(solution)/shard_map/ppermute | solution.py:491
  11.9 11.3 %copy-start.1 = (bf16[768,768]{1,0:T(8,128)(2,1)S(1)}, bf16[768,768]{1,0:T(8,128)(2,1)}, u32[]{:S(2)}) copy-start(bf16[768,768]{1,0:T(8,128)(2,1)} %down.1) | copy-start | bytes 3538948
  23.2 3.5 %copy-start.6 = (bf16[768,3,192]{0,2,1:T(8,128)(2,1)S(1)}, bf16[768,3,192]{0,2,1:T(8,128)(2,1)}, u32[]{:S(2)}) copy-start(bf16[768,3,192]{0,2,1:T(8,128)(2,1)} %param.15) | copy-start | bytes 2654212
  24.7 3.3 %copy-start = (bf16[768,768]{1,0:T(8,128)(2,1)S(1)}, bf16[768,768]{1,0:T(8,128)(2,1)}, u32[]{:S(2)}) copy-start(bf16[768,768]{1,0:T(8,128)(2,1)} %up.7) | copy-start | bytes 3538948
  28.0 1.5 copy-start.21
  28.0 5.9 %copy-start.20 = (bf16[768]{0:T(1024)(128)(2,1)S(1)}, bf16[768]{0:T(1024)(128)(2,1)}, u32[]{:S(2)}) copy-start(bf16[768]{0:T(1024)(128)(2,1)} %param.19) | copy-start | bytes 4612
  28.0 6.8 %copy-start.22 = (bf16[192]{0:T(256)(128)(2,1)S(1)}, bf16[192]{0:T(256)(128)(2,1)}, u32[]{:S(2)}) copy-start(bf16[192]{0:T(256)(128)(2,1)} %param.21) | copy-start | bytes 1156
  28.0 8.0 %copy-start.23 = (s32[4]{0:T(128)S(1)}, s32[4]{0:T(128)}, u32[]{:S(2)}) copy-start(s32[4]{0:T(128)} %constant.117.clone) | copy-start | bytes 52
  29.6 8.9 %copy-start.17 = (bf16[192,128]{1,0:T(8,128)(2,1)}, bf16[192,128]{1,0:T(8,128)(2,1)S(1)}, u32[]{:S(2)}) copy-start(bf16[192,128]{1,0:T(8,128)(2,1)S(1)} %collective-permute-done.1.gain_y) | copy-start | bytes 147460
  29.6 8.9 %copy-start.18 = (bf16[192,128]{1,0:T(8,128)(2,1)}, bf16[192,128]{1,0:T(8,128)(2,1)S(1)}, u32[]{:S(2)}) copy-start(bf16[192,128]{1,0:T(8,128)(2,1)S(1)} %collective-permute-done.2.gain_c) | copy-start | bytes 147460
  33.0 5.4 %copy-start.8 = (bf16[192,3072]{1,0:T(8,128)(2,1)}, bf16[192,3072]{1,0:T(8,128)(2,1)S(1)}, u32[]{:S(2)}) copy-start(bf16[192,3072]{1,0:T(8,128)(2,1)S(1)} %collective-permute-done.flip_y) | copy-start | bytes 3538948
  35.5 2.9 %collective-permute-start.4 = (bf16[192,3072]{1,0:T(8,128)(2,1)S(1)}, bf16[192,3072]{1,0:T(8,128)(2,1)S(1)}, u32[]{:S(2)}, u32[]{:S(2)}) collective-permute-start(bf16[192,3072]{1,0:T(8,128)(2,1)S(1)} %collective-permute-done.flip_y), channel_id=1, source_target_pairs={{0,1},{1,0},{2,3},{3,2},{4,5},{5,4},{6,7},{7,6},{8,9},{9,8},{10,11... | collective-permute-start | bytes 3538952 | tf_op jit(solution)/shard_map/ppermute | solution.py:491
  35.5 2.9 %collective-permute-start.5 = (bf16[192,128]{1,0:T(8,128)(2,1)S(1)}, bf16[192,128]{1,0:T(8,128)(2,1)S(1)}, u32[]{:S(2)}, u32[]{:S(2)}) collective-permute-start(bf16[192,128]{1,0:T(8,128)(2,1)S(1)} %collective-permute-done.1.gain_y), channel_id=1, source_target_pairs={{0,1},{1,0},{2,3},{3,2},{4,5},{5,4},{6,7},{7,6},{8,9},{9,8},{10,11... | collective-permute-start | bytes 147464 | tf_op jit(solution)/shard_map/ppermute | solution.py:491
  38.4 0.6 copy-start.19
  39.1 1.0 copy-start.9
  64.3 60.0 %all-to-all-start = ((bf16[8,192,768]{2,1,0:T(8,128)(2,1)}), bf16[8,192,768]{2,1,0:T(8,128)(2,1)S(1)}, u32[]{:S(2)}, u32[]{:S(2)}) async-start(bf16[8,192,768]{2,1,0:T(8,128)(2,1)} %bitcast.39), calls=%async_computation | async-start | bytes 4718592 | tf_op jit(solution)/shard_map/all_to_all | solution.py:514
  70.1 38.0 %copy-start.14 = (f32[768,128]{1,0:T(8,128)S(1)}, f32[768,128]{1,0:T(8,128)}, u32[]{:S(2)}) copy-start(f32[768,128]{1,0:T(8,128)} %get-tuple-element.158) | copy-start | bytes 1179652
  110.3 9.8 %collective-permute-start.6 = (f32[2,192]{1,0:T(2,128)S(1)}, f32[2,192]{1,0:T(2,128)S(1)}, u32[]{:S(2)}, u32[]{:S(2)}) collective-permute-start(f32[2,192]{1,0:T(2,128)S(1)} %pad_maximum_fusion), channel_id=1, source_target_pairs={{0,1},{1,0},{2,3},{3,2},{4,5},{5,4},{6,7},{7,6},{8,9},{9,8},{10,11... | collective-permute-start | bytes 4616 | tf_op jit(solution)/shard_map/ppermute | solution.py:491
  120.1 10.5 %copy-start.16 = (f32[192,128]{1,0:T(8,128)S(1)}, f32[192,128]{1,0:T(8,128)}, u32[]{:S(2)}) copy-start(f32[192,128]{1,0:T(8,128)} %get-tuple-element.186) | copy-start | bytes 294916
  120.1 11.5 %copy-start.15 = (f32[384,128]{1,0:T(8,128)S(1)}, f32[384,128]{1,0:T(8,128)}, u32[]{:S(2)}) copy-start(f32[384,128]{1,0:T(8,128)} %get-tuple-element.184) | copy-start | bytes 589828
  120.1 11.6 %copy-start.13 = (f32[768,128]{1,0:T(8,128)S(1)}, f32[768,128]{1,0:T(8,128)}, u32[]{:S(2)}) copy-start(f32[768,128]{1,0:T(8,128)} %get-tuple-element.185) | copy-start | bytes 1179652
  125.4 18.8 %collective-permute-start.10 = (bf16[1,2,400,1024]{3,2,1,0:T(8,128)(2,1)}, bf16[1,2,400,1024]{3,2,1,0:T(8,128)(2,1)S(1)}, u32[]{:S(2)}, u32[]{:S(2)}) collective-permute-start(bf16[1,2,400,1024]{3,2,1,0:T(8,128)(2,1)} %get-tuple-element.180), channel_id=1, source_target_pairs={{0,1},{1,0},{2,3},{3,2},{4,5},{5,4},{6,7},{7,6},{8,9},{9,8},{10,11... | collective-permute-start | bytes 4915208 | tf_op jit(solution)/shard_map/ppermute | solution.py:491
  125.4 16.4 %collective-permute-start.7 = (bf16[384,768]{1,0:T(8,128)(2,1)}, bf16[384,768]{1,0:T(8,128)(2,1)}, u32[]{:S(2)}, u32[]{:S(2)}) collective-permute-start(bf16[384,768]{1,0:T(8,128)(2,1)} %constant_dynamic-slice_fusion.4), channel_id=1, source_target_pairs={{0,4},{4,0},{8,12},{12,8},{16,20},{20,16},{24,28},{28,24},{1,5},{5... | collective-permute-start | bytes 1769480 | tf_op jit(solution)/shard_map/ppermute | solution.py:491
  126.8 17.3 %collective-permute-start.8 = (bf16[192,768]{1,0:T(8,128)(2,1)}, bf16[192,768]{1,0:T(8,128)(2,1)}, u32[]{:S(2)}, u32[]{:S(2)}) collective-permute-start(bf16[192,768]{1,0:T(8,128)(2,1)} %reduce_sum.75), channel_id=1, source_target_pairs={{0,16},{4,20},{8,24},{12,28},{16,0},{20,4},{24,8},{28,12},{1,17},{... | collective-permute-start | bytes 884744 | tf_op jit(solution)/shard_map/ppermute | solution.py:491
  130.7 11.1 %collective-permute-start.9 = (f32[192]{0:T(256)S(1)}, f32[192]{0:T(256)S(1)}, u32[]{:S(2)}, u32[]{:S(2)}) collective-permute-start(f32[192]{0:T(256)S(1)} %bitcast.42), channel_id=1, source_target_pairs={{0,2},{1,3},{2,0},{3,1},{4,6},{5,7},{6,4},{7,5},{8,10},{9,11},{10,... | collective-permute-start | bytes 2312 | tf_op jit(solution)/shard_map/ppermute | solution.py:491
  131.9 12.3 %copy-start.4 = (bf16[1,2,400,1024]{3,2,1,0:T(8,128)(2,1)S(1)}, bf16[1,2,400,1024]{3,2,1,0:T(8,128)(2,1)}, u32[]{:S(2)}) copy-start(bf16[1,2,400,1024]{3,2,1,0:T(8,128)(2,1)} %get-tuple-element.187.keep) | copy-start | bytes 4915204
  144.1 2.6 %copy-start.5 = (bf16[1,2,400,1024]{3,2,1,0:T(8,128)(2,1)}, bf16[1,2,400,1024]{3,2,1,0:T(8,128)(2,1)S(1)}, u32[]{:S(2)}) copy-start(bf16[1,2,400,1024]{3,2,1,0:T(8,128)(2,1)S(1)} %collective-permute-done.10.from_core) | copy-start | bytes 4915204
  144.2 2.6 %copy-start.10 = (bf16[768,768]{1,0:T(8,128)(2,1)S(1)}, bf16[768,768]{1,0:T(8,128)(2,1)}, u32[]{:S(2)}) copy-start(bf16[768,768]{1,0:T(8,128)(2,1)} %get-tuple-element.156) | copy-start | bytes 3538948
  148.9 22.6 %collective-permute-start.15 = (bf16[1,2,400,1024]{3,2,1,0:T(8,128)(2,1)}, bf16[1,2,400,1024]{3,2,1,0:T(8,128)(2,1)}, u32[]{:S(2)}, u32[]{:S(2)}) collective-permute-start(bf16[1,2,400,1024]{3,2,1,0:T(8,128)(2,1)} %get-tuple-element.198), channel_id=1, source_target_pairs={{0,1},{1,0},{2,3},{3,2},{4,5},{5,4},{6,7},{7,6},{8,9},{9,8},{10,11... | collective-permute-start | bytes 4915208 | tf_op jit(solution)/shard_map/ppermute | solution.py:491
  148.9 22.6 %collective-permute-start.14 = (bf16[1,1,400,1024]{3,2,1,0:T(8,128)(2,1)}, bf16[1,1,400,1024]{3,2,1,0:T(8,128)(2,1)S(1)}, u32[]{:S(2)}, u32[]{:S(2)}) collective-permute-start(bf16[1,1,400,1024]{3,2,1,0:T(8,128)(2,1)} %add_convert_fusion.2), channel_id=1, source_target_pairs={{0,2},{1,3},{2,0},{3,1},{4,6},{5,7},{6,4},{7,5},{8,10},{9,11},{10,... | collective-permute-start | bytes 2457608 | tf_op jit(solution)/shard_map/ppermute | solution.py:491
  149.7 21.7 %collective-permute-start.12 = (bf16[384,768]{1,0:T(8,128)(2,1)S(1)}, bf16[384,768]{1,0:T(8,128)(2,1)S(1)}, u32[]{:S(2)}, u32[]{:S(2)}) collective-permute-start(bf16[384,768]{1,0:T(8,128)(2,1)S(1)} %maximum_select_fusion.3), channel_id=1, source_target_pairs={{0,8},{4,12},{8,0},{12,4},{16,24},{20,28},{24,16},{28,20},{1,9},{5... | collective-permute-start | bytes 1769480 | tf_op jit(solution)/shard_map/ppermute | solution.py:491
  150.4 21.0 %collective-permute-start.11 = (bf16[192,768]{1,0:T(8,128)(2,1)}, bf16[192,768]{1,0:T(8,128)(2,1)S(1)}, u32[]{:S(2)}, u32[]{:S(2)}) collective-permute-start(bf16[192,768]{1,0:T(8,128)(2,1)} %get-tuple-element.194), channel_id=1, source_target_pairs={{0,8},{4,12},{8,0},{12,4},{16,24},{20,28},{24,16},{28,20},{1,9},{5... | collective-permute-start | bytes 884744 | tf_op jit(solution)/shard_map/ppermute | solution.py:491
  151.8 10.9 %collective-permute-start.13 = (f32[1536]{0:T(1024)S(1)}, f32[1536]{0:T(1024)S(1)}, u32[]{:S(2)}, u32[]{:S(2)}) collective-permute-start(f32[1536]{0:T(1024)S(1)} %concatenate.41), channel_id=1, source_target_pairs={{0,4},{4,0},{8,12},{12,8},{16,20},{20,16},{24,28},{28,24},{1,5},{5... | collective-permute-start | bytes 18440 | tf_op jit(solution)/shard_map/ppermute | solution.py:491
  162.7 10.8 %copy-start.2 = (bf16[1,2,400,1024]{3,2,1,0:T(8,128)(2,1)S(1)}, bf16[1,2,400,1024]{3,2,1,0:T(8,128)(2,1)}, u32[]{:S(2)}) copy-start(bf16[1,2,400,1024]{3,2,1,0:T(8,128)(2,1)} %get-tuple-element.207.keep) | copy-start | bytes 4915204
  171.5 0.9 copy-start.11
  176.5 10.6 %collective-permute-start.16 = (bf16[1,2,400,1024]{3,2,1,0:T(8,128)(2,1)}, bf16[1,2,400,1024]{3,2,1,0:T(8,128)(2,1)}, u32[]{:S(2)}, u32[]{:S(2)}) collective-permute-start(bf16[1,2,400,1024]{3,2,1,0:T(8,128)(2,1)} %get-tuple-element.212), channel_id=1, source_target_pairs={{0,1},{1,0},{2,3},{3,2},{4,5},{5,4},{6,7},{7,6},{8,9},{9,8},{10,11... | collective-permute-start | bytes 4915208 | tf_op jit(solution)/shard_map/ppermute | solution.py:491
  176.5 10.6 %collective-permute-start.17 = (bf16[96,768]{1,0:T(8,128)(2,1)}, bf16[96,768]{1,0:T(8,128)(2,1)S(1)}, u32[]{:S(2)}, u32[]{:S(2)}) collective-permute-start(bf16[96,768]{1,0:T(8,128)(2,1)} %add_convert_fusion.7), channel_id=1, source_target_pairs={{0,16},{4,20},{8,24},{12,28},{16,0},{20,4},{24,8},{28,12},{1,17},{... | collective-permute-start | bytes 442376 | tf_op jit(solution)/shard_map/ppermute | solution.py:491
  178.9 28.2 %collective-permute-start.23 = (bf16[768,768]{1,0:T(8,128)(2,1)S(1)}, bf16[768,768]{1,0:T(8,128)(2,1)}, u32[]{:S(2)}, u32[]{:S(2)}) collective-permute-start(bf16[768,768]{1,0:T(8,128)(2,1)S(1)} %maximum_select_fusion.1), channel_id=1, source_target_pairs={{0,4},{4,0},{8,12},{12,8},{16,20},{20,16},{24,28},{28,24},{1,5},{5... | collective-permute-start | bytes 3538952 | tf_op jit(solution)/shard_map/ppermute | solution.py:491
  179.7 7.4 %collective-permute-start.18 = (f32[1536]{0:T(1024)}, f32[1536]{0:T(1024)}, u32[]{:S(2)}, u32[]{:S(2)}) collective-permute-start(f32[1536]{0:T(1024)} %add.133), channel_id=1, source_target_pairs={{0,8},{4,12},{8,0},{12,4},{16,24},{20,28},{24,16},{28,20},{1,9},{5... | collective-permute-start | bytes 18440 | tf_op jit(solution)/shard_map/ppermute | solution.py:491
  181.5 22.9 %collective-permute-start.22 = (bf16[1,1,400,1024]{3,2,1,0:T(8,128)(2,1)}, bf16[1,1,400,1024]{3,2,1,0:T(8,128)(2,1)}, u32[]{:S(2)}, u32[]{:S(2)}) collective-permute-start(bf16[1,1,400,1024]{3,2,1,0:T(8,128)(2,1)} %add_convert_fusion.1), channel_id=1, source_target_pairs={{0,2},{1,3},{2,0},{3,1},{4,6},{5,7},{6,4},{7,5},{8,10},{9,11},{10,... | collective-permute-start | bytes 2457608 | tf_op jit(solution)/shard_map/ppermute | solution.py:491
  182.7 4.4 %copy-start.3 = (bf16[1,2,400,1024]{3,2,1,0:T(8,128)(2,1)S(1)}, bf16[1,2,400,1024]{3,2,1,0:T(8,128)(2,1)}, u32[]{:S(2)}) copy-start(bf16[1,2,400,1024]{3,2,1,0:T(8,128)(2,1)} %get-tuple-element.199.keep) | copy-start | bytes 4915204
  190.3 9.9 %collective-permute-start.19 = (bf16[96,768]{1,0:T(8,128)(2,1)S(1)}, bf16[96,768]{1,0:T(8,128)(2,1)S(1)}, u32[]{:S(2)}, u32[]{:S(2)}) collective-permute-start(bf16[96,768]{1,0:T(8,128)(2,1)S(1)} %add_convert_fusion.5), channel_id=1, source_target_pairs={{0,16},{4,20},{8,24},{12,28},{16,0},{20,4},{24,8},{28,12},{1,17},{... | collective-permute-start | bytes 442376 | tf_op jit(solution)/shard_map/ppermute | solution.py:491
  190.4 9.8 %collective-permute-start.20 = (f32[1536]{0:T(1024)S(1)}, f32[1536]{0:T(1024)S(1)}, u32[]{:S(2)}, u32[]{:S(2)}) collective-permute-start(f32[1536]{0:T(1024)S(1)} %add.137), channel_id=1, source_target_pairs={{0,16},{4,20},{8,24},{12,28},{16,0},{20,4},{24,8},{28,12},{1,17},{... | collective-permute-start | bytes 18440 | tf_op jit(solution)/shard_map/ppermute | solution.py:491
  200.2 8.0 %collective-permute-start.21 = (bf16[192,768]{1,0:T(8,128)(2,1)S(1)}, bf16[192,768]{1,0:T(8,128)(2,1)S(1)}, u32[]{:S(2)}, u32[]{:S(2)}) collective-permute-start(bf16[192,768]{1,0:T(8,128)(2,1)S(1)} %maximum_select_fusion.5), channel_id=1, source_target_pairs={{0,8},{4,12},{8,0},{12,4},{16,24},{20,28},{24,16},{28,20},{1,9},{5... | collective-permute-start | bytes 884744 | tf_op jit(solution)/shard_map/ppermute | solution.py:491
  200.3 19.4 %collective-permute-start.24 = (bf16[1,1,400,1024]{3,2,1,0:T(8,128)(2,1)}, bf16[1,1,400,1024]{3,2,1,0:T(8,128)(2,1)S(1)}, u32[]{:S(2)}, u32[]{:S(2)}) collective-permute-start(bf16[1,1,400,1024]{3,2,1,0:T(8,128)(2,1)} %add_convert_fusion), channel_id=1, source_target_pairs={{0,2},{1,3},{2,0},{3,1},{4,6},{5,7},{6,4},{7,5},{8,10},{9,11},{10,... | collective-permute-start | bytes 2457608 | tf_op jit(solution)/shard_map/ppermute | solution.py:491
  208.4 16.5 %collective-permute-start.25 = (bf16[384,768]{1,0:T(8,128)(2,1)S(1)}, bf16[384,768]{1,0:T(8,128)(2,1)S(1)}, u32[]{:S(2)}, u32[]{:S(2)}) collective-permute-start(bf16[384,768]{1,0:T(8,128)(2,1)S(1)} %maximum_select_fusion.4), channel_id=1, source_target_pairs={{0,4},{4,0},{8,12},{12,8},{16,20},{20,16},{24,28},{28,24},{1,5},{5... | collective-permute-start | bytes 1769480 | tf_op jit(solution)/shard_map/ppermute | solution.py:491
  219.7 0.9 copy-start.12

commit v7 on v6

--- a/solution.py
+++ b/solution.py
@@ -86,20 +86,38 @@
 
 
 def mlp_kernel(
-    pieces_order, place, own, flip_y, flip_c, flip_cy, gain_own, gain_y, gain_c, gain_cy, up_t, up_bias, d_act, cot, up,
-    normed, active, d_pre, stats, bias_sum, gain_all, up_row, grads, low, high
+    pieces_order, opening, closing, place, own, flip_y, flip_c, flip_cy, gain_own, gain_y, gain_c, gain_cy, up_t, up_bias,
+    d_act, cot, *rest
 ):
+    if closing:
+        up, rest = rest[0], rest[1:]
+    if not opening:
+        held, rest = rest[4:6], rest[6:]
+    normed, active, d_pre, stats, bias_sum, gain_all, *rest = rest
+    if closing:
+        up_row, grads, low, high, low_sem, high_sem = rest
+    else:
+        low, high = rest
     pieces = (own, flip_y, flip_c, flip_cy)
     part = own.shape[0]
     width = part * 4
     first = pl.program_id(0) == 0
     last = pl.program_id(0) == pl.num_programs(0) - 1
+    copies = []
+    if not opening:
+        copies = [
+            pltpu.make_async_copy(held[0], low, low_sem),
+            pltpu.make_async_copy(held[1], high, high_sem),
+        ]
 
     @pl.when(first)
     def _():
+        for copy in copies:
+            copy.start()
         bias_sum[...] = jnp.zeros_like(bias_sum)
-        low[...] = jnp.zeros_like(low)
-        high[...] = jnp.zeros_like(high)
+        if opening:
+            low[...] = jnp.zeros_like(low)
+            high[...] = jnp.zeros_like(high)
         for slot, piece in enumerate((gain_own, gain_y, gain_c, gain_cy)):
             gain_all[pl.ds(pl.multiple_of(place[slot], part), part), :] = piece[...].astype(F32)
 
@@ -126,6 +144,13 @@
         return dot(up_t[here, :], normed[...]) + up_bias[here, :1].astype(F32)
 
     ahead = lift(0)
+    if copies:
+
+        @pl.when(first)
+        def _():
+            for copy in copies:
+                copy.wait()
+
     for start in range(0, up_t.shape[0], 256):
         here = slice(start, start + 256)
         pre = ahead
@@ -142,6 +167,9 @@
         low[here, :] += dot(act, cot[...])
         high[:, here] += dot(normed[...], grad, NT)
 
+    if not closing:
+        return
+
     @pl.when(last)
     def _():
         up_row[...] = fold_lanes(high[...] * up[...].astype(F32))
@@ -152,55 +180,75 @@
             grads[slot * size : (slot + 1) * size, :] = source[start : start + size, :].astype(BF16)
 
 
-def mlp_call(pieces_order, place, pieces, gains, up_t, up_bias, d_act, cot, up, block=512):
-    part, tokens = pieces[0].shape
+def mlp_call(pieces_order, place, pieces, gains, up_t, up_bias, d_act, cot, up, before, held, begin, block=512):
+    part = pieces[0].shape[0]
     width = 4 * part
     seqs, hidden, _ = d_act.shape
+    assert hidden == width
     steps = LEN // block
+    grid = pieces[0].shape[1] // block
+    opening = begin == 0
+    closing = begin + grid // steps == seqs
     lanes = lambda i, *_: (0, i)
-    by_seq = lambda i, *_: (i // steps, 0, i % steps)
+    tokens = lambda i, *_: (0, begin * steps + i)
+    by_seq = lambda i, *_: (begin + i // steps, 0, i % steps)
     fixed = lambda i, *_: (0, 0)
-    grid_spec = pltpu.PrefetchScalarGridSpec(
-        num_scalar_prefetch=1,
-        grid=(tokens // block,),
-        in_specs=[pl.BlockSpec((part, block), lanes)] * 4
+    square = jax.ShapeDtypeStruct((hidden, width), F32)
+    in_specs = (
+        [pl.BlockSpec((part, block), lanes)] * 4
         + [pl.BlockSpec((part, 128), fixed)] * 4
         + [
             pl.BlockSpec((hidden, width), fixed),
             pl.BlockSpec((hidden, 128), fixed),
             pl.BlockSpec((None, hidden, block), by_seq),
-            pl.BlockSpec((block, width), lambda i, *_: (i, 0)),
-            pl.BlockSpec((width, hidden), fixed),
-        ],
-        out_specs=[
-            pl.BlockSpec((None, width, block), by_seq),
-            pl.BlockSpec((None, hidden, block), by_seq),
-            pl.BlockSpec((None, hidden, block), by_seq),
-            pl.BlockSpec((8, block), lanes),
-            pl.BlockSpec((hidden, 128), fixed),
-            pl.BlockSpec((width, 128), fixed),
-            pl.BlockSpec((width, 128), fixed),
-            pl.BlockSpec((hidden + width, width), fixed),
-        ],
-        scratch_shapes=[pltpu.VMEM((hidden, width), F32), pltpu.VMEM((width, hidden), F32)],
-    )
-    assert hidden == width
-    return pl.pallas_call(
-        functools.partial(mlp_kernel, pieces_order),
-        grid_spec=grid_spec,
-        out_shape=[
-            jax.ShapeDtypeStruct((seqs, width, LEN), BF16),
-            jax.ShapeDtypeStruct((seqs, hidden, LEN), BF16),
-            jax.ShapeDtypeStruct((seqs, hidden, LEN), BF16),
-            jax.ShapeDtypeStruct((8, tokens), F32),
-            jax.ShapeDtypeStruct((hidden, 128), F32),
-            jax.ShapeDtypeStruct((width, 128), F32),
+            pl.BlockSpec((block, width), lambda i, *_: (begin * steps + i, 0)),
+        ]
+        + ([pl.BlockSpec((width, hidden), fixed)] if closing else [])
+    )
+    out_specs = [
+        pl.BlockSpec((None, width, block), by_seq),
+        pl.BlockSpec((None, hidden, block), by_seq),
+        pl.BlockSpec((None, hidden, block), by_seq),
+        pl.BlockSpec((8, block), tokens),
+        pl.BlockSpec((hidden, 128), fixed),
+        pl.BlockSpec((width, 128), fixed),
+    ]
+    out_shape = [
+        jax.ShapeDtypeStruct((seqs, width, LEN), BF16),
+        jax.ShapeDtypeStruct((seqs, hidden, LEN), BF16),
+        jax.ShapeDtypeStruct((seqs, hidden, LEN), BF16),
+        jax.ShapeDtypeStruct((8, seqs * LEN), F32),
+        jax.ShapeDtypeStruct((hidden, 128), F32),
+        jax.ShapeDtypeStruct((width, 128), F32),
+    ]
+    scratch = []
+    if closing:
+        out_specs += [pl.BlockSpec((width, 128), fixed), pl.BlockSpec((hidden + width, width), fixed)]
+        out_shape += [
             jax.ShapeDtypeStruct((width, 128), F32),
             jax.ShapeDtypeStruct((hidden + width, width), BF16),
-        ],
+        ]
+        scratch = [pltpu.VMEM(square.shape, F32)] * 2 + [pltpu.SemaphoreType.DMA(())] * 2
+    else:
+        out_specs += [pl.BlockSpec(square.shape, fixed)] * 2
+        out_shape += [square] * 2
+    extra = [*before, *held]
+    grid_spec = pltpu.PrefetchScalarGridSpec(
+        num_scalar_prefetch=1,
+        grid=(grid,),
+        in_specs=in_specs + [ANY] * len(extra),
+        out_specs=out_specs,
+        scratch_shapes=scratch,
+    )
+    start = 1 + len(in_specs)
+    return pl.pallas_call(
+        functools.partial(mlp_kernel, pieces_order, opening, closing),
+        grid_spec=grid_spec,
+        out_shape=out_shape,
+        input_output_aliases={start + i: i for i in range(len(before))},
         cost_estimate=cost(20, 30_000_000),
         name="mlp",
-    )(place, *pieces, *gains, up_t, up_bias, d_act, cot, up)
+    )(place, *pieces, *gains, up_t, up_bias, d_act, cot, *([up] if closing else []), *extra)
 
 
 def attention_kernel(
@@ -457,7 +505,7 @@
     token_grad[...] = cot[...].astype(F32) + inner * scale
 
 
-def finish_call(keep, from_core, from_y, own_t, cot, stats, gain, bias, before, begin, block=256):
+def finish_call(keep, from_core, from_y, own_t, cot, stats, gain, bias, before, begin, block=512):
     part, tokens = own_t.shape
     steps = LEN // block
     size = keep.shape[0]
@@ -652,52 +700,64 @@
     place = jnp.bitwise_xor(shard, jnp.array([0, 2, 1, 3], jnp.int32)) * part
 
     own_t = tokens.T
-    from_y = flip(own_t, "mp", 4, 2)
+    cuts = [(0, 1), (1, seqs)] if seqs > 1 else [(0, seqs)]
+    owns = [own_t[:, lo * LEN : hi * LEN] for lo, hi in cuts]
+    across = [flip(own, "mp", 4, 2) for own in owns]
     gain_own = jnp.broadcast_to(norm_gain[:, None], (part, 128))
     gain_y = flip(gain_own, "mp", 4, 2)
     gain_c = flip(gain_own, "mp", 4, 1)
 
-    mixed_t = jnp.transpose(qkv_weight, (1, 2, 0)).reshape(3 * part, width)
-    mixed = mixed_t.T
-    up_t = up_weight.T
-    down_t = down_weight.T
-    attn_t = attn_weight.T
     def column(vector):
         return jnp.broadcast_to(vector[:, None], (vector.shape[0], 128))
 
-    up_bias_col = column(up_bias)
-    head_gains = column(qk_gain.astype(F32).reshape(2 * part))
-
-    slots = jnp.arange(IMAGE_SLOTS, dtype=jnp.int32)[None, :, None]
-    same = image_ids[:, None, :] == slots
-    mask_q = same.astype(BF16)
-    mask_k = jnp.where(same | (slots >= 8), 0.0, -PENALTY).astype(BF16)
-    block_first = image_ids[:, ::BI]
-    block_last = image_ids[:, BI - 1 :: BI]
-    starts = jnp.sum(image_ids[:, None, :] < block_first[:, :, None], axis=2, dtype=jnp.int32)
-    ends = jnp.sum(image_ids[:, None, :] <= block_last[:, :, None], axis=2, dtype=jnp.int32)
-    first = starts // 128
-    count = ((ends + 127) // 128 - first + BJ // 128 - 1) // (BJ // 128)
-    first = jnp.minimum(first, (LEN - count * BJ) // 128).reshape(-1)
-    count = count.reshape(-1)
+    def prepare(qkv_weight, down_weight, attn_weight, qk_gain, down_bias, image_ids):
+        mixed_t = jnp.transpose(qkv_weight, (1, 2, 0)).reshape(3 * part, width)
+        slots = jnp.arange(IMAGE_SLOTS, dtype=jnp.int32)[None, :, None]
+        same = image_ids[:, None, :] == slots
+        mask_q = same.astype(BF16)
+        mask_k = jnp.where(same | (slots >= 8), 0.0, -PENALTY).astype(BF16)
+        block_first = image_ids[:, ::BI]
+        block_last = image_ids[:, BI - 1 :: BI]
+        starts = jnp.sum(image_ids[:, None, :] < block_first[:, :, None], axis=2, dtype=jnp.int32)
+        ends = jnp.sum(image_ids[:, None, :] <= block_last[:, :, None], axis=2, dtype=jnp.int32)
+        first = starts // 128
+        count = ((ends + 127) // 128 - first + BJ // 128 - 1) // (BJ // 128)
+        first = jnp.minimum(first, (LEN - count * BJ) // 128)
+        head_gains = column(qk_gain.astype(F32).reshape(2 * part))
+        return (
+            mixed_t, mixed_t.T, down_weight.T, attn_weight.T, head_gains, column(down_bias), mask_q, mask_k,
+            first.reshape(-1), count.reshape(-1),
+        )
 
     pick = (jnp.arange(part)[:, None] + me * part == jnp.arange(width)[None, :]).astype(BF16)
     d_act, d_att, cot_own, cot_sum = early_call(cotangent, down_weight, attn_weight, pick)
-    bias_col = column(down_bias)
-    prepared = (
-        d_act, d_att, mixed_t, mixed, up_t, down_t, attn_t, up_bias_col, head_gains, mask_q, mask_k, first, count,
-        bias_col,
-    )
-    prepared, (from_y, gain_y, gain_c) = tie(prepared, (from_y, gain_y, gain_c))
+    (d_act, up_t, up_bias_col), (across[0], gain_y, gain_c) = tie(
+        (d_act, up_weight.T, column(up_bias)), (across[0], gain_y, gain_c)
+    )
     gains = (gain_own, gain_y, gain_c, flip(gain_y, "mp", 4, 1))
-    (
-        d_act, d_att, mixed_t, mixed, up_t, down_t, attn_t, up_bias_col, head_gains, mask_q, mask_k, first, count,
-        bias_col,
-    ) = prepared
-    pieces = (own_t, from_y, flip(own_t, "mp", 4, 1), flip(from_y, "mp", 4, 1))
-    normed, active, d_pre, stats, upbias_part, gain_all, up_row, mlp_part = mlp_call(
-        tuple(piece_order(dp_size)), place, pieces, gains, up_t, up_bias_col, d_act, cotangent, up_weight
-    )
+    before = held = ()
+    bias_parts = 0.0
+    for number, (lo, _) in enumerate(cuts):
+        own, from_y = owns[number], across[number]
+        pieces = (own, from_y, flip(own, "mp", 4, 1), flip(from_y, "mp", 4, 1))
+        if number == 1:
+            prepared, pieces = tie(prepared, pieces)
+        *before, bias_part, gain_all, left, right = mlp_call(
+            tuple(piece_order(dp_size)), place, pieces, gains, up_t, up_bias_col, d_act, cotangent, up_weight, before,
+            held, lo,
+        )
+        held = (left, right)
+        bias_parts = bias_parts + bias_part
+        if number == 0:
+            (before, held), raw = tie(
+                (before, held), (qkv_weight, down_weight, attn_weight, qk_gain, down_bias, image_ids)
+            )
+            prepared = prepare(*raw)
+        if number + 1 < len(cuts):
+            (before, held), across[number + 1] = tie((before, held), across[number + 1])
+    mixed_t, mixed, down_t, attn_t, head_gains, bias_col, mask_q, mask_k, first, count = prepared
+    normed, active, d_pre, stats = before
+    up_row, mlp_part = held
     mlp_sum = SumOverDp(mlp_part, dp_size, dp)
 
     (states,), flying = launch([mlp_sum], (normed,))
@@ -712,7 +772,7 @@
     short = ShortSums(
         jnp.stack([norm_parts[0], norm_parts[2]]),
         jnp.stack([norm_parts[1], norm_parts[3]]),
-        jnp.concatenate([jnp.sum(qk_part, axis=1), jnp.sum(upbias_part, axis=1), jnp.sum(cot_sum, axis=1)]),
+        jnp.concatenate([jnp.sum(qk_part, axis=1), jnp.sum(bias_parts, axis=1), jnp.sum(cot_sum, axis=1)]),
         dp_size,
     )
 

time: 229 us -> 245 us (1.070)
  waiting for transfers between devices: 32.4 us -> 45.4 us
  Pallas kernels: 115 us -> 119 us
    ppermute x26 -> x29, waiting for transfers between devices: 28.3 us -> 40.7 us  [flip(): return lax.ppermute(value, axis, [(i, i ^ bit) for i in range(size)])]
    pallas_call x1 -> x2, Pallas kernels: 24.2 us -> 32.3 us  [mlp_call(): pl.pallas_call(functools.partial(mlp_kernel, pieces_order, opening, closi...]
    unnamed x51 -> x65, local copies, waits for them, and re-layouts: 8.43 us -> 4.68 us
    pallas_call x3, Pallas kernels: 12.8 us -> 9.38 us  [finish_call(): pl.pallas_call(finish_kernel, grid=(size * steps,), in_specs=[packed, pac...]
    select_n x3, other arithmetic: 3.78 us -> 6.33 us  [take(): jnp.where(self.index & step > 0, jnp.concatenate([arrived, self.keep], ax...]
    ppermute x26 -> x29, starting transfers between devices: 26.3 us -> 25.4 us  [flip(): return lax.ppermute(value, axis, [(i, i ^ bit) for i in range(size)])]
  transfers between devices with their start and end apart: 27 -> 30, of which waited for: 9 -> 10; matrix products, arithmetic and copies ran while one was open for 13% -> 11% of each run, Pallas kernels for 40% -> 40%
where the time goes in v7:
time: 245 us; the launch traced here: 244 us
  Pallas kernels  119 us (49%)
  waiting for transfers between devices  45.4 us (19%)
  starting transfers between devices  31.5 us (13%)
  other arithmetic  27.2 us (11%)
  local copies, waits for them, and re-layouts  19.9 us (8%)
    ppermute x29, waiting for transfers between devices, flip(): return lax.ppermute(value, axis, [(i, i ^ bit) for i in range(size)])  40.7 us
    pallas_call x1, Pallas kernels, attention_call(): pl.pallas_call(attention_kernel, grid_spec=grid_spec, out_shape=[jax.Shap...  36.6 us
    pallas_call x2, Pallas kernels, mlp_call(): pl.pallas_call(functools.partial(mlp_kernel, pieces_order, opening, closi...  32.3 us
    pallas_call x3, Pallas kernels, project_call(): pl.pallas_call(project_kernel, grid_spec=grid_spec, out_shape=[jax.ShapeD...  29.5 us
    ppermute x29, starting transfers between devices, flip(): return lax.ppermute(value, axis, [(i, i ^ bit) for i in range(size)])  25.4 us
    pallas_call x1, Pallas kernels, early_call(): pl.pallas_call(early_kernel, grid=(tokens // block,), in_specs=[pl.BlockS...  11.3 us
    pallas_call x3, Pallas kernels, finish_call(): pl.pallas_call(finish_kernel, grid=(size * steps,), in_specs=[packed, pac...  9.38 us
    select_n x3, other arithmetic, take(): jnp.where(self.index & step > 0, jnp.concatenate([arrived, self.keep], ax...  6.33 us
  transfers between devices with their start and end apart: 30, of which 10 were waited for; matrix products, arithmetic and copies ran while one was open for 11% of the time, Pallas kernels for 40%

profile of v7, /device:TPU:0, one launch (start us, length us, event | category | flops | bytes accessed | tf_op | source)
XLA Modules:
  0.0 244.2 jit_solution(4876645230381044864)
XLA Ops:
  0.7 1.0 slice.95.own
  1.7 3.0 %collective-permute-start = (bf16[192,1024]{1,0:T(8,128)(2,1)S(1)}, bf16[192,1024]{1,0:T(8,128)(2,1)S(1)}, u32[]{:S(2)}, u32[]{:S(2)}) collective-permute-start(bf16[192,1024]{1,0:T(8,128)(2,1)S(1)} %slice.95.own), channel_id=1, source_target_pairs={{0,2},{1,3},{2,0},{3,1},{4,6},{5,7},{6,4},{7,5},{8,10},{9,11},{10,... | collective-permute-start | bytes 1179656 | tf_op jit(solution)/shard_map/ppermute | solution.py:539
  4.7 1.2 slice.96.own
  6.3 2.0 collective-permute-start.1
  8.4 0.8 fusion.1.pick
  9.3 11.3 %early.1 = (bf16[3,768,1024]{2,1,0:T(8,128)(2,1)}, bf16[3,192,1024]{2,1,0:T(8,128)(2,1)}, bf16[192,3072]{1,0:T(8,128)(2,1)}, f32[192,128]{1,0:T(8,128)}) custom-call(bf16[3072,768]{1,0:T(8,128)(2,1)} %cot.7, bf16[768,768]{1,0:T(8,128)(2,1)} %down.1, bf16[192,768]{1,0:T(8,128)(2,1)} %attn.1, bf16[192,768]{1,0:T(8,128)(2,1)} %fusion.1.pick), custom_call_target="tpu_custom_call" | custom-call | flops 10000 | bytes 12000 | tf_op jit(solution)/shard_map/early/pallas_call | solution.py:62
  20.6 1.5 copy.39
  22.0 9.7 %collective-permute-done.1.gain_y = bf16[192,128]{1,0:T(8,128)(2,1)S(1)} collective-permute-done((bf16[192,128]{1,0:T(8,128)(2,1)S(1)}, bf16[192,128]{1,0:T(8,128)(2,1)S(1)}, u32[]{:S(2)}, u32[]{:S(2)}) %collective-permute-start.1) | collective-permute-done | bytes 49184 | tf_op jit(solution)/shard_map/ppermute | solution.py:539
  31.8 0.8 broadcast_in_dim.24.up_bias
  34.2 1.0 collective-permute-done.5.gain_cy
  35.8 0.7 copy-done.17
  36.5 12.0 %mlp.2 = (bf16[3,768,1024]{2,1,0:T(8,128)(2,1)}, bf16[3,768,1024]{2,1,0:T(8,128)(2,1)}, bf16[3,768,1024]{2,1,0:T(8,128)(2,1)}, f32[8,3072]{1,0:T(8,128)}, f32[76...) custom-call(s32[4]{0:T(128)} %xor_multiply_fusion.place, ...), custom_call_target="tpu_custom_call" | custom-call | flops 20000 | bytes 30000 | tf_op jit(solution)/shard_map/mlp/pallas_call | solution.py:244
  49.4 0.8 reshape.72
  50.3 0.9 copy.42
  51.3 1.3 copy.40
  52.6 1.4 copy.41
  55.3 0.7 select_convert_fusion.mask_k
  56.0 0.7 broadcast_in_dim.53.bias
  56.8 0.8 broadcast_in_dim.52.gains
  57.6 20.3 %mlp.3 = (bf16[3,768,1024]{2,1,0:T(8,128)(2,1)}, bf16[3,768,1024]{2,1,0:T(8,128)(2,1)}, bf16[3,768,1024]{2,1,0:T(8,128)(2,1)}, f32[8,3072]{1,0:T(8,128)}, f32[76...) custom-call(s32[4]{0:T(128)} %xor_multiply_fusion.place, ...), custom_call_target="tpu_custom_call", output_to_operand_aliasing={{0}: (14, {}), {1}: (15, {}), {2}: (16, {}), {3}: (17, {})} | custom-call | flops 20000 | bytes 30000 | tf_op jit(solution)/shard_map/mlp/pallas_call | solution.py:244
  77.9 6.0 %all-to-all-start = ((bf16[8,192,768]{2,1,0:T(8,128)(2,1)}), bf16[8,192,768]{2,1,0:T(8,128)(2,1)S(1)}, u32[]{:S(2)}, u32[]{:S(2)}) async-start(bf16[8,192,768]{2,1,0:T(8,128)(2,1)} %bitcast.39), calls=%async_computation | async-start | bytes 4718592 | tf_op jit(solution)/shard_map/all_to_all | solution.py:562
  84.0 36.6 %attention.1 = (bf16[3,192,1024]{2,1,0:T(8,128)(2,1)}, bf16[3,576,1024]{2,1,0:T(8,128)(2,1)}, f32[384,128]{1,0:T(8,128)}, f32[1,768]{1,0:T(1,128)}, bf16[768,768]{1,0:T(8,128)(2,1)}) custom-call(s32[12]{0:T(128)} %get-tuple-element.201.first, s32[12]{0:T(128)} %get-tuple-element.202.count, bf16[3,768,1024]{2,1,0:T(8,128)(2,1)} %get-tuple-element.205.normed, ...), custom_call_target="tpu_custom_call" | custom-call | flops 18000 | bytes 5000 | tf_op jit(solution)/shard_map/attention/pallas_call | solution.py:405
  120.8 0.7 reduce.1
  121.6 1.9 constant_dynamic-slice_fusion.4
  123.6 9.8 %project.3 = (bf16[1,2,400,1024]{3,2,1,0:T(8,128)(2,1)}, bf16[1,2,400,1024]{3,2,1,0:T(8,128)(2,1)}) custom-call(s32[1]{0:T(128)} %bitcast.shard, bf16[3,768,1024]{2,1,0:T(8,128)(2,1)} %get-tuple-element.200.active, bf16[3,192,1024]{2,1,0:T(8,128)(2,1)} %get-tuple-element.248.attended, bf16[3,768,1024]{2,1,0:T(8,128)(2,1)} %get-tuple-element.217.d_pre, ...), custom_call_target="tpu_custom_call" | custom-call | flops 8000 | bytes 16000 | tf_op jit(solution)/shard_map/project/pallas_call | solution.py:480
  133.4 4.7 %all-to-all-done = bf16[8,192,768]{2,1,0:T(8,128)(2,1)S(1)} async-done(((bf16[8,192,768]{2,1,0:T(8,128)(2,1)}), bf16[8,192,768]{2,1,0:T(8,128)(2,1)S(1)}, u32[]{:S(2)}, u32[]{:S(2)}) %all-to-all-start) | async-done | bytes 2359328 | tf_op jit(solution)/shard_map/all_to_all | solution.py:562
  138.1 1.1 reduce_sum.75
  139.3 1.5 collective-permute-start.10
  140.7 4.2 %collective-permute-start.11 = (bf16[192,768]{1,0:T(8,128)(2,1)}, bf16[192,768]{1,0:T(8,128)(2,1)}, u32[]{:S(2)}, u32[]{:S(2)}) collective-permute-start(bf16[192,768]{1,0:T(8,128)(2,1)} %reduce_sum.75), channel_id=1, source_target_pairs={{0,16},{4,20},{8,24},{12,28},{16,0},{20,4},{24,8},{28,12},{1,17},{... | collective-permute-start | bytes 884744 | tf_op jit(solution)/shard_map/ppermute | solution.py:539
  145.1 1.6 collective-permute-start.12
  147.0 9.9 %project.4 = (bf16[1,2,400,1024]{3,2,1,0:T(8,128)(2,1)}, bf16[1,2,400,1024]{3,2,1,0:T(8,128)(2,1)}) custom-call(s32[1]{0:T(128)} %bitcast.shard, bf16[3,768,1024]{2,1,0:T(8,128)(2,1)} %get-tuple-element.200.active, bf16[3,192,1024]{2,1,0:T(8,128)(2,1)} %get-tuple-element.248.attended, bf16[3,768,1024]{2,1,0:T(8,128)(2,1)} %get-tuple-element.217.d_pre, ...), custom_call_target="tpu_custom_call" | custom-call | flops 8000 | bytes 16000 | tf_op jit(solution)/shard_map/project/pallas_call | solution.py:480
  157.0 0.9 collective-permute-done.11
  157.9 2.8 %maximum_select_fusion.3 = bf16[384,768]{1,0:T(8,128)(2,1)} fusion(bf16[192,768]{1,0:T(8,128)(2,1)} %reduce_sum.75, bf16[192,768]{1,0:T(8,128)(2,1)} %collective-permute-done.11, pred[]{:T(512)S(6)} %gt.8), kind=kLoop, calls=%fused_computation.9 | loop fusion | flops 2654208 | bytes 1179649 | tf_op jit(solution)/shard_map/jit(_where)/select_n | solution.py:571
  160.7 1.2 add_convert_fusion.2
  161.9 2.0 add_convert_fusion.3
  164.0 1.6 collective-permute-start.17
  165.6 2.0 collective-permute-start.14
  167.9 9.8 %project.5 = (bf16[1,2,400,1024]{3,2,1,0:T(8,128)(2,1)}, bf16[1,2,400,1024]{3,2,1,0:T(8,128)(2,1)}) custom-call(s32[1]{0:T(128)} %bitcast.shard, bf16[3,768,1024]{2,1,0:T(8,128)(2,1)} %get-tuple-element.200.active, bf16[3,192,1024]{2,1,0:T(8,128)(2,1)} %get-tuple-element.248.attended, bf16[3,768,1024]{2,1,0:T(8,128)(2,1)} %get-tuple-element.217.d_pre, ...), custom_call_target="tpu_custom_call" | custom-call | flops 8000 | bytes 16000 | tf_op jit(solution)/shard_map/project/pallas_call | solution.py:480
  177.8 9.5 %collective-permute-done.14 = bf16[192,768]{1,0:T(8,128)(2,1)S(1)} collective-permute-done((bf16[192,768]{1,0:T(8,128)(2,1)}, bf16[192,768]{1,0:T(8,128)(2,1)S(1)}, u32[]{:S(2)}, u32[]{:S(2)}) %collective-permute-start.14) | collective-permute-done | bytes 294944 | tf_op jit(solution)/shard_map/ppermute | solution.py:539
  187.4 0.9 copy-done.14
  188.8 1.6 maximum_select_fusion.1
  190.5 2.4 add_convert_fusion.1
  192.8 0.7 add_convert_fusion.7
  193.5 1.5 collective-permute-start.20
  195.0 1.2 collective-permute-start.26
  196.2 0.8 collective-permute-start.21
  197.5 3.1 %finish.3 = (bf16[192,3072]{1,0:T(8,128)(2,1)}, f32[192,3072]{1,0:T(8,128)}) custom-call(bf16[1,2,400,1024]{3,2,1,0:T(8,128)(2,1)} %get-tuple-element.245.keep, bf16[1,2,400,1024]{3,2,1,0:T(8,128)(2,1)} %copy-done.5, bf16[1,1,400,1024]{3,2,1,0:T(8,128)(2,1)} %copy-done.14, bf16[192,3072]{1,0:T(8,128)(2,1)} %bitcast.24, ...), custom_call_target="tpu_custom_call" | custom-call | flops 3000 | bytes 5000 | tf_op jit(solution)/shard_map/finish/pallas_call | solution.py:516
  200.7 3.4 %collective-permute-done.20 = bf16[96,768]{1,0:T(8,128)(2,1)S(1)} collective-permute-done((bf16[96,768]{1,0:T(8,128)(2,1)}, bf16[96,768]{1,0:T(8,128)(2,1)S(1)}, u32[]{:S(2)}, u32[]{:S(2)}) %collective-permute-start.20) | collective-permute-done | bytes 147488 | tf_op jit(solution)/shard_map/ppermute | solution.py:539
  204.1 2.3 add_convert_fusion
  206.4 0.7 add.141
  207.3 2.9 %collective-permute-start.23 = (f32[1536]{0:T(1024)S(1)}, f32[1536]{0:T(1024)S(1)}, u32[]{:S(2)}, u32[]{:S(2)}) collective-permute-start(f32[1536]{0:T(1024)S(1)} %add.141), channel_id=1, source_target_pairs={{0,16},{4,20},{8,24},{12,28},{16,0},{20,4},{24,8},{28,12},{1,17},{... | collective-permute-start | bytes 18440 | tf_op jit(solution)/shard_map/ppermute | solution.py:539
  210.2 7.0 %collective-permute-done.23 = f32[1536]{0:T(1024)S(1)} collective-permute-done((f32[1536]{0:T(1024)S(1)}, f32[1536]{0:T(1024)S(1)}, u32[]{:S(2)}, u32[]{:S(2)}) %collective-permute-start.23) | collective-permute-done | bytes 6176 | tf_op jit(solution)/shard_map/ppermute | solution.py:539
  218.0 0.7 slice.105
  219.3 1.3 fusion.5
  220.6 2.6 %collective-permute-done.26 = bf16[768,768]{1,0:T(8,128)(2,1)} collective-permute-done((bf16[768,768]{1,0:T(8,128)(2,1)S(1)}, bf16[768,768]{1,0:T(8,128)(2,1)}, u32[]{:S(2)}, u32[]{:S(2)}) %collective-permute-start.26) | collective-permute-done | bytes 1179680 | tf_op jit(solution)/shard_map/ppermute | solution.py:539
  223.2 3.1 %collective-permute-done.24 = bf16[192,768]{1,0:T(8,128)(2,1)S(1)} collective-permute-done((bf16[192,768]{1,0:T(8,128)(2,1)S(1)}, bf16[192,768]{1,0:T(8,128)(2,1)S(1)}, u32[]{:S(2)}, u32[]{:S(2)}) %collective-permute-start.24) | collective-permute-done | bytes 294944 | tf_op jit(solution)/shard_map/ppermute | solution.py:539
  226.7 3.1 %finish.4 = (bf16[192,3072]{1,0:T(8,128)(2,1)}, f32[192,3072]{1,0:T(8,128)}) custom-call(bf16[1,2,400,1024]{3,2,1,0:T(8,128)(2,1)} %get-tuple-element.265.keep, bf16[1,2,400,1024]{3,2,1,0:T(8,128)(2,1)} %collective-permute-done.18.from_core, bf16[1,1,400,1024]{3,2,1,0:T(8,128)(2,1)} %collective-permute-done.25.from_y, ...), custom_call_target="tpu_custom_call", output_to_operand_aliasing={{0}: (8, {}), {1}: (9, {})} | custom-call | flops 3000 | bytes 5000 | tf_op jit(solution)/shard_map/finish/pallas_call | solution.py:516
  229.8 1.9 maximum_select_fusion
  231.8 2.5 %slice_convert_fusion = (f32[768,768]{1,0:T(8,128)}, f32[768,768]{1,0:T(8,128)}) fusion(bf16[1536,768]{1,0:T(8,128)(2,1)S(1)} %maximum_select_fusion), kind=kLoop, calls=%fused_computation.4 | loop fusion | flops 1179648 | bytes 7077888 | tf_op jit(solution)/shard_map/convert_element_type | solution.py:834
  234.3 3.5 %collective-permute-done.27.from_y = bf16[1,1,400,1024]{3,2,1,0:T(8,128)(2,1)S(1)} collective-permute-done((bf16[1,1,400,1024]{3,2,1,0:T(8,128)(2,1)}, bf16[1,1,400,1024]{3,2,1,0:T(8,128)(2,1)S(1)}, u32[]{:S(2)}, u32[]{:S(2)}) %collective-permute-start.27) | collective-permute-done | bytes 819232 | tf_op jit(solution)/shard_map/ppermute | solution.py:539
  237.8 0.9 copy-done.15
  238.7 3.1 %finish.5 = (bf16[192,3072]{1,0:T(8,128)(2,1)}, f32[192,3072]{1,0:T(8,128)}) custom-call(bf16[1,2,400,1024]{3,2,1,0:T(8,128)(2,1)} %get-tuple-element.257.keep, bf16[1,2,400,1024]{3,2,1,0:T(8,128)(2,1)} %collective-permute-done.19.from_core, bf16[1,1,400,1024]{3,2,1,0:T(8,128)(2,1)} %copy-done.15, ...), custom_call_target="tpu_custom_call", output_to_operand_aliasing={{0}: (8, {}), {1}: (9, {})} | custom-call | flops 3000 | bytes 5000 | tf_op jit(solution)/shard_map/finish/pallas_call | solution.py:516
  242.0 0.9 slice.104
  242.9 1.3 slice.102
  (132 shorter events, 9.6 us)
Async XLA Ops:
  0.6 5.4 %copy-start.28 = (bf16[192]{0:T(256)(128)(2,1)S(1)}, bf16[192]{0:T(256)(128)(2,1)}, u32[]{:S(2)}) copy-start(bf16[192]{0:T(256)(128)(2,1)} %param.14) | copy-start | bytes 1156
  1.7 18.9 %copy-start.11 = (bf16[192,1024]{1,0:T(8,128)(2,1)}, bf16[192,1024]{1,0:T(8,128)(2,1)S(1)}, u32[]{:S(2)}) copy-start(bf16[192,1024]{1,0:T(8,128)(2,1)S(1)} %slice.95.own) | copy-start | bytes 1179652
  1.7 30.1 %collective-permute-start = (bf16[192,1024]{1,0:T(8,128)(2,1)S(1)}, bf16[192,1024]{1,0:T(8,128)(2,1)S(1)}, u32[]{:S(2)}, u32[]{:S(2)}) collective-permute-start(bf16[192,1024]{1,0:T(8,128)(2,1)S(1)} %slice.95.own), channel_id=1, source_target_pairs={{0,2},{1,3},{2,0},{3,1},{4,6},{5,7},{6,4},{7,5},{8,10},{9,11},{10,... | collective-permute-start | bytes 1179656 | tf_op jit(solution)/shard_map/ppermute | solution.py:539
  5.9 26.7 %copy-start.7 = (bf16[192,2048]{1,0:T(8,128)(2,1)}, bf16[192,2048]{1,0:T(8,128)(2,1)S(1)}, u32[]{:S(2)}) copy-start(bf16[192,2048]{1,0:T(8,128)(2,1)S(1)} %slice.96.own) | copy-start | bytes 2359300
  5.9 42.8 %collective-permute-start.6 = (bf16[192,2048]{1,0:T(8,128)(2,1)S(1)}, bf16[192,2048]{1,0:T(8,128)(2,1)}, u32[]{:S(2)}, u32[]{:S(2)}) collective-permute-start(bf16[192,2048]{1,0:T(8,128)(2,1)S(1)} %slice.96.own), channel_id=1, source_target_pairs={{0,2},{1,3},{2,0},{3,1},{4,6},{5,7},{6,4},{7,5},{8,10},{9,11},{10,... | collective-permute-start | bytes 2359304 | tf_op jit(solution)/shard_map/ppermute | solution.py:539
  6.2 14.4 %copy-start.10 = (bf16[192,128]{1,0:T(8,128)(2,1)}, bf16[192,128]{1,0:T(8,128)(2,1)S(1)}, u32[]{:S(2)}) copy-start(bf16[192,128]{1,0:T(8,128)(2,1)S(1)} %broadcast_in_dim.25.gain_own.gain) | copy-start | bytes 147460
  6.2 15.9 %collective-permute-start.2 = (bf16[192,128]{1,0:T(8,128)(2,1)S(1)}, bf16[192,128]{1,0:T(8,128)(2,1)S(1)}, u32[]{:S(2)}, u32[]{:S(2)}) collective-permute-start(bf16[192,128]{1,0:T(8,128)(2,1)S(1)} %broadcast_in_dim.25.gain_own.gain), channel_id=1, source_target_pairs={{0,1},{1,0},{2,3},{3,2},{4,5},{5,4},{6,7},{7,6},{8,9},{9,8},{10,11... | collective-permute-start | bytes 147464 | tf_op jit(solution)/shard_map/ppermute | solution.py:539
  6.3 25.5 %collective-permute-start.1 = (bf16[192,128]{1,0:T(8,128)(2,1)S(1)}, bf16[192,128]{1,0:T(8,128)(2,1)S(1)}, u32[]{:S(2)}, u32[]{:S(2)}) collective-permute-start(bf16[192,128]{1,0:T(8,128)(2,1)S(1)} %broadcast_in_dim.25.gain_own.gain), channel_id=1, source_target_pairs={{0,2},{1,3},{2,0},{3,1},{4,6},{5,7},{6,4},{7,5},{8,10},{9,11},{10,... | collective-permute-start | bytes 147464 | tf_op jit(solution)/shard_map/ppermute | solution.py:539
  8.3 25.9 %collective-permute-start.3 = (bf16[192,1024]{1,0:T(8,128)(2,1)S(1)}, bf16[192,1024]{1,0:T(8,128)(2,1)}, u32[]{:S(2)}, u32[]{:S(2)}) collective-permute-start(bf16[192,1024]{1,0:T(8,128)(2,1)S(1)} %slice.95.own), channel_id=1, source_target_pairs={{0,1},{1,0},{2,3},{3,2},{4,5},{5,4},{6,7},{7,6},{8,9},{9,8},{10,11... | collective-permute-start | bytes 1179656 | tf_op jit(solution)/shard_map/ppermute | solution.py:539
  9.3 11.3 %copy-start = (bf16[768,768]{1,0:T(8,128)(2,1)S(1)}, bf16[768,768]{1,0:T(8,128)(2,1)}, u32[]{:S(2)}) copy-start(bf16[768,768]{1,0:T(8,128)(2,1)} %up.5) | copy-start | bytes 3538948
  20.6 11.2 %copy-start.27 = (bf16[768]{0:T(1024)(128)(2,1)S(1)}, bf16[768]{0:T(1024)(128)(2,1)}, u32[]{:S(2)}) copy-start(bf16[768]{0:T(1024)(128)(2,1)} %param.19) | copy-start | bytes 4612
  20.6 12.6 %copy-start.31 = (s32[4]{0:T(128)S(1)}, s32[4]{0:T(128)}, u32[]{:S(2)}) copy-start(s32[4]{0:T(128)} %constant.117.clone) | copy-start | bytes 52
  22.0 13.1 %copy-start.22 = (bf16[192,128]{1,0:T(8,128)(2,1)}, bf16[192,128]{1,0:T(8,128)(2,1)S(1)}, u32[]{:S(2)}) copy-start(bf16[192,128]{1,0:T(8,128)(2,1)S(1)} %collective-permute-done.2.gain_c) | copy-start | bytes 147460
  31.8 3.4 %copy-start.23 = (bf16[192,128]{1,0:T(8,128)(2,1)}, bf16[192,128]{1,0:T(8,128)(2,1)S(1)}, u32[]{:S(2)}) copy-start(bf16[192,128]{1,0:T(8,128)(2,1)S(1)} %collective-permute-done.1.gain_y) | copy-start | bytes 147460
  31.8 3.4 %copy-start.16 = (bf16[192,1024]{1,0:T(8,128)(2,1)}, bf16[192,1024]{1,0:T(8,128)(2,1)S(1)}, u32[]{:S(2)}) copy-start(bf16[192,1024]{1,0:T(8,128)(2,1)S(1)} %collective-permute-done.flip_y) | copy-start | bytes 1179652
  32.6 2.6 %collective-permute-start.4 = (bf16[192,1024]{1,0:T(8,128)(2,1)S(1)}, bf16[192,1024]{1,0:T(8,128)(2,1)S(1)}, u32[]{:S(2)}, u32[]{:S(2)}) collective-permute-start(bf16[192,1024]{1,0:T(8,128)(2,1)S(1)} %collective-permute-done.flip_y), channel_id=1, source_target_pairs={{0,1},{1,0},{2,3},{3,2},{4,5},{5,4},{6,7},{7,6},{8,9},{9,8},{10,11... | collective-permute-start | bytes 1179656 | tf_op jit(solution)/shard_map/ppermute | solution.py:539
  32.6 23.4 %collective-permute-start.7 = (bf16[192,2048]{1,0:T(8,128)(2,1)S(1)}, bf16[192,2048]{1,0:T(8,128)(2,1)}, u32[]{:S(2)}, u32[]{:S(2)}) collective-permute-start(bf16[192,2048]{1,0:T(8,128)(2,1)S(1)} %slice.96.own), channel_id=1, source_target_pairs={{0,1},{1,0},{2,3},{3,2},{4,5},{5,4},{6,7},{7,6},{8,9},{9,8},{10,11... | collective-permute-start | bytes 2359304 | tf_op jit(solution)/shard_map/ppermute | solution.py:539
  33.6 1.5 collective-permute-start.5
  34.2 14.4 %copy-start.25 = (s32[3,1024]{1,0:T(4,128)S(1)}, s32[3,1024]{1,0:T(4,128)}, u32[]{:S(2)}) copy-start(s32[3,1024]{1,0:T(4,128)} %param.13) | copy-start | bytes 36868
  34.2 16.2 %copy-start.12 = (bf16[192,768]{1,0:T(8,128)(2,1)S(1)}, bf16[192,768]{1,0:T(8,128)(2,1)}, u32[]{:S(2)}) copy-start(bf16[192,768]{1,0:T(8,128)(2,1)} %attn.1) | copy-start | bytes 884740
  34.2 17.1 %copy-start.6 = (bf16[768,3,192]{0,2,1:T(8,128)(2,1)S(1)}, bf16[768,3,192]{0,2,1:T(8,128)(2,1)}, u32[]{:S(2)}) copy-start(bf16[768,3,192]{0,2,1:T(8,128)(2,1)} %param.15) | copy-start | bytes 2654212
  35.2 0.6 copy-start.24
  35.8 0.7 copy-start.17
  48.5 4.1 %copy-start.1 = (bf16[768,768]{1,0:T(8,128)(2,1)S(1)}, bf16[768,768]{1,0:T(8,128)(2,1)}, u32[]{:S(2)}) copy-start(bf16[768,768]{1,0:T(8,128)(2,1)} %down.1) | copy-start | bytes 3538948
  48.7 7.3 %collective-permute-start.8 = (bf16[192,2048]{1,0:T(8,128)(2,1)}, bf16[192,2048]{1,0:T(8,128)(2,1)}, u32[]{:S(2)}, u32[]{:S(2)}) collective-permute-start(bf16[192,2048]{1,0:T(8,128)(2,1)} %collective-permute-done.6.flip_y), channel_id=1, source_target_pairs={{0,1},{1,0},{2,3},{3,2},{4,5},{5,4},{6,7},{7,6},{8,9},{9,8},{10,11... | collective-permute-start | bytes 2359304 | tf_op jit(solution)/shard_map/ppermute | solution.py:539
  52.6 2.7 %copy-start.30 = (pred[16]{0:T(512)(128)(4,1)S(1)}, pred[16]{0:T(512)(128)(4,1)}, u32[]{:S(2)}) copy-start(pred[16]{0:T(512)(128)(4,1)} %iota_compare_fusion.2) | copy-start | bytes 52
  52.6 3.5 %copy-start.29 = (bf16[192]{0:T(256)(128)(2,1)S(1)}, bf16[192]{0:T(256)(128)(2,1)}, u32[]{:S(2)}) copy-start(bf16[192]{0:T(256)(128)(2,1)} %param.21) | copy-start | bytes 1156
  77.9 60.2 %all-to-all-start = ((bf16[8,192,768]{2,1,0:T(8,128)(2,1)}), bf16[8,192,768]{2,1,0:T(8,128)(2,1)S(1)}, u32[]{:S(2)}, u32[]{:S(2)}) async-start(bf16[8,192,768]{2,1,0:T(8,128)(2,1)} %bitcast.39), calls=%async_computation | async-start | bytes 4718592 | tf_op jit(solution)/shard_map/all_to_all | solution.py:562
  83.9 36.6 %copy-start.20 = (f32[768,128]{1,0:T(8,128)S(1)}, f32[768,128]{1,0:T(8,128)}, u32[]{:S(2)}) copy-start(f32[768,128]{1,0:T(8,128)} %get-tuple-element.215) | copy-start | bytes 1179652
  123.6 9.8 %collective-permute-start.9 = (f32[2,192]{1,0:T(2,128)S(1)}, f32[2,192]{1,0:T(2,128)S(1)}, u32[]{:S(2)}, u32[]{:S(2)}) collective-permute-start(f32[2,192]{1,0:T(2,128)S(1)} %pad_maximum_fusion), channel_id=1, source_target_pairs={{0,1},{1,0},{2,3},{3,2},{4,5},{5,4},{6,7},{7,6},{8,9},{9,8},{10,11... | collective-permute-start | bytes 4616 | tf_op jit(solution)/shard_map/ppermute | solution.py:539
  133.4 11.6 %copy-start.26 = (f32[192,128]{1,0:T(8,128)S(1)}, f32[192,128]{1,0:T(8,128)}, u32[]{:S(2)}) copy-start(f32[192,128]{1,0:T(8,128)} %get-tuple-element.244) | copy-start | bytes 294916
  133.4 13.3 %copy-start.18 = (f32[768,128]{1,0:T(8,128)S(1)}, f32[768,128]{1,0:T(8,128)}, u32[]{:S(2)}) copy-start(f32[768,128]{1,0:T(8,128)} %get-tuple-element.242) | copy-start | bytes 1179652
  133.4 13.3 %copy-start.19 = (f32[768,128]{1,0:T(8,128)S(1)}, f32[768,128]{1,0:T(8,128)}, u32[]{:S(2)}) copy-start(f32[768,128]{1,0:T(8,128)} %get-tuple-element.243) | copy-start | bytes 1179652
  138.1 8.7 %copy-start.21 = (f32[384,128]{1,0:T(8,128)S(1)}, f32[384,128]{1,0:T(8,128)}, u32[]{:S(2)}) copy-start(f32[384,128]{1,0:T(8,128)} %get-tuple-element.241) | copy-start | bytes 589828
  139.3 18.6 %collective-permute-start.13 = (bf16[1,2,400,1024]{3,2,1,0:T(8,128)(2,1)}, bf16[1,2,400,1024]{3,2,1,0:T(8,128)(2,1)S(1)}, u32[]{:S(2)}, u32[]{:S(2)}) collective-permute-start(bf16[1,2,400,1024]{3,2,1,0:T(8,128)(2,1)} %get-tuple-element.237), channel_id=1, source_target_pairs={{0,1},{1,0},{2,3},{3,2},{4,5},{5,4},{6,7},{7,6},{8,9},{9,8},{10,11... | collective-permute-start | bytes 4915208 | tf_op jit(solution)/shard_map/ppermute | solution.py:539
  139.3 17.7 %collective-permute-start.10 = (bf16[384,768]{1,0:T(8,128)(2,1)}, bf16[384,768]{1,0:T(8,128)(2,1)}, u32[]{:S(2)}, u32[]{:S(2)}) collective-permute-start(bf16[384,768]{1,0:T(8,128)(2,1)} %constant_dynamic-slice_fusion.4), channel_id=1, source_target_pairs={{0,4},{4,0},{8,12},{12,8},{16,20},{20,16},{24,28},{28,24},{1,5},{5... | collective-permute-start | bytes 1769480 | tf_op jit(solution)/shard_map/ppermute | solution.py:539
  140.7 17.1 %collective-permute-start.11 = (bf16[192,768]{1,0:T(8,128)(2,1)}, bf16[192,768]{1,0:T(8,128)(2,1)}, u32[]{:S(2)}, u32[]{:S(2)}) collective-permute-start(bf16[192,768]{1,0:T(8,128)(2,1)} %reduce_sum.75), channel_id=1, source_target_pairs={{0,16},{4,20},{8,24},{12,28},{16,0},{20,4},{24,8},{28,12},{1,17},{... | collective-permute-start | bytes 884744 | tf_op jit(solution)/shard_map/ppermute | solution.py:539
  145.1 11.9 %collective-permute-start.12 = (f32[192]{0:T(256)S(1)}, f32[192]{0:T(256)S(1)}, u32[]{:S(2)}, u32[]{:S(2)}) collective-permute-start(f32[192]{0:T(256)S(1)} %bitcast.42), channel_id=1, source_target_pairs={{0,2},{1,3},{2,0},{3,1},{4,6},{5,7},{6,4},{7,5},{8,10},{9,11},{10,... | collective-permute-start | bytes 2312 | tf_op jit(solution)/shard_map/ppermute | solution.py:539
  147.0 13.6 %copy-start.4 = (bf16[1,2,400,1024]{3,2,1,0:T(8,128)(2,1)S(1)}, bf16[1,2,400,1024]{3,2,1,0:T(8,128)(2,1)}, u32[]{:S(2)}) copy-start(bf16[1,2,400,1024]{3,2,1,0:T(8,128)(2,1)} %get-tuple-element.245.keep) | copy-start | bytes 4915204
  157.8 4.0 %copy-start.5 = (bf16[1,2,400,1024]{3,2,1,0:T(8,128)(2,1)}, bf16[1,2,400,1024]{3,2,1,0:T(8,128)(2,1)S(1)}, u32[]{:S(2)}) copy-start(bf16[1,2,400,1024]{3,2,1,0:T(8,128)(2,1)S(1)} %collective-permute-done.13.from_core) | copy-start | bytes 4915204
  157.9 4.0 %copy-start.13 = (bf16[768,768]{1,0:T(8,128)(2,1)S(1)}, bf16[768,768]{1,0:T(8,128)(2,1)}, u32[]{:S(2)}) copy-start(bf16[768,768]{1,0:T(8,128)(2,1)} %get-tuple-element.213) | copy-start | bytes 3538948
  161.9 3.7 %copy-start.8 = (bf16[384,768]{1,0:T(8,128)(2,1)S(1)}, bf16[384,768]{1,0:T(8,128)(2,1)}, u32[]{:S(2)}) copy-start(bf16[384,768]{1,0:T(8,128)(2,1)} %maximum_select_fusion.3) | copy-start | bytes 1769476
  164.0 23.3 %collective-permute-start.18 = (bf16[1,2,400,1024]{3,2,1,0:T(8,128)(2,1)}, bf16[1,2,400,1024]{3,2,1,0:T(8,128)(2,1)}, u32[]{:S(2)}, u32[]{:S(2)}) collective-permute-start(bf16[1,2,400,1024]{3,2,1,0:T(8,128)(2,1)} %get-tuple-element.256), channel_id=1, source_target_pairs={{0,1},{1,0},{2,3},{3,2},{4,5},{5,4},{6,7},{7,6},{8,9},{9,8},{10,11... | collective-permute-start | bytes 4915208 | tf_op jit(solution)/shard_map/ppermute | solution.py:539
  164.0 23.3 %collective-permute-start.17 = (bf16[1,1,400,1024]{3,2,1,0:T(8,128)(2,1)}, bf16[1,1,400,1024]{3,2,1,0:T(8,128)(2,1)S(1)}, u32[]{:S(2)}, u32[]{:S(2)}) collective-permute-start(bf16[1,1,400,1024]{3,2,1,0:T(8,128)(2,1)} %add_convert_fusion.2), channel_id=1, source_target_pairs={{0,2},{1,3},{2,0},{3,1},{4,6},{5,7},{6,4},{7,5},{8,10},{9,11},{10,... | collective-permute-start | bytes 2457608 | tf_op jit(solution)/shard_map/ppermute | solution.py:539
  165.6 21.7 %collective-permute-start.15 = (bf16[384,768]{1,0:T(8,128)(2,1)S(1)}, bf16[384,768]{1,0:T(8,128)(2,1)}, u32[]{:S(2)}, u32[]{:S(2)}) collective-permute-start(bf16[384,768]{1,0:T(8,128)(2,1)S(1)} %copy-done.8), channel_id=1, source_target_pairs={{0,8},{4,12},{8,0},{12,4},{16,24},{20,28},{24,16},{28,20},{1,9},{5... | collective-permute-start | bytes 1769480 | tf_op jit(solution)/shard_map/ppermute | solution.py:539
  165.6 21.7 %collective-permute-start.14 = (bf16[192,768]{1,0:T(8,128)(2,1)}, bf16[192,768]{1,0:T(8,128)(2,1)S(1)}, u32[]{:S(2)}, u32[]{:S(2)}) collective-permute-start(bf16[192,768]{1,0:T(8,128)(2,1)} %get-tuple-element.252), channel_id=1, source_target_pairs={{0,8},{4,12},{8,0},{12,4},{16,24},{20,28},{24,16},{28,20},{1,9},{5... | collective-permute-start | bytes 884744 | tf_op jit(solution)/shard_map/ppermute | solution.py:539
  167.7 10.1 %collective-permute-start.16 = (f32[1536]{0:T(1024)S(1)}, f32[1536]{0:T(1024)S(1)}, u32[]{:S(2)}, u32[]{:S(2)}) collective-permute-start(f32[1536]{0:T(1024)S(1)} %concatenate.41), channel_id=1, source_target_pairs={{0,4},{4,0},{8,12},{12,8},{16,20},{20,16},{24,28},{28,24},{1,5},{5... | collective-permute-start | bytes 18440 | tf_op jit(solution)/shard_map/ppermute | solution.py:539
  167.9 20.9 %copy-start.9 = (bf16[384,768]{1,0:T(8,128)(2,1)S(1)}, bf16[384,768]{1,0:T(8,128)(2,1)}, u32[]{:S(2)}) copy-start(bf16[384,768]{1,0:T(8,128)(2,1)} %maximum_select_fusion.3) | copy-start | bytes 1769476
  177.8 12.7 %copy-start.2 = (bf16[1,2,400,1024]{3,2,1,0:T(8,128)(2,1)S(1)}, bf16[1,2,400,1024]{3,2,1,0:T(8,128)(2,1)}, u32[]{:S(2)}) copy-start(bf16[1,2,400,1024]{3,2,1,0:T(8,128)(2,1)} %get-tuple-element.265.keep) | copy-start | bytes 4915204
  187.4 0.9 copy-start.14
  193.5 10.5 %collective-permute-start.19 = (bf16[1,2,400,1024]{3,2,1,0:T(8,128)(2,1)}, bf16[1,2,400,1024]{3,2,1,0:T(8,128)(2,1)}, u32[]{:S(2)}, u32[]{:S(2)}) collective-permute-start(bf16[1,2,400,1024]{3,2,1,0:T(8,128)(2,1)} %get-tuple-element.270), channel_id=1, source_target_pairs={{0,1},{1,0},{2,3},{3,2},{4,5},{5,4},{6,7},{7,6},{8,9},{9,8},{10,11... | collective-permute-start | bytes 4915208 | tf_op jit(solution)/shard_map/ppermute | solution.py:539
  193.5 10.5 %collective-permute-start.20 = (bf16[96,768]{1,0:T(8,128)(2,1)}, bf16[96,768]{1,0:T(8,128)(2,1)S(1)}, u32[]{:S(2)}, u32[]{:S(2)}) collective-permute-start(bf16[96,768]{1,0:T(8,128)(2,1)} %add_convert_fusion.7), channel_id=1, source_target_pairs={{0,16},{4,20},{8,24},{12,28},{16,0},{20,4},{24,8},{28,12},{1,17},{... | collective-permute-start | bytes 442376 | tf_op jit(solution)/shard_map/ppermute | solution.py:539
  195.0 28.2 %collective-permute-start.26 = (bf16[768,768]{1,0:T(8,128)(2,1)S(1)}, bf16[768,768]{1,0:T(8,128)(2,1)}, u32[]{:S(2)}, u32[]{:S(2)}) collective-permute-start(bf16[768,768]{1,0:T(8,128)(2,1)S(1)} %maximum_select_fusion.1), channel_id=1, source_target_pairs={{0,4},{4,0},{8,12},{12,8},{16,20},{20,16},{24,28},{28,24},{1,5},{5... | collective-permute-start | bytes 3538952 | tf_op jit(solution)/shard_map/ppermute | solution.py:539
  196.2 4.4 %collective-permute-start.21 = (f32[1536]{0:T(1024)}, f32[1536]{0:T(1024)}, u32[]{:S(2)}, u32[]{:S(2)}) collective-permute-start(f32[1536]{0:T(1024)} %add.137), channel_id=1, source_target_pairs={{0,8},{4,12},{8,0},{12,4},{16,24},{20,28},{24,16},{28,20},{1,9},{5... | collective-permute-start | bytes 18440 | tf_op jit(solution)/shard_map/ppermute | solution.py:539
  197.0 23.6 %collective-permute-start.25 = (bf16[1,1,400,1024]{3,2,1,0:T(8,128)(2,1)}, bf16[1,1,400,1024]{3,2,1,0:T(8,128)(2,1)}, u32[]{:S(2)}, u32[]{:S(2)}) collective-permute-start(bf16[1,1,400,1024]{3,2,1,0:T(8,128)(2,1)} %add_convert_fusion.1), channel_id=1, source_target_pairs={{0,2},{1,3},{2,0},{3,1},{4,6},{5,7},{6,4},{7,5},{8,10},{9,11},{10,... | collective-permute-start | bytes 2457608 | tf_op jit(solution)/shard_map/ppermute | solution.py:539
  197.5 6.5 %copy-start.3 = (bf16[1,2,400,1024]{3,2,1,0:T(8,128)(2,1)S(1)}, bf16[1,2,400,1024]{3,2,1,0:T(8,128)(2,1)}, u32[]{:S(2)}) copy-start(bf16[1,2,400,1024]{3,2,1,0:T(8,128)(2,1)} %get-tuple-element.257.keep) | copy-start | bytes 4915204
  207.2 10.0 %collective-permute-start.22 = (bf16[96,768]{1,0:T(8,128)(2,1)S(1)}, bf16[96,768]{1,0:T(8,128)(2,1)S(1)}, u32[]{:S(2)}, u32[]{:S(2)}) collective-permute-start(bf16[96,768]{1,0:T(8,128)(2,1)S(1)} %add_convert_fusion.5), channel_id=1, source_target_pairs={{0,16},{4,20},{8,24},{12,28},{16,0},{20,4},{24,8},{28,12},{1,17},{... | collective-permute-start | bytes 442376 | tf_op jit(solution)/shard_map/ppermute | solution.py:539
  207.3 9.9 %collective-permute-start.23 = (f32[1536]{0:T(1024)S(1)}, f32[1536]{0:T(1024)S(1)}, u32[]{:S(2)}, u32[]{:S(2)}) collective-permute-start(f32[1536]{0:T(1024)S(1)} %add.141), channel_id=1, source_target_pairs={{0,16},{4,20},{8,24},{12,28},{16,0},{20,4},{24,8},{28,12},{1,17},{... | collective-permute-start | bytes 18440 | tf_op jit(solution)/shard_map/ppermute | solution.py:539
  217.3 9.0 %collective-permute-start.24 = (bf16[192,768]{1,0:T(8,128)(2,1)S(1)}, bf16[192,768]{1,0:T(8,128)(2,1)S(1)}, u32[]{:S(2)}, u32[]{:S(2)}) collective-permute-start(bf16[192,768]{1,0:T(8,128)(2,1)S(1)} %maximum_select_fusion.5), channel_id=1, source_target_pairs={{0,8},{4,12},{8,0},{12,4},{16,24},{20,28},{24,16},{28,20},{1,9},{5... | collective-permute-start | bytes 884744 | tf_op jit(solution)/shard_map/ppermute | solution.py:539
  217.3 20.4 %collective-permute-start.27 = (bf16[1,1,400,1024]{3,2,1,0:T(8,128)(2,1)}, bf16[1,1,400,1024]{3,2,1,0:T(8,128)(2,1)S(1)}, u32[]{:S(2)}, u32[]{:S(2)}) collective-permute-start(bf16[1,1,400,1024]{3,2,1,0:T(8,128)(2,1)} %add_convert_fusion), channel_id=1, source_target_pairs={{0,2},{1,3},{2,0},{3,1},{4,6},{5,7},{6,4},{7,5},{8,10},{9,11},{10,... | collective-permute-start | bytes 2457608 | tf_op jit(solution)/shard_map/ppermute | solution.py:539
  226.4 15.4 %collective-permute-start.28 = (bf16[384,768]{1,0:T(8,128)(2,1)S(1)}, bf16[384,768]{1,0:T(8,128)(2,1)S(1)}, u32[]{:S(2)}, u32[]{:S(2)}) collective-permute-start(bf16[384,768]{1,0:T(8,128)(2,1)S(1)} %maximum_select_fusion.4), channel_id=1, source_target_pairs={{0,4},{4,0},{8,12},{12,8},{16,20},{20,16},{24,28},{28,24},{1,5},{5... | collective-permute-start | bytes 1769480 | tf_op jit(solution)/shard_map/ppermute | solution.py:539
  237.8 0.9 copy-start.15

commit v8 on v6

--- a/solution.py
+++ b/solution.py
@@ -242,23 +242,26 @@
     dka[...] = jnp.zeros_like(dka)
     dva[...] = jnp.zeros_like(dva)
 
-    def straight(trips, i0, base):
+    def straight(units, i0, base):
         icols = pl.ds(i0, BI)
-        places = [pl.ds(pl.multiple_of(base + j * BJ, 128), BJ) for j in range(trips)]
+        edges = [(at, min(BJ, units * 128 - at)) for at in range(0, units * 128, BJ)]
+        trips = len(edges)
+        spots = [slice(at, at + size) for at, size in edges]
+        places = [pl.ds(pl.multiple_of(base + at, 128), size) for at, size in edges]
 
         def scores(head, j, sums):
             rows = slice(head * DH, (head + 1) * DH)
             e = jnp.exp(dot(kx[head, places[j], :], qx[head, :, icols]))
             p = dot(vn[head, places[j], :], d_att[rows, icols])
-            es[head % 2, j * BJ : (j + 1) * BJ, :] = e
-            ps[head % 2, j * BJ : (j + 1) * BJ, :] = p
+            es[head % 2, spots[j], :] = e
+            ps[head % 2, spots[j], :] = p
             more = (jnp.sum(e, axis=0, keepdims=True), jnp.sum(e * p, axis=0, keepdims=True))
             return more if sums is None else (sums[0] + more[0], sums[1] + more[1])
 
         def row_grads(head, j, inverse, inner, held):
             rows = slice(head * DH, (head + 1) * DH)
-            w = es[head % 2, j * BJ : (j + 1) * BJ, :] * inverse
-            d = (w * (ps[head % 2, j * BJ : (j + 1) * BJ, :] - inner)).astype(BF16)
+            w = es[head % 2, spots[j], :] * inverse
+            d = (w * (ps[head % 2, spots[j], :] - inner)).astype(BF16)
             w = w.astype(BF16)
             out = dot(vt[rows, places[j]], w)
             query = dot(kt[rows, places[j]], d)
@@ -286,7 +289,7 @@
         i0 = pl.multiple_of(ib * BI, BI)
         base = first[seq * (LEN // BI) + ib] * 128
         trips = count[seq * (LEN // BI) + ib]
-        for number in range(1, LEN // BJ + 1):
+        for number in range(BI // 128, LEN // 128 + 1):
             pl.when(trips == number)(functools.partial(straight, number, i0, base))
         return 0
 
@@ -457,7 +460,7 @@
     token_grad[...] = cot[...].astype(F32) + inner * scale
 
 
-def finish_call(keep, from_core, from_y, own_t, cot, stats, gain, bias, before, begin, block=256):
+def finish_call(keep, from_core, from_y, own_t, cot, stats, gain, bias, before, begin, block=512):
     part, tokens = own_t.shape
     steps = LEN // block
     size = keep.shape[0]
@@ -495,6 +498,12 @@
     return lax.optimization_barrier(trees)
 
 
+def joined(swap, held, arrived):
+    return jnp.where(
+        swap, jnp.concatenate([arrived, held], axis=0), jnp.concatenate([held, arrived], axis=0)
+    )
+
+
 def piece_order(size):
     bits = size.bit_length() - 1
     return [sum(((i >> b) & 1) << (bits - 1 - b) for b in range(bits)) for i in range(size)]
@@ -520,11 +529,8 @@
             shares = arrived.reshape(self.size, -1, arrived.shape[1]).astype(F32)
             self.keep = jnp.sum(shares, axis=0).astype(BF16)
         else:
-            self.keep = jnp.where(
-                (self.index & step) > 0,
-                jnp.concatenate([arrived, self.keep], axis=0),
-                jnp.concatenate([self.keep, arrived], axis=0),
-            )
+            self.last = ((self.index & step) > 0, self.keep, arrived)
+            self.keep = joined(*self.last)
         self.send = self.keep
 
 
@@ -562,12 +568,8 @@
         if kind == "sum":
             self.prepare(self.keep, arrived)
             return
-        self.keep = jnp.where(
-            (self.index & bit) > 0,
-            jnp.concatenate([arrived, self.keep], axis=0),
-            jnp.concatenate([self.keep, arrived], axis=0),
-        )
-        self.send = self.keep
+        self.last = ((self.index & bit) > 0, self.keep, arrived)
+        self.keep = self.send = joined(*self.last)
 
 
 class ScatterOverMp:
@@ -665,8 +667,7 @@
     def column(vector):
         return jnp.broadcast_to(vector[:, None], (vector.shape[0], 128))
 
-    up_bias_col = column(up_bias)
-    head_gains = column(qk_gain.astype(F32).reshape(2 * part))
+    columns = (column(up_bias), column(qk_gain.astype(F32).reshape(2 * part)), column(down_bias))
 
     slots = jnp.arange(IMAGE_SLOTS, dtype=jnp.int32)[None, :, None]
     same = image_ids[:, None, :] == slots
@@ -677,19 +678,20 @@
     starts = jnp.sum(image_ids[:, None, :] < block_first[:, :, None], axis=2, dtype=jnp.int32)
     ends = jnp.sum(image_ids[:, None, :] <= block_last[:, :, None], axis=2, dtype=jnp.int32)
     first = starts // 128
-    count = ((ends + 127) // 128 - first + BJ // 128 - 1) // (BJ // 128)
-    first = jnp.minimum(first, (LEN - count * BJ) // 128).reshape(-1)
-    count = count.reshape(-1)
+    count = ((ends + 127) // 128 - first).reshape(-1)
+    first = first.reshape(-1)
 
     pick = (jnp.arange(part)[:, None] + me * part == jnp.arange(width)[None, :]).astype(BF16)
+    pick, place, columns, (gain_y, gain_c) = tie(pick, place, columns, (gain_y, gain_c))
+    up_bias_col, head_gains, bias_col = columns
+    gain_cy = flip(gain_y, "mp", 4, 1)
     d_act, d_att, cot_own, cot_sum = early_call(cotangent, down_weight, attn_weight, pick)
-    bias_col = column(down_bias)
     prepared = (
         d_act, d_att, mixed_t, mixed, up_t, down_t, attn_t, up_bias_col, head_gains, mask_q, mask_k, first, count,
         bias_col,
     )
-    prepared, (from_y, gain_y, gain_c) = tie(prepared, (from_y, gain_y, gain_c))
-    gains = (gain_own, gain_y, gain_c, flip(gain_y, "mp", 4, 1))
+    prepared, (from_y, gain_cy) = tie(prepared, (from_y, gain_cy))
+    gains = (gain_own, gain_y, gain_c, gain_cy)
     (
         d_act, d_att, mixed_t, mixed, up_t, down_t, attn_t, up_bias_col, head_gains, mask_q, mask_k, first, count,
         bias_col,
@@ -770,13 +772,19 @@
         finished, wide_grads = land(now, (finished, wide_grads))
         flying = [f for f in flying if f not in now]
         if not mlp_sum.more() and not wide_grads:
-            split = up_weight.shape[1]
-            wide_grads = (mlp_sum.keep[:split].astype(F32), mlp_sum.keep[split:].astype(F32))
+            swap, held, arrived = mlp_sum.last
+            wide_grads = (
+                jnp.where(swap, arrived, held).astype(F32),
+                jnp.where(swap, held, arrived).astype(F32),
+            )
     finished = finish_ready(finished)
     block_out, token_grad = finished
     block_out, token_grad = block_out.T, token_grad.T
-    mixed_grad = mix_sum.keep.astype(F32)
-    qkv_grad = jnp.transpose(mixed_grad[: 3 * part].reshape(3, part, width), (2, 0, 1))
+    swap, held, arrived = mix_sum.last
+    left = 3 * part - held.shape[0]
+    qkv_rows = joined(swap, held, arrived)[: 3 * part].astype(F32)
+    attn_grad = jnp.where(swap, held[left:], arrived[left:]).astype(F32)
+    qkv_grad = jnp.transpose(qkv_rows.reshape(3, part, width), (2, 0, 1))
 
     gain_grad = short.norm / norm_gain.astype(F32)
     rest = short.rest
@@ -787,7 +795,7 @@
         gain_grad,
         qkv_grad,
         rest[: 2 * part].reshape(2, part),
-        mixed_grad[3 * part :],
+        attn_grad,
         wide_grads[1],
         rest[2 * part : split],
         wide_grads[0],

time: 229 us -> 226 us (0.987)
  starting transfers between devices: 32.1 us -> 29.4 us
  waiting for transfers between devices: 32.4 us -> 34.9 us
  other arithmetic: 26.2 us -> 28.5 us
    ppermute x26, waiting for transfers between devices: 28.3 us -> 31.8 us  [flip(): return lax.ppermute(value, axis, [(i, i ^ bit) for i in range(size)])]
    pallas_call x3, Pallas kernels: 12.8 us -> 9.4 us  [finish_call(): pl.pallas_call(finish_kernel, grid=(size * steps,), in_specs=[packed, pac...]
    ppermute x26, starting transfers between devices: 26.3 us -> 23.2 us  [flip(): return lax.ppermute(value, axis, [(i, i ^ bit) for i in range(size)])]
    unnamed x51 -> x43, local copies, waits for them, and re-layouts: 8.43 us -> 6.8 us
  transfers between devices with their start and end apart: 27 -> 27, of which waited for: 9 -> 10; matrix products, arithmetic and copies ran while one was open for 13% -> 14% of each run, Pallas kernels for 40% -> 39%
where the time goes in v8:
time: 226 us; the launch traced here: 225 us
  Pallas kernels  113 us (50%)
  waiting for transfers between devices  34.9 us (15%)
  starting transfers between devices  29.4 us (13%)
  other arithmetic  28.5 us (13%)
  local copies, waits for them, and re-layouts  18.8 us (8%)
    pallas_call x1, Pallas kernels, attention_call(): pl.pallas_call(attention_kernel, grid_spec=grid_spec, out_shape=[jax.Shap...  38.3 us
    ppermute x26, waiting for transfers between devices, flip(): return lax.ppermute(value, axis, [(i, i ^ bit) for i in range(size)])  31.8 us
    pallas_call x3, Pallas kernels, project_call(): pl.pallas_call(project_kernel, grid_spec=grid_spec, out_shape=[jax.ShapeD...  29.5 us
    pallas_call x1, Pallas kernels, mlp_call(): pl.pallas_call(functools.partial(mlp_kernel, pieces_order), grid_spec=gri...  24.2 us
    ppermute x26, starting transfers between devices, flip(): return lax.ppermute(value, axis, [(i, i ^ bit) for i in range(size)])  23.2 us
    pallas_call x1, Pallas kernels, early_call(): pl.pallas_call(early_kernel, grid=(tokens // block,), in_specs=[pl.BlockS...  11.2 us
    pallas_call x3, Pallas kernels, finish_call(): pl.pallas_call(finish_kernel, grid=(size * steps,), in_specs=[packed, pac...  9.4 us
    unnamed x43, local copies, waits for them, and re-layouts  6.8 us
  transfers between devices with their start and end apart: 27, of which 10 were waited for; matrix products, arithmetic and copies ran while one was open for 14% of the time, Pallas kernels for 39%

profile of v8, /device:TPU:0, one launch (start us, length us, event | category | flops | bytes accessed | tf_op | source)
XLA Modules:
  0.0 225.1 jit_solution(365881144384278940)
XLA Ops:
  0.7 0.9 broadcast_in_dim.53.gain_own.gain
  1.6 3.0 %collective-permute-start = (bf16[192,128]{1,0:T(8,128)(2,1)S(1)}, bf16[192,128]{1,0:T(8,128)(2,1)S(1)}, u32[]{:S(2)}, u32[]{:S(2)}) collective-permute-start(bf16[192,128]{1,0:T(8,128)(2,1)S(1)} %broadcast_in_dim.53.gain_own.gain), channel_id=1, source_target_pairs={{0,2},{1,3},{2,0},{3,1},{4,6},{5,7},{6,4},{7,5},{8,10},{9,11},{10,... | collective-permute-start | bytes 147464 | tf_op jit(solution)/shard_map/ppermute | solution.py:494
  5.1 0.8 slice.65
  5.9 0.8 slice.66
  6.7 1.0 convert_reduce_fusion
  7.7 1.4 fusion.4.mask_q
  9.1 1.5 select_convert_fusion.2.mask_k
  10.6 0.8 fusion.1.pick
  11.4 1.2 xor_multiply_fusion.place
  12.6 0.8 reshape.72
  13.5 0.8 broadcast_in_dim.27.gains
  14.3 1.5 broadcast_in_dim.24.up_bias
  15.9 1.4 broadcast_in_dim.52.bias
  17.9 1.3 copy.35
  19.3 1.4 copy.36
  20.7 1.5 copy.37
  22.3 0.9 copy.38
  23.2 11.2 %early.1 = (bf16[3,768,1024]{2,1,0:T(8,128)(2,1)}, bf16[3,192,1024]{2,1,0:T(8,128)(2,1)}, bf16[192,3072]{1,0:T(8,128)(2,1)}, f32[192,128]{1,0:T(8,128)}) custom-call(bf16[3072,768]{1,0:T(8,128)(2,1)} %cot.5, bf16[768,768]{1,0:T(8,128)(2,1)} %down.1, bf16[192,768]{1,0:T(8,128)(2,1)} %attn.1, bf16[192,768]{1,0:T(8,128)(2,1)} %fusion.1.pick), custom_call_target="tpu_custom_call" | custom-call | flops 10000 | bytes 12000 | tf_op jit(solution)/shard_map/early/pallas_call | solution.py:62
  34.8 2.7 %collective-permute-done.5.flip_cy = bf16[192,3072]{1,0:T(8,128)(2,1)S(1)} collective-permute-done((bf16[192,3072]{1,0:T(8,128)(2,1)}, bf16[192,3072]{1,0:T(8,128)(2,1)S(1)}, u32[]{:S(2)}, u32[]{:S(2)}) %collective-permute-start.5) | collective-permute-done | bytes 1179680 | tf_op jit(solution)/shard_map/ppermute | solution.py:494
  37.5 1.0 copy-done.8
  38.5 24.2 %mlp.1 = (bf16[3,768,1024]{2,1,0:T(8,128)(2,1)}, bf16[3,768,1024]{2,1,0:T(8,128)(2,1)}, bf16[3,768,1024]{2,1,0:T(8,128)(2,1)}, f32[8,3072]{1,0:T(8,128)}, f32[76...) custom-call(s32[4]{0:T(128)} %xor_multiply_fusion.place, ...), custom_call_target="tpu_custom_call" | custom-call | flops 20000 | bytes 30000 | tf_op jit(solution)/shard_map/mlp/pallas_call | solution.py:188
  62.7 6.2 %all-to-all-start = ((bf16[8,192,768]{2,1,0:T(8,128)(2,1)}), bf16[8,192,768]{2,1,0:T(8,128)(2,1)S(1)}, u32[]{:S(2)}, u32[]{:S(2)}) async-start(bf16[8,192,768]{2,1,0:T(8,128)(2,1)} %bitcast.41), calls=%async_computation | async-start | bytes 4718592 | tf_op jit(solution)/shard_map/all_to_all | solution.py:523
  68.9 38.3 %attention.1 = (bf16[3,192,1024]{2,1,0:T(8,128)(2,1)}, bf16[3,576,1024]{2,1,0:T(8,128)(2,1)}, f32[384,128]{1,0:T(8,128)}, f32[1,768]{1,0:T(1,128)}, bf16[768,768]{1,0:T(8,128)(2,1)}) custom-call(s32[12]{0:T(128)} %get-tuple-element.156.first, s32[12]{0:T(128)} %get-tuple-element.157.count, bf16[3,768,1024]{2,1,0:T(8,128)(2,1)} %get-tuple-element.160.normed, ...), custom_call_target="tpu_custom_call" | custom-call | flops 18000 | bytes 5000 | tf_op jit(solution)/shard_map/attention/pallas_call | solution.py:360
  107.2 0.7 reduce.1
  108.3 1.9 constant_dynamic-slice_fusion.4
  110.2 9.8 %project.3 = (bf16[1,2,400,1024]{3,2,1,0:T(8,128)(2,1)}, bf16[1,2,400,1024]{3,2,1,0:T(8,128)(2,1)}) custom-call(s32[1]{0:T(128)} %bitcast.shard, bf16[3,768,1024]{2,1,0:T(8,128)(2,1)} %get-tuple-element.155.active, bf16[3,192,1024]{2,1,0:T(8,128)(2,1)} %get-tuple-element.202.attended, bf16[3,768,1024]{2,1,0:T(8,128)(2,1)} %get-tuple-element.172.d_pre, ...), custom_call_target="tpu_custom_call" | custom-call | flops 8000 | bytes 16000 | tf_op jit(solution)/shard_map/project/pallas_call | solution.py:435
  120.0 3.1 %all-to-all-done = bf16[8,192,768]{2,1,0:T(8,128)(2,1)S(1)} async-done(((bf16[8,192,768]{2,1,0:T(8,128)(2,1)}), bf16[8,192,768]{2,1,0:T(8,128)(2,1)S(1)}, u32[]{:S(2)}, u32[]{:S(2)}) %all-to-all-start) | async-done | bytes 2359328 | tf_op jit(solution)/shard_map/all_to_all | solution.py:523
  123.2 1.1 reduce_sum.75
  124.3 1.5 collective-permute-start.7
  125.7 0.7 collective-permute-start.8
  126.5 1.5 collective-permute-start.9
  128.4 9.9 %project.4 = (bf16[1,2,400,1024]{3,2,1,0:T(8,128)(2,1)}, bf16[1,2,400,1024]{3,2,1,0:T(8,128)(2,1)}) custom-call(s32[1]{0:T(128)} %bitcast.shard, bf16[3,768,1024]{2,1,0:T(8,128)(2,1)} %get-tuple-element.155.active, bf16[3,192,1024]{2,1,0:T(8,128)(2,1)} %get-tuple-element.202.attended, bf16[3,768,1024]{2,1,0:T(8,128)(2,1)} %get-tuple-element.172.d_pre, ...), custom_call_target="tpu_custom_call" | custom-call | flops 8000 | bytes 16000 | tf_op jit(solution)/shard_map/project/pallas_call | solution.py:435
  138.4 2.0 collective-permute-done.7
  140.3 1.3 collective-permute-done.8
  141.7 1.2 add_convert_fusion.2
  142.9 1.4 maximum_select_fusion.1
  144.3 2.0 add_convert_fusion.3
  146.4 1.6 collective-permute-start.14
  148.0 2.0 collective-permute-start.11
  150.0 1.4 collective-permute-start.13
  151.3 9.8 %project.5 = (bf16[1,2,400,1024]{3,2,1,0:T(8,128)(2,1)}, bf16[1,2,400,1024]{3,2,1,0:T(8,128)(2,1)}) custom-call(s32[1]{0:T(128)} %bitcast.shard, bf16[3,768,1024]{2,1,0:T(8,128)(2,1)} %get-tuple-element.155.active, bf16[3,192,1024]{2,1,0:T(8,128)(2,1)} %get-tuple-element.202.attended, bf16[3,768,1024]{2,1,0:T(8,128)(2,1)} %get-tuple-element.172.d_pre, ...), custom_call_target="tpu_custom_call" | custom-call | flops 8000 | bytes 16000 | tf_op jit(solution)/shard_map/project/pallas_call | solution.py:435
  161.1 8.6 %collective-permute-done.11 = bf16[192,768]{1,0:T(8,128)(2,1)S(1)} collective-permute-done((bf16[192,768]{1,0:T(8,128)(2,1)}, bf16[192,768]{1,0:T(8,128)(2,1)S(1)}, u32[]{:S(2)}, u32[]{:S(2)}) %collective-permute-start.11) | collective-permute-done | bytes 294944 | tf_op jit(solution)/shard_map/ppermute | solution.py:494
  169.7 0.9 copy-done.11
  171.7 2.4 %add_convert_fusion.1 = bf16[1,1,400,1024]{3,2,1,0:T(8,128)(2,1)} fusion(bf16[1,2,400,1024]{3,2,1,0:T(8,128)(2,1)} %collective-permute-done.15.from_core, bf16[1,2,400,1024]{3,2,1,0:T(8,128)(2,1)S(1)} %copy-done.2), kind=kLoop, calls=%fused_computation.2 | loop fusion | flops 1638400 | bytes 2457600 | tf_op jit(solution)/shard_map/convert_element_type | solution.py:590
  174.7 1.0 collective-permute-start.17
  175.8 1.7 collective-permute-start.23
  177.5 1.7 collective-permute-start.18
  179.8 3.1 %finish.3 = (bf16[192,3072]{1,0:T(8,128)(2,1)}, f32[192,3072]{1,0:T(8,128)}) custom-call(bf16[1,2,400,1024]{3,2,1,0:T(8,128)(2,1)} %get-tuple-element.199.keep, bf16[1,2,400,1024]{3,2,1,0:T(8,128)(2,1)} %copy-done.5, bf16[1,1,400,1024]{3,2,1,0:T(8,128)(2,1)} %copy-done.11, bf16[192,3072]{1,0:T(8,128)(2,1)} %bitcast.23, ...), custom_call_target="tpu_custom_call" | custom-call | flops 3000 | bytes 5000 | tf_op jit(solution)/shard_map/finish/pallas_call | solution.py:471
  182.9 2.1 collective-permute-done.17
  185.0 2.4 %add_convert_fusion = bf16[1,1,400,1024]{3,2,1,0:T(8,128)(2,1)} fusion(bf16[1,2,400,1024]{3,2,1,0:T(8,128)(2,1)} %collective-permute-done.16.from_core, bf16[1,2,400,1024]{3,2,1,0:T(8,128)(2,1)S(1)} %copy-done.3), kind=kLoop, calls=%fused_computation.1 | loop fusion | flops 1638400 | bytes 2457600 | tf_op jit(solution)/shard_map/convert_element_type | solution.py:590
  187.4 0.7 add.122
  188.3 2.9 %collective-permute-start.20 = (f32[1536]{0:T(1024)S(1)}, f32[1536]{0:T(1024)S(1)}, u32[]{:S(2)}, u32[]{:S(2)}) collective-permute-start(f32[1536]{0:T(1024)S(1)} %add.122), channel_id=1, source_target_pairs={{0,16},{4,20},{8,24},{12,28},{16,0},{20,4},{24,8},{28,12},{1,17},{... | collective-permute-start | bytes 18440 | tf_op jit(solution)/shard_map/ppermute | solution.py:494
  191.2 6.9 %collective-permute-done.20 = f32[1536]{0:T(1024)S(1)} collective-permute-done((f32[1536]{0:T(1024)S(1)}, f32[1536]{0:T(1024)S(1)}, u32[]{:S(2)}, u32[]{:S(2)}) %collective-permute-start.20) | collective-permute-done | bytes 6176 | tf_op jit(solution)/shard_map/ppermute | solution.py:494
  200.1 3.8 %collective-permute-done.23 = bf16[768,768]{1,0:T(8,128)(2,1)} collective-permute-done((bf16[768,768]{1,0:T(8,128)(2,1)S(1)}, bf16[768,768]{1,0:T(8,128)(2,1)}, u32[]{:S(2)}, u32[]{:S(2)}) %collective-permute-start.23) | collective-permute-done | bytes 1179680 | tf_op jit(solution)/shard_map/ppermute | solution.py:494
  204.0 3.1 %collective-permute-done.21 = bf16[192,768]{1,0:T(8,128)(2,1)S(1)} collective-permute-done((bf16[192,768]{1,0:T(8,128)(2,1)S(1)}, bf16[192,768]{1,0:T(8,128)(2,1)S(1)}, u32[]{:S(2)}, u32[]{:S(2)}) %collective-permute-start.21) | collective-permute-done | bytes 294944 | tf_op jit(solution)/shard_map/ppermute | solution.py:494
  207.3 1.8 collective-permute-start.25
  209.1 1.3 fusion.6
  210.4 3.1 %finish.4 = (bf16[192,3072]{1,0:T(8,128)(2,1)}, f32[192,3072]{1,0:T(8,128)}) custom-call(bf16[1,2,400,1024]{3,2,1,0:T(8,128)(2,1)} %get-tuple-element.219.keep, bf16[1,2,400,1024]{3,2,1,0:T(8,128)(2,1)} %collective-permute-done.15.from_core, bf16[1,1,400,1024]{3,2,1,0:T(8,128)(2,1)} %collective-permute-done.22.from_y, ...), custom_call_target="tpu_custom_call", output_to_operand_aliasing={{0}: (8, {}), {1}: (9, {})} | custom-call | flops 3000 | bytes 5000 | tf_op jit(solution)/shard_map/finish/pallas_call | solution.py:471
  213.5 3.8 %select_convert_fusion = (f32[768,768]{1,0:T(8,128)}, f32[768,768]{1,0:T(8,128)}) fusion(bf16[768,768]{1,0:T(8,128)(2,1)S(1)} %maximum_select_fusion, bf16[768,768]{1,0:T(8,128)(2,1)} %collective-permute-done.23, pred[]{:T(512)S(6)} %gt.7), kind=kLoop, calls=%fused_computation.5 | loop fusion | flops 2359296 | bytes 7077889 | tf_op jit(solution)/shard_map/convert_element_type | solution.py:778
  217.3 1.3 collective-permute-done.24.from_y
  218.6 0.9 copy-done.12
  219.5 3.1 %finish.5 = (bf16[192,3072]{1,0:T(8,128)(2,1)}, f32[192,3072]{1,0:T(8,128)}) custom-call(bf16[1,2,400,1024]{3,2,1,0:T(8,128)(2,1)} %get-tuple-element.211.keep, bf16[1,2,400,1024]{3,2,1,0:T(8,128)(2,1)} %collective-permute-done.16.from_core, bf16[1,1,400,1024]{3,2,1,0:T(8,128)(2,1)} %copy-done.12, ...), custom_call_target="tpu_custom_call", output_to_operand_aliasing={{0}: (8, {}), {1}: (9, {})} | custom-call | flops 3000 | bytes 5000 | tf_op jit(solution)/shard_map/finish/pallas_call | solution.py:471
  222.6 0.9 fusion.2
  223.8 1.4 convert_bitcast_fusion
  (98 shorter events, 7.8 us)
Async XLA Ops:
  0.6 17.3 %copy-start.6 = (bf16[768,3,192]{0,2,1:T(8,128)(2,1)S(1)}, bf16[768,3,192]{0,2,1:T(8,128)(2,1)}, u32[]{:S(2)}) copy-start(bf16[768,3,192]{0,2,1:T(8,128)(2,1)} %param.15) | copy-start | bytes 2654212
  0.7 18.6 %copy-start = (bf16[768,768]{1,0:T(8,128)(2,1)S(1)}, bf16[768,768]{1,0:T(8,128)(2,1)}, u32[]{:S(2)}) copy-start(bf16[768,768]{1,0:T(8,128)(2,1)} %up.7) | copy-start | bytes 3538948
  1.6 19.2 %copy-start.7 = (bf16[192,128]{1,0:T(8,128)(2,1)}, bf16[192,128]{1,0:T(8,128)(2,1)S(1)}, u32[]{:S(2)}) copy-start(bf16[192,128]{1,0:T(8,128)(2,1)S(1)} %broadcast_in_dim.53.gain_own.gain) | copy-start | bytes 147460
  1.6 11.9 %collective-permute-start = (bf16[192,128]{1,0:T(8,128)(2,1)S(1)}, bf16[192,128]{1,0:T(8,128)(2,1)S(1)}, u32[]{:S(2)}, u32[]{:S(2)}) collective-permute-start(bf16[192,128]{1,0:T(8,128)(2,1)S(1)} %broadcast_in_dim.53.gain_own.gain), channel_id=1, source_target_pairs={{0,2},{1,3},{2,0},{3,1},{4,6},{5,7},{6,4},{7,5},{8,10},{9,11},{10,... | collective-permute-start | bytes 147464 | tf_op jit(solution)/shard_map/ppermute | solution.py:494
  4.6 8.9 %collective-permute-start.1 = (bf16[192,128]{1,0:T(8,128)(2,1)S(1)}, bf16[192,128]{1,0:T(8,128)(2,1)S(1)}, u32[]{:S(2)}, u32[]{:S(2)}) collective-permute-start(bf16[192,128]{1,0:T(8,128)(2,1)S(1)} %broadcast_in_dim.53.gain_own.gain), channel_id=1, source_target_pairs={{0,1},{1,0},{2,3},{3,2},{4,5},{5,4},{6,7},{7,6},{8,9},{9,8},{10,11... | collective-permute-start | bytes 147464 | tf_op jit(solution)/shard_map/ppermute | solution.py:494
  4.6 29.8 %collective-permute-start.2 = (bf16[192,3072]{1,0:T(8,128)(2,1)}, bf16[192,3072]{1,0:T(8,128)(2,1)}, u32[]{:S(2)}, u32[]{:S(2)}) collective-permute-start(bf16[192,3072]{1,0:T(8,128)(2,1)} %bitcast.20), channel_id=1, source_target_pairs={{0,2},{1,3},{2,0},{3,1},{4,6},{5,7},{6,4},{7,5},{8,10},{9,11},{10,... | collective-permute-start | bytes 3538952 | tf_op jit(solution)/shard_map/ppermute | solution.py:494
  4.8 30.1 %collective-permute-start.4 = (bf16[192,3072]{1,0:T(8,128)(2,1)}, bf16[192,3072]{1,0:T(8,128)(2,1)}, u32[]{:S(2)}, u32[]{:S(2)}) collective-permute-start(bf16[192,3072]{1,0:T(8,128)(2,1)} %bitcast.21), channel_id=1, source_target_pairs={{0,1},{1,0},{2,3},{3,2},{4,5},{5,4},{6,7},{7,6},{8,9},{9,8},{10,11... | collective-permute-start | bytes 3538952 | tf_op jit(solution)/shard_map/ppermute | solution.py:494
  13.5 7.2 %copy-start.17 = (bf16[192,128]{1,0:T(8,128)(2,1)}, bf16[192,128]{1,0:T(8,128)(2,1)S(1)}, u32[]{:S(2)}) copy-start(bf16[192,128]{1,0:T(8,128)(2,1)S(1)} %collective-permute-done.gain_y) | copy-start | bytes 147460
  13.5 7.2 %copy-start.18 = (bf16[192,128]{1,0:T(8,128)(2,1)}, bf16[192,128]{1,0:T(8,128)(2,1)S(1)}, u32[]{:S(2)}) copy-start(bf16[192,128]{1,0:T(8,128)(2,1)S(1)} %collective-permute-done.1.gain_c) | copy-start | bytes 147460
  17.2 17.1 %collective-permute-start.3 = (bf16[192,128]{1,0:T(8,128)(2,1)S(1)}, bf16[192,128]{1,0:T(8,128)(2,1)S(1)}, u32[]{:S(2)}, u32[]{:S(2)}) collective-permute-start(bf16[192,128]{1,0:T(8,128)(2,1)S(1)} %collective-permute-done.gain_y), channel_id=1, source_target_pairs={{0,1},{1,0},{2,3},{3,2},{4,5},{5,4},{6,7},{7,6},{8,9},{9,8},{10,11... | collective-permute-start | bytes 147464 | tf_op jit(solution)/shard_map/ppermute | solution.py:494
  19.3 1.5 copy-start.1
  20.7 1.5 copy-start.9
  34.4 3.1 %copy-start.19 = (bf16[192,128]{1,0:T(8,128)(2,1)}, bf16[192,128]{1,0:T(8,128)(2,1)S(1)}, u32[]{:S(2)}) copy-start(bf16[192,128]{1,0:T(8,128)(2,1)S(1)} %collective-permute-done.3.gain_cy) | copy-start | bytes 147460
  34.4 3.1 %collective-permute-start.5 = (bf16[192,3072]{1,0:T(8,128)(2,1)}, bf16[192,3072]{1,0:T(8,128)(2,1)S(1)}, u32[]{:S(2)}, u32[]{:S(2)}) collective-permute-start(bf16[192,3072]{1,0:T(8,128)(2,1)} %collective-permute-done.2.flip_y), channel_id=1, source_target_pairs={{0,1},{1,0},{2,3},{3,2},{4,5},{5,4},{6,7},{7,6},{8,9},{9,8},{10,11... | collective-permute-start | bytes 3538952 | tf_op jit(solution)/shard_map/ppermute | solution.py:494
  37.5 1.0 copy-start.8
  62.7 60.4 %all-to-all-start = ((bf16[8,192,768]{2,1,0:T(8,128)(2,1)}), bf16[8,192,768]{2,1,0:T(8,128)(2,1)S(1)}, u32[]{:S(2)}, u32[]{:S(2)}) async-start(bf16[8,192,768]{2,1,0:T(8,128)(2,1)} %bitcast.41), calls=%async_computation | async-start | bytes 4718592 | tf_op jit(solution)/shard_map/all_to_all | solution.py:523
  68.9 39.1 %copy-start.14 = (f32[768,128]{1,0:T(8,128)S(1)}, f32[768,128]{1,0:T(8,128)}, u32[]{:S(2)}) copy-start(f32[768,128]{1,0:T(8,128)} %get-tuple-element.170) | copy-start | bytes 1179652
  110.2 9.8 %collective-permute-start.6 = (f32[2,192]{1,0:T(2,128)S(1)}, f32[2,192]{1,0:T(2,128)S(1)}, u32[]{:S(2)}, u32[]{:S(2)}) collective-permute-start(f32[2,192]{1,0:T(2,128)S(1)} %pad_maximum_fusion.2), channel_id=1, source_target_pairs={{0,1},{1,0},{2,3},{3,2},{4,5},{5,4},{6,7},{7,6},{8,9},{9,8},{10,11... | collective-permute-start | bytes 4616 | tf_op jit(solution)/shard_map/ppermute | solution.py:494
  120.0 8.0 %copy-start.16 = (f32[192,128]{1,0:T(8,128)S(1)}, f32[192,128]{1,0:T(8,128)}, u32[]{:S(2)}) copy-start(f32[192,128]{1,0:T(8,128)} %get-tuple-element.198) | copy-start | bytes 294916
  120.0 8.1 %copy-start.15 = (f32[384,128]{1,0:T(8,128)S(1)}, f32[384,128]{1,0:T(8,128)}, u32[]{:S(2)}) copy-start(f32[384,128]{1,0:T(8,128)} %get-tuple-element.196) | copy-start | bytes 589828
  120.0 8.2 %copy-start.13 = (f32[768,128]{1,0:T(8,128)S(1)}, f32[768,128]{1,0:T(8,128)}, u32[]{:S(2)}) copy-start(f32[768,128]{1,0:T(8,128)} %get-tuple-element.197) | copy-start | bytes 1179652
  124.3 17.4 %collective-permute-start.10 = (bf16[1,2,400,1024]{3,2,1,0:T(8,128)(2,1)}, bf16[1,2,400,1024]{3,2,1,0:T(8,128)(2,1)S(1)}, u32[]{:S(2)}, u32[]{:S(2)}) collective-permute-start(bf16[1,2,400,1024]{3,2,1,0:T(8,128)(2,1)} %get-tuple-element.192), channel_id=1, source_target_pairs={{0,1},{1,0},{2,3},{3,2},{4,5},{5,4},{6,7},{7,6},{8,9},{9,8},{10,11... | collective-permute-start | bytes 4915208 | tf_op jit(solution)/shard_map/ppermute | solution.py:494
  124.3 16.1 %collective-permute-start.7 = (bf16[384,768]{1,0:T(8,128)(2,1)}, bf16[384,768]{1,0:T(8,128)(2,1)}, u32[]{:S(2)}, u32[]{:S(2)}) collective-permute-start(bf16[384,768]{1,0:T(8,128)(2,1)} %constant_dynamic-slice_fusion.4), channel_id=1, source_target_pairs={{0,4},{4,0},{8,12},{12,8},{16,20},{20,16},{24,28},{28,24},{1,5},{5... | collective-permute-start | bytes 1769480 | tf_op jit(solution)/shard_map/ppermute | solution.py:494
  125.7 15.9 %collective-permute-start.8 = (bf16[192,768]{1,0:T(8,128)(2,1)}, bf16[192,768]{1,0:T(8,128)(2,1)}, u32[]{:S(2)}, u32[]{:S(2)}) collective-permute-start(bf16[192,768]{1,0:T(8,128)(2,1)} %reduce_sum.75), channel_id=1, source_target_pairs={{0,16},{4,20},{8,24},{12,28},{16,0},{20,4},{24,8},{28,12},{1,17},{... | collective-permute-start | bytes 884744 | tf_op jit(solution)/shard_map/ppermute | solution.py:494
  126.5 13.9 %collective-permute-start.9 = (f32[192]{0:T(256)S(1)}, f32[192]{0:T(256)S(1)}, u32[]{:S(2)}, u32[]{:S(2)}) collective-permute-start(f32[192]{0:T(256)S(1)} %bitcast.43), channel_id=1, source_target_pairs={{0,2},{1,3},{2,0},{3,1},{4,6},{5,7},{6,4},{7,5},{8,10},{9,11},{10,... | collective-permute-start | bytes 2312 | tf_op jit(solution)/shard_map/ppermute | solution.py:494
  128.4 13.2 %copy-start.4 = (bf16[1,2,400,1024]{3,2,1,0:T(8,128)(2,1)S(1)}, bf16[1,2,400,1024]{3,2,1,0:T(8,128)(2,1)}, u32[]{:S(2)}) copy-start(bf16[1,2,400,1024]{3,2,1,0:T(8,128)(2,1)} %get-tuple-element.199.keep) | copy-start | bytes 4915204
  141.6 2.6 %copy-start.5 = (bf16[1,2,400,1024]{3,2,1,0:T(8,128)(2,1)}, bf16[1,2,400,1024]{3,2,1,0:T(8,128)(2,1)S(1)}, u32[]{:S(2)}) copy-start(bf16[1,2,400,1024]{3,2,1,0:T(8,128)(2,1)S(1)} %collective-permute-done.10.from_core) | copy-start | bytes 4915204
  141.6 2.6 %copy-start.10 = (bf16[768,768]{1,0:T(8,128)(2,1)S(1)}, bf16[768,768]{1,0:T(8,128)(2,1)}, u32[]{:S(2)}) copy-start(bf16[768,768]{1,0:T(8,128)(2,1)} %get-tuple-element.168) | copy-start | bytes 3538948
  146.4 23.3 %collective-permute-start.15 = (bf16[1,2,400,1024]{3,2,1,0:T(8,128)(2,1)}, bf16[1,2,400,1024]{3,2,1,0:T(8,128)(2,1)}, u32[]{:S(2)}, u32[]{:S(2)}) collective-permute-start(bf16[1,2,400,1024]{3,2,1,0:T(8,128)(2,1)} %get-tuple-element.210), channel_id=1, source_target_pairs={{0,1},{1,0},{2,3},{3,2},{4,5},{5,4},{6,7},{7,6},{8,9},{9,8},{10,11... | collective-permute-start | bytes 4915208 | tf_op jit(solution)/shard_map/ppermute | solution.py:494
  146.4 23.3 %collective-permute-start.14 = (bf16[1,1,400,1024]{3,2,1,0:T(8,128)(2,1)}, bf16[1,1,400,1024]{3,2,1,0:T(8,128)(2,1)S(1)}, u32[]{:S(2)}, u32[]{:S(2)}) collective-permute-start(bf16[1,1,400,1024]{3,2,1,0:T(8,128)(2,1)} %add_convert_fusion.2), channel_id=1, source_target_pairs={{0,2},{1,3},{2,0},{3,1},{4,6},{5,7},{6,4},{7,5},{8,10},{9,11},{10,... | collective-permute-start | bytes 2457608 | tf_op jit(solution)/shard_map/ppermute | solution.py:494
  148.0 21.7 %collective-permute-start.12 = (bf16[384,768]{1,0:T(8,128)(2,1)S(1)}, bf16[384,768]{1,0:T(8,128)(2,1)S(1)}, u32[]{:S(2)}, u32[]{:S(2)}) collective-permute-start(bf16[384,768]{1,0:T(8,128)(2,1)S(1)} %maximum_select_fusion.1), channel_id=1, source_target_pairs={{0,8},{4,12},{8,0},{12,4},{16,24},{20,28},{24,16},{28,20},{1,9},{5... | collective-permute-start | bytes 1769480 | tf_op jit(solution)/shard_map/ppermute | solution.py:494
  148.0 21.7 %collective-permute-start.11 = (bf16[192,768]{1,0:T(8,128)(2,1)}, bf16[192,768]{1,0:T(8,128)(2,1)S(1)}, u32[]{:S(2)}, u32[]{:S(2)}) collective-permute-start(bf16[192,768]{1,0:T(8,128)(2,1)} %get-tuple-element.206), channel_id=1, source_target_pairs={{0,8},{4,12},{8,0},{12,4},{16,24},{20,28},{24,16},{28,20},{1,9},{5... | collective-permute-start | bytes 884744 | tf_op jit(solution)/shard_map/ppermute | solution.py:494
  150.0 11.1 %collective-permute-start.13 = (f32[1536]{0:T(1024)S(1)}, f32[1536]{0:T(1024)S(1)}, u32[]{:S(2)}, u32[]{:S(2)}) collective-permute-start(f32[1536]{0:T(1024)S(1)} %concatenate.35), channel_id=1, source_target_pairs={{0,4},{4,0},{8,12},{12,8},{16,20},{20,16},{24,28},{28,24},{1,5},{5... | collective-permute-start | bytes 18440 | tf_op jit(solution)/shard_map/ppermute | solution.py:494
  161.1 10.6 %copy-start.2 = (bf16[1,2,400,1024]{3,2,1,0:T(8,128)(2,1)S(1)}, bf16[1,2,400,1024]{3,2,1,0:T(8,128)(2,1)}, u32[]{:S(2)}) copy-start(bf16[1,2,400,1024]{3,2,1,0:T(8,128)(2,1)} %get-tuple-element.219.keep) | copy-start | bytes 4915204
  169.7 0.9 copy-start.11
  174.7 10.3 %collective-permute-start.16 = (bf16[1,2,400,1024]{3,2,1,0:T(8,128)(2,1)}, bf16[1,2,400,1024]{3,2,1,0:T(8,128)(2,1)}, u32[]{:S(2)}, u32[]{:S(2)}) collective-permute-start(bf16[1,2,400,1024]{3,2,1,0:T(8,128)(2,1)} %get-tuple-element.224), channel_id=1, source_target_pairs={{0,1},{1,0},{2,3},{3,2},{4,5},{5,4},{6,7},{7,6},{8,9},{9,8},{10,11... | collective-permute-start | bytes 4915208 | tf_op jit(solution)/shard_map/ppermute | solution.py:494
  174.7 10.2 %collective-permute-start.17 = (bf16[96,768]{1,0:T(8,128)(2,1)}, bf16[96,768]{1,0:T(8,128)(2,1)S(1)}, u32[]{:S(2)}, u32[]{:S(2)}) collective-permute-start(bf16[96,768]{1,0:T(8,128)(2,1)} %add_convert_fusion.7), channel_id=1, source_target_pairs={{0,16},{4,20},{8,24},{12,28},{16,0},{20,4},{24,8},{28,12},{1,17},{... | collective-permute-start | bytes 442376 | tf_op jit(solution)/shard_map/ppermute | solution.py:494
  175.8 28.2 %collective-permute-start.23 = (bf16[768,768]{1,0:T(8,128)(2,1)S(1)}, bf16[768,768]{1,0:T(8,128)(2,1)}, u32[]{:S(2)}, u32[]{:S(2)}) collective-permute-start(bf16[768,768]{1,0:T(8,128)(2,1)S(1)} %maximum_select_fusion), channel_id=1, source_target_pairs={{0,4},{4,0},{8,12},{12,8},{16,20},{20,16},{24,28},{28,24},{1,5},{5... | collective-permute-start | bytes 3538952 | tf_op jit(solution)/shard_map/ppermute | solution.py:494
  177.5 5.4 %collective-permute-start.18 = (f32[1536]{0:T(1024)}, f32[1536]{0:T(1024)}, u32[]{:S(2)}, u32[]{:S(2)}) collective-permute-start(f32[1536]{0:T(1024)} %add.118), channel_id=1, source_target_pairs={{0,8},{4,12},{8,0},{12,4},{16,24},{20,28},{24,16},{28,20},{1,9},{5... | collective-permute-start | bytes 18440 | tf_op jit(solution)/shard_map/ppermute | solution.py:494
  179.2 20.9 %collective-permute-start.22 = (bf16[1,1,400,1024]{3,2,1,0:T(8,128)(2,1)}, bf16[1,1,400,1024]{3,2,1,0:T(8,128)(2,1)}, u32[]{:S(2)}, u32[]{:S(2)}) collective-permute-start(bf16[1,1,400,1024]{3,2,1,0:T(8,128)(2,1)} %add_convert_fusion.1), channel_id=1, source_target_pairs={{0,2},{1,3},{2,0},{3,1},{4,6},{5,7},{6,4},{7,5},{8,10},{9,11},{10,... | collective-permute-start | bytes 2457608 | tf_op jit(solution)/shard_map/ppermute | solution.py:494
  179.7 5.2 %copy-start.3 = (bf16[1,2,400,1024]{3,2,1,0:T(8,128)(2,1)S(1)}, bf16[1,2,400,1024]{3,2,1,0:T(8,128)(2,1)}, u32[]{:S(2)}) copy-start(bf16[1,2,400,1024]{3,2,1,0:T(8,128)(2,1)} %get-tuple-element.211.keep) | copy-start | bytes 4915204
  188.2 9.9 %collective-permute-start.19 = (bf16[96,768]{1,0:T(8,128)(2,1)S(1)}, bf16[96,768]{1,0:T(8,128)(2,1)S(1)}, u32[]{:S(2)}, u32[]{:S(2)}) collective-permute-start(bf16[96,768]{1,0:T(8,128)(2,1)S(1)} %add_convert_fusion.5), channel_id=1, source_target_pairs={{0,16},{4,20},{8,24},{12,28},{16,0},{20,4},{24,8},{28,12},{1,17},{... | collective-permute-start | bytes 442376 | tf_op jit(solution)/shard_map/ppermute | solution.py:494
  188.3 9.8 %collective-permute-start.20 = (f32[1536]{0:T(1024)S(1)}, f32[1536]{0:T(1024)S(1)}, u32[]{:S(2)}, u32[]{:S(2)}) collective-permute-start(f32[1536]{0:T(1024)S(1)} %add.122), channel_id=1, source_target_pairs={{0,16},{4,20},{8,24},{12,28},{16,0},{20,4},{24,8},{28,12},{1,17},{... | collective-permute-start | bytes 18440 | tf_op jit(solution)/shard_map/ppermute | solution.py:494
  198.1 9.0 %collective-permute-start.21 = (bf16[192,768]{1,0:T(8,128)(2,1)S(1)}, bf16[192,768]{1,0:T(8,128)(2,1)S(1)}, u32[]{:S(2)}, u32[]{:S(2)}) collective-permute-start(bf16[192,768]{1,0:T(8,128)(2,1)S(1)} %maximum_select_fusion.3), channel_id=1, source_target_pairs={{0,8},{4,12},{8,0},{12,4},{16,24},{20,28},{24,16},{28,20},{1,9},{5... | collective-permute-start | bytes 884744 | tf_op jit(solution)/shard_map/ppermute | solution.py:494
  198.2 20.4 %collective-permute-start.24 = (bf16[1,1,400,1024]{3,2,1,0:T(8,128)(2,1)}, bf16[1,1,400,1024]{3,2,1,0:T(8,128)(2,1)S(1)}, u32[]{:S(2)}, u32[]{:S(2)}) collective-permute-start(bf16[1,1,400,1024]{3,2,1,0:T(8,128)(2,1)} %add_convert_fusion), channel_id=1, source_target_pairs={{0,2},{1,3},{2,0},{3,1},{4,6},{5,7},{6,4},{7,5},{8,10},{9,11},{10,... | collective-permute-start | bytes 2457608 | tf_op jit(solution)/shard_map/ppermute | solution.py:494
  207.3 15.4 %collective-permute-start.25 = (bf16[384,768]{1,0:T(8,128)(2,1)S(1)}, bf16[384,768]{1,0:T(8,128)(2,1)S(1)}, u32[]{:S(2)}, u32[]{:S(2)}) collective-permute-start(bf16[384,768]{1,0:T(8,128)(2,1)S(1)} %maximum_select_fusion.2), channel_id=1, source_target_pairs={{0,4},{4,0},{8,12},{12,8},{16,20},{20,16},{24,28},{28,24},{1,5},{5... | collective-permute-start | bytes 1769480 | tf_op jit(solution)/shard_map/ppermute | solution.py:494
  218.6 0.9 copy-start.12

commit v9 on v8

--- a/solution.py
+++ b/solution.py
@@ -20,6 +20,7 @@
 
 NN = (((1,), (0,)), ((), ()))
 NT = (((1,), (1,)), ((), ()))
+TN = (((0,), (0,)), ((), ()))
 ANY = pl.BlockSpec(memory_space=pl.ANY)
 
 
@@ -86,7 +87,7 @@
 
 
 def mlp_kernel(
-    pieces_order, place, own, flip_y, flip_c, flip_cy, gain_own, gain_y, gain_c, gain_cy, up_t, up_bias, d_act, cot, up,
+    pieces_order, place, own, flip_y, flip_c, flip_cy, gain_own, gain_y, gain_c, gain_cy, up, up_bias, d_act, cot,
     normed, active, d_pre, stats, bias_sum, gain_all, up_row, grads, low, high
 ):
     pieces = (own, flip_y, flip_c, flip_cy)
@@ -123,13 +124,13 @@
     c1 = 0.044715 * c0
     def lift(start):
         here = slice(start, start + 256)
-        return dot(up_t[here, :], normed[...]) + up_bias[here, :1].astype(F32)
+        return dot(up[:, here], normed[...], TN) + up_bias[here, :1].astype(F32)
 
     ahead = lift(0)
-    for start in range(0, up_t.shape[0], 256):
+    for start in range(0, up.shape[1], 256):
         here = slice(start, start + 256)
         pre = ahead
-        if start + 256 < up_t.shape[0]:
+        if start + 256 < up.shape[1]:
             ahead = lift(start + 256)
         square = pre * pre
         half = 0.5 * jnp.tanh(pre * (c0 + c1 * square)) + 0.5
@@ -152,7 +153,7 @@
             grads[slot * size : (slot + 1) * size, :] = source[start : start + size, :].astype(BF16)
 
 
-def mlp_call(pieces_order, place, pieces, gains, up_t, up_bias, d_act, cot, up, block=512):
+def mlp_call(pieces_order, place, pieces, gains, up, up_bias, d_act, cot, block=512):
     part, tokens = pieces[0].shape
     width = 4 * part
     seqs, hidden, _ = d_act.shape
@@ -166,11 +167,10 @@
         in_specs=[pl.BlockSpec((part, block), lanes)] * 4
         + [pl.BlockSpec((part, 128), fixed)] * 4
         + [
-            pl.BlockSpec((hidden, width), fixed),
+            pl.BlockSpec((width, hidden), fixed),
             pl.BlockSpec((hidden, 128), fixed),
             pl.BlockSpec((None, hidden, block), by_seq),
             pl.BlockSpec((block, width), lambda i, *_: (i, 0)),
-            pl.BlockSpec((width, hidden), fixed),
         ],
         out_specs=[
             pl.BlockSpec((None, width, block), by_seq),
@@ -200,7 +200,7 @@
         ],
         cost_estimate=cost(20, 30_000_000),
         name="mlp",
-    )(place, *pieces, *gains, up_t, up_bias, d_act, cot, up)
+    )(place, *pieces, *gains, up, up_bias, d_act, cot)
 
 
 def attention_kernel(
@@ -373,12 +373,12 @@
 
 
 def project_kernel(
-    shard, active, attended, d_pre, d_mixed, normed, down_t, attn_t, up, mixed, gain, keep, send
+    shard, active, attended, d_pre, d_mixed, normed, down, attn, up, mixed_t, gain, keep, send
 ):
     me = shard[0]
     part = attended.shape[0]
-    out = dot(down_t[...], active[...]) + dot(attn_t[...], attended[...])
-    grad = dot(up[...], d_pre[...]) + dot(mixed[...], d_mixed[...])
+    out = dot(down[...], active[...], TN) + dot(attn[...], attended[...], TN)
+    grad = dot(up[...], d_pre[...]) + dot(mixed_t[...], d_mixed[...], TN)
     product = grad * normed[...].astype(F32)
     sums = []
     for row in (jnp.sum(grad * gain[:, :1], axis=0, keepdims=True), jnp.sum(product, axis=0, keepdims=True)):
@@ -404,8 +404,8 @@
             send[slot, part : 2 * part, :] = grad[rows].astype(BF16)
 
 
-def project_call(shard, active, attended, d_pre, d_mixed, normed, down_t, attn_t, up, mixed, gain, begin, size, block=256):
-    width, hidden = down_t.shape
+def project_call(shard, active, attended, d_pre, d_mixed, normed, down, attn, up, mixed_t, gain, begin, size, block=256):
+    hidden, width = down.shape
     part = attended.shape[1]
     steps = LEN // block
     ours = lambda i, *_: (begin + i // steps, 0, i % steps)
@@ -421,10 +421,10 @@
             pl.BlockSpec((None, hidden, block), ours),
             pl.BlockSpec((None, 3 * part, block), ours),
             pl.BlockSpec((None, width, block), ours),
+            pl.BlockSpec((hidden, width), fixed),
+            pl.BlockSpec((part, width), fixed),
             pl.BlockSpec((width, hidden), fixed),
-            pl.BlockSpec((width, part), fixed),
-            pl.BlockSpec((width, hidden), fixed),
-            pl.BlockSpec((width, 3 * part), fixed),
+            pl.BlockSpec((3 * part, width), fixed),
             pl.BlockSpec((width, 128), fixed),
         ],
         out_specs=[
@@ -441,7 +441,7 @@
         ],
         cost_estimate=cost(8, 16_000_000),
         name="project",
-    )(shard, active, attended, d_pre, d_mixed, normed, down_t, attn_t, up, mixed, gain)
+    )(shard, active, attended, d_pre, d_mixed, normed, down, attn, up, mixed_t, gain)
 
 
 def finish_kernel(keep, from_core, from_y, own_t, cot, stats, gain, bias, *rest):
@@ -592,6 +592,15 @@
             self.from_y = arrived
 
 
+def land_then(flights, final, outputs):
+    outputs = land(flights, outputs)
+    movers = [f[0] for f in flights]
+    outputs, sends = land(final, (outputs, [m.send for m in movers]))
+    for mover, send in zip(movers, sends):
+        mover.send = send
+    return outputs
+
+
 class ShortSums:
     def __init__(self, keep, send, rest, size):
         self.keep, self.send, self.rest, self.size = keep, send, rest, size
@@ -660,10 +669,6 @@
     gain_c = flip(gain_own, "mp", 4, 1)
 
     mixed_t = jnp.transpose(qkv_weight, (1, 2, 0)).reshape(3 * part, width)
-    mixed = mixed_t.T
-    up_t = up_weight.T
-    down_t = down_weight.T
-    attn_t = attn_weight.T
     def column(vector):
         return jnp.broadcast_to(vector[:, None], (vector.shape[0], 128))
 
@@ -687,18 +692,18 @@
     gain_cy = flip(gain_y, "mp", 4, 1)
     d_act, d_att, cot_own, cot_sum = early_call(cotangent, down_weight, attn_weight, pick)
     prepared = (
-        d_act, d_att, mixed_t, mixed, up_t, down_t, attn_t, up_bias_col, head_gains, mask_q, mask_k, first, count,
+        d_act, d_att, mixed_t, up_bias_col, head_gains, mask_q, mask_k, first, count,
         bias_col,
     )
     prepared, (from_y, gain_cy) = tie(prepared, (from_y, gain_cy))
     gains = (gain_own, gain_y, gain_c, gain_cy)
     (
-        d_act, d_att, mixed_t, mixed, up_t, down_t, attn_t, up_bias_col, head_gains, mask_q, mask_k, first, count,
+        d_act, d_att, mixed_t, up_bias_col, head_gains, mask_q, mask_k, first, count,
         bias_col,
     ) = prepared
     pieces = (own_t, from_y, flip(own_t, "mp", 4, 1), flip(from_y, "mp", 4, 1))
     normed, active, d_pre, stats, upbias_part, gain_all, up_row, mlp_part = mlp_call(
-        tuple(piece_order(dp_size)), place, pieces, gains, up_t, up_bias_col, d_act, cotangent, up_weight
+        tuple(piece_order(dp_size)), place, pieces, gains, up_weight, up_bias_col, d_act, cotangent
     )
     mlp_sum = SumOverDp(mlp_part, dp_size, dp)
 
@@ -726,10 +731,11 @@
         (att, dm), flights = launch(along, (attended, d_mixed))
         flying = flying + flights
         sent = project_call(
-            shard, active, att, d_pre, dm, normed, down_t, attn_t, up_weight, mixed, gain_all, begin, size
+            shard, active, att, d_pre, dm, normed, down_weight, attn_weight, up_weight, mixed_t, gain_all, begin, size
         )
         late = [f for f in flights if begin == 0 and f[0] is mix_sum]
-        keep, send = land([f for f in flying if f not in late], sent)
+        final = [f for f in flying if f[0] is mix_sum and f not in late]
+        keep, send = land_then([f for f in flying if f not in late + final], final, sent)
         flying = late
         scatters.append(ScatterOverMp(keep, send))
 
@@ -769,7 +775,8 @@
             now = across + wide + rest or chain
         else:
             now = chain + rest or flying
-        finished, wide_grads = land(now, (finished, wide_grads))
+        final = [f for f in now if f[0] is mix_sum]
+        finished, wide_grads = land_then([f for f in now if f not in final], final, (finished, wide_grads))
         flying = [f for f in flying if f not in now]
         if not mlp_sum.more() and not wide_grads:
             swap, held, arrived = mlp_sum.last

time: 226 us -> 221 us (0.978)
  local copies, waits for them, and re-layouts: 18.8 us -> 13.4 us
  other arithmetic: 28.5 us -> 33.3 us
  waiting for transfers between devices: 34.9 us -> 31 us
    unnamed x43 -> x32, local copies, waits for them, and re-layouts: 6.8 us -> 2.86 us
    ppermute x26, waiting for transfers between devices: 31.8 us -> 28.6 us  [flip(): return lax.ppermute(value, axis, [(i, i ^ bit) for i in range(size)])]
    select_n x5, other arithmetic: 2.36 us -> 5.12 us  [joined(): jnp.where(swap, jnp.concatenate([arrived, held], axis=0), jnp.concatenate...]
  transfers between devices with their start and end apart: 27 -> 27, of which waited for: 10 -> 10; matrix products, arithmetic and copies ran while one was open for 14% -> 17% of each run, Pallas kernels for 39% -> 41%
where the time goes in v9:
time: 221 us; the launch traced here: 220 us
  Pallas kernels  113 us (51%)
  other arithmetic  33.3 us (15%)
  waiting for transfers between devices  31 us (14%)
  starting transfers between devices  28 us (13%)
  local copies, waits for them, and re-layouts  13.4 us (6%)
    pallas_call x1, Pallas kernels, attention_call(): pl.pallas_call(attention_kernel, grid_spec=grid_spec, out_shape=[jax.Shap...  38.7 us
    pallas_call x3, Pallas kernels, project_call(): pl.pallas_call(project_kernel, grid_spec=grid_spec, out_shape=[jax.ShapeD...  29.8 us
    ppermute x26, waiting for transfers between devices, flip(): return lax.ppermute(value, axis, [(i, i ^ bit) for i in range(size)])  28.6 us
    pallas_call x1, Pallas kernels, mlp_call(): pl.pallas_call(functools.partial(mlp_kernel, pieces_order), grid_spec=gri...  23.9 us
    ppermute x26, starting transfers between devices, flip(): return lax.ppermute(value, axis, [(i, i ^ bit) for i in range(size)])  22.1 us
    pallas_call x1, Pallas kernels, early_call(): pl.pallas_call(early_kernel, grid=(tokens // block,), in_specs=[pl.BlockS...  11.2 us
    pallas_call x3, Pallas kernels, finish_call(): pl.pallas_call(finish_kernel, grid=(size * steps,), in_specs=[packed, pac...  9.42 us
    convert_element_type x3, other arithmetic, take(): (self.keep[:, 1:].astype(F32) + arrived[:, 1:].astype(F32)).astype(BF16)  5.9 us
  transfers between devices with their start and end apart: 27, of which 10 were waited for; matrix products, arithmetic and copies ran while one was open for 17% of the time, Pallas kernels for 41%

profile of v9, /device:TPU:0, one launch (start us, length us, event | category | flops | bytes accessed | tf_op | source)
XLA Modules:
  0.0 219.8 jit_solution(3614236834019173046)
XLA Ops:
  0.6 0.7 broadcast_in_dim.53.gain_own.gain
  1.4 3.0 %collective-permute-start = (bf16[192,128]{1,0:T(8,128)(2,1)S(1)}, bf16[192,128]{1,0:T(8,128)(2,1)S(1)}, u32[]{:S(2)}, u32[]{:S(2)}) collective-permute-start(bf16[192,128]{1,0:T(8,128)(2,1)S(1)} %broadcast_in_dim.53.gain_own.gain), channel_id=1, source_target_pairs={{0,2},{1,3},{2,0},{3,1},{4,6},{5,7},{6,4},{7,5},{8,10},{9,11},{10,... | collective-permute-start | bytes 147464 | tf_op jit(solution)/shard_map/ppermute | solution.py:494
  4.9 0.8 slice.65
  5.8 0.8 slice.66
  6.6 1.0 convert_reduce_fusion
  7.6 1.4 fusion.4.mask_q
  8.9 1.4 select_convert_fusion.2.mask_k
  10.4 0.8 fusion.1.pick
  11.2 1.2 xor_multiply_fusion.place
  12.4 0.8 reshape.72
  13.3 0.8 broadcast_in_dim.27.gains
  14.1 1.5 broadcast_in_dim.24.up_bias
  15.7 1.4 broadcast_in_dim.52.bias
  17.8 11.2 %early.1 = (bf16[3,768,1024]{2,1,0:T(8,128)(2,1)}, bf16[3,192,1024]{2,1,0:T(8,128)(2,1)}, bf16[192,3072]{1,0:T(8,128)(2,1)}, f32[192,128]{1,0:T(8,128)}) custom-call(bf16[3072,768]{1,0:T(8,128)(2,1)} %cot.5, bf16[768,768]{1,0:T(8,128)(2,1)} %down.7, bf16[192,768]{1,0:T(8,128)(2,1)} %attn.7, bf16[192,768]{1,0:T(8,128)(2,1)} %fusion.1.pick), custom_call_target="tpu_custom_call" | custom-call | flops 10000 | bytes 12000 | tf_op jit(solution)/shard_map/early/pallas_call | solution.py:63
  29.0 4.0 %collective-permute-done.2.flip_y = bf16[192,3072]{1,0:T(8,128)(2,1)S(1)} collective-permute-done((bf16[192,3072]{1,0:T(8,128)(2,1)}, bf16[192,3072]{1,0:T(8,128)(2,1)S(1)}, u32[]{:S(2)}, u32[]{:S(2)}) %collective-permute-start.2) | collective-permute-done | bytes 1179680 | tf_op jit(solution)/shard_map/ppermute | solution.py:494
  33.1 2.8 %collective-permute-done.5.flip_cy = bf16[192,3072]{1,0:T(8,128)(2,1)S(1)} collective-permute-done((bf16[192,3072]{1,0:T(8,128)(2,1)S(1)}, bf16[192,3072]{1,0:T(8,128)(2,1)S(1)}, u32[]{:S(2)}, u32[]{:S(2)}) %collective-permute-start.5) | collective-permute-done | bytes 1179680 | tf_op jit(solution)/shard_map/ppermute | solution.py:494
  35.9 1.0 copy-done.7
  36.9 23.9 %mlp.1 = (bf16[3,768,1024]{2,1,0:T(8,128)(2,1)}, bf16[3,768,1024]{2,1,0:T(8,128)(2,1)}, bf16[3,768,1024]{2,1,0:T(8,128)(2,1)}, f32[8,3072]{1,0:T(8,128)}, f32[76...) custom-call(s32[4]{0:T(128)} %xor_multiply_fusion.place, ...), custom_call_target="tpu_custom_call" | custom-call | flops 20000 | bytes 30000 | tf_op jit(solution)/shard_map/mlp/pallas_call | solution.py:188
  60.8 5.8 %all-to-all-start = ((bf16[8,192,768]{2,1,0:T(8,128)(2,1)}), bf16[8,192,768]{2,1,0:T(8,128)(2,1)S(1)}, u32[]{:S(2)}, u32[]{:S(2)}) async-start(bf16[8,192,768]{2,1,0:T(8,128)(2,1)} %bitcast.29), calls=%async_computation | async-start | bytes 4718592 | tf_op jit(solution)/shard_map/all_to_all | solution.py:523
  66.6 38.7 %attention.1 = (bf16[3,192,1024]{2,1,0:T(8,128)(2,1)}, bf16[3,576,1024]{2,1,0:T(8,128)(2,1)}, f32[384,128]{1,0:T(8,128)}, f32[1,768]{1,0:T(1,128)}, bf16[768,768]{1,0:T(8,128)(2,1)}) custom-call(s32[12]{0:T(128)} %get-tuple-element.181.first, s32[12]{0:T(128)} %get-tuple-element.182.count, bf16[3,768,1024]{2,1,0:T(8,128)(2,1)} %get-tuple-element.185.normed, ...), custom_call_target="tpu_custom_call" | custom-call | flops 18000 | bytes 5000 | tf_op jit(solution)/shard_map/attention/pallas_call | solution.py:360
  105.4 0.7 reduce.1
  106.4 1.9 constant_dynamic-slice_fusion.4
  108.4 9.9 %project.3 = (bf16[1,2,400,1024]{3,2,1,0:T(8,128)(2,1)}, bf16[1,2,400,1024]{3,2,1,0:T(8,128)(2,1)}) custom-call(s32[1]{0:T(128)} %bitcast.shard, bf16[3,768,1024]{2,1,0:T(8,128)(2,1)} %get-tuple-element.180.active, bf16[3,192,1024]{2,1,0:T(8,128)(2,1)} %get-tuple-element.233.attended, bf16[3,768,1024]{2,1,0:T(8,128)(2,1)} %get-tuple-element.197.d_pre, ...), custom_call_target="tpu_custom_call" | custom-call | flops 8000 | bytes 16000 | tf_op jit(solution)/shard_map/project/pallas_call | solution.py:435
  118.3 2.5 %all-to-all-done = bf16[8,192,768]{2,1,0:T(8,128)(2,1)S(1)} async-done(((bf16[8,192,768]{2,1,0:T(8,128)(2,1)}), bf16[8,192,768]{2,1,0:T(8,128)(2,1)S(1)}, u32[]{:S(2)}, u32[]{:S(2)}) %all-to-all-start) | async-done | bytes 2359328 | tf_op jit(solution)/shard_map/all_to_all | solution.py:523
  120.8 1.1 reduce_sum.75
  122.3 3.9 %collective-permute-start.10 = (bf16[384,768]{1,0:T(8,128)(2,1)}, bf16[384,768]{1,0:T(8,128)(2,1)}, u32[]{:S(2)}, u32[]{:S(2)}) collective-permute-start(bf16[384,768]{1,0:T(8,128)(2,1)} %constant_dynamic-slice_fusion.4), channel_id=1, source_target_pairs={{0,4},{4,0},{8,12},{12,8},{16,20},{20,16},{24,28},{28,24},{1,5},{5... | collective-permute-start | bytes 1769480 | tf_op jit(solution)/shard_map/ppermute | solution.py:494
  126.2 0.8 collective-permute-start.8
  127.0 1.0 reduce_sum.78
  128.1 1.2 reduce_sum.77
  129.3 10.0 %project.4 = (bf16[1,2,400,1024]{3,2,1,0:T(8,128)(2,1)}, bf16[1,2,400,1024]{3,2,1,0:T(8,128)(2,1)}) custom-call(s32[1]{0:T(128)} %bitcast.shard, bf16[3,768,1024]{2,1,0:T(8,128)(2,1)} %get-tuple-element.180.active, bf16[3,192,1024]{2,1,0:T(8,128)(2,1)} %get-tuple-element.233.attended, bf16[3,768,1024]{2,1,0:T(8,128)(2,1)} %get-tuple-element.197.d_pre, ...), custom_call_target="tpu_custom_call" | custom-call | flops 8000 | bytes 16000 | tf_op jit(solution)/shard_map/project/pallas_call | solution.py:435
  139.5 2.7 %maximum_select_fusion.1 = bf16[384,768]{1,0:T(8,128)(2,1)} fusion(bf16[192,768]{1,0:T(8,128)(2,1)} %reduce_sum.75, bf16[192,768]{1,0:T(8,128)(2,1)} %collective-permute-done.7, pred[]{:T(512)S(6)} %gt.8), kind=kLoop, calls=%fused_computation.10 | loop fusion | flops 2654208 | bytes 1179649 | tf_op jit(solution)/shard_map/jit(_where)/select_n | solution.py:502
  142.2 1.2 add_convert_fusion.2
  143.4 2.0 add_convert_fusion.3
  145.4 1.3 collective-permute-start.13
  147.3 1.9 collective-permute-start.15
  149.2 9.9 %project.5 = (bf16[1,2,400,1024]{3,2,1,0:T(8,128)(2,1)}, bf16[1,2,400,1024]{3,2,1,0:T(8,128)(2,1)}) custom-call(s32[1]{0:T(128)} %bitcast.shard, bf16[3,768,1024]{2,1,0:T(8,128)(2,1)} %get-tuple-element.180.active, bf16[3,192,1024]{2,1,0:T(8,128)(2,1)} %get-tuple-element.233.attended, bf16[3,768,1024]{2,1,0:T(8,128)(2,1)} %get-tuple-element.197.d_pre, ...), custom_call_target="tpu_custom_call" | custom-call | flops 8000 | bytes 16000 | tf_op jit(solution)/shard_map/project/pallas_call | solution.py:435
  159.1 4.1 %collective-permute-done.11 = bf16[384,768]{1,0:T(8,128)(2,1)} collective-permute-done((bf16[384,768]{1,0:T(8,128)(2,1)}, bf16[384,768]{1,0:T(8,128)(2,1)}, u32[]{:S(2)}, u32[]{:S(2)}) %collective-permute-start.11) | collective-permute-done | bytes 589856 | tf_op jit(solution)/shard_map/ppermute | solution.py:494
  163.1 3.1 %collective-permute-done.13.from_y = bf16[1,1,400,1024]{3,2,1,0:T(8,128)(2,1)S(1)} collective-permute-done((bf16[1,1,400,1024]{3,2,1,0:T(8,128)(2,1)}, bf16[1,1,400,1024]{3,2,1,0:T(8,128)(2,1)S(1)}, u32[]{:S(2)}, u32[]{:S(2)}) %collective-permute-start.13) | collective-permute-done | bytes 819232 | tf_op jit(solution)/shard_map/ppermute | solution.py:494
  166.3 0.9 copy-done.9
  167.2 1.9 maximum_select_fusion
  169.7 2.3 %add_convert_fusion.1 = bf16[1,1,400,1024]{3,2,1,0:T(8,128)(2,1)} fusion(bf16[1,2,400,1024]{3,2,1,0:T(8,128)(2,1)} %collective-permute-done.14.from_core, bf16[1,2,400,1024]{3,2,1,0:T(8,128)(2,1)S(1)} %copy-done), kind=kLoop, calls=%fused_computation.2 | loop fusion | flops 1638400 | bytes 2457600 | tf_op jit(solution)/shard_map/convert_element_type | solution.py:590
  172.1 1.1 collective-permute-start.22
  173.2 2.0 collective-permute-start.18
  175.2 0.8 collective-permute-start.21
  176.0 3.1 %finish.3 = (bf16[192,3072]{1,0:T(8,128)(2,1)}, f32[192,3072]{1,0:T(8,128)}) custom-call(bf16[1,2,400,1024]{3,2,1,0:T(8,128)(2,1)} %get-tuple-element.225.keep, bf16[1,2,400,1024]{3,2,1,0:T(8,128)(2,1)} %copy-done.3, bf16[1,1,400,1024]{3,2,1,0:T(8,128)(2,1)} %copy-done.9, bf16[192,3072]{1,0:T(8,128)(2,1)} %bitcast.19, ...), custom_call_target="tpu_custom_call" | custom-call | flops 3000 | bytes 5000 | tf_op jit(solution)/shard_map/finish/pallas_call | solution.py:471
  179.2 2.3 %add_convert_fusion = bf16[1,1,400,1024]{3,2,1,0:T(8,128)(2,1)} fusion(bf16[1,2,400,1024]{3,2,1,0:T(8,128)(2,1)} %collective-permute-done.16.from_core, bf16[1,2,400,1024]{3,2,1,0:T(8,128)(2,1)S(1)} %copy-done.1), kind=kLoop, calls=%fused_computation.1 | loop fusion | flops 1638400 | bytes 2457600 | tf_op jit(solution)/shard_map/convert_element_type | solution.py:590
  181.6 0.7 add.120
  182.3 1.0 collective-permute-done.18
  183.3 1.0 add_convert_fusion.5
  184.3 2.9 %collective-permute-start.19 = (f32[1536]{0:T(1024)S(1)}, f32[1536]{0:T(1024)S(1)}, u32[]{:S(2)}, u32[]{:S(2)}) collective-permute-start(f32[1536]{0:T(1024)S(1)} %add.120), channel_id=1, source_target_pairs={{0,16},{4,20},{8,24},{12,28},{16,0},{20,4},{24,8},{28,12},{1,17},{... | collective-permute-start | bytes 18440 | tf_op jit(solution)/shard_map/ppermute | solution.py:494
  187.2 5.4 %collective-permute-done.19 = f32[1536]{0:T(1024)S(1)} collective-permute-done((f32[1536]{0:T(1024)S(1)}, f32[1536]{0:T(1024)S(1)}, u32[]{:S(2)}, u32[]{:S(2)}) %collective-permute-start.19) | collective-permute-done | bytes 6176 | tf_op jit(solution)/shard_map/ppermute | solution.py:494
  192.8 1.2 collective-permute-start.24
  194.0 0.7 slice.88
  195.3 5.3 %collective-permute-done.22 = bf16[768,768]{1,0:T(8,128)(2,1)} collective-permute-done((bf16[768,768]{1,0:T(8,128)(2,1)S(1)}, bf16[768,768]{1,0:T(8,128)(2,1)}, u32[]{:S(2)}, u32[]{:S(2)}) %collective-permute-start.22) | collective-permute-done | bytes 1179680 | tf_op jit(solution)/shard_map/ppermute | solution.py:494
  200.6 1.1 collective-permute-done.23
  201.9 1.4 collective-permute-start.25
  203.3 1.3 fusion.6
  204.6 3.8 %select_convert_fusion = (f32[768,768]{1,0:T(8,128)}, f32[768,768]{1,0:T(8,128)}) fusion(bf16[768,768]{1,0:T(8,128)(2,1)S(1)} %maximum_select_fusion, bf16[768,768]{1,0:T(8,128)(2,1)} %collective-permute-done.22, pred[]{:T(512)S(6)} %gt.7), kind=kLoop, calls=%fused_computation.5 | loop fusion | flops 2359296 | bytes 7077889 | tf_op jit(solution)/shard_map/convert_element_type | solution.py:785
  208.4 3.1 %finish.4 = (bf16[192,3072]{1,0:T(8,128)(2,1)}, f32[192,3072]{1,0:T(8,128)}) custom-call(bf16[1,2,400,1024]{3,2,1,0:T(8,128)(2,1)} %get-tuple-element.245.keep, bf16[1,2,400,1024]{3,2,1,0:T(8,128)(2,1)} %collective-permute-done.14.from_core, bf16[1,1,400,1024]{3,2,1,0:T(8,128)(2,1)} %collective-permute-done.21.from_y, ...), custom_call_target="tpu_custom_call", output_to_operand_aliasing={{0}: (8, {}), {1}: (9, {})} | custom-call | flops 3000 | bytes 5000 | tf_op jit(solution)/shard_map/finish/pallas_call | solution.py:471
  211.5 1.7 collective-permute-done.24.from_y
  213.2 0.9 copy-done.10
  214.1 3.1 %finish.5 = (bf16[192,3072]{1,0:T(8,128)(2,1)}, f32[192,3072]{1,0:T(8,128)}) custom-call(bf16[1,2,400,1024]{3,2,1,0:T(8,128)(2,1)} %get-tuple-element.248.keep, bf16[1,2,400,1024]{3,2,1,0:T(8,128)(2,1)} %collective-permute-done.16.from_core, bf16[1,1,400,1024]{3,2,1,0:T(8,128)(2,1)} %copy-done.10, ...), custom_call_target="tpu_custom_call", output_to_operand_aliasing={{0}: (8, {}), {1}: (9, {})} | custom-call | flops 3000 | bytes 5000 | tf_op jit(solution)/shard_map/finish/pallas_call | solution.py:471
  217.3 0.9 fusion.2
  218.4 1.4 convert_bitcast_fusion
  (86 shorter events, 5.2 us)
Async XLA Ops:
  1.4 27.6 %copy-start.4 = (bf16[192,128]{1,0:T(8,128)(2,1)}, bf16[192,128]{1,0:T(8,128)(2,1)S(1)}, u32[]{:S(2)}) copy-start(bf16[192,128]{1,0:T(8,128)(2,1)S(1)} %broadcast_in_dim.53.gain_own.gain) | copy-start | bytes 147460
  1.4 11.9 %collective-permute-start = (bf16[192,128]{1,0:T(8,128)(2,1)S(1)}, bf16[192,128]{1,0:T(8,128)(2,1)S(1)}, u32[]{:S(2)}, u32[]{:S(2)}) collective-permute-start(bf16[192,128]{1,0:T(8,128)(2,1)S(1)} %broadcast_in_dim.53.gain_own.gain), channel_id=1, source_target_pairs={{0,2},{1,3},{2,0},{3,1},{4,6},{5,7},{6,4},{7,5},{8,10},{9,11},{10,... | collective-permute-start | bytes 147464 | tf_op jit(solution)/shard_map/ppermute | solution.py:494
  4.4 8.9 %collective-permute-start.1 = (bf16[192,128]{1,0:T(8,128)(2,1)S(1)}, bf16[192,128]{1,0:T(8,128)(2,1)S(1)}, u32[]{:S(2)}, u32[]{:S(2)}) collective-permute-start(bf16[192,128]{1,0:T(8,128)(2,1)S(1)} %broadcast_in_dim.53.gain_own.gain), channel_id=1, source_target_pairs={{0,1},{1,0},{2,3},{3,2},{4,5},{5,4},{6,7},{7,6},{8,9},{9,8},{10,11... | collective-permute-start | bytes 147464 | tf_op jit(solution)/shard_map/ppermute | solution.py:494
  4.4 28.6 %collective-permute-start.2 = (bf16[192,3072]{1,0:T(8,128)(2,1)}, bf16[192,3072]{1,0:T(8,128)(2,1)S(1)}, u32[]{:S(2)}, u32[]{:S(2)}) collective-permute-start(bf16[192,3072]{1,0:T(8,128)(2,1)} %bitcast.16), channel_id=1, source_target_pairs={{0,2},{1,3},{2,0},{3,1},{4,6},{5,7},{6,4},{7,5},{8,10},{9,11},{10,... | collective-permute-start | bytes 3538952 | tf_op jit(solution)/shard_map/ppermute | solution.py:494
  4.6 28.4 %collective-permute-start.4 = (bf16[192,3072]{1,0:T(8,128)(2,1)}, bf16[192,3072]{1,0:T(8,128)(2,1)S(1)}, u32[]{:S(2)}, u32[]{:S(2)}) collective-permute-start(bf16[192,3072]{1,0:T(8,128)(2,1)} %bitcast.17), channel_id=1, source_target_pairs={{0,1},{1,0},{2,3},{3,2},{4,5},{5,4},{6,7},{7,6},{8,9},{9,8},{10,11... | collective-permute-start | bytes 3538952 | tf_op jit(solution)/shard_map/ppermute | solution.py:494
  13.3 15.7 %copy-start.13 = (bf16[192,128]{1,0:T(8,128)(2,1)}, bf16[192,128]{1,0:T(8,128)(2,1)S(1)}, u32[]{:S(2)}) copy-start(bf16[192,128]{1,0:T(8,128)(2,1)S(1)} %collective-permute-done.gain_y) | copy-start | bytes 147460
  13.3 15.7 %copy-start.14 = (bf16[192,128]{1,0:T(8,128)(2,1)}, bf16[192,128]{1,0:T(8,128)(2,1)S(1)}, u32[]{:S(2)}) copy-start(bf16[192,128]{1,0:T(8,128)(2,1)S(1)} %collective-permute-done.1.gain_c) | copy-start | bytes 147460
  17.0 12.0 %collective-permute-start.3 = (bf16[192,128]{1,0:T(8,128)(2,1)S(1)}, bf16[192,128]{1,0:T(8,128)(2,1)S(1)}, u32[]{:S(2)}, u32[]{:S(2)}) collective-permute-start(bf16[192,128]{1,0:T(8,128)(2,1)S(1)} %collective-permute-done.gain_y), channel_id=1, source_target_pairs={{0,1},{1,0},{2,3},{3,2},{4,5},{5,4},{6,7},{7,6},{8,9},{9,8},{10,11... | collective-permute-start | bytes 147464 | tf_op jit(solution)/shard_map/ppermute | solution.py:494
  29.0 4.0 %copy-start.15 = (bf16[192,128]{1,0:T(8,128)(2,1)}, bf16[192,128]{1,0:T(8,128)(2,1)S(1)}, u32[]{:S(2)}) copy-start(bf16[192,128]{1,0:T(8,128)(2,1)S(1)} %collective-permute-done.3.gain_cy) | copy-start | bytes 147460
  33.0 2.9 %copy-start.5 = (bf16[192,3072]{1,0:T(8,128)(2,1)}, bf16[192,3072]{1,0:T(8,128)(2,1)S(1)}, u32[]{:S(2)}) copy-start(bf16[192,3072]{1,0:T(8,128)(2,1)S(1)} %collective-permute-done.2.flip_y) | copy-start | bytes 3538948
  33.0 2.8 %collective-permute-start.5 = (bf16[192,3072]{1,0:T(8,128)(2,1)S(1)}, bf16[192,3072]{1,0:T(8,128)(2,1)S(1)}, u32[]{:S(2)}, u32[]{:S(2)}) collective-permute-start(bf16[192,3072]{1,0:T(8,128)(2,1)S(1)} %collective-permute-done.2.flip_y), channel_id=1, source_target_pairs={{0,1},{1,0},{2,3},{3,2},{4,5},{5,4},{6,7},{7,6},{8,9},{9,8},{10,11... | collective-permute-start | bytes 3538952 | tf_op jit(solution)/shard_map/ppermute | solution.py:494
  33.1 2.8 %copy-start.6 = (bf16[192,3072]{1,0:T(8,128)(2,1)}, bf16[192,3072]{1,0:T(8,128)(2,1)S(1)}, u32[]{:S(2)}) copy-start(bf16[192,3072]{1,0:T(8,128)(2,1)S(1)} %collective-permute-done.4.flip_c) | copy-start | bytes 3538948
  35.9 1.0 copy-start.7
  60.8 60.0 %all-to-all-start = ((bf16[8,192,768]{2,1,0:T(8,128)(2,1)}), bf16[8,192,768]{2,1,0:T(8,128)(2,1)S(1)}, u32[]{:S(2)}, u32[]{:S(2)}) async-start(bf16[8,192,768]{2,1,0:T(8,128)(2,1)} %bitcast.29), calls=%async_computation | async-start | bytes 4718592 | tf_op jit(solution)/shard_map/all_to_all | solution.py:523
  66.6 39.5 %copy-start.11 = (f32[768,128]{1,0:T(8,128)S(1)}, f32[768,128]{1,0:T(8,128)}, u32[]{:S(2)}) copy-start(f32[768,128]{1,0:T(8,128)} %get-tuple-element.195) | copy-start | bytes 1179652
  108.4 10.0 %collective-permute-start.6 = (f32[2,192]{1,0:T(2,128)S(1)}, f32[2,192]{1,0:T(2,128)S(1)}, u32[]{:S(2)}, u32[]{:S(2)}) collective-permute-start(f32[2,192]{1,0:T(2,128)S(1)} %pad_maximum_fusion.2), channel_id=1, source_target_pairs={{0,1},{1,0},{2,3},{3,2},{4,5},{5,4},{6,7},{7,6},{8,9},{9,8},{10,11... | collective-permute-start | bytes 4616 | tf_op jit(solution)/shard_map/ppermute | solution.py:494
  118.3 9.7 %copy-start.12 = (f32[384,128]{1,0:T(8,128)S(1)}, f32[384,128]{1,0:T(8,128)}, u32[]{:S(2)}) copy-start(f32[384,128]{1,0:T(8,128)} %get-tuple-element.222) | copy-start | bytes 589828
  121.9 17.4 %collective-permute-start.9 = (bf16[1,2,400,1024]{3,2,1,0:T(8,128)(2,1)}, bf16[1,2,400,1024]{3,2,1,0:T(8,128)(2,1)S(1)}, u32[]{:S(2)}, u32[]{:S(2)}) collective-permute-start(bf16[1,2,400,1024]{3,2,1,0:T(8,128)(2,1)} %get-tuple-element.217), channel_id=1, source_target_pairs={{0,1},{1,0},{2,3},{3,2},{4,5},{5,4},{6,7},{7,6},{8,9},{9,8},{10,11... | collective-permute-start | bytes 4915208 | tf_op jit(solution)/shard_map/ppermute | solution.py:494
  121.9 17.4 %collective-permute-start.7 = (bf16[192,768]{1,0:T(8,128)(2,1)}, bf16[192,768]{1,0:T(8,128)(2,1)}, u32[]{:S(2)}, u32[]{:S(2)}) collective-permute-start(bf16[192,768]{1,0:T(8,128)(2,1)} %reduce_sum.75), channel_id=1, source_target_pairs={{0,16},{4,20},{8,24},{12,28},{16,0},{20,4},{24,8},{28,12},{1,17},{... | collective-permute-start | bytes 884744 | tf_op jit(solution)/shard_map/ppermute | solution.py:494
  122.3 21.1 %collective-permute-start.10 = (bf16[384,768]{1,0:T(8,128)(2,1)}, bf16[384,768]{1,0:T(8,128)(2,1)}, u32[]{:S(2)}, u32[]{:S(2)}) collective-permute-start(bf16[384,768]{1,0:T(8,128)(2,1)} %constant_dynamic-slice_fusion.4), channel_id=1, source_target_pairs={{0,4},{4,0},{8,12},{12,8},{16,20},{20,16},{24,28},{28,24},{1,5},{5... | collective-permute-start | bytes 1769480 | tf_op jit(solution)/shard_map/ppermute | solution.py:494
  126.2 13.1 %collective-permute-start.8 = (f32[192]{0:T(256)S(1)}, f32[192]{0:T(256)S(1)}, u32[]{:S(2)}, u32[]{:S(2)}) collective-permute-start(f32[192]{0:T(256)S(1)} %bitcast.31), channel_id=1, source_target_pairs={{0,2},{1,3},{2,0},{3,1},{4,6},{5,7},{6,4},{7,5},{8,10},{9,11},{10,... | collective-permute-start | bytes 2312 | tf_op jit(solution)/shard_map/ppermute | solution.py:494
  129.3 12.9 %copy-start.2 = (bf16[1,2,400,1024]{3,2,1,0:T(8,128)(2,1)S(1)}, bf16[1,2,400,1024]{3,2,1,0:T(8,128)(2,1)}, u32[]{:S(2)}) copy-start(bf16[1,2,400,1024]{3,2,1,0:T(8,128)(2,1)} %get-tuple-element.225.keep) | copy-start | bytes 4915204
  139.4 4.0 %copy-start.3 = (bf16[1,2,400,1024]{3,2,1,0:T(8,128)(2,1)}, bf16[1,2,400,1024]{3,2,1,0:T(8,128)(2,1)S(1)}, u32[]{:S(2)}) copy-start(bf16[1,2,400,1024]{3,2,1,0:T(8,128)(2,1)S(1)} %collective-permute-done.9.from_core) | copy-start | bytes 4915204
  139.5 3.9 %copy-start.8 = (bf16[768,768]{1,0:T(8,128)(2,1)S(1)}, bf16[768,768]{1,0:T(8,128)(2,1)}, u32[]{:S(2)}) copy-start(bf16[768,768]{1,0:T(8,128)(2,1)} %get-tuple-element.193) | copy-start | bytes 3538948
  145.4 20.9 %collective-permute-start.14 = (bf16[1,2,400,1024]{3,2,1,0:T(8,128)(2,1)}, bf16[1,2,400,1024]{3,2,1,0:T(8,128)(2,1)}, u32[]{:S(2)}, u32[]{:S(2)}) collective-permute-start(bf16[1,2,400,1024]{3,2,1,0:T(8,128)(2,1)} %get-tuple-element.240), channel_id=1, source_target_pairs={{0,1},{1,0},{2,3},{3,2},{4,5},{5,4},{6,7},{7,6},{8,9},{9,8},{10,11... | collective-permute-start | bytes 4915208 | tf_op jit(solution)/shard_map/ppermute | solution.py:494
  145.4 20.9 %collective-permute-start.13 = (bf16[1,1,400,1024]{3,2,1,0:T(8,128)(2,1)}, bf16[1,1,400,1024]{3,2,1,0:T(8,128)(2,1)S(1)}, u32[]{:S(2)}, u32[]{:S(2)}) collective-permute-start(bf16[1,1,400,1024]{3,2,1,0:T(8,128)(2,1)} %add_convert_fusion.2), channel_id=1, source_target_pairs={{0,2},{1,3},{2,0},{3,1},{4,6},{5,7},{6,4},{7,5},{8,10},{9,11},{10,... | collective-permute-start | bytes 2457608 | tf_op jit(solution)/shard_map/ppermute | solution.py:494
  146.7 16.5 %collective-permute-start.11 = (bf16[384,768]{1,0:T(8,128)(2,1)}, bf16[384,768]{1,0:T(8,128)(2,1)}, u32[]{:S(2)}, u32[]{:S(2)}) collective-permute-start(bf16[384,768]{1,0:T(8,128)(2,1)} %maximum_select_fusion.1), channel_id=1, source_target_pairs={{0,8},{4,12},{8,0},{12,4},{16,24},{20,28},{24,16},{28,20},{1,9},{5... | collective-permute-start | bytes 1769480 | tf_op jit(solution)/shard_map/ppermute | solution.py:494
  146.7 12.4 %collective-permute-start.12 = (f32[1536]{0:T(1024)S(1)}, f32[1536]{0:T(1024)S(1)}, u32[]{:S(2)}, u32[]{:S(2)}) collective-permute-start(f32[1536]{0:T(1024)S(1)} %concatenate.37), channel_id=1, source_target_pairs={{0,4},{4,0},{8,12},{12,8},{16,20},{20,16},{24,28},{28,24},{1,5},{5... | collective-permute-start | bytes 18440 | tf_op jit(solution)/shard_map/ppermute | solution.py:494
  147.3 24.7 %collective-permute-start.15 = (bf16[192,768]{1,0:T(8,128)(2,1)}, bf16[192,768]{1,0:T(8,128)(2,1)S(1)}, u32[]{:S(2)}, u32[]{:S(2)}) collective-permute-start(bf16[192,768]{1,0:T(8,128)(2,1)} %get-tuple-element.247), channel_id=1, source_target_pairs={{0,8},{4,12},{8,0},{12,4},{16,24},{20,28},{24,16},{28,20},{1,9},{5... | collective-permute-start | bytes 884744 | tf_op jit(solution)/shard_map/ppermute | solution.py:494
  159.1 10.6 %copy-start = (bf16[1,2,400,1024]{3,2,1,0:T(8,128)(2,1)S(1)}, bf16[1,2,400,1024]{3,2,1,0:T(8,128)(2,1)}, u32[]{:S(2)}) copy-start(bf16[1,2,400,1024]{3,2,1,0:T(8,128)(2,1)} %get-tuple-element.245.keep) | copy-start | bytes 4915204
  166.3 0.9 copy-start.9
  172.1 7.1 %collective-permute-start.16 = (bf16[1,2,400,1024]{3,2,1,0:T(8,128)(2,1)}, bf16[1,2,400,1024]{3,2,1,0:T(8,128)(2,1)}, u32[]{:S(2)}, u32[]{:S(2)}) collective-permute-start(bf16[1,2,400,1024]{3,2,1,0:T(8,128)(2,1)} %get-tuple-element.260), channel_id=1, source_target_pairs={{0,1},{1,0},{2,3},{3,2},{4,5},{5,4},{6,7},{7,6},{8,9},{9,8},{10,11... | collective-permute-start | bytes 4915208 | tf_op jit(solution)/shard_map/ppermute | solution.py:494
  172.1 28.5 %collective-permute-start.22 = (bf16[768,768]{1,0:T(8,128)(2,1)S(1)}, bf16[768,768]{1,0:T(8,128)(2,1)}, u32[]{:S(2)}, u32[]{:S(2)}) collective-permute-start(bf16[768,768]{1,0:T(8,128)(2,1)S(1)} %maximum_select_fusion), channel_id=1, source_target_pairs={{0,4},{4,0},{8,12},{12,8},{16,20},{20,16},{24,28},{28,24},{1,5},{5... | collective-permute-start | bytes 3538952 | tf_op jit(solution)/shard_map/ppermute | solution.py:494
  173.2 6.0 %collective-permute-start.17 = (f32[1536]{0:T(1024)}, f32[1536]{0:T(1024)}, u32[]{:S(2)}, u32[]{:S(2)}) collective-permute-start(f32[1536]{0:T(1024)} %add.114), channel_id=1, source_target_pairs={{0,8},{4,12},{8,0},{12,4},{16,24},{20,28},{24,16},{28,20},{1,9},{5... | collective-permute-start | bytes 18440 | tf_op jit(solution)/shard_map/ppermute | solution.py:494
  173.2 10.1 %collective-permute-start.18 = (bf16[96,768]{1,0:T(8,128)(2,1)S(1)}, bf16[96,768]{1,0:T(8,128)(2,1)}, u32[]{:S(2)}, u32[]{:S(2)}) collective-permute-start(bf16[96,768]{1,0:T(8,128)(2,1)S(1)} %add_convert_fusion.7), channel_id=1, source_target_pairs={{0,16},{4,20},{8,24},{12,28},{16,0},{20,4},{24,8},{28,12},{1,17},{... | collective-permute-start | bytes 442376 | tf_op jit(solution)/shard_map/ppermute | solution.py:494
  175.2 20.1 %collective-permute-start.21 = (bf16[1,1,400,1024]{3,2,1,0:T(8,128)(2,1)}, bf16[1,1,400,1024]{3,2,1,0:T(8,128)(2,1)}, u32[]{:S(2)}, u32[]{:S(2)}) collective-permute-start(bf16[1,1,400,1024]{3,2,1,0:T(8,128)(2,1)} %add_convert_fusion.1), channel_id=1, source_target_pairs={{0,2},{1,3},{2,0},{3,1},{4,6},{5,7},{6,4},{7,5},{8,10},{9,11},{10,... | collective-permute-start | bytes 2457608 | tf_op jit(solution)/shard_map/ppermute | solution.py:494
  176.0 3.2 %copy-start.1 = (bf16[1,2,400,1024]{3,2,1,0:T(8,128)(2,1)S(1)}, bf16[1,2,400,1024]{3,2,1,0:T(8,128)(2,1)}, u32[]{:S(2)}) copy-start(bf16[1,2,400,1024]{3,2,1,0:T(8,128)(2,1)} %get-tuple-element.248.keep) | copy-start | bytes 4915204
  184.3 8.4 %collective-permute-start.20 = (bf16[96,768]{1,0:T(8,128)(2,1)S(1)}, bf16[96,768]{1,0:T(8,128)(2,1)S(1)}, u32[]{:S(2)}, u32[]{:S(2)}) collective-permute-start(bf16[96,768]{1,0:T(8,128)(2,1)S(1)} %add_convert_fusion.5), channel_id=1, source_target_pairs={{0,16},{4,20},{8,24},{12,28},{16,0},{20,4},{24,8},{28,12},{1,17},{... | collective-permute-start | bytes 442376 | tf_op jit(solution)/shard_map/ppermute | solution.py:494
  184.3 8.3 %collective-permute-start.19 = (f32[1536]{0:T(1024)S(1)}, f32[1536]{0:T(1024)S(1)}, u32[]{:S(2)}, u32[]{:S(2)}) collective-permute-start(f32[1536]{0:T(1024)S(1)} %add.120), channel_id=1, source_target_pairs={{0,16},{4,20},{8,24},{12,28},{16,0},{20,4},{24,8},{28,12},{1,17},{... | collective-permute-start | bytes 18440 | tf_op jit(solution)/shard_map/ppermute | solution.py:494
  192.7 9.0 %collective-permute-start.23 = (bf16[192,768]{1,0:T(8,128)(2,1)S(1)}, bf16[192,768]{1,0:T(8,128)(2,1)S(1)}, u32[]{:S(2)}, u32[]{:S(2)}) collective-permute-start(bf16[192,768]{1,0:T(8,128)(2,1)S(1)} %maximum_select_fusion.3), channel_id=1, source_target_pairs={{0,8},{4,12},{8,0},{12,4},{16,24},{20,28},{24,16},{28,20},{1,9},{5... | collective-permute-start | bytes 884744 | tf_op jit(solution)/shard_map/ppermute | solution.py:494
  192.8 20.4 %collective-permute-start.24 = (bf16[1,1,400,1024]{3,2,1,0:T(8,128)(2,1)}, bf16[1,1,400,1024]{3,2,1,0:T(8,128)(2,1)S(1)}, u32[]{:S(2)}, u32[]{:S(2)}) collective-permute-start(bf16[1,1,400,1024]{3,2,1,0:T(8,128)(2,1)} %add_convert_fusion), channel_id=1, source_target_pairs={{0,2},{1,3},{2,0},{3,1},{4,6},{5,7},{6,4},{7,5},{8,10},{9,11},{10,... | collective-permute-start | bytes 2457608 | tf_op jit(solution)/shard_map/ppermute | solution.py:494
  201.9 15.4 %collective-permute-start.25 = (bf16[384,768]{1,0:T(8,128)(2,1)S(1)}, bf16[384,768]{1,0:T(8,128)(2,1)S(1)}, u32[]{:S(2)}, u32[]{:S(2)}) collective-permute-start(bf16[384,768]{1,0:T(8,128)(2,1)S(1)} %maximum_select_fusion.2), channel_id=1, source_target_pairs={{0,4},{4,0},{8,12},{12,8},{16,20},{20,16},{24,28},{28,24},{1,5},{5... | collective-permute-start | bytes 1769480 | tf_op jit(solution)/shard_map/ppermute | solution.py:494
  213.2 0.9 copy-start.10

commit v10 on v9

--- a/solution.py
+++ b/solution.py
@@ -592,12 +592,15 @@
             self.from_y = arrived
 
 
-def land_then(flights, final, outputs):
-    outputs = land(flights, outputs)
-    movers = [f[0] for f in flights]
-    outputs, sends = land(final, (outputs, [m.send for m in movers]))
-    for mover, send in zip(movers, sends):
-        mover.send = send
+def land_in_turn(phases, outputs):
+    movers = []
+    for flights in phases:
+        outputs, sends, arrivals = tie(outputs, [m.send for m in movers], [f[1] for f in flights])
+        for mover, send in zip(movers, sends):
+            mover.send = send
+        for (mover, _), arrived in zip(flights, arrivals):
+            mover.take(arrived)
+        movers += [f[0] for f in flights]
     return outputs
 
 
@@ -733,9 +736,16 @@
         sent = project_call(
             shard, active, att, d_pre, dm, normed, down_weight, attn_weight, up_weight, mixed_t, gain_all, begin, size
         )
-        late = [f for f in flights if begin == 0 and f[0] is mix_sum]
-        final = [f for f in flying if f[0] is mix_sum and f not in late]
-        keep, send = land_then([f for f in flying if f not in late + final], final, sent)
+        final = seqs - 1
+        late = [f for f in flights if begin == 0 and f[0] is mix_sum or begin == final and f[0] is scatters[0]]
+        wide = [f for f in flying if f[0] is mlp_sum]
+        chain = [f for f in flying if f[0] is mix_sum and f not in late]
+        quick = [f for f in flying if f not in late + wide + chain]
+        keep, send = land_in_turn([quick, wide, chain], sent)
+        if begin == final and begin > 0:
+            _, ahead = launch([mix_sum], ())
+            (keep, send), *_ = (land(late, (keep, send)),)
+            late = ahead
         flying = late
         scatters.append(ScatterOverMp(keep, send))
 
@@ -776,7 +786,7 @@
         else:
             now = chain + rest or flying
         final = [f for f in now if f[0] is mix_sum]
-        finished, wide_grads = land_then([f for f in now if f not in final], final, (finished, wide_grads))
+        finished, wide_grads = land_in_turn([[f for f in now if f not in final], final], (finished, wide_grads))
         flying = [f for f in flying if f not in now]
         if not mlp_sum.more() and not wide_grads:
             swap, held, arrived = mlp_sum.last

time: 221 us -> 216 us (0.977)
  no operation moved by 1% of the time
where the time goes in v10:
time: 216 us; the launch traced here: 215 us
  Pallas kernels  113 us (52%)
  other arithmetic  31.5 us (15%)
  waiting for transfers between devices  29.3 us (14%)
  starting transfers between devices  27.7 us (13%)
  local copies, waits for them, and re-layouts  12.5 us (6%)
    pallas_call x1, Pallas kernels, attention_call(): pl.pallas_call(attention_kernel, grid_spec=grid_spec, out_shape=[jax.Shap...  38.3 us
    pallas_call x3, Pallas kernels, project_call(): pl.pallas_call(project_kernel, grid_spec=grid_spec, out_shape=[jax.ShapeD...  29.8 us
    ppermute x26, waiting for transfers between devices, flip(): return lax.ppermute(value, axis, [(i, i ^ bit) for i in range(size)])  26.4 us
    pallas_call x1, Pallas kernels, mlp_call(): pl.pallas_call(functools.partial(mlp_kernel, pieces_order), grid_spec=gri...  23.9 us
    ppermute x26, starting transfers between devices, flip(): return lax.ppermute(value, axis, [(i, i ^ bit) for i in range(size)])  21.9 us
    pallas_call x1, Pallas kernels, early_call(): pl.pallas_call(early_kernel, grid=(tokens // block,), in_specs=[pl.BlockS...  11.2 us
    pallas_call x3, Pallas kernels, finish_call(): pl.pallas_call(finish_kernel, grid=(size * steps,), in_specs=[packed, pac...  9.4 us
    convert_element_type x3, other arithmetic, take(): (self.keep[:, 1:].astype(F32) + arrived[:, 1:].astype(F32)).astype(BF16)  5.9 us
  transfers between devices with their start and end apart: 27, of which 10 were waited for; matrix products, arithmetic and copies ran while one was open for 17% of the time, Pallas kernels for 41%

profile of v10, /device:TPU:0, one launch (start us, length us, event | category | flops | bytes accessed | tf_op | source)
XLA Modules:
  0.0 214.6 jit_solution(10217477008880423379)
XLA Ops:
  0.6 0.7 broadcast_in_dim.53.gain_own.gain
  1.4 3.0 %collective-permute-start = (bf16[192,128]{1,0:T(8,128)(2,1)S(1)}, bf16[192,128]{1,0:T(8,128)(2,1)S(1)}, u32[]{:S(2)}, u32[]{:S(2)}) collective-permute-start(bf16[192,128]{1,0:T(8,128)(2,1)S(1)} %broadcast_in_dim.53.gain_own.gain), channel_id=1, source_target_pairs={{0,2},{1,3},{2,0},{3,1},{4,6},{5,7},{6,4},{7,5},{8,10},{9,11},{10,... | collective-permute-start | bytes 147464 | tf_op jit(solution)/shard_map/ppermute | solution.py:494
  4.9 0.8 slice.65
  5.8 0.8 slice.66
  6.6 1.0 convert_reduce_fusion
  7.6 1.4 fusion.4.mask_q
  8.9 1.4 select_convert_fusion.2.mask_k
  10.4 0.8 fusion.1.pick
  11.2 1.2 xor_multiply_fusion.place
  12.4 0.8 reshape.72
  13.3 0.8 broadcast_in_dim.27.gains
  14.1 1.5 broadcast_in_dim.24.up_bias
  15.7 1.4 broadcast_in_dim.52.bias
  17.7 11.2 %early.1 = (bf16[3,768,1024]{2,1,0:T(8,128)(2,1)}, bf16[3,192,1024]{2,1,0:T(8,128)(2,1)}, bf16[192,3072]{1,0:T(8,128)(2,1)}, f32[192,128]{1,0:T(8,128)}) custom-call(bf16[3072,768]{1,0:T(8,128)(2,1)} %cot.5, bf16[768,768]{1,0:T(8,128)(2,1)} %down.7, bf16[192,768]{1,0:T(8,128)(2,1)} %attn.7, bf16[192,768]{1,0:T(8,128)(2,1)} %fusion.1.pick), custom_call_target="tpu_custom_call" | custom-call | flops 10000 | bytes 12000 | tf_op jit(solution)/shard_map/early/pallas_call | solution.py:63
  28.9 4.1 %collective-permute-done.2.flip_y = bf16[192,3072]{1,0:T(8,128)(2,1)S(1)} collective-permute-done((bf16[192,3072]{1,0:T(8,128)(2,1)}, bf16[192,3072]{1,0:T(8,128)(2,1)S(1)}, u32[]{:S(2)}, u32[]{:S(2)}) %collective-permute-start.2) | collective-permute-done | bytes 1179680 | tf_op jit(solution)/shard_map/ppermute | solution.py:494
  33.1 2.8 %collective-permute-done.5.flip_cy = bf16[192,3072]{1,0:T(8,128)(2,1)S(1)} collective-permute-done((bf16[192,3072]{1,0:T(8,128)(2,1)S(1)}, bf16[192,3072]{1,0:T(8,128)(2,1)S(1)}, u32[]{:S(2)}, u32[]{:S(2)}) %collective-permute-start.5) | collective-permute-done | bytes 1179680 | tf_op jit(solution)/shard_map/ppermute | solution.py:494
  35.9 1.0 copy-done.9
  36.9 23.9 %mlp.1 = (bf16[3,768,1024]{2,1,0:T(8,128)(2,1)}, bf16[3,768,1024]{2,1,0:T(8,128)(2,1)}, bf16[3,768,1024]{2,1,0:T(8,128)(2,1)}, f32[8,3072]{1,0:T(8,128)}, f32[76...) custom-call(s32[4]{0:T(128)} %xor_multiply_fusion.place, ...), custom_call_target="tpu_custom_call" | custom-call | flops 20000 | bytes 30000 | tf_op jit(solution)/shard_map/mlp/pallas_call | solution.py:188
  60.8 5.8 %all-to-all-start = ((bf16[8,192,768]{2,1,0:T(8,128)(2,1)}), bf16[8,192,768]{2,1,0:T(8,128)(2,1)S(1)}, u32[]{:S(2)}, u32[]{:S(2)}) async-start(bf16[8,192,768]{2,1,0:T(8,128)(2,1)} %bitcast.29), calls=%async_computation | async-start | bytes 4718592 | tf_op jit(solution)/shard_map/all_to_all | solution.py:523
  66.6 38.3 %attention.1 = (bf16[3,192,1024]{2,1,0:T(8,128)(2,1)}, bf16[3,576,1024]{2,1,0:T(8,128)(2,1)}, f32[384,128]{1,0:T(8,128)}, f32[1,768]{1,0:T(1,128)}, bf16[768,768]{1,0:T(8,128)(2,1)}) custom-call(s32[12]{0:T(128)} %get-tuple-element.193.first, s32[12]{0:T(128)} %get-tuple-element.194.count, bf16[3,768,1024]{2,1,0:T(8,128)(2,1)} %get-tuple-element.197.normed, ...), custom_call_target="tpu_custom_call" | custom-call | flops 18000 | bytes 5000 | tf_op jit(solution)/shard_map/attention/pallas_call | solution.py:360
  104.9 0.7 reduce.1
  106.0 1.9 constant_dynamic-slice_fusion.4
  107.9 9.9 %project.3 = (bf16[1,2,400,1024]{3,2,1,0:T(8,128)(2,1)}, bf16[1,2,400,1024]{3,2,1,0:T(8,128)(2,1)}) custom-call(s32[1]{0:T(128)} %bitcast.shard, bf16[3,768,1024]{2,1,0:T(8,128)(2,1)} %get-tuple-element.192.active, bf16[3,192,1024]{2,1,0:T(8,128)(2,1)} %get-tuple-element.252.attended, bf16[3,768,1024]{2,1,0:T(8,128)(2,1)} %get-tuple-element.209.d_pre, ...), custom_call_target="tpu_custom_call" | custom-call | flops 8000 | bytes 16000 | tf_op jit(solution)/shard_map/project/pallas_call | solution.py:435
  117.9 2.9 %all-to-all-done = bf16[8,192,768]{2,1,0:T(8,128)(2,1)S(1)} async-done(((bf16[8,192,768]{2,1,0:T(8,128)(2,1)}), bf16[8,192,768]{2,1,0:T(8,128)(2,1)S(1)}, u32[]{:S(2)}, u32[]{:S(2)}) %all-to-all-start) | async-done | bytes 2359328 | tf_op jit(solution)/shard_map/all_to_all | solution.py:523
  120.8 1.1 reduce_sum.75
  121.9 1.5 collective-permute-start.10
  123.4 3.0 %collective-permute-start.9 = (bf16[192,768]{1,0:T(8,128)(2,1)}, bf16[192,768]{1,0:T(8,128)(2,1)}, u32[]{:S(2)}, u32[]{:S(2)}) collective-permute-start(bf16[192,768]{1,0:T(8,128)(2,1)} %reduce_sum.75), channel_id=1, source_target_pairs={{0,16},{4,20},{8,24},{12,28},{16,0},{20,4},{24,8},{28,12},{1,17},{... | collective-permute-start | bytes 884744 | tf_op jit(solution)/shard_map/ppermute | solution.py:494
  126.4 0.8 collective-permute-start.7
  127.2 1.0 reduce_sum.78
  128.4 1.2 reduce_sum.77
  129.5 10.0 %project.4 = (bf16[1,2,400,1024]{3,2,1,0:T(8,128)(2,1)}, bf16[1,2,400,1024]{3,2,1,0:T(8,128)(2,1)}) custom-call(s32[1]{0:T(128)} %bitcast.shard, bf16[3,768,1024]{2,1,0:T(8,128)(2,1)} %get-tuple-element.192.active, bf16[3,192,1024]{2,1,0:T(8,128)(2,1)} %get-tuple-element.252.attended, bf16[3,768,1024]{2,1,0:T(8,128)(2,1)} %get-tuple-element.209.d_pre, ...), custom_call_target="tpu_custom_call" | custom-call | flops 8000 | bytes 16000 | tf_op jit(solution)/shard_map/project/pallas_call | solution.py:435
  139.7 1.2 add_convert_fusion.2
  140.9 1.3 maximum_select_fusion.1
  142.2 2.2 %add_convert_fusion.3 = (bf16[192,768]{1,0:T(8,128)(2,1)S(1)}, bf16[192,768]{1,0:T(8,128)(2,1)}) fusion(bf16[384,768]{1,0:T(8,128)(2,1)} %collective-permute-done.10, s32[]{:T(128)S(6)} %mul.38, bf16[768,768]{1,0:T(8,128)(2,1)S(1)} %copy-done.10, s32[]{:T(128)S(6)} %dynamic_slice.55, s32[]{:T(128)S(6)} %select_n.103, s32[]{:T(128)S(6)} %dynamic_slice.47), kind=kLoop, calls=%fused_computation.12 | loop fusion | flops 1179648 | bytes 1769488 | tf_op jit(solution)/shard_map/convert_element_type | solution.py:550
  144.4 1.2 collective-permute-start.15
  145.7 0.9 collective-permute-start.13
  146.5 1.5 collective-permute-start.14
  148.0 9.9 %project.5 = (bf16[1,2,400,1024]{3,2,1,0:T(8,128)(2,1)}, bf16[1,2,400,1024]{3,2,1,0:T(8,128)(2,1)}) custom-call(s32[1]{0:T(128)} %bitcast.shard, bf16[3,768,1024]{2,1,0:T(8,128)(2,1)} %get-tuple-element.192.active, bf16[3,192,1024]{2,1,0:T(8,128)(2,1)} %get-tuple-element.252.attended, bf16[3,768,1024]{2,1,0:T(8,128)(2,1)} %get-tuple-element.209.d_pre, ...), custom_call_target="tpu_custom_call" | custom-call | flops 8000 | bytes 16000 | tf_op jit(solution)/shard_map/project/pallas_call | solution.py:435
  158.5 2.3 %add_convert_fusion.1 = bf16[1,1,400,1024]{3,2,1,0:T(8,128)(2,1)} fusion(bf16[1,2,400,1024]{3,2,1,0:T(8,128)(2,1)} %collective-permute-done.12.from_core, bf16[1,2,400,1024]{3,2,1,0:T(8,128)(2,1)S(1)} %copy-done), kind=kLoop, calls=%fused_computation.2 | loop fusion | flops 1638400 | bytes 2457600 | tf_op jit(solution)/shard_map/convert_element_type | solution.py:590
  160.9 1.1 collective-permute-done.13
  161.9 1.6 maximum_select_fusion
  163.6 3.9 %collective-permute-done.14 = bf16[192,768]{1,0:T(8,128)(2,1)S(1)} collective-permute-done((bf16[192,768]{1,0:T(8,128)(2,1)}, bf16[192,768]{1,0:T(8,128)(2,1)S(1)}, u32[]{:S(2)}, u32[]{:S(2)}) %collective-permute-start.14) | collective-permute-done | bytes 294944 | tf_op jit(solution)/shard_map/ppermute | solution.py:494
  167.4 0.9 collective-permute-start.17
  168.3 0.7 add_convert_fusion.7
  169.0 1.5 collective-permute-start.18
  170.5 1.2 collective-permute-start.21
  171.8 3.1 %finish.3 = (bf16[192,3072]{1,0:T(8,128)(2,1)}, f32[192,3072]{1,0:T(8,128)}) custom-call(bf16[1,2,400,1024]{3,2,1,0:T(8,128)(2,1)} %get-tuple-element.238.keep, bf16[1,2,400,1024]{3,2,1,0:T(8,128)(2,1)} %copy-done.3, bf16[1,1,400,1024]{3,2,1,0:T(8,128)(2,1)} %collective-permute-done.15.from_y, bf16[192,3072]{1,0:T(8,128)(2,1)} %bitcast.19, ...), custom_call_target="tpu_custom_call" | custom-call | flops 3000 | bytes 5000 | tf_op jit(solution)/shard_map/finish/pallas_call | solution.py:471
  174.9 2.3 %add_convert_fusion = bf16[1,1,400,1024]{3,2,1,0:T(8,128)(2,1)} fusion(bf16[1,2,400,1024]{3,2,1,0:T(8,128)(2,1)} %collective-permute-done.16.from_core, bf16[1,2,400,1024]{3,2,1,0:T(8,128)(2,1)S(1)} %copy-done.1), kind=kLoop, calls=%fused_computation.1 | loop fusion | flops 1638400 | bytes 2457600 | tf_op jit(solution)/shard_map/convert_element_type | solution.py:590
  177.3 0.7 add.117
  178.0 1.3 collective-permute-done.18
  179.4 2.9 %collective-permute-start.19 = (f32[1536]{0:T(1024)S(1)}, f32[1536]{0:T(1024)S(1)}, u32[]{:S(2)}, u32[]{:S(2)}) collective-permute-start(f32[1536]{0:T(1024)S(1)} %add.117), channel_id=1, source_target_pairs={{0,16},{4,20},{8,24},{12,28},{16,0},{20,4},{24,8},{28,12},{1,17},{... | collective-permute-start | bytes 18440 | tf_op jit(solution)/shard_map/ppermute | solution.py:494
  182.3 5.1 %collective-permute-done.19 = f32[1536]{0:T(1024)S(1)} collective-permute-done((f32[1536]{0:T(1024)S(1)}, f32[1536]{0:T(1024)S(1)}, u32[]{:S(2)}, u32[]{:S(2)}) %collective-permute-start.19) | collective-permute-done | bytes 6176 | tf_op jit(solution)/shard_map/ppermute | solution.py:494
  187.5 0.9 collective-permute-start.24
  189.8 0.9 collective-permute-done.21.from_y
  190.7 5.8 %collective-permute-done.22 = bf16[768,768]{1,0:T(8,128)(2,1)} collective-permute-done((bf16[768,768]{1,0:T(8,128)(2,1)S(1)}, bf16[768,768]{1,0:T(8,128)(2,1)}, u32[]{:S(2)}, u32[]{:S(2)}) %collective-permute-start.22) | collective-permute-done | bytes 1179680 | tf_op jit(solution)/shard_map/ppermute | solution.py:494
  196.7 1.7 collective-permute-start.25
  198.5 1.3 fusion.6
  199.7 3.8 %select_convert_fusion = (f32[768,768]{1,0:T(8,128)}, f32[768,768]{1,0:T(8,128)}) fusion(bf16[768,768]{1,0:T(8,128)(2,1)S(1)} %maximum_select_fusion, bf16[768,768]{1,0:T(8,128)(2,1)} %collective-permute-done.22, pred[]{:T(512)S(6)} %gt.7), kind=kLoop, calls=%fused_computation.5 | loop fusion | flops 2359296 | bytes 7077889 | tf_op jit(solution)/shard_map/convert_element_type | solution.py:795
  203.5 3.1 %finish.4 = (bf16[192,3072]{1,0:T(8,128)(2,1)}, f32[192,3072]{1,0:T(8,128)}) custom-call(bf16[1,2,400,1024]{3,2,1,0:T(8,128)(2,1)} %get-tuple-element.261.keep, bf16[1,2,400,1024]{3,2,1,0:T(8,128)(2,1)} %collective-permute-done.12.from_core, bf16[1,1,400,1024]{3,2,1,0:T(8,128)(2,1)} %collective-permute-done.21.from_y, ...), custom_call_target="tpu_custom_call", output_to_operand_aliasing={{0}: (8, {}), {1}: (9, {})} | custom-call | flops 3000 | bytes 5000 | tf_op jit(solution)/shard_map/finish/pallas_call | solution.py:471
  206.6 1.5 collective-permute-done.24.from_y
  208.1 0.9 copy-done.12
  209.0 3.1 %finish.5 = (bf16[192,3072]{1,0:T(8,128)(2,1)}, f32[192,3072]{1,0:T(8,128)}) custom-call(bf16[1,2,400,1024]{3,2,1,0:T(8,128)(2,1)} %get-tuple-element.273.keep, bf16[1,2,400,1024]{3,2,1,0:T(8,128)(2,1)} %collective-permute-done.16.from_core, bf16[1,1,400,1024]{3,2,1,0:T(8,128)(2,1)} %copy-done.12, ...), custom_call_target="tpu_custom_call", output_to_operand_aliasing={{0}: (8, {}), {1}: (9, {})} | custom-call | flops 3000 | bytes 5000 | tf_op jit(solution)/shard_map/finish/pallas_call | solution.py:471
  212.1 0.9 fusion.2
  213.3 1.4 convert_bitcast_fusion
  (90 shorter events, 4.8 us)
Async XLA Ops:
  1.4 27.5 %copy-start.6 = (bf16[192,128]{1,0:T(8,128)(2,1)}, bf16[192,128]{1,0:T(8,128)(2,1)S(1)}, u32[]{:S(2)}) copy-start(bf16[192,128]{1,0:T(8,128)(2,1)S(1)} %broadcast_in_dim.53.gain_own.gain) | copy-start | bytes 147460
  1.4 11.9 %collective-permute-start = (bf16[192,128]{1,0:T(8,128)(2,1)S(1)}, bf16[192,128]{1,0:T(8,128)(2,1)S(1)}, u32[]{:S(2)}, u32[]{:S(2)}) collective-permute-start(bf16[192,128]{1,0:T(8,128)(2,1)S(1)} %broadcast_in_dim.53.gain_own.gain), channel_id=1, source_target_pairs={{0,2},{1,3},{2,0},{3,1},{4,6},{5,7},{6,4},{7,5},{8,10},{9,11},{10,... | collective-permute-start | bytes 147464 | tf_op jit(solution)/shard_map/ppermute | solution.py:494
  4.4 8.9 %collective-permute-start.1 = (bf16[192,128]{1,0:T(8,128)(2,1)S(1)}, bf16[192,128]{1,0:T(8,128)(2,1)S(1)}, u32[]{:S(2)}, u32[]{:S(2)}) collective-permute-start(bf16[192,128]{1,0:T(8,128)(2,1)S(1)} %broadcast_in_dim.53.gain_own.gain), channel_id=1, source_target_pairs={{0,1},{1,0},{2,3},{3,2},{4,5},{5,4},{6,7},{7,6},{8,9},{9,8},{10,11... | collective-permute-start | bytes 147464 | tf_op jit(solution)/shard_map/ppermute | solution.py:494
  4.4 28.6 %collective-permute-start.2 = (bf16[192,3072]{1,0:T(8,128)(2,1)}, bf16[192,3072]{1,0:T(8,128)(2,1)S(1)}, u32[]{:S(2)}, u32[]{:S(2)}) collective-permute-start(bf16[192,3072]{1,0:T(8,128)(2,1)} %bitcast.16), channel_id=1, source_target_pairs={{0,2},{1,3},{2,0},{3,1},{4,6},{5,7},{6,4},{7,5},{8,10},{9,11},{10,... | collective-permute-start | bytes 3538952 | tf_op jit(solution)/shard_map/ppermute | solution.py:494
  4.6 28.4 %collective-permute-start.4 = (bf16[192,3072]{1,0:T(8,128)(2,1)}, bf16[192,3072]{1,0:T(8,128)(2,1)S(1)}, u32[]{:S(2)}, u32[]{:S(2)}) collective-permute-start(bf16[192,3072]{1,0:T(8,128)(2,1)} %bitcast.17), channel_id=1, source_target_pairs={{0,1},{1,0},{2,3},{3,2},{4,5},{5,4},{6,7},{7,6},{8,9},{9,8},{10,11... | collective-permute-start | bytes 3538952 | tf_op jit(solution)/shard_map/ppermute | solution.py:494
  13.3 15.6 %copy-start.15 = (bf16[192,128]{1,0:T(8,128)(2,1)}, bf16[192,128]{1,0:T(8,128)(2,1)S(1)}, u32[]{:S(2)}) copy-start(bf16[192,128]{1,0:T(8,128)(2,1)S(1)} %collective-permute-done.gain_y) | copy-start | bytes 147460
  13.3 15.6 %copy-start.16 = (bf16[192,128]{1,0:T(8,128)(2,1)}, bf16[192,128]{1,0:T(8,128)(2,1)S(1)}, u32[]{:S(2)}) copy-start(bf16[192,128]{1,0:T(8,128)(2,1)S(1)} %collective-permute-done.1.gain_c) | copy-start | bytes 147460
  17.0 11.9 %collective-permute-start.3 = (bf16[192,128]{1,0:T(8,128)(2,1)S(1)}, bf16[192,128]{1,0:T(8,128)(2,1)S(1)}, u32[]{:S(2)}, u32[]{:S(2)}) collective-permute-start(bf16[192,128]{1,0:T(8,128)(2,1)S(1)} %collective-permute-done.gain_y), channel_id=1, source_target_pairs={{0,1},{1,0},{2,3},{3,2},{4,5},{5,4},{6,7},{7,6},{8,9},{9,8},{10,11... | collective-permute-start | bytes 147464 | tf_op jit(solution)/shard_map/ppermute | solution.py:494
  28.9 4.1 %copy-start.17 = (bf16[192,128]{1,0:T(8,128)(2,1)}, bf16[192,128]{1,0:T(8,128)(2,1)S(1)}, u32[]{:S(2)}) copy-start(bf16[192,128]{1,0:T(8,128)(2,1)S(1)} %collective-permute-done.3.gain_cy) | copy-start | bytes 147460
  33.0 2.9 %copy-start.7 = (bf16[192,3072]{1,0:T(8,128)(2,1)}, bf16[192,3072]{1,0:T(8,128)(2,1)S(1)}, u32[]{:S(2)}) copy-start(bf16[192,3072]{1,0:T(8,128)(2,1)S(1)} %collective-permute-done.2.flip_y) | copy-start | bytes 3538948
  33.0 2.8 %collective-permute-start.5 = (bf16[192,3072]{1,0:T(8,128)(2,1)S(1)}, bf16[192,3072]{1,0:T(8,128)(2,1)S(1)}, u32[]{:S(2)}, u32[]{:S(2)}) collective-permute-start(bf16[192,3072]{1,0:T(8,128)(2,1)S(1)} %collective-permute-done.2.flip_y), channel_id=1, source_target_pairs={{0,1},{1,0},{2,3},{3,2},{4,5},{5,4},{6,7},{7,6},{8,9},{9,8},{10,11... | collective-permute-start | bytes 3538952 | tf_op jit(solution)/shard_map/ppermute | solution.py:494
  33.1 2.8 %copy-start.8 = (bf16[192,3072]{1,0:T(8,128)(2,1)}, bf16[192,3072]{1,0:T(8,128)(2,1)S(1)}, u32[]{:S(2)}) copy-start(bf16[192,3072]{1,0:T(8,128)(2,1)S(1)} %collective-permute-done.4.flip_c) | copy-start | bytes 3538948
  35.9 1.0 copy-start.9
  60.8 60.0 %all-to-all-start = ((bf16[8,192,768]{2,1,0:T(8,128)(2,1)}), bf16[8,192,768]{2,1,0:T(8,128)(2,1)S(1)}, u32[]{:S(2)}, u32[]{:S(2)}) async-start(bf16[8,192,768]{2,1,0:T(8,128)(2,1)} %bitcast.29), calls=%async_computation | async-start | bytes 4718592 | tf_op jit(solution)/shard_map/all_to_all | solution.py:523
  66.6 39.1 %copy-start.13 = (f32[768,128]{1,0:T(8,128)S(1)}, f32[768,128]{1,0:T(8,128)}, u32[]{:S(2)}) copy-start(f32[768,128]{1,0:T(8,128)} %get-tuple-element.207) | copy-start | bytes 1179652
  107.9 10.0 %collective-permute-start.6 = (f32[2,192]{1,0:T(2,128)S(1)}, f32[2,192]{1,0:T(2,128)S(1)}, u32[]{:S(2)}, u32[]{:S(2)}) collective-permute-start(f32[2,192]{1,0:T(2,128)S(1)} %pad_maximum_fusion.2), channel_id=1, source_target_pairs={{0,1},{1,0},{2,3},{3,2},{4,5},{5,4},{6,7},{7,6},{8,9},{9,8},{10,11... | collective-permute-start | bytes 4616 | tf_op jit(solution)/shard_map/ppermute | solution.py:494
  117.9 10.3 %copy-start.14 = (f32[384,128]{1,0:T(8,128)S(1)}, f32[384,128]{1,0:T(8,128)}, u32[]{:S(2)}) copy-start(f32[384,128]{1,0:T(8,128)} %get-tuple-element.235) | copy-start | bytes 589828
  121.9 17.7 %collective-permute-start.8 = (bf16[1,2,400,1024]{3,2,1,0:T(8,128)(2,1)}, bf16[1,2,400,1024]{3,2,1,0:T(8,128)(2,1)S(1)}, u32[]{:S(2)}, u32[]{:S(2)}) collective-permute-start(bf16[1,2,400,1024]{3,2,1,0:T(8,128)(2,1)} %get-tuple-element.231), channel_id=1, source_target_pairs={{0,1},{1,0},{2,3},{3,2},{4,5},{5,4},{6,7},{7,6},{8,9},{9,8},{10,11... | collective-permute-start | bytes 4915208 | tf_op jit(solution)/shard_map/ppermute | solution.py:494
  121.9 20.3 %collective-permute-start.10 = (bf16[384,768]{1,0:T(8,128)(2,1)}, bf16[384,768]{1,0:T(8,128)(2,1)}, u32[]{:S(2)}, u32[]{:S(2)}) collective-permute-start(bf16[384,768]{1,0:T(8,128)(2,1)} %constant_dynamic-slice_fusion.4), channel_id=1, source_target_pairs={{0,4},{4,0},{8,12},{12,8},{16,20},{20,16},{24,28},{28,24},{1,5},{5... | collective-permute-start | bytes 1769480 | tf_op jit(solution)/shard_map/ppermute | solution.py:494
  123.4 17.5 %collective-permute-start.9 = (bf16[192,768]{1,0:T(8,128)(2,1)}, bf16[192,768]{1,0:T(8,128)(2,1)}, u32[]{:S(2)}, u32[]{:S(2)}) collective-permute-start(bf16[192,768]{1,0:T(8,128)(2,1)} %reduce_sum.75), channel_id=1, source_target_pairs={{0,16},{4,20},{8,24},{12,28},{16,0},{20,4},{24,8},{28,12},{1,17},{... | collective-permute-start | bytes 884744 | tf_op jit(solution)/shard_map/ppermute | solution.py:494
  126.4 13.1 %collective-permute-start.7 = (f32[192]{0:T(256)S(1)}, f32[192]{0:T(256)S(1)}, u32[]{:S(2)}, u32[]{:S(2)}) collective-permute-start(f32[192]{0:T(256)S(1)} %bitcast.31), channel_id=1, source_target_pairs={{0,2},{1,3},{2,0},{3,1},{4,6},{5,7},{6,4},{7,5},{8,10},{9,11},{10,... | collective-permute-start | bytes 2312 | tf_op jit(solution)/shard_map/ppermute | solution.py:494
  129.5 10.1 %copy-start.2 = (bf16[1,2,400,1024]{3,2,1,0:T(8,128)(2,1)S(1)}, bf16[1,2,400,1024]{3,2,1,0:T(8,128)(2,1)}, u32[]{:S(2)}) copy-start(bf16[1,2,400,1024]{3,2,1,0:T(8,128)(2,1)} %get-tuple-element.238.keep) | copy-start | bytes 4915204
  139.6 2.6 %copy-start.3 = (bf16[1,2,400,1024]{3,2,1,0:T(8,128)(2,1)}, bf16[1,2,400,1024]{3,2,1,0:T(8,128)(2,1)S(1)}, u32[]{:S(2)}) copy-start(bf16[1,2,400,1024]{3,2,1,0:T(8,128)(2,1)S(1)} %collective-permute-done.8.from_core) | copy-start | bytes 4915204
  139.7 1.2 copy-start.11
  139.7 2.5 %copy-start.10 = (bf16[768,768]{1,0:T(8,128)(2,1)S(1)}, bf16[768,768]{1,0:T(8,128)(2,1)}, u32[]{:S(2)}) copy-start(bf16[768,768]{1,0:T(8,128)(2,1)} %get-tuple-element.205) | copy-start | bytes 3538948
  142.2 15.7 %copy-start.4 = (bf16[384,768]{1,0:T(8,128)(2,1)}, bf16[384,768]{1,0:T(8,128)(2,1)S(1)}, u32[]{:S(2)}) copy-start(bf16[384,768]{1,0:T(8,128)(2,1)S(1)} %maximum_select_fusion.1) | copy-start | bytes 1769476
  144.4 14.1 %copy-start = (bf16[1,2,400,1024]{3,2,1,0:T(8,128)(2,1)S(1)}, bf16[1,2,400,1024]{3,2,1,0:T(8,128)(2,1)}, u32[]{:S(2)}) copy-start(bf16[1,2,400,1024]{3,2,1,0:T(8,128)(2,1)} %get-tuple-element.261.keep) | copy-start | bytes 4915204
  144.4 13.5 %collective-permute-start.12 = (bf16[1,2,400,1024]{3,2,1,0:T(8,128)(2,1)}, bf16[1,2,400,1024]{3,2,1,0:T(8,128)(2,1)}, u32[]{:S(2)}, u32[]{:S(2)}) collective-permute-start(bf16[1,2,400,1024]{3,2,1,0:T(8,128)(2,1)} %get-tuple-element.257), channel_id=1, source_target_pairs={{0,1},{1,0},{2,3},{3,2},{4,5},{5,4},{6,7},{7,6},{8,9},{9,8},{10,11... | collective-permute-start | bytes 4915208 | tf_op jit(solution)/shard_map/ppermute | solution.py:494
  144.4 23.0 %collective-permute-start.15 = (bf16[1,1,400,1024]{3,2,1,0:T(8,128)(2,1)}, bf16[1,1,400,1024]{3,2,1,0:T(8,128)(2,1)}, u32[]{:S(2)}, u32[]{:S(2)}) collective-permute-start(bf16[1,1,400,1024]{3,2,1,0:T(8,128)(2,1)} %add_convert_fusion.2), channel_id=1, source_target_pairs={{0,2},{1,3},{2,0},{3,1},{4,6},{5,7},{6,4},{7,5},{8,10},{9,11},{10,... | collective-permute-start | bytes 2457608 | tf_op jit(solution)/shard_map/ppermute | solution.py:494
  145.7 16.3 %collective-permute-start.13 = (bf16[384,768]{1,0:T(8,128)(2,1)S(1)}, bf16[384,768]{1,0:T(8,128)(2,1)}, u32[]{:S(2)}, u32[]{:S(2)}) collective-permute-start(bf16[384,768]{1,0:T(8,128)(2,1)S(1)} %maximum_select_fusion.1), channel_id=1, source_target_pairs={{0,8},{4,12},{8,0},{12,4},{16,24},{20,28},{24,16},{28,20},{1,9},{5... | collective-permute-start | bytes 1769480 | tf_op jit(solution)/shard_map/ppermute | solution.py:494
  146.5 11.4 %collective-permute-start.11 = (f32[1536]{0:T(1024)S(1)}, f32[1536]{0:T(1024)S(1)}, u32[]{:S(2)}, u32[]{:S(2)}) collective-permute-start(f32[1536]{0:T(1024)S(1)} %concatenate.35), channel_id=1, source_target_pairs={{0,4},{4,0},{8,12},{12,8},{16,20},{20,16},{24,28},{28,24},{1,5},{5... | collective-permute-start | bytes 18440 | tf_op jit(solution)/shard_map/ppermute | solution.py:494
  146.5 20.9 %collective-permute-start.14 = (bf16[192,768]{1,0:T(8,128)(2,1)}, bf16[192,768]{1,0:T(8,128)(2,1)S(1)}, u32[]{:S(2)}, u32[]{:S(2)}) collective-permute-start(bf16[192,768]{1,0:T(8,128)(2,1)} %get-tuple-element.269), channel_id=1, source_target_pairs={{0,8},{4,12},{8,0},{12,4},{16,24},{20,28},{24,16},{28,20},{1,9},{5... | collective-permute-start | bytes 884744 | tf_op jit(solution)/shard_map/ppermute | solution.py:494
  157.9 4.0 %copy-start.5 = (bf16[384,768]{1,0:T(8,128)(2,1)S(1)}, bf16[384,768]{1,0:T(8,128)(2,1)}, u32[]{:S(2)}) copy-start(bf16[384,768]{1,0:T(8,128)(2,1)} %copy-done.4) | copy-start | bytes 1769476
  167.4 7.5 %collective-permute-start.16 = (bf16[1,2,400,1024]{3,2,1,0:T(8,128)(2,1)}, bf16[1,2,400,1024]{3,2,1,0:T(8,128)(2,1)}, u32[]{:S(2)}, u32[]{:S(2)}) collective-permute-start(bf16[1,2,400,1024]{3,2,1,0:T(8,128)(2,1)} %get-tuple-element.284), channel_id=1, source_target_pairs={{0,1},{1,0},{2,3},{3,2},{4,5},{5,4},{6,7},{7,6},{8,9},{9,8},{10,11... | collective-permute-start | bytes 4915208 | tf_op jit(solution)/shard_map/ppermute | solution.py:494
  167.4 7.5 %collective-permute-start.17 = (f32[1536]{0:T(1024)}, f32[1536]{0:T(1024)}, u32[]{:S(2)}, u32[]{:S(2)}) collective-permute-start(f32[1536]{0:T(1024)} %add.114), channel_id=1, source_target_pairs={{0,8},{4,12},{8,0},{12,4},{16,24},{20,28},{24,16},{28,20},{1,9},{5... | collective-permute-start | bytes 18440 | tf_op jit(solution)/shard_map/ppermute | solution.py:494
  168.3 28.2 %collective-permute-start.22 = (bf16[768,768]{1,0:T(8,128)(2,1)S(1)}, bf16[768,768]{1,0:T(8,128)(2,1)}, u32[]{:S(2)}, u32[]{:S(2)}) collective-permute-start(bf16[768,768]{1,0:T(8,128)(2,1)S(1)} %maximum_select_fusion), channel_id=1, source_target_pairs={{0,4},{4,0},{8,12},{12,8},{16,20},{20,16},{24,28},{28,24},{1,5},{5... | collective-permute-start | bytes 3538952 | tf_op jit(solution)/shard_map/ppermute | solution.py:494
  169.0 10.2 %collective-permute-start.18 = (bf16[96,768]{1,0:T(8,128)(2,1)}, bf16[96,768]{1,0:T(8,128)(2,1)S(1)}, u32[]{:S(2)}, u32[]{:S(2)}) collective-permute-start(bf16[96,768]{1,0:T(8,128)(2,1)} %add_convert_fusion.7), channel_id=1, source_target_pairs={{0,16},{4,20},{8,24},{12,28},{16,0},{20,4},{24,8},{28,12},{1,17},{... | collective-permute-start | bytes 442376 | tf_op jit(solution)/shard_map/ppermute | solution.py:494
  170.5 20.2 %collective-permute-start.21 = (bf16[1,1,400,1024]{3,2,1,0:T(8,128)(2,1)}, bf16[1,1,400,1024]{3,2,1,0:T(8,128)(2,1)}, u32[]{:S(2)}, u32[]{:S(2)}) collective-permute-start(bf16[1,1,400,1024]{3,2,1,0:T(8,128)(2,1)} %add_convert_fusion.1), channel_id=1, source_target_pairs={{0,2},{1,3},{2,0},{3,1},{4,6},{5,7},{6,4},{7,5},{8,10},{9,11},{10,... | collective-permute-start | bytes 2457608 | tf_op jit(solution)/shard_map/ppermute | solution.py:494
  171.8 3.2 %copy-start.1 = (bf16[1,2,400,1024]{3,2,1,0:T(8,128)(2,1)S(1)}, bf16[1,2,400,1024]{3,2,1,0:T(8,128)(2,1)}, u32[]{:S(2)}) copy-start(bf16[1,2,400,1024]{3,2,1,0:T(8,128)(2,1)} %get-tuple-element.273.keep) | copy-start | bytes 4915204
  179.3 8.1 %collective-permute-start.20 = (bf16[96,768]{1,0:T(8,128)(2,1)S(1)}, bf16[96,768]{1,0:T(8,128)(2,1)S(1)}, u32[]{:S(2)}, u32[]{:S(2)}) collective-permute-start(bf16[96,768]{1,0:T(8,128)(2,1)S(1)} %add_convert_fusion.5), channel_id=1, source_target_pairs={{0,16},{4,20},{8,24},{12,28},{16,0},{20,4},{24,8},{28,12},{1,17},{... | collective-permute-start | bytes 442376 | tf_op jit(solution)/shard_map/ppermute | solution.py:494
  179.4 8.0 %collective-permute-start.19 = (f32[1536]{0:T(1024)S(1)}, f32[1536]{0:T(1024)S(1)}, u32[]{:S(2)}, u32[]{:S(2)}) collective-permute-start(f32[1536]{0:T(1024)S(1)} %add.117), channel_id=1, source_target_pairs={{0,16},{4,20},{8,24},{12,28},{16,0},{20,4},{24,8},{28,12},{1,17},{... | collective-permute-start | bytes 18440 | tf_op jit(solution)/shard_map/ppermute | solution.py:494
  187.5 9.1 %collective-permute-start.23 = (bf16[192,768]{1,0:T(8,128)(2,1)S(1)}, bf16[192,768]{1,0:T(8,128)(2,1)S(1)}, u32[]{:S(2)}, u32[]{:S(2)}) collective-permute-start(bf16[192,768]{1,0:T(8,128)(2,1)S(1)} %maximum_select_fusion.3), channel_id=1, source_target_pairs={{0,8},{4,12},{8,0},{12,4},{16,24},{20,28},{24,16},{28,20},{1,9},{5... | collective-permute-start | bytes 884744 | tf_op jit(solution)/shard_map/ppermute | solution.py:494
  187.5 20.6 %collective-permute-start.24 = (bf16[1,1,400,1024]{3,2,1,0:T(8,128)(2,1)}, bf16[1,1,400,1024]{3,2,1,0:T(8,128)(2,1)S(1)}, u32[]{:S(2)}, u32[]{:S(2)}) collective-permute-start(bf16[1,1,400,1024]{3,2,1,0:T(8,128)(2,1)} %add_convert_fusion), channel_id=1, source_target_pairs={{0,2},{1,3},{2,0},{3,1},{4,6},{5,7},{6,4},{7,5},{8,10},{9,11},{10,... | collective-permute-start | bytes 2457608 | tf_op jit(solution)/shard_map/ppermute | solution.py:494
  196.7 15.4 %collective-permute-start.25 = (bf16[384,768]{1,0:T(8,128)(2,1)S(1)}, bf16[384,768]{1,0:T(8,128)(2,1)S(1)}, u32[]{:S(2)}, u32[]{:S(2)}) collective-permute-start(bf16[384,768]{1,0:T(8,128)(2,1)S(1)} %maximum_select_fusion.2), channel_id=1, source_target_pairs={{0,4},{4,0},{8,12},{12,8},{16,20},{20,16},{24,28},{28,24},{1,5},{5... | collective-permute-start | bytes 1769480 | tf_op jit(solution)/shard_map/ppermute | solution.py:494
  208.1 0.9 copy-start.12

commit v11 on v10

--- a/solution.py
+++ b/solution.py
@@ -780,9 +780,9 @@
         if near:
             now = near + chain + rest
         elif left == 2:
-            now = chain + across[:1] + wide + rest
+            now = chain + across[:1] + rest
         elif left == 1:
-            now = across + wide + rest or chain
+            now = wide + rest or across[:1] or chain
         else:
             now = chain + rest or flying
         final = [f for f in now if f[0] is mix_sum]

time: 216 us -> 216 us (level)
  waiting for transfers between devices: 29.3 us -> 32.5 us
  Pallas kernels: 113 us -> 110 us
    pallas_call x1, Pallas kernels: 38.3 us -> 36 us  [attention_call(): pl.pallas_call(attention_kernel, grid_spec=grid_spec, out_shape=[jax.Shap...]
    all_to_all x1, waiting for transfers between devices: 2.88 us -> 5.14 us  [move(): return lax.all_to_all(send, 'dp', 0, 0, tiled=True)]
  transfers between devices with their start and end apart: 27 -> 27, of which waited for: 10 -> 11; matrix products, arithmetic and copies ran while one was open for 17% -> 17% of each run, Pallas kernels for 41% -> 40%
where the time goes in v11:
time: 216 us; the launch traced here: 214 us
  Pallas kernels  110 us (51%)
  waiting for transfers between devices  32.5 us (15%)
  other arithmetic  31.8 us (15%)
  starting transfers between devices  26.1 us (12%)
  local copies, waits for them, and re-layouts  12.5 us (6%)
    pallas_call x1, Pallas kernels, attention_call(): pl.pallas_call(attention_kernel, grid_spec=grid_spec, out_shape=[jax.Shap...  36 us
    pallas_call x3, Pallas kernels, project_call(): pl.pallas_call(project_kernel, grid_spec=grid_spec, out_shape=[jax.ShapeD...  29.8 us
    ppermute x26, waiting for transfers between devices, flip(): return lax.ppermute(value, axis, [(i, i ^ bit) for i in range(size)])  27.3 us
    pallas_call x1, Pallas kernels, mlp_call(): pl.pallas_call(functools.partial(mlp_kernel, pieces_order), grid_spec=gri...  23.9 us
    ppermute x26, starting transfers between devices, flip(): return lax.ppermute(value, axis, [(i, i ^ bit) for i in range(size)])  20.3 us
    pallas_call x1, Pallas kernels, early_call(): pl.pallas_call(early_kernel, grid=(tokens // block,), in_specs=[pl.BlockS...  11.2 us
    pallas_call x3, Pallas kernels, finish_call(): pl.pallas_call(finish_kernel, grid=(size * steps,), in_specs=[packed, pac...  9.4 us
    convert_element_type x3, other arithmetic, take(): (self.keep[:, 1:].astype(F32) + arrived[:, 1:].astype(F32)).astype(BF16)  6.04 us
  transfers between devices with their start and end apart: 27, of which 11 were waited for; matrix products, arithmetic and copies ran while one was open for 17% of the time, Pallas kernels for 40%

profile of v11, /device:TPU:0, one launch (start us, length us, event | category | flops | bytes accessed | tf_op | source)
XLA Modules:
  0.0 214.2 jit_solution(15863190011491052348)
XLA Ops:
  0.6 0.7 broadcast_in_dim.53.gain_own.gain
  1.4 3.0 %collective-permute-start = (bf16[192,128]{1,0:T(8,128)(2,1)S(1)}, bf16[192,128]{1,0:T(8,128)(2,1)S(1)}, u32[]{:S(2)}, u32[]{:S(2)}) collective-permute-start(bf16[192,128]{1,0:T(8,128)(2,1)S(1)} %broadcast_in_dim.53.gain_own.gain), channel_id=1, source_target_pairs={{0,2},{1,3},{2,0},{3,1},{4,6},{5,7},{6,4},{7,5},{8,10},{9,11},{10,... | collective-permute-start | bytes 147464 | tf_op jit(solution)/shard_map/ppermute | solution.py:494
  4.9 0.8 slice.65
  5.8 0.8 slice.66
  6.6 1.0 convert_reduce_fusion
  7.6 1.4 fusion.4.mask_q
  8.9 1.5 select_convert_fusion.2.mask_k
  10.4 0.8 fusion.1.pick
  11.2 1.2 xor_multiply_fusion.place
  12.4 0.8 reshape.72
  13.3 0.8 broadcast_in_dim.27.gains
  14.1 1.5 broadcast_in_dim.24.up_bias
  15.7 1.4 broadcast_in_dim.52.bias
  17.8 11.2 %early.1 = (bf16[3,768,1024]{2,1,0:T(8,128)(2,1)}, bf16[3,192,1024]{2,1,0:T(8,128)(2,1)}, bf16[192,3072]{1,0:T(8,128)(2,1)}, f32[192,128]{1,0:T(8,128)}) custom-call(bf16[3072,768]{1,0:T(8,128)(2,1)} %cot.5, bf16[768,768]{1,0:T(8,128)(2,1)} %down.7, bf16[192,768]{1,0:T(8,128)(2,1)} %attn.7, bf16[192,768]{1,0:T(8,128)(2,1)} %fusion.1.pick), custom_call_target="tpu_custom_call" | custom-call | flops 10000 | bytes 12000 | tf_op jit(solution)/shard_map/early/pallas_call | solution.py:63
  29.0 4.0 %collective-permute-done.2.flip_y = bf16[192,3072]{1,0:T(8,128)(2,1)S(1)} collective-permute-done((bf16[192,3072]{1,0:T(8,128)(2,1)}, bf16[192,3072]{1,0:T(8,128)(2,1)S(1)}, u32[]{:S(2)}, u32[]{:S(2)}) %collective-permute-start.2) | collective-permute-done | bytes 1179680 | tf_op jit(solution)/shard_map/ppermute | solution.py:494
  33.1 2.8 %collective-permute-done.5.flip_cy = bf16[192,3072]{1,0:T(8,128)(2,1)S(1)} collective-permute-done((bf16[192,3072]{1,0:T(8,128)(2,1)S(1)}, bf16[192,3072]{1,0:T(8,128)(2,1)S(1)}, u32[]{:S(2)}, u32[]{:S(2)}) %collective-permute-start.5) | collective-permute-done | bytes 1179680 | tf_op jit(solution)/shard_map/ppermute | solution.py:494
  35.9 1.0 copy-done.9
  36.9 23.9 %mlp.1 = (bf16[3,768,1024]{2,1,0:T(8,128)(2,1)}, bf16[3,768,1024]{2,1,0:T(8,128)(2,1)}, bf16[3,768,1024]{2,1,0:T(8,128)(2,1)}, f32[8,3072]{1,0:T(8,128)}, f32[76...) custom-call(s32[4]{0:T(128)} %xor_multiply_fusion.place, ...), custom_call_target="tpu_custom_call" | custom-call | flops 20000 | bytes 30000 | tf_op jit(solution)/shard_map/mlp/pallas_call | solution.py:188
  60.8 5.8 %all-to-all-start = ((bf16[8,192,768]{2,1,0:T(8,128)(2,1)}), bf16[8,192,768]{2,1,0:T(8,128)(2,1)S(1)}, u32[]{:S(2)}, u32[]{:S(2)}) async-start(bf16[8,192,768]{2,1,0:T(8,128)(2,1)} %bitcast.29), calls=%async_computation | async-start | bytes 4718592 | tf_op jit(solution)/shard_map/all_to_all | solution.py:523
  66.6 36.0 %attention.1 = (bf16[3,192,1024]{2,1,0:T(8,128)(2,1)}, bf16[3,576,1024]{2,1,0:T(8,128)(2,1)}, f32[384,128]{1,0:T(8,128)}, f32[1,768]{1,0:T(1,128)}, bf16[768,768]{1,0:T(8,128)(2,1)}) custom-call(s32[12]{0:T(128)} %get-tuple-element.197.first, s32[12]{0:T(128)} %get-tuple-element.198.count, bf16[3,768,1024]{2,1,0:T(8,128)(2,1)} %get-tuple-element.201.normed, ...), custom_call_target="tpu_custom_call" | custom-call | flops 18000 | bytes 5000 | tf_op jit(solution)/shard_map/attention/pallas_call | solution.py:360
  102.7 0.7 reduce.1
  103.7 1.9 constant_dynamic-slice_fusion.4
  105.7 9.9 %project.3 = (bf16[1,2,400,1024]{3,2,1,0:T(8,128)(2,1)}, bf16[1,2,400,1024]{3,2,1,0:T(8,128)(2,1)}) custom-call(s32[1]{0:T(128)} %bitcast.shard, bf16[3,768,1024]{2,1,0:T(8,128)(2,1)} %get-tuple-element.196.active, bf16[3,192,1024]{2,1,0:T(8,128)(2,1)} %get-tuple-element.256.attended, bf16[3,768,1024]{2,1,0:T(8,128)(2,1)} %get-tuple-element.213.d_pre, ...), custom_call_target="tpu_custom_call" | custom-call | flops 8000 | bytes 16000 | tf_op jit(solution)/shard_map/project/pallas_call | solution.py:435
  115.7 5.1 %all-to-all-done = bf16[8,192,768]{2,1,0:T(8,128)(2,1)S(1)} async-done(((bf16[8,192,768]{2,1,0:T(8,128)(2,1)}), bf16[8,192,768]{2,1,0:T(8,128)(2,1)S(1)}, u32[]{:S(2)}, u32[]{:S(2)}) %all-to-all-start) | async-done | bytes 2359328 | tf_op jit(solution)/shard_map/all_to_all | solution.py:523
  120.8 1.1 reduce_sum.75
  121.9 1.5 collective-permute-start.10
  123.4 0.8 collective-permute-start.9
  124.2 0.8 collective-permute-start.7
  125.0 1.0 reduce_sum.78
  126.2 1.2 reduce_sum.77
  127.3 10.0 %project.4 = (bf16[1,2,400,1024]{3,2,1,0:T(8,128)(2,1)}, bf16[1,2,400,1024]{3,2,1,0:T(8,128)(2,1)}) custom-call(s32[1]{0:T(128)} %bitcast.shard, bf16[3,768,1024]{2,1,0:T(8,128)(2,1)} %get-tuple-element.196.active, bf16[3,192,1024]{2,1,0:T(8,128)(2,1)} %get-tuple-element.256.attended, bf16[3,768,1024]{2,1,0:T(8,128)(2,1)} %get-tuple-element.213.d_pre, ...), custom_call_target="tpu_custom_call" | custom-call | flops 8000 | bytes 16000 | tf_op jit(solution)/shard_map/project/pallas_call | solution.py:435
  137.5 1.3 add_convert_fusion.2
  138.7 1.3 collective-permute-done.9
  140.0 1.3 maximum_select_fusion.1
  141.3 2.2 %add_convert_fusion.3 = (bf16[192,768]{1,0:T(8,128)(2,1)S(1)}, bf16[192,768]{1,0:T(8,128)(2,1)}) fusion(bf16[384,768]{1,0:T(8,128)(2,1)} %collective-permute-done.10, s32[]{:T(128)S(6)} %mul.38, bf16[768,768]{1,0:T(8,128)(2,1)S(1)} %copy-done.10, s32[]{:T(128)S(6)} %dynamic_slice.55, s32[]{:T(128)S(6)} %select_n.103, s32[]{:T(128)S(6)} %dynamic_slice.47), kind=kLoop, calls=%fused_computation.12 | loop fusion | flops 1179648 | bytes 1769488 | tf_op jit(solution)/shard_map/convert_element_type | solution.py:550
  143.5 0.8 collective-permute-start.15
  144.3 0.9 collective-permute-start.13
  145.2 2.0 collective-permute-start.11
  147.3 9.9 %project.5 = (bf16[1,2,400,1024]{3,2,1,0:T(8,128)(2,1)}, bf16[1,2,400,1024]{3,2,1,0:T(8,128)(2,1)}) custom-call(s32[1]{0:T(128)} %bitcast.shard, bf16[3,768,1024]{2,1,0:T(8,128)(2,1)} %get-tuple-element.196.active, bf16[3,192,1024]{2,1,0:T(8,128)(2,1)} %get-tuple-element.256.attended, bf16[3,768,1024]{2,1,0:T(8,128)(2,1)} %get-tuple-element.213.d_pre, ...), custom_call_target="tpu_custom_call" | custom-call | flops 8000 | bytes 16000 | tf_op jit(solution)/shard_map/project/pallas_call | solution.py:435
  157.8 2.4 %add_convert_fusion.1 = bf16[1,1,400,1024]{3,2,1,0:T(8,128)(2,1)} fusion(bf16[1,2,400,1024]{3,2,1,0:T(8,128)(2,1)} %collective-permute-done.12.from_core, bf16[1,2,400,1024]{3,2,1,0:T(8,128)(2,1)S(1)} %copy-done), kind=kLoop, calls=%fused_computation.2 | loop fusion | flops 1638400 | bytes 2457600 | tf_op jit(solution)/shard_map/convert_element_type | solution.py:590
  160.6 1.8 maximum_select_fusion
  162.4 3.7 %collective-permute-done.14 = bf16[192,768]{1,0:T(8,128)(2,1)S(1)} collective-permute-done((bf16[192,768]{1,0:T(8,128)(2,1)}, bf16[192,768]{1,0:T(8,128)(2,1)S(1)}, u32[]{:S(2)}, u32[]{:S(2)}) %collective-permute-start.14) | collective-permute-done | bytes 294944 | tf_op jit(solution)/shard_map/ppermute | solution.py:494
  166.1 0.9 collective-permute-start.17
  167.7 2.1 collective-permute-start.18
  169.9 0.8 collective-permute-start.21
  170.6 3.1 %finish.3 = (bf16[192,3072]{1,0:T(8,128)(2,1)}, f32[192,3072]{1,0:T(8,128)}) custom-call(bf16[1,2,400,1024]{3,2,1,0:T(8,128)(2,1)} %get-tuple-element.242.keep, bf16[1,2,400,1024]{3,2,1,0:T(8,128)(2,1)} %copy-done.3, bf16[1,1,400,1024]{3,2,1,0:T(8,128)(2,1)} %collective-permute-done.15.from_y, bf16[192,3072]{1,0:T(8,128)(2,1)} %bitcast.19, ...), custom_call_target="tpu_custom_call" | custom-call | flops 3000 | bytes 5000 | tf_op jit(solution)/shard_map/finish/pallas_call | solution.py:471
  173.8 2.4 %add_convert_fusion = bf16[1,1,400,1024]{3,2,1,0:T(8,128)(2,1)} fusion(bf16[1,2,400,1024]{3,2,1,0:T(8,128)(2,1)} %collective-permute-done.16.from_core, bf16[1,2,400,1024]{3,2,1,0:T(8,128)(2,1)S(1)} %copy-done.1), kind=kLoop, calls=%fused_computation.1 | loop fusion | flops 1638400 | bytes 2457600 | tf_op jit(solution)/shard_map/convert_element_type | solution.py:590
  176.2 0.7 add.117
  176.9 1.0 collective-permute-done.18
  178.0 1.9 collective-permute-start.20
  179.9 1.1 collective-permute-start.19
  181.0 5.9 %collective-permute-done.19 = f32[1536]{0:T(1024)S(1)} collective-permute-done((f32[1536]{0:T(1024)S(1)}, f32[1536]{0:T(1024)S(1)}, u32[]{:S(2)}, u32[]{:S(2)}) %collective-permute-start.19) | collective-permute-done | bytes 6176 | tf_op jit(solution)/shard_map/ppermute | solution.py:494
  187.0 1.3 collective-permute-start.24
  189.7 0.8 collective-permute-done.21.from_y
  190.4 5.5 %collective-permute-done.22 = bf16[192,768]{1,0:T(8,128)(2,1)S(1)} collective-permute-done((bf16[192,768]{1,0:T(8,128)(2,1)S(1)}, bf16[192,768]{1,0:T(8,128)(2,1)S(1)}, u32[]{:S(2)}, u32[]{:S(2)}) %collective-permute-start.22) | collective-permute-done | bytes 294944 | tf_op jit(solution)/shard_map/ppermute | solution.py:494
  196.1 1.6 collective-permute-start.25
  197.7 1.3 fusion.6
  199.0 3.1 %finish.4 = (bf16[192,3072]{1,0:T(8,128)(2,1)}, f32[192,3072]{1,0:T(8,128)}) custom-call(bf16[1,2,400,1024]{3,2,1,0:T(8,128)(2,1)} %get-tuple-element.265.keep, bf16[1,2,400,1024]{3,2,1,0:T(8,128)(2,1)} %collective-permute-done.12.from_core, bf16[1,1,400,1024]{3,2,1,0:T(8,128)(2,1)} %collective-permute-done.21.from_y, ...), custom_call_target="tpu_custom_call", output_to_operand_aliasing={{0}: (8, {}), {1}: (9, {})} | custom-call | flops 3000 | bytes 5000 | tf_op jit(solution)/shard_map/finish/pallas_call | solution.py:471
  202.1 3.8 %select_convert_fusion = (f32[768,768]{1,0:T(8,128)}, f32[768,768]{1,0:T(8,128)}) fusion(bf16[768,768]{1,0:T(8,128)(2,1)S(1)} %maximum_select_fusion, bf16[768,768]{1,0:T(8,128)(2,1)} %collective-permute-done.23, pred[]{:T(512)S(6)} %gt.7), kind=kLoop, calls=%fused_computation.5 | loop fusion | flops 2359296 | bytes 7077889 | tf_op jit(solution)/shard_map/convert_element_type | solution.py:795
  205.9 1.8 collective-permute-done.24.from_y
  207.7 0.9 copy-done.12
  208.6 3.1 %finish.5 = (bf16[192,3072]{1,0:T(8,128)(2,1)}, f32[192,3072]{1,0:T(8,128)}) custom-call(bf16[1,2,400,1024]{3,2,1,0:T(8,128)(2,1)} %get-tuple-element.277.keep, bf16[1,2,400,1024]{3,2,1,0:T(8,128)(2,1)} %collective-permute-done.16.from_core, bf16[1,1,400,1024]{3,2,1,0:T(8,128)(2,1)} %copy-done.12, ...), custom_call_target="tpu_custom_call", output_to_operand_aliasing={{0}: (8, {}), {1}: (9, {})} | custom-call | flops 3000 | bytes 5000 | tf_op jit(solution)/shard_map/finish/pallas_call | solution.py:471
  211.7 0.9 fusion.2
  212.9 1.4 convert_bitcast_fusion
  (90 shorter events, 5.9 us)
Async XLA Ops:
  1.4 27.6 %copy-start.6 = (bf16[192,128]{1,0:T(8,128)(2,1)}, bf16[192,128]{1,0:T(8,128)(2,1)S(1)}, u32[]{:S(2)}) copy-start(bf16[192,128]{1,0:T(8,128)(2,1)S(1)} %broadcast_in_dim.53.gain_own.gain) | copy-start | bytes 147460
  1.4 11.9 %collective-permute-start = (bf16[192,128]{1,0:T(8,128)(2,1)S(1)}, bf16[192,128]{1,0:T(8,128)(2,1)S(1)}, u32[]{:S(2)}, u32[]{:S(2)}) collective-permute-start(bf16[192,128]{1,0:T(8,128)(2,1)S(1)} %broadcast_in_dim.53.gain_own.gain), channel_id=1, source_target_pairs={{0,2},{1,3},{2,0},{3,1},{4,6},{5,7},{6,4},{7,5},{8,10},{9,11},{10,... | collective-permute-start | bytes 147464 | tf_op jit(solution)/shard_map/ppermute | solution.py:494
  4.4 8.9 %collective-permute-start.1 = (bf16[192,128]{1,0:T(8,128)(2,1)S(1)}, bf16[192,128]{1,0:T(8,128)(2,1)S(1)}, u32[]{:S(2)}, u32[]{:S(2)}) collective-permute-start(bf16[192,128]{1,0:T(8,128)(2,1)S(1)} %broadcast_in_dim.53.gain_own.gain), channel_id=1, source_target_pairs={{0,1},{1,0},{2,3},{3,2},{4,5},{5,4},{6,7},{7,6},{8,9},{9,8},{10,11... | collective-permute-start | bytes 147464 | tf_op jit(solution)/shard_map/ppermute | solution.py:494
  4.4 28.6 %collective-permute-start.2 = (bf16[192,3072]{1,0:T(8,128)(2,1)}, bf16[192,3072]{1,0:T(8,128)(2,1)S(1)}, u32[]{:S(2)}, u32[]{:S(2)}) collective-permute-start(bf16[192,3072]{1,0:T(8,128)(2,1)} %bitcast.16), channel_id=1, source_target_pairs={{0,2},{1,3},{2,0},{3,1},{4,6},{5,7},{6,4},{7,5},{8,10},{9,11},{10,... | collective-permute-start | bytes 3538952 | tf_op jit(solution)/shard_map/ppermute | solution.py:494
  4.6 28.4 %collective-permute-start.4 = (bf16[192,3072]{1,0:T(8,128)(2,1)}, bf16[192,3072]{1,0:T(8,128)(2,1)S(1)}, u32[]{:S(2)}, u32[]{:S(2)}) collective-permute-start(bf16[192,3072]{1,0:T(8,128)(2,1)} %bitcast.17), channel_id=1, source_target_pairs={{0,1},{1,0},{2,3},{3,2},{4,5},{5,4},{6,7},{7,6},{8,9},{9,8},{10,11... | collective-permute-start | bytes 3538952 | tf_op jit(solution)/shard_map/ppermute | solution.py:494
  13.3 15.6 %copy-start.15 = (bf16[192,128]{1,0:T(8,128)(2,1)}, bf16[192,128]{1,0:T(8,128)(2,1)S(1)}, u32[]{:S(2)}) copy-start(bf16[192,128]{1,0:T(8,128)(2,1)S(1)} %collective-permute-done.gain_y) | copy-start | bytes 147460
  13.3 15.6 %copy-start.16 = (bf16[192,128]{1,0:T(8,128)(2,1)}, bf16[192,128]{1,0:T(8,128)(2,1)S(1)}, u32[]{:S(2)}) copy-start(bf16[192,128]{1,0:T(8,128)(2,1)S(1)} %collective-permute-done.1.gain_c) | copy-start | bytes 147460
  17.0 11.9 %collective-permute-start.3 = (bf16[192,128]{1,0:T(8,128)(2,1)S(1)}, bf16[192,128]{1,0:T(8,128)(2,1)S(1)}, u32[]{:S(2)}, u32[]{:S(2)}) collective-permute-start(bf16[192,128]{1,0:T(8,128)(2,1)S(1)} %collective-permute-done.gain_y), channel_id=1, source_target_pairs={{0,1},{1,0},{2,3},{3,2},{4,5},{5,4},{6,7},{7,6},{8,9},{9,8},{10,11... | collective-permute-start | bytes 147464 | tf_op jit(solution)/shard_map/ppermute | solution.py:494
  29.0 4.0 %copy-start.17 = (bf16[192,128]{1,0:T(8,128)(2,1)}, bf16[192,128]{1,0:T(8,128)(2,1)S(1)}, u32[]{:S(2)}) copy-start(bf16[192,128]{1,0:T(8,128)(2,1)S(1)} %collective-permute-done.3.gain_cy) | copy-start | bytes 147460
  33.0 2.9 %copy-start.7 = (bf16[192,3072]{1,0:T(8,128)(2,1)}, bf16[192,3072]{1,0:T(8,128)(2,1)S(1)}, u32[]{:S(2)}) copy-start(bf16[192,3072]{1,0:T(8,128)(2,1)S(1)} %collective-permute-done.2.flip_y) | copy-start | bytes 3538948
  33.0 2.8 %collective-permute-start.5 = (bf16[192,3072]{1,0:T(8,128)(2,1)S(1)}, bf16[192,3072]{1,0:T(8,128)(2,1)S(1)}, u32[]{:S(2)}, u32[]{:S(2)}) collective-permute-start(bf16[192,3072]{1,0:T(8,128)(2,1)S(1)} %collective-permute-done.2.flip_y), channel_id=1, source_target_pairs={{0,1},{1,0},{2,3},{3,2},{4,5},{5,4},{6,7},{7,6},{8,9},{9,8},{10,11... | collective-permute-start | bytes 3538952 | tf_op jit(solution)/shard_map/ppermute | solution.py:494
  33.1 2.8 %copy-start.8 = (bf16[192,3072]{1,0:T(8,128)(2,1)}, bf16[192,3072]{1,0:T(8,128)(2,1)S(1)}, u32[]{:S(2)}) copy-start(bf16[192,3072]{1,0:T(8,128)(2,1)S(1)} %collective-permute-done.4.flip_c) | copy-start | bytes 3538948
  35.9 1.0 copy-start.9
  60.8 60.0 %all-to-all-start = ((bf16[8,192,768]{2,1,0:T(8,128)(2,1)}), bf16[8,192,768]{2,1,0:T(8,128)(2,1)S(1)}, u32[]{:S(2)}, u32[]{:S(2)}) async-start(bf16[8,192,768]{2,1,0:T(8,128)(2,1)} %bitcast.29), calls=%async_computation | async-start | bytes 4718592 | tf_op jit(solution)/shard_map/all_to_all | solution.py:523
  66.6 36.8 %copy-start.13 = (f32[768,128]{1,0:T(8,128)S(1)}, f32[768,128]{1,0:T(8,128)}, u32[]{:S(2)}) copy-start(f32[768,128]{1,0:T(8,128)} %get-tuple-element.211) | copy-start | bytes 1179652
  105.7 10.0 %collective-permute-start.6 = (f32[2,192]{1,0:T(2,128)S(1)}, f32[2,192]{1,0:T(2,128)S(1)}, u32[]{:S(2)}, u32[]{:S(2)}) collective-permute-start(f32[2,192]{1,0:T(2,128)S(1)} %pad_maximum_fusion.2), channel_id=1, source_target_pairs={{0,1},{1,0},{2,3},{3,2},{4,5},{5,4},{6,7},{7,6},{8,9},{9,8},{10,11... | collective-permute-start | bytes 4616 | tf_op jit(solution)/shard_map/ppermute | solution.py:494
  115.6 10.4 %copy-start.14 = (f32[384,128]{1,0:T(8,128)S(1)}, f32[384,128]{1,0:T(8,128)}, u32[]{:S(2)}) copy-start(f32[384,128]{1,0:T(8,128)} %get-tuple-element.239) | copy-start | bytes 589828
  121.9 15.5 %collective-permute-start.8 = (bf16[1,2,400,1024]{3,2,1,0:T(8,128)(2,1)}, bf16[1,2,400,1024]{3,2,1,0:T(8,128)(2,1)S(1)}, u32[]{:S(2)}, u32[]{:S(2)}) collective-permute-start(bf16[1,2,400,1024]{3,2,1,0:T(8,128)(2,1)} %get-tuple-element.235), channel_id=1, source_target_pairs={{0,1},{1,0},{2,3},{3,2},{4,5},{5,4},{6,7},{7,6},{8,9},{9,8},{10,11... | collective-permute-start | bytes 4915208 | tf_op jit(solution)/shard_map/ppermute | solution.py:494
  121.9 19.4 %collective-permute-start.10 = (bf16[384,768]{1,0:T(8,128)(2,1)}, bf16[384,768]{1,0:T(8,128)(2,1)}, u32[]{:S(2)}, u32[]{:S(2)}) collective-permute-start(bf16[384,768]{1,0:T(8,128)(2,1)} %constant_dynamic-slice_fusion.4), channel_id=1, source_target_pairs={{0,4},{4,0},{8,12},{12,8},{16,20},{20,16},{24,28},{28,24},{1,5},{5... | collective-permute-start | bytes 1769480 | tf_op jit(solution)/shard_map/ppermute | solution.py:494
  123.4 16.7 %collective-permute-start.9 = (bf16[192,768]{1,0:T(8,128)(2,1)}, bf16[192,768]{1,0:T(8,128)(2,1)}, u32[]{:S(2)}, u32[]{:S(2)}) collective-permute-start(bf16[192,768]{1,0:T(8,128)(2,1)} %reduce_sum.75), channel_id=1, source_target_pairs={{0,16},{4,20},{8,24},{12,28},{16,0},{20,4},{24,8},{28,12},{1,17},{... | collective-permute-start | bytes 884744 | tf_op jit(solution)/shard_map/ppermute | solution.py:494
  124.2 13.1 %collective-permute-start.7 = (f32[192]{0:T(256)S(1)}, f32[192]{0:T(256)S(1)}, u32[]{:S(2)}, u32[]{:S(2)}) collective-permute-start(f32[192]{0:T(256)S(1)} %bitcast.31), channel_id=1, source_target_pairs={{0,2},{1,3},{2,0},{3,1},{4,6},{5,7},{6,4},{7,5},{8,10},{9,11},{10,... | collective-permute-start | bytes 2312 | tf_op jit(solution)/shard_map/ppermute | solution.py:494
  127.3 10.1 %copy-start.2 = (bf16[1,2,400,1024]{3,2,1,0:T(8,128)(2,1)S(1)}, bf16[1,2,400,1024]{3,2,1,0:T(8,128)(2,1)}, u32[]{:S(2)}) copy-start(bf16[1,2,400,1024]{3,2,1,0:T(8,128)(2,1)} %get-tuple-element.242.keep) | copy-start | bytes 4915204
  137.4 3.9 %copy-start.3 = (bf16[1,2,400,1024]{3,2,1,0:T(8,128)(2,1)}, bf16[1,2,400,1024]{3,2,1,0:T(8,128)(2,1)S(1)}, u32[]{:S(2)}) copy-start(bf16[1,2,400,1024]{3,2,1,0:T(8,128)(2,1)S(1)} %collective-permute-done.8.from_core) | copy-start | bytes 4915204
  137.5 2.6 %copy-start.11 = (bf16[192,768]{1,0:T(8,128)(2,1)S(1)}, bf16[192,768]{1,0:T(8,128)(2,1)}, u32[]{:S(2)}) copy-start(bf16[192,768]{1,0:T(8,128)(2,1)} %reduce_sum.75) | copy-start | bytes 884740
  137.5 3.9 %copy-start.10 = (bf16[768,768]{1,0:T(8,128)(2,1)S(1)}, bf16[768,768]{1,0:T(8,128)(2,1)}, u32[]{:S(2)}) copy-start(bf16[768,768]{1,0:T(8,128)(2,1)} %get-tuple-element.209) | copy-start | bytes 3538948
  141.3 15.8 %copy-start.4 = (bf16[384,768]{1,0:T(8,128)(2,1)}, bf16[384,768]{1,0:T(8,128)(2,1)S(1)}, u32[]{:S(2)}) copy-start(bf16[384,768]{1,0:T(8,128)(2,1)S(1)} %maximum_select_fusion.1) | copy-start | bytes 1769476
  143.5 14.3 %copy-start = (bf16[1,2,400,1024]{3,2,1,0:T(8,128)(2,1)S(1)}, bf16[1,2,400,1024]{3,2,1,0:T(8,128)(2,1)}, u32[]{:S(2)}) copy-start(bf16[1,2,400,1024]{3,2,1,0:T(8,128)(2,1)} %get-tuple-element.265.keep) | copy-start | bytes 4915204
  143.5 13.7 %collective-permute-start.12 = (bf16[1,2,400,1024]{3,2,1,0:T(8,128)(2,1)}, bf16[1,2,400,1024]{3,2,1,0:T(8,128)(2,1)}, u32[]{:S(2)}, u32[]{:S(2)}) collective-permute-start(bf16[1,2,400,1024]{3,2,1,0:T(8,128)(2,1)} %get-tuple-element.261), channel_id=1, source_target_pairs={{0,1},{1,0},{2,3},{3,2},{4,5},{5,4},{6,7},{7,6},{8,9},{9,8},{10,11... | collective-permute-start | bytes 4915208 | tf_op jit(solution)/shard_map/ppermute | solution.py:494
  143.5 22.6 %collective-permute-start.15 = (bf16[1,1,400,1024]{3,2,1,0:T(8,128)(2,1)}, bf16[1,1,400,1024]{3,2,1,0:T(8,128)(2,1)}, u32[]{:S(2)}, u32[]{:S(2)}) collective-permute-start(bf16[1,1,400,1024]{3,2,1,0:T(8,128)(2,1)} %add_convert_fusion.2), channel_id=1, source_target_pairs={{0,2},{1,3},{2,0},{3,1},{4,6},{5,7},{6,4},{7,5},{8,10},{9,11},{10,... | collective-permute-start | bytes 2457608 | tf_op jit(solution)/shard_map/ppermute | solution.py:494
  144.3 16.3 %collective-permute-start.13 = (bf16[384,768]{1,0:T(8,128)(2,1)S(1)}, bf16[384,768]{1,0:T(8,128)(2,1)}, u32[]{:S(2)}, u32[]{:S(2)}) collective-permute-start(bf16[384,768]{1,0:T(8,128)(2,1)S(1)} %maximum_select_fusion.1), channel_id=1, source_target_pairs={{0,8},{4,12},{8,0},{12,4},{16,24},{20,28},{24,16},{28,20},{1,9},{5... | collective-permute-start | bytes 1769480 | tf_op jit(solution)/shard_map/ppermute | solution.py:494
  145.2 11.9 %collective-permute-start.11 = (f32[1536]{0:T(1024)S(1)}, f32[1536]{0:T(1024)S(1)}, u32[]{:S(2)}, u32[]{:S(2)}) collective-permute-start(f32[1536]{0:T(1024)S(1)} %concatenate.35), channel_id=1, source_target_pairs={{0,4},{4,0},{8,12},{12,8},{16,20},{20,16},{24,28},{28,24},{1,5},{5... | collective-permute-start | bytes 18440 | tf_op jit(solution)/shard_map/ppermute | solution.py:494
  147.3 18.8 %collective-permute-start.14 = (bf16[192,768]{1,0:T(8,128)(2,1)}, bf16[192,768]{1,0:T(8,128)(2,1)S(1)}, u32[]{:S(2)}, u32[]{:S(2)}) collective-permute-start(bf16[192,768]{1,0:T(8,128)(2,1)} %get-tuple-element.273), channel_id=1, source_target_pairs={{0,8},{4,12},{8,0},{12,4},{16,24},{20,28},{24,16},{28,20},{1,9},{5... | collective-permute-start | bytes 884744 | tf_op jit(solution)/shard_map/ppermute | solution.py:494
  157.2 3.4 %copy-start.5 = (bf16[384,768]{1,0:T(8,128)(2,1)S(1)}, bf16[384,768]{1,0:T(8,128)(2,1)}, u32[]{:S(2)}) copy-start(bf16[384,768]{1,0:T(8,128)(2,1)} %copy-done.4) | copy-start | bytes 1769476
  166.1 7.7 %collective-permute-start.16 = (bf16[1,2,400,1024]{3,2,1,0:T(8,128)(2,1)}, bf16[1,2,400,1024]{3,2,1,0:T(8,128)(2,1)}, u32[]{:S(2)}, u32[]{:S(2)}) collective-permute-start(bf16[1,2,400,1024]{3,2,1,0:T(8,128)(2,1)} %get-tuple-element.288), channel_id=1, source_target_pairs={{0,1},{1,0},{2,3},{3,2},{4,5},{5,4},{6,7},{7,6},{8,9},{9,8},{10,11... | collective-permute-start | bytes 4915208 | tf_op jit(solution)/shard_map/ppermute | solution.py:494
  166.1 7.7 %collective-permute-start.17 = (f32[1536]{0:T(1024)}, f32[1536]{0:T(1024)}, u32[]{:S(2)}, u32[]{:S(2)}) collective-permute-start(f32[1536]{0:T(1024)} %add.114), channel_id=1, source_target_pairs={{0,8},{4,12},{8,0},{12,4},{16,24},{20,28},{24,16},{28,20},{1,9},{5... | collective-permute-start | bytes 18440 | tf_op jit(solution)/shard_map/ppermute | solution.py:494
  167.7 10.2 %collective-permute-start.18 = (bf16[96,768]{1,0:T(8,128)(2,1)}, bf16[96,768]{1,0:T(8,128)(2,1)S(1)}, u32[]{:S(2)}, u32[]{:S(2)}) collective-permute-start(bf16[96,768]{1,0:T(8,128)(2,1)} %add_convert_fusion.7), channel_id=1, source_target_pairs={{0,16},{4,20},{8,24},{12,28},{16,0},{20,4},{24,8},{28,12},{1,17},{... | collective-permute-start | bytes 442376 | tf_op jit(solution)/shard_map/ppermute | solution.py:494
  169.9 20.6 %collective-permute-start.21 = (bf16[1,1,400,1024]{3,2,1,0:T(8,128)(2,1)}, bf16[1,1,400,1024]{3,2,1,0:T(8,128)(2,1)}, u32[]{:S(2)}, u32[]{:S(2)}) collective-permute-start(bf16[1,1,400,1024]{3,2,1,0:T(8,128)(2,1)} %add_convert_fusion.1), channel_id=1, source_target_pairs={{0,2},{1,3},{2,0},{3,1},{4,6},{5,7},{6,4},{7,5},{8,10},{9,11},{10,... | collective-permute-start | bytes 2457608 | tf_op jit(solution)/shard_map/ppermute | solution.py:494
  170.6 31.5 %collective-permute-start.23 = (bf16[768,768]{1,0:T(8,128)(2,1)S(1)}, bf16[768,768]{1,0:T(8,128)(2,1)}, u32[]{:S(2)}, u32[]{:S(2)}) collective-permute-start(bf16[768,768]{1,0:T(8,128)(2,1)S(1)} %maximum_select_fusion), channel_id=1, source_target_pairs={{0,4},{4,0},{8,12},{12,8},{16,20},{20,16},{24,28},{28,24},{1,5},{5... | collective-permute-start | bytes 3538952 | tf_op jit(solution)/shard_map/ppermute | solution.py:494
  170.6 3.2 %copy-start.1 = (bf16[1,2,400,1024]{3,2,1,0:T(8,128)(2,1)S(1)}, bf16[1,2,400,1024]{3,2,1,0:T(8,128)(2,1)}, u32[]{:S(2)}) copy-start(bf16[1,2,400,1024]{3,2,1,0:T(8,128)(2,1)} %get-tuple-element.277.keep) | copy-start | bytes 4915204
  178.0 8.9 %collective-permute-start.20 = (bf16[96,768]{1,0:T(8,128)(2,1)S(1)}, bf16[96,768]{1,0:T(8,128)(2,1)S(1)}, u32[]{:S(2)}, u32[]{:S(2)}) collective-permute-start(bf16[96,768]{1,0:T(8,128)(2,1)S(1)} %add_convert_fusion.5), channel_id=1, source_target_pairs={{0,16},{4,20},{8,24},{12,28},{16,0},{20,4},{24,8},{28,12},{1,17},{... | collective-permute-start | bytes 442376 | tf_op jit(solution)/shard_map/ppermute | solution.py:494
  179.9 7.0 %collective-permute-start.19 = (f32[1536]{0:T(1024)S(1)}, f32[1536]{0:T(1024)S(1)}, u32[]{:S(2)}, u32[]{:S(2)}) collective-permute-start(f32[1536]{0:T(1024)S(1)} %add.117), channel_id=1, source_target_pairs={{0,16},{4,20},{8,24},{12,28},{16,0},{20,4},{24,8},{28,12},{1,17},{... | collective-permute-start | bytes 18440 | tf_op jit(solution)/shard_map/ppermute | solution.py:494
  186.9 9.0 %collective-permute-start.22 = (bf16[192,768]{1,0:T(8,128)(2,1)S(1)}, bf16[192,768]{1,0:T(8,128)(2,1)S(1)}, u32[]{:S(2)}, u32[]{:S(2)}) collective-permute-start(bf16[192,768]{1,0:T(8,128)(2,1)S(1)} %maximum_select_fusion.3), channel_id=1, source_target_pairs={{0,8},{4,12},{8,0},{12,4},{16,24},{20,28},{24,16},{28,20},{1,9},{5... | collective-permute-start | bytes 884744 | tf_op jit(solution)/shard_map/ppermute | solution.py:494
  187.0 20.7 %collective-permute-start.24 = (bf16[1,1,400,1024]{3,2,1,0:T(8,128)(2,1)}, bf16[1,1,400,1024]{3,2,1,0:T(8,128)(2,1)S(1)}, u32[]{:S(2)}, u32[]{:S(2)}) collective-permute-start(bf16[1,1,400,1024]{3,2,1,0:T(8,128)(2,1)} %add_convert_fusion), channel_id=1, source_target_pairs={{0,2},{1,3},{2,0},{3,1},{4,6},{5,7},{6,4},{7,5},{8,10},{9,11},{10,... | collective-permute-start | bytes 2457608 | tf_op jit(solution)/shard_map/ppermute | solution.py:494
  196.1 15.6 %collective-permute-start.25 = (bf16[384,768]{1,0:T(8,128)(2,1)S(1)}, bf16[384,768]{1,0:T(8,128)(2,1)S(1)}, u32[]{:S(2)}, u32[]{:S(2)}) collective-permute-start(bf16[384,768]{1,0:T(8,128)(2,1)S(1)} %maximum_select_fusion.2), channel_id=1, source_target_pairs={{0,4},{4,0},{8,12},{12,8},{16,20},{20,16},{24,28},{28,24},{1,5},{5... | collective-permute-start | bytes 1769480 | tf_op jit(solution)/shard_map/ppermute | solution.py:494
  207.7 0.9 copy-start.12

commit v12 on v11

--- a/solution.py
+++ b/solution.py
@@ -486,6 +486,7 @@
         ],
         input_output_aliases={8 + i: i for i in range(len(before))},
         cost_estimate=cost(3, 5_000_000),
+        compiler_params=pltpu.CompilerParams(vmem_limit_bytes=40 << 20),
         name="finish",
     )(keep, from_core, from_y, own_t, cot, stats, gain, bias, *before)
 

time: 216 us -> 219 us (1.014)
  local copies, waits for them, and re-layouts: 12.5 us -> 16.9 us
  waiting for transfers between devices: 32.5 us -> 28.5 us
    unnamed x36 -> x54, local copies, waits for them, and re-layouts: 1.98 us -> 7 us
    select_n x5, other arithmetic: 3.54 us -> 7.61 us  [joined(): jnp.where(swap, jnp.concatenate([arrived, held], axis=0), jnp.concatenate...]
    pallas_call x3, Pallas kernels: 9.4 us -> 6.85 us  [finish_call(): pl.pallas_call(finish_kernel, grid=(size * steps,), in_specs=[packed, pac...]
  transfers between devices with their start and end apart: 27 -> 27, of which waited for: 11 -> 9; matrix products, arithmetic and copies ran while one was open for 17% -> 17% of each run, Pallas kernels for 40% -> 40%
where the time goes in v12:
time: 219 us; the launch traced here: 217 us
  Pallas kernels  110 us (50%)
  other arithmetic  33.9 us (15%)
  waiting for transfers between devices  28.5 us (13%)
  starting transfers between devices  26.8 us (12%)
  local copies, waits for them, and re-layouts  16.9 us (8%)
    pallas_call x1, Pallas kernels, attention_call(): pl.pallas_call(attention_kernel, grid_spec=grid_spec, out_shape=[jax.Shap...  38.1 us
    pallas_call x3, Pallas kernels, project_call(): pl.pallas_call(project_kernel, grid_spec=grid_spec, out_shape=[jax.ShapeD...  29.8 us
    ppermute x26, waiting for transfers between devices, flip(): return lax.ppermute(value, axis, [(i, i ^ bit) for i in range(size)])  25.5 us
    pallas_call x1, Pallas kernels, mlp_call(): pl.pallas_call(functools.partial(mlp_kernel, pieces_order), grid_spec=gri...  23.9 us
    ppermute x26, starting transfers between devices, flip(): return lax.ppermute(value, axis, [(i, i ^ bit) for i in range(size)])  20.9 us
    pallas_call x1, Pallas kernels, early_call(): pl.pallas_call(early_kernel, grid=(tokens // block,), in_specs=[pl.BlockS...  11.2 us
    select_n x5, other arithmetic, joined(): jnp.where(swap, jnp.concatenate([arrived, held], axis=0), jnp.concatenate...  7.61 us
    unnamed x54, local copies, waits for them, and re-layouts  7 us
  transfers between devices with their start and end apart: 27, of which 9 were waited for; matrix products, arithmetic and copies ran while one was open for 17% of the time, Pallas kernels for 40%

profile of v12, /device:TPU:0, one launch (start us, length us, event | category | flops | bytes accessed | tf_op | source)
XLA Modules:
  0.0 216.9 jit_solution(8547498656487460384)
XLA Ops:
  0.6 0.7 broadcast_in_dim.53.gain_own.gain
  1.4 3.0 %collective-permute-start = (bf16[192,128]{1,0:T(8,128)(2,1)S(1)}, bf16[192,128]{1,0:T(8,128)(2,1)S(1)}, u32[]{:S(2)}, u32[]{:S(2)}) collective-permute-start(bf16[192,128]{1,0:T(8,128)(2,1)S(1)} %broadcast_in_dim.53.gain_own.gain), channel_id=1, source_target_pairs={{0,2},{1,3},{2,0},{3,1},{4,6},{5,7},{6,4},{7,5},{8,10},{9,11},{10,... | collective-permute-start | bytes 147464 | tf_op jit(solution)/shard_map/ppermute | solution.py:495
  4.9 0.8 slice.65
  5.8 0.8 slice.66
  6.6 1.0 convert_reduce_fusion
  7.6 1.4 fusion.4.mask_q
  8.9 1.4 select_convert_fusion.2.mask_k
  10.4 0.8 fusion.1.pick
  11.2 1.2 xor_multiply_fusion.place
  12.4 0.8 reshape.72
  13.3 0.8 broadcast_in_dim.27.gains
  14.1 1.5 broadcast_in_dim.24.up_bias
  17.1 11.2 %early.1 = (bf16[3,768,1024]{2,1,0:T(8,128)(2,1)}, bf16[3,192,1024]{2,1,0:T(8,128)(2,1)}, bf16[192,3072]{1,0:T(8,128)(2,1)}, f32[192,128]{1,0:T(8,128)}) custom-call(bf16[3072,768]{1,0:T(8,128)(2,1)} %cot.5, bf16[768,768]{1,0:T(8,128)(2,1)} %down.7, bf16[192,768]{1,0:T(8,128)(2,1)} %attn.7, bf16[192,768]{1,0:T(8,128)(2,1)} %fusion.1.pick), custom_call_target="tpu_custom_call" | custom-call | flops 10000 | bytes 12000 | tf_op jit(solution)/shard_map/early/pallas_call | solution.py:63
  28.3 4.7 %collective-permute-done.2.flip_y = bf16[192,3072]{1,0:T(8,128)(2,1)S(1)} collective-permute-done((bf16[192,3072]{1,0:T(8,128)(2,1)}, bf16[192,3072]{1,0:T(8,128)(2,1)S(1)}, u32[]{:S(2)}, u32[]{:S(2)}) %collective-permute-start.2) | collective-permute-done | bytes 1179680 | tf_op jit(solution)/shard_map/ppermute | solution.py:495
  33.1 3.0 %collective-permute-done.5.flip_cy = bf16[192,3072]{1,0:T(8,128)(2,1)} collective-permute-done((bf16[192,3072]{1,0:T(8,128)(2,1)S(1)}, bf16[192,3072]{1,0:T(8,128)(2,1)}, u32[]{:S(2)}, u32[]{:S(2)}) %collective-permute-start.5) | collective-permute-done | bytes 1179680 | tf_op jit(solution)/shard_map/ppermute | solution.py:495
  36.0 23.9 %mlp.1 = (bf16[3,768,1024]{2,1,0:T(8,128)(2,1)}, bf16[3,768,1024]{2,1,0:T(8,128)(2,1)}, bf16[3,768,1024]{2,1,0:T(8,128)(2,1)}, f32[8,3072]{1,0:T(8,128)}, f32[76...) custom-call(s32[4]{0:T(128)} %xor_multiply_fusion.place, ...), custom_call_target="tpu_custom_call" | custom-call | flops 20000 | bytes 30000 | tf_op jit(solution)/shard_map/mlp/pallas_call | solution.py:188
  60.0 5.8 %all-to-all-start = ((bf16[8,192,768]{2,1,0:T(8,128)(2,1)}), bf16[8,192,768]{2,1,0:T(8,128)(2,1)S(1)}, u32[]{:S(2)}, u32[]{:S(2)}) async-start(bf16[8,192,768]{2,1,0:T(8,128)(2,1)} %bitcast.29), calls=%async_computation | async-start | bytes 4718592 | tf_op jit(solution)/shard_map/all_to_all | solution.py:524
  65.8 38.1 %attention.1 = (bf16[3,192,1024]{2,1,0:T(8,128)(2,1)}, bf16[3,576,1024]{2,1,0:T(8,128)(2,1)}, f32[384,128]{1,0:T(8,128)}, f32[1,768]{1,0:T(1,128)}, bf16[768,768]{1,0:T(8,128)(2,1)}) custom-call(s32[12]{0:T(128)} %get-tuple-element.197.first, s32[12]{0:T(128)} %get-tuple-element.198.count, bf16[3,768,1024]{2,1,0:T(8,128)(2,1)} %get-tuple-element.201.normed, ...), custom_call_target="tpu_custom_call" | custom-call | flops 18000 | bytes 5000 | tf_op jit(solution)/shard_map/attention/pallas_call | solution.py:360
  105.0 1.9 constant_dynamic-slice_fusion.4
  106.9 9.9 %project.3 = (bf16[1,2,400,1024]{3,2,1,0:T(8,128)(2,1)}, bf16[1,2,400,1024]{3,2,1,0:T(8,128)(2,1)}) custom-call(s32[1]{0:T(128)} %bitcast.shard, bf16[3,768,1024]{2,1,0:T(8,128)(2,1)} %get-tuple-element.196.active, bf16[3,192,1024]{2,1,0:T(8,128)(2,1)} %get-tuple-element.256.attended, bf16[3,768,1024]{2,1,0:T(8,128)(2,1)} %get-tuple-element.213.d_pre, ...), custom_call_target="tpu_custom_call" | custom-call | flops 8000 | bytes 16000 | tf_op jit(solution)/shard_map/project/pallas_call | solution.py:435
  116.9 3.0 %all-to-all-done = bf16[8,192,768]{2,1,0:T(8,128)(2,1)S(1)} async-done(((bf16[8,192,768]{2,1,0:T(8,128)(2,1)}), bf16[8,192,768]{2,1,0:T(8,128)(2,1)S(1)}, u32[]{:S(2)}, u32[]{:S(2)}) %all-to-all-start) | async-done | bytes 2359328 | tf_op jit(solution)/shard_map/all_to_all | solution.py:524
  119.9 1.1 reduce_sum.75
  121.0 1.5 collective-permute-start.10
  122.5 0.9 collective-permute-start.9
  123.4 0.8 collective-permute-start.7
  124.3 1.1 reduce_sum.76
  125.4 1.2 reduce_sum.77
  126.6 10.0 %project.4 = (bf16[1,2,400,1024]{3,2,1,0:T(8,128)(2,1)}, bf16[1,2,400,1024]{3,2,1,0:T(8,128)(2,1)}) custom-call(s32[1]{0:T(128)} %bitcast.shard, bf16[3,768,1024]{2,1,0:T(8,128)(2,1)} %get-tuple-element.196.active, bf16[3,192,1024]{2,1,0:T(8,128)(2,1)} %get-tuple-element.256.attended, bf16[3,768,1024]{2,1,0:T(8,128)(2,1)} %get-tuple-element.213.d_pre, ...), custom_call_target="tpu_custom_call" | custom-call | flops 8000 | bytes 16000 | tf_op jit(solution)/shard_map/project/pallas_call | solution.py:435
  136.7 1.2 add_convert_fusion.2
  138.2 2.1 maximum_select_fusion.1
  140.3 2.1 add_convert_fusion.3
  142.5 0.9 collective-permute-start.15
  143.4 1.1 collective-permute-start.13
  144.5 1.4 collective-permute-start.11
  146.4 9.9 %project.5 = (bf16[1,2,400,1024]{3,2,1,0:T(8,128)(2,1)}, bf16[1,2,400,1024]{3,2,1,0:T(8,128)(2,1)}) custom-call(s32[1]{0:T(128)} %bitcast.shard, bf16[3,768,1024]{2,1,0:T(8,128)(2,1)} %get-tuple-element.196.active, bf16[3,192,1024]{2,1,0:T(8,128)(2,1)} %get-tuple-element.256.attended, bf16[3,768,1024]{2,1,0:T(8,128)(2,1)} %get-tuple-element.213.d_pre, ...), custom_call_target="tpu_custom_call" | custom-call | flops 8000 | bytes 16000 | tf_op jit(solution)/shard_map/project/pallas_call | solution.py:435
  156.3 1.2 add_convert_fusion.1
  157.6 1.2 copy-done.6
  158.8 1.1 collective-permute-done.13
  159.9 3.0 %maximum_select_fusion = bf16[768,768]{1,0:T(8,128)(2,1)} fusion(bf16[384,768]{1,0:T(8,128)(2,1)} %maximum_select_fusion.1, bf16[384,768]{1,0:T(8,128)(2,1)} %collective-permute-done.13, pred[]{:T(512)S(6)} %gt.6), kind=kLoop, calls=%fused_computation.4 | loop fusion | flops 5308416 | bytes 2359297 | tf_op jit(solution)/shard_map/jit(_where)/select_n | solution.py:503
  162.9 2.6 %collective-permute-done.14 = bf16[192,768]{1,0:T(8,128)(2,1)} collective-permute-done((bf16[192,768]{1,0:T(8,128)(2,1)}, bf16[192,768]{1,0:T(8,128)(2,1)}, u32[]{:S(2)}, u32[]{:S(2)}) %collective-permute-start.14) | collective-permute-done | bytes 294944 | tf_op jit(solution)/shard_map/ppermute | solution.py:495
  165.5 1.1 collective-permute-start.17
  166.6 1.0 add_convert_fusion.7
  167.7 1.6 collective-permute-start.18
  169.3 1.2 collective-permute-start.21
  170.9 1.4 copy-done.9
  172.4 1.4 copy-done.11
  173.8 2.6 %finish.3 = (bf16[192,3072]{1,0:T(8,128)(2,1)}, f32[192,3072]{1,0:T(8,128)}) custom-call(bf16[1,2,400,1024]{3,2,1,0:T(8,128)(2,1)S(1)} %copy-done.9, bf16[1,2,400,1024]{3,2,1,0:T(8,128)(2,1)S(1)} %copy-done.11, bf16[1,1,400,1024]{3,2,1,0:T(8,128)(2,1)} %collective-permute-done.15.from_y, bf16[192,3072]{1,0:T(8,128)(2,1)S(1)} %bitcast.19, ...), custom_call_target="tpu_custom_call" | custom-call | flops 3000 | bytes 5000 | tf_op jit(solution)/shard_map/finish/pallas_call | solution.py:471
  176.4 2.4 %add_convert_fusion = bf16[1,1,400,1024]{3,2,1,0:T(8,128)(2,1)} fusion(bf16[1,2,400,1024]{3,2,1,0:T(8,128)(2,1)} %collective-permute-done.16.from_core, bf16[1,2,400,1024]{3,2,1,0:T(8,128)(2,1)S(1)} %copy-done.4), kind=kLoop, calls=%fused_computation.1 | loop fusion | flops 1638400 | bytes 2457600 | tf_op jit(solution)/shard_map/convert_element_type | solution.py:591
  178.8 1.0 add_convert_fusion.5
  179.8 2.0 collective-permute-start.20
  181.8 1.0 collective-permute-start.19
  182.8 6.6 %collective-permute-done.19 = f32[1536]{0:T(1024)S(1)} collective-permute-done((f32[1536]{0:T(1024)S(1)}, f32[1536]{0:T(1024)S(1)}, u32[]{:S(2)}, u32[]{:S(2)}) %collective-permute-start.19) | collective-permute-done | bytes 6176 | tf_op jit(solution)/shard_map/ppermute | solution.py:495
  189.4 0.8 maximum_select_fusion.3
  190.2 0.8 collective-permute-start.24
  192.4 6.5 %collective-permute-done.22 = bf16[192,768]{1,0:T(8,128)(2,1)} collective-permute-done((bf16[192,768]{1,0:T(8,128)(2,1)}, bf16[192,768]{1,0:T(8,128)(2,1)}, u32[]{:S(2)}, u32[]{:S(2)}) %collective-permute-start.22) | collective-permute-done | bytes 294944 | tf_op jit(solution)/shard_map/ppermute | solution.py:495
  198.9 1.5 maximum_select_fusion.2
  200.3 1.9 collective-permute-start.25
  202.8 1.4 copy-done.3
  204.3 1.4 copy-done.7
  205.7 1.7 finish.4
  207.4 3.9 %select_convert_fusion = (f32[768,768]{1,0:T(8,128)}, f32[768,768]{1,0:T(8,128)}) fusion(bf16[768,768]{1,0:T(8,128)(2,1)S(1)} %copy-done.15, bf16[768,768]{1,0:T(8,128)(2,1)} %collective-permute-done.23, pred[]{:T(512)S(6)} %gt.7), kind=kLoop, calls=%fused_computation.5 | loop fusion | flops 2359296 | bytes 7077889 | tf_op jit(solution)/shard_map/convert_element_type | solution.py:796
  211.3 2.6 %finish.5 = (bf16[192,3072]{1,0:T(8,128)(2,1)}, f32[192,3072]{1,0:T(8,128)}) custom-call(bf16[1,2,400,1024]{3,2,1,0:T(8,128)(2,1)S(1)} %copy-done.5, bf16[1,2,400,1024]{3,2,1,0:T(8,128)(2,1)} %collective-permute-done.16.from_core, bf16[1,1,400,1024]{3,2,1,0:T(8,128)(2,1)} %collective-permute-done.24.from_y, ...), custom_call_target="tpu_custom_call", output_to_operand_aliasing={{0}: (8, {}), {1}: (9, {})} | custom-call | flops 3000 | bytes 5000 | tf_op jit(solution)/shard_map/finish/pallas_call | solution.py:471
  214.4 0.9 fusion.2
  215.5 1.4 convert_bitcast_fusion
  (108 shorter events, 7.7 us)
Async XLA Ops:
  1.4 26.9 %copy-start.12 = (bf16[192,128]{1,0:T(8,128)(2,1)}, bf16[192,128]{1,0:T(8,128)(2,1)S(1)}, u32[]{:S(2)}) copy-start(bf16[192,128]{1,0:T(8,128)(2,1)S(1)} %broadcast_in_dim.53.gain_own.gain) | copy-start | bytes 147460
  1.4 11.9 %collective-permute-start = (bf16[192,128]{1,0:T(8,128)(2,1)S(1)}, bf16[192,128]{1,0:T(8,128)(2,1)S(1)}, u32[]{:S(2)}, u32[]{:S(2)}) collective-permute-start(bf16[192,128]{1,0:T(8,128)(2,1)S(1)} %broadcast_in_dim.53.gain_own.gain), channel_id=1, source_target_pairs={{0,2},{1,3},{2,0},{3,1},{4,6},{5,7},{6,4},{7,5},{8,10},{9,11},{10,... | collective-permute-start | bytes 147464 | tf_op jit(solution)/shard_map/ppermute | solution.py:495
  4.4 8.9 %collective-permute-start.1 = (bf16[192,128]{1,0:T(8,128)(2,1)S(1)}, bf16[192,128]{1,0:T(8,128)(2,1)S(1)}, u32[]{:S(2)}, u32[]{:S(2)}) collective-permute-start(bf16[192,128]{1,0:T(8,128)(2,1)S(1)} %broadcast_in_dim.53.gain_own.gain), channel_id=1, source_target_pairs={{0,1},{1,0},{2,3},{3,2},{4,5},{5,4},{6,7},{7,6},{8,9},{9,8},{10,11... | collective-permute-start | bytes 147464 | tf_op jit(solution)/shard_map/ppermute | solution.py:495
  4.4 28.6 %collective-permute-start.2 = (bf16[192,3072]{1,0:T(8,128)(2,1)}, bf16[192,3072]{1,0:T(8,128)(2,1)S(1)}, u32[]{:S(2)}, u32[]{:S(2)}) collective-permute-start(bf16[192,3072]{1,0:T(8,128)(2,1)} %bitcast.16), channel_id=1, source_target_pairs={{0,2},{1,3},{2,0},{3,1},{4,6},{5,7},{6,4},{7,5},{8,10},{9,11},{10,... | collective-permute-start | bytes 3538952 | tf_op jit(solution)/shard_map/ppermute | solution.py:495
  4.6 28.4 %collective-permute-start.4 = (bf16[192,3072]{1,0:T(8,128)(2,1)}, bf16[192,3072]{1,0:T(8,128)(2,1)S(1)}, u32[]{:S(2)}, u32[]{:S(2)}) collective-permute-start(bf16[192,3072]{1,0:T(8,128)(2,1)} %bitcast.17), channel_id=1, source_target_pairs={{0,1},{1,0},{2,3},{3,2},{4,5},{5,4},{6,7},{7,6},{8,9},{9,8},{10,11... | collective-permute-start | bytes 3538952 | tf_op jit(solution)/shard_map/ppermute | solution.py:495
  13.3 15.0 %copy-start.23 = (bf16[192,128]{1,0:T(8,128)(2,1)}, bf16[192,128]{1,0:T(8,128)(2,1)S(1)}, u32[]{:S(2)}) copy-start(bf16[192,128]{1,0:T(8,128)(2,1)S(1)} %collective-permute-done.gain_y) | copy-start | bytes 147460
  13.3 15.0 %copy-start.24 = (bf16[192,128]{1,0:T(8,128)(2,1)}, bf16[192,128]{1,0:T(8,128)(2,1)S(1)}, u32[]{:S(2)}) copy-start(bf16[192,128]{1,0:T(8,128)(2,1)S(1)} %collective-permute-done.1.gain_c) | copy-start | bytes 147460
  16.4 11.9 %collective-permute-start.3 = (bf16[192,128]{1,0:T(8,128)(2,1)S(1)}, bf16[192,128]{1,0:T(8,128)(2,1)S(1)}, u32[]{:S(2)}, u32[]{:S(2)}) collective-permute-start(bf16[192,128]{1,0:T(8,128)(2,1)S(1)} %collective-permute-done.gain_y), channel_id=1, source_target_pairs={{0,1},{1,0},{2,3},{3,2},{4,5},{5,4},{6,7},{7,6},{8,9},{9,8},{10,11... | collective-permute-start | bytes 147464 | tf_op jit(solution)/shard_map/ppermute | solution.py:495
  28.3 7.7 %copy-start.25 = (bf16[192,128]{1,0:T(8,128)(2,1)}, bf16[192,128]{1,0:T(8,128)(2,1)S(1)}, u32[]{:S(2)}) copy-start(bf16[192,128]{1,0:T(8,128)(2,1)S(1)} %collective-permute-done.3.gain_cy) | copy-start | bytes 147460
  33.0 3.0 %copy-start.16 = (bf16[192,3072]{1,0:T(8,128)(2,1)}, bf16[192,3072]{1,0:T(8,128)(2,1)S(1)}, u32[]{:S(2)}) copy-start(bf16[192,3072]{1,0:T(8,128)(2,1)S(1)} %collective-permute-done.2.flip_y) | copy-start | bytes 3538948
  33.0 3.0 %collective-permute-start.5 = (bf16[192,3072]{1,0:T(8,128)(2,1)S(1)}, bf16[192,3072]{1,0:T(8,128)(2,1)}, u32[]{:S(2)}, u32[]{:S(2)}) collective-permute-start(bf16[192,3072]{1,0:T(8,128)(2,1)S(1)} %collective-permute-done.2.flip_y), channel_id=1, source_target_pairs={{0,1},{1,0},{2,3},{3,2},{4,5},{5,4},{6,7},{7,6},{8,9},{9,8},{10,11... | collective-permute-start | bytes 3538952 | tf_op jit(solution)/shard_map/ppermute | solution.py:495
  33.0 3.0 %copy-start.17 = (bf16[192,3072]{1,0:T(8,128)(2,1)}, bf16[192,3072]{1,0:T(8,128)(2,1)S(1)}, u32[]{:S(2)}) copy-start(bf16[192,3072]{1,0:T(8,128)(2,1)S(1)} %collective-permute-done.4.flip_c) | copy-start | bytes 3538948
  60.0 59.9 %all-to-all-start = ((bf16[8,192,768]{2,1,0:T(8,128)(2,1)}), bf16[8,192,768]{2,1,0:T(8,128)(2,1)S(1)}, u32[]{:S(2)}, u32[]{:S(2)}) async-start(bf16[8,192,768]{2,1,0:T(8,128)(2,1)} %bitcast.29), calls=%async_computation | async-start | bytes 4718592 | tf_op jit(solution)/shard_map/all_to_all | solution.py:524
  65.8 38.9 %copy-start.21 = (f32[768,128]{1,0:T(8,128)S(1)}, f32[768,128]{1,0:T(8,128)}, u32[]{:S(2)}) copy-start(f32[768,128]{1,0:T(8,128)} %get-tuple-element.211) | copy-start | bytes 1179652
  106.9 10.0 %collective-permute-start.6 = (f32[2,192]{1,0:T(2,128)S(1)}, f32[2,192]{1,0:T(2,128)S(1)}, u32[]{:S(2)}, u32[]{:S(2)}) collective-permute-start(f32[2,192]{1,0:T(2,128)S(1)} %pad_maximum_fusion.2), channel_id=1, source_target_pairs={{0,1},{1,0},{2,3},{3,2},{4,5},{5,4},{6,7},{7,6},{8,9},{9,8},{10,11... | collective-permute-start | bytes 4616 | tf_op jit(solution)/shard_map/ppermute | solution.py:495
  116.9 7.3 %copy-start.22 = (f32[192,128]{1,0:T(8,128)S(1)}, f32[192,128]{1,0:T(8,128)}, u32[]{:S(2)}) copy-start(f32[192,128]{1,0:T(8,128)} %get-tuple-element.241) | copy-start | bytes 294916
  121.0 15.6 %collective-permute-start.8 = (bf16[1,2,400,1024]{3,2,1,0:T(8,128)(2,1)}, bf16[1,2,400,1024]{3,2,1,0:T(8,128)(2,1)S(1)}, u32[]{:S(2)}, u32[]{:S(2)}) collective-permute-start(bf16[1,2,400,1024]{3,2,1,0:T(8,128)(2,1)} %get-tuple-element.235), channel_id=1, source_target_pairs={{0,1},{1,0},{2,3},{3,2},{4,5},{5,4},{6,7},{7,6},{8,9},{9,8},{10,11... | collective-permute-start | bytes 4915208 | tf_op jit(solution)/shard_map/ppermute | solution.py:495
  121.0 19.3 %collective-permute-start.10 = (bf16[384,768]{1,0:T(8,128)(2,1)}, bf16[384,768]{1,0:T(8,128)(2,1)}, u32[]{:S(2)}, u32[]{:S(2)}) collective-permute-start(bf16[384,768]{1,0:T(8,128)(2,1)} %constant_dynamic-slice_fusion.4), channel_id=1, source_target_pairs={{0,4},{4,0},{8,12},{12,8},{16,20},{20,16},{24,28},{28,24},{1,5},{5... | collective-permute-start | bytes 1769480 | tf_op jit(solution)/shard_map/ppermute | solution.py:495
  122.5 15.7 %collective-permute-start.9 = (bf16[192,768]{1,0:T(8,128)(2,1)}, bf16[192,768]{1,0:T(8,128)(2,1)}, u32[]{:S(2)}, u32[]{:S(2)}) collective-permute-start(bf16[192,768]{1,0:T(8,128)(2,1)} %reduce_sum.75), channel_id=1, source_target_pairs={{0,16},{4,20},{8,24},{12,28},{16,0},{20,4},{24,8},{28,12},{1,17},{... | collective-permute-start | bytes 884744 | tf_op jit(solution)/shard_map/ppermute | solution.py:495
  123.4 13.2 %collective-permute-start.7 = (f32[192]{0:T(256)S(1)}, f32[192]{0:T(256)S(1)}, u32[]{:S(2)}, u32[]{:S(2)}) collective-permute-start(f32[192]{0:T(256)S(1)} %bitcast.31), channel_id=1, source_target_pairs={{0,2},{1,3},{2,0},{3,1},{4,6},{5,7},{6,4},{7,5},{8,10},{9,11},{10,... | collective-permute-start | bytes 2312 | tf_op jit(solution)/shard_map/ppermute | solution.py:495
  126.6 10.1 %copy-start.8 = (bf16[1,2,400,1024]{3,2,1,0:T(8,128)(2,1)S(1)}, bf16[1,2,400,1024]{3,2,1,0:T(8,128)(2,1)}, u32[]{:S(2)}) copy-start(bf16[1,2,400,1024]{3,2,1,0:T(8,128)(2,1)} %get-tuple-element.242.keep) | copy-start | bytes 4915204
  136.6 3.8 %copy-start.10 = (bf16[1,2,400,1024]{3,2,1,0:T(8,128)(2,1)}, bf16[1,2,400,1024]{3,2,1,0:T(8,128)(2,1)S(1)}, u32[]{:S(2)}) copy-start(bf16[1,2,400,1024]{3,2,1,0:T(8,128)(2,1)S(1)} %collective-permute-done.8.from_core) | copy-start | bytes 4915204
  136.7 1.5 copy-start.20
  136.7 3.6 %copy-start.18 = (bf16[768,768]{1,0:T(8,128)(2,1)S(1)}, bf16[768,768]{1,0:T(8,128)(2,1)}, u32[]{:S(2)}) copy-start(bf16[768,768]{1,0:T(8,128)(2,1)} %get-tuple-element.209) | copy-start | bytes 3538948
  142.4 13.9 %copy-start.2 = (bf16[1,2,400,1024]{3,2,1,0:T(8,128)(2,1)S(1)}, bf16[1,2,400,1024]{3,2,1,0:T(8,128)(2,1)}, u32[]{:S(2)}) copy-start(bf16[1,2,400,1024]{3,2,1,0:T(8,128)(2,1)} %get-tuple-element.265.keep) | copy-start | bytes 4915204
  142.4 13.9 %collective-permute-start.12 = (bf16[1,2,400,1024]{3,2,1,0:T(8,128)(2,1)}, bf16[1,2,400,1024]{3,2,1,0:T(8,128)(2,1)S(1)}, u32[]{:S(2)}, u32[]{:S(2)}) collective-permute-start(bf16[1,2,400,1024]{3,2,1,0:T(8,128)(2,1)} %get-tuple-element.261), channel_id=1, source_target_pairs={{0,1},{1,0},{2,3},{3,2},{4,5},{5,4},{6,7},{7,6},{8,9},{9,8},{10,11... | collective-permute-start | bytes 4915208 | tf_op jit(solution)/shard_map/ppermute | solution.py:495
  142.5 23.0 %collective-permute-start.15 = (bf16[1,1,400,1024]{3,2,1,0:T(8,128)(2,1)}, bf16[1,1,400,1024]{3,2,1,0:T(8,128)(2,1)}, u32[]{:S(2)}, u32[]{:S(2)}) collective-permute-start(bf16[1,1,400,1024]{3,2,1,0:T(8,128)(2,1)} %add_convert_fusion.2), channel_id=1, source_target_pairs={{0,2},{1,3},{2,0},{3,1},{4,6},{5,7},{6,4},{7,5},{8,10},{9,11},{10,... | collective-permute-start | bytes 2457608 | tf_op jit(solution)/shard_map/ppermute | solution.py:495
  143.4 16.5 %collective-permute-start.13 = (bf16[384,768]{1,0:T(8,128)(2,1)}, bf16[384,768]{1,0:T(8,128)(2,1)}, u32[]{:S(2)}, u32[]{:S(2)}) collective-permute-start(bf16[384,768]{1,0:T(8,128)(2,1)} %maximum_select_fusion.1), channel_id=1, source_target_pairs={{0,8},{4,12},{8,0},{12,4},{16,24},{20,28},{24,16},{28,20},{1,9},{5... | collective-permute-start | bytes 1769480 | tf_op jit(solution)/shard_map/ppermute | solution.py:495
  144.5 11.8 %collective-permute-start.11 = (f32[1536]{0:T(1024)S(1)}, f32[1536]{0:T(1024)S(1)}, u32[]{:S(2)}, u32[]{:S(2)}) collective-permute-start(f32[1536]{0:T(1024)S(1)} %concatenate.35), channel_id=1, source_target_pairs={{0,4},{4,0},{8,12},{12,8},{16,20},{20,16},{24,28},{28,24},{1,5},{5... | collective-permute-start | bytes 18440 | tf_op jit(solution)/shard_map/ppermute | solution.py:495
  145.9 19.6 %collective-permute-start.14 = (bf16[192,768]{1,0:T(8,128)(2,1)}, bf16[192,768]{1,0:T(8,128)(2,1)}, u32[]{:S(2)}, u32[]{:S(2)}) collective-permute-start(bf16[192,768]{1,0:T(8,128)(2,1)} %get-tuple-element.273), channel_id=1, source_target_pairs={{0,8},{4,12},{8,0},{12,4},{16,24},{20,28},{24,16},{28,20},{1,9},{5... | collective-permute-start | bytes 884744 | tf_op jit(solution)/shard_map/ppermute | solution.py:495
  157.6 1.2 copy-start.6
  158.8 12.2 %copy-start = (bf16[3072,192]{0,1:T(8,128)(2,1)S(1)}, bf16[3072,192]{0,1:T(8,128)(2,1)}, u32[]{:S(2)}) copy-start(bf16[3072,192]{0,1:T(8,128)(2,1)} %param.12) | copy-start | bytes 3538948
  158.8 12.2 %copy-start.1 = (bf16[192,3072]{1,0:T(8,128)(2,1)S(1)}, bf16[192,3072]{1,0:T(8,128)(2,1)}, u32[]{:S(2)}) copy-start(bf16[192,3072]{1,0:T(8,128)(2,1)} %get-tuple-element.279.cot) | copy-start | bytes 3538948
  158.8 12.2 %copy-start.13 = (bf16[192,128]{1,0:T(8,128)(2,1)S(1)}, bf16[192,128]{1,0:T(8,128)(2,1)}, u32[]{:S(2)}) copy-start(bf16[192,128]{1,0:T(8,128)(2,1)} %copy-done.12) | copy-start | bytes 147460
  158.8 12.2 %copy-start.14 = (f32[8,3072]{1,0:T(8,128)S(1)}, f32[8,3072]{1,0:T(8,128)}, u32[]{:S(2)}) copy-start(f32[8,3072]{1,0:T(8,128)} %get-tuple-element.280.stats) | copy-start | bytes 294916
  165.5 10.9 %collective-permute-start.16 = (bf16[1,2,400,1024]{3,2,1,0:T(8,128)(2,1)}, bf16[1,2,400,1024]{3,2,1,0:T(8,128)(2,1)}, u32[]{:S(2)}, u32[]{:S(2)}) collective-permute-start(bf16[1,2,400,1024]{3,2,1,0:T(8,128)(2,1)} %get-tuple-element.288), channel_id=1, source_target_pairs={{0,1},{1,0},{2,3},{3,2},{4,5},{5,4},{6,7},{7,6},{8,9},{9,8},{10,11... | collective-permute-start | bytes 4915208 | tf_op jit(solution)/shard_map/ppermute | solution.py:495
  165.5 10.9 %collective-permute-start.17 = (f32[1536]{0:T(1024)S(1)}, f32[1536]{0:T(1024)S(1)}, u32[]{:S(2)}, u32[]{:S(2)}) collective-permute-start(f32[1536]{0:T(1024)S(1)} %add.114), channel_id=1, source_target_pairs={{0,8},{4,12},{8,0},{12,4},{16,24},{20,28},{24,16},{28,20},{1,9},{5... | collective-permute-start | bytes 18440 | tf_op jit(solution)/shard_map/ppermute | solution.py:495
  167.7 11.2 %collective-permute-start.18 = (bf16[96,768]{1,0:T(8,128)(2,1)S(1)}, bf16[96,768]{1,0:T(8,128)(2,1)S(1)}, u32[]{:S(2)}, u32[]{:S(2)}) collective-permute-start(bf16[96,768]{1,0:T(8,128)(2,1)S(1)} %add_convert_fusion.7), channel_id=1, source_target_pairs={{0,16},{4,20},{8,24},{12,28},{16,0},{20,4},{24,8},{28,12},{1,17},{... | collective-permute-start | bytes 442376 | tf_op jit(solution)/shard_map/ppermute | solution.py:495
  169.3 23.1 %collective-permute-start.21 = (bf16[1,1,400,1024]{3,2,1,0:T(8,128)(2,1)}, bf16[1,1,400,1024]{3,2,1,0:T(8,128)(2,1)S(1)}, u32[]{:S(2)}, u32[]{:S(2)}) collective-permute-start(bf16[1,1,400,1024]{3,2,1,0:T(8,128)(2,1)} %add_convert_fusion.1), channel_id=1, source_target_pairs={{0,2},{1,3},{2,0},{3,1},{4,6},{5,7},{6,4},{7,5},{8,10},{9,11},{10,... | collective-permute-start | bytes 2457608 | tf_op jit(solution)/shard_map/ppermute | solution.py:495
  170.5 36.9 %collective-permute-start.23 = (bf16[768,768]{1,0:T(8,128)(2,1)}, bf16[768,768]{1,0:T(8,128)(2,1)}, u32[]{:S(2)}, u32[]{:S(2)}) collective-permute-start(bf16[768,768]{1,0:T(8,128)(2,1)} %maximum_select_fusion), channel_id=1, source_target_pairs={{0,4},{4,0},{8,12},{12,8},{16,20},{20,16},{24,28},{28,24},{1,5},{5... | collective-permute-start | bytes 3538952 | tf_op jit(solution)/shard_map/ppermute | solution.py:495
  170.9 1.4 copy-start.9
  172.4 1.4 copy-start.11
  173.8 2.6 %copy-start.4 = (bf16[1,2,400,1024]{3,2,1,0:T(8,128)(2,1)S(1)}, bf16[1,2,400,1024]{3,2,1,0:T(8,128)(2,1)}, u32[]{:S(2)}) copy-start(bf16[1,2,400,1024]{3,2,1,0:T(8,128)(2,1)} %get-tuple-element.277.keep) | copy-start | bytes 4915204
  176.4 2.4 %copy-start.19 = (bf16[192,768]{1,0:T(8,128)(2,1)S(1)}, bf16[192,768]{1,0:T(8,128)(2,1)}, u32[]{:S(2)}) copy-start(bf16[192,768]{1,0:T(8,128)(2,1)} %get-tuple-element.362) | copy-start | bytes 884740
  178.8 23.4 %copy-start.26 = (bf16[192]{0:T(256)(128)(2,1)S(1)}, bf16[192]{0:T(256)(128)(2,1)}, u32[]{:S(2)}) copy-start(bf16[192]{0:T(256)(128)(2,1)} %param.14) | copy-start | bytes 1156
  179.8 9.6 %collective-permute-start.20 = (bf16[96,768]{1,0:T(8,128)(2,1)S(1)}, bf16[96,768]{1,0:T(8,128)(2,1)S(1)}, u32[]{:S(2)}, u32[]{:S(2)}) collective-permute-start(bf16[96,768]{1,0:T(8,128)(2,1)S(1)} %add_convert_fusion.5), channel_id=1, source_target_pairs={{0,16},{4,20},{8,24},{12,28},{16,0},{20,4},{24,8},{28,12},{1,17},{... | collective-permute-start | bytes 442376 | tf_op jit(solution)/shard_map/ppermute | solution.py:495
  181.8 7.7 %collective-permute-start.19 = (f32[1536]{0:T(1024)S(1)}, f32[1536]{0:T(1024)S(1)}, u32[]{:S(2)}, u32[]{:S(2)}) collective-permute-start(f32[1536]{0:T(1024)S(1)} %add.117), channel_id=1, source_target_pairs={{0,16},{4,20},{8,24},{12,28},{16,0},{20,4},{24,8},{28,12},{1,17},{... | collective-permute-start | bytes 18440 | tf_op jit(solution)/shard_map/ppermute | solution.py:495
  190.2 8.7 %collective-permute-start.22 = (bf16[192,768]{1,0:T(8,128)(2,1)}, bf16[192,768]{1,0:T(8,128)(2,1)}, u32[]{:S(2)}, u32[]{:S(2)}) collective-permute-start(bf16[192,768]{1,0:T(8,128)(2,1)} %maximum_select_fusion.3), channel_id=1, source_target_pairs={{0,8},{4,12},{8,0},{12,4},{16,24},{20,28},{24,16},{28,20},{1,9},{5... | collective-permute-start | bytes 884744 | tf_op jit(solution)/shard_map/ppermute | solution.py:495
  190.2 21.1 %collective-permute-start.24 = (bf16[1,1,400,1024]{3,2,1,0:T(8,128)(2,1)}, bf16[1,1,400,1024]{3,2,1,0:T(8,128)(2,1)}, u32[]{:S(2)}, u32[]{:S(2)}) collective-permute-start(bf16[1,1,400,1024]{3,2,1,0:T(8,128)(2,1)} %add_convert_fusion), channel_id=1, source_target_pairs={{0,2},{1,3},{2,0},{3,1},{4,6},{5,7},{6,4},{7,5},{8,10},{9,11},{10,... | collective-permute-start | bytes 2457608 | tf_op jit(solution)/shard_map/ppermute | solution.py:495
  200.3 14.1 %collective-permute-start.25 = (bf16[384,768]{1,0:T(8,128)(2,1)S(1)}, bf16[384,768]{1,0:T(8,128)(2,1)S(1)}, u32[]{:S(2)}, u32[]{:S(2)}) collective-permute-start(bf16[384,768]{1,0:T(8,128)(2,1)S(1)} %maximum_select_fusion.2), channel_id=1, source_target_pairs={{0,4},{4,0},{8,12},{12,8},{16,20},{20,16},{24,28},{28,24},{1,5},{5... | collective-permute-start | bytes 1769480 | tf_op jit(solution)/shard_map/ppermute | solution.py:495
  202.8 1.4 copy-start.3
  204.3 1.4 copy-start.7
  205.7 1.7 copy-start.15
  207.4 3.9 %copy-start.5 = (bf16[1,2,400,1024]{3,2,1,0:T(8,128)(2,1)S(1)}, bf16[1,2,400,1024]{3,2,1,0:T(8,128)(2,1)}, u32[]{:S(2)}) copy-start(bf16[1,2,400,1024]{3,2,1,0:T(8,128)(2,1)} %get-tuple-element.277.keep) | copy-start | bytes 4915204

commit v13 on v11

--- a/solution.py
+++ b/solution.py
@@ -786,7 +786,8 @@
         else:
             now = chain + rest or flying
         final = [f for f in now if f[0] is mix_sum]
-        finished, wide_grads = land_in_turn([[f for f in now if f not in final], final], (finished, wide_grads))
+        phases = [[f for f in now if f not in final], final]
+        finished, wide_grads = land_in_turn(phases[::-1] if near else phases, (finished, wide_grads))
         flying = [f for f in flying if f not in now]
         if not mlp_sum.more() and not wide_grads:
             swap, held, arrived = mlp_sum.last

time: 216 us -> 219 us (1.014)
  Pallas kernels: 110 us -> 115 us
    all_to_all x1, waiting for transfers between devices: 5.14 us -> 0.7 us  [move(): return lax.all_to_all(send, 'dp', 0, 0, tiled=True)]
    pallas_call x1, Pallas kernels: 36 us -> 40.5 us  [attention_call(): pl.pallas_call(attention_kernel, grid_spec=grid_spec, out_shape=[jax.Shap...]
    ppermute x26, waiting for transfers between devices: 27.3 us -> 30.1 us  [flip(): return lax.ppermute(value, axis, [(i, i ^ bit) for i in range(size)])]
  transfers between devices with their start and end apart: 27 -> 27, of which waited for: 11 -> 9; matrix products, arithmetic and copies ran while one was open for 17% -> 16% of each run, Pallas kernels for 40% -> 42%
where the time goes in v13:
time: 219 us; the launch traced here: 218 us
  Pallas kernels  115 us (53%)
  other arithmetic  31 us (14%)
  waiting for transfers between devices  30.8 us (14%)
  starting transfers between devices  27.9 us (13%)
  local copies, waits for them, and re-layouts  12.5 us (6%)
    pallas_call x1, Pallas kernels, attention_call(): pl.pallas_call(attention_kernel, grid_spec=grid_spec, out_shape=[jax.Shap...  40.5 us
    ppermute x26, waiting for transfers between devices, flip(): return lax.ppermute(value, axis, [(i, i ^ bit) for i in range(size)])  30.1 us
    pallas_call x3, Pallas kernels, project_call(): pl.pallas_call(project_kernel, grid_spec=grid_spec, out_shape=[jax.ShapeD...  29.8 us
    pallas_call x1, Pallas kernels, mlp_call(): pl.pallas_call(functools.partial(mlp_kernel, pieces_order), grid_spec=gri...  23.9 us
    ppermute x26, starting transfers between devices, flip(): return lax.ppermute(value, axis, [(i, i ^ bit) for i in range(size)])  22.1 us
    pallas_call x1, Pallas kernels, early_call(): pl.pallas_call(early_kernel, grid=(tokens // block,), in_specs=[pl.BlockS...  11.2 us
    pallas_call x3, Pallas kernels, finish_call(): pl.pallas_call(finish_kernel, grid=(size * steps,), in_specs=[packed, pac...  9.4 us
    convert_element_type x3, other arithmetic, take(): (self.keep[:, 1:].astype(F32) + arrived[:, 1:].astype(F32)).astype(BF16)  6.03 us
  transfers between devices with their start and end apart: 27, of which 9 were waited for; matrix products, arithmetic and copies ran while one was open for 16% of the time, Pallas kernels for 42%

profile of v13, /device:TPU:0, one launch (start us, length us, event | category | flops | bytes accessed | tf_op | source)
XLA Modules:
  0.0 218.0 jit_solution(17277012516505921346)
XLA Ops:
  0.6 0.7 broadcast_in_dim.53.gain_own.gain
  1.4 3.0 %collective-permute-start = (bf16[192,128]{1,0:T(8,128)(2,1)S(1)}, bf16[192,128]{1,0:T(8,128)(2,1)S(1)}, u32[]{:S(2)}, u32[]{:S(2)}) collective-permute-start(bf16[192,128]{1,0:T(8,128)(2,1)S(1)} %broadcast_in_dim.53.gain_own.gain), channel_id=1, source_target_pairs={{0,2},{1,3},{2,0},{3,1},{4,6},{5,7},{6,4},{7,5},{8,10},{9,11},{10,... | collective-permute-start | bytes 147464 | tf_op jit(solution)/shard_map/ppermute | solution.py:494
  4.9 0.8 slice.65
  5.8 0.8 slice.66
  6.6 1.0 convert_reduce_fusion
  7.6 1.4 fusion.4.mask_q
  8.9 1.4 select_convert_fusion.2.mask_k
  10.4 0.8 fusion.1.pick
  11.2 1.2 xor_multiply_fusion.place
  12.4 0.8 reshape.72
  13.3 0.8 broadcast_in_dim.27.gains
  14.1 1.5 broadcast_in_dim.24.up_bias
  15.7 1.4 broadcast_in_dim.52.bias
  17.7 11.2 %early.1 = (bf16[3,768,1024]{2,1,0:T(8,128)(2,1)}, bf16[3,192,1024]{2,1,0:T(8,128)(2,1)}, bf16[192,3072]{1,0:T(8,128)(2,1)}, f32[192,128]{1,0:T(8,128)}) custom-call(bf16[3072,768]{1,0:T(8,128)(2,1)} %cot.5, bf16[768,768]{1,0:T(8,128)(2,1)} %down.7, bf16[192,768]{1,0:T(8,128)(2,1)} %attn.7, bf16[192,768]{1,0:T(8,128)(2,1)} %fusion.1.pick), custom_call_target="tpu_custom_call" | custom-call | flops 10000 | bytes 12000 | tf_op jit(solution)/shard_map/early/pallas_call | solution.py:63
  28.9 4.1 %collective-permute-done.2.flip_y = bf16[192,3072]{1,0:T(8,128)(2,1)S(1)} collective-permute-done((bf16[192,3072]{1,0:T(8,128)(2,1)}, bf16[192,3072]{1,0:T(8,128)(2,1)S(1)}, u32[]{:S(2)}, u32[]{:S(2)}) %collective-permute-start.2) | collective-permute-done | bytes 1179680 | tf_op jit(solution)/shard_map/ppermute | solution.py:494
  33.1 2.8 %collective-permute-done.5.flip_cy = bf16[192,3072]{1,0:T(8,128)(2,1)S(1)} collective-permute-done((bf16[192,3072]{1,0:T(8,128)(2,1)S(1)}, bf16[192,3072]{1,0:T(8,128)(2,1)S(1)}, u32[]{:S(2)}, u32[]{:S(2)}) %collective-permute-start.5) | collective-permute-done | bytes 1179680 | tf_op jit(solution)/shard_map/ppermute | solution.py:494
  35.9 1.0 copy-done.9
  36.9 23.9 %mlp.1 = (bf16[3,768,1024]{2,1,0:T(8,128)(2,1)}, bf16[3,768,1024]{2,1,0:T(8,128)(2,1)}, bf16[3,768,1024]{2,1,0:T(8,128)(2,1)}, f32[8,3072]{1,0:T(8,128)}, f32[76...) custom-call(s32[4]{0:T(128)} %xor_multiply_fusion.place, ...), custom_call_target="tpu_custom_call" | custom-call | flops 20000 | bytes 30000 | tf_op jit(solution)/shard_map/mlp/pallas_call | solution.py:188
  60.8 5.8 %all-to-all-start = ((bf16[8,192,768]{2,1,0:T(8,128)(2,1)}), bf16[8,192,768]{2,1,0:T(8,128)(2,1)S(1)}, u32[]{:S(2)}, u32[]{:S(2)}) async-start(bf16[8,192,768]{2,1,0:T(8,128)(2,1)} %bitcast.29), calls=%async_computation | async-start | bytes 4718592 | tf_op jit(solution)/shard_map/all_to_all | solution.py:523
  66.6 40.5 %attention.1 = (bf16[3,192,1024]{2,1,0:T(8,128)(2,1)}, bf16[3,576,1024]{2,1,0:T(8,128)(2,1)}, f32[384,128]{1,0:T(8,128)}, f32[1,768]{1,0:T(1,128)}, bf16[768,768]{1,0:T(8,128)(2,1)}) custom-call(s32[12]{0:T(128)} %get-tuple-element.196.first, s32[12]{0:T(128)} %get-tuple-element.197.count, bf16[3,768,1024]{2,1,0:T(8,128)(2,1)} %get-tuple-element.200.normed, ...), custom_call_target="tpu_custom_call" | custom-call | flops 18000 | bytes 5000 | tf_op jit(solution)/shard_map/attention/pallas_call | solution.py:360
  107.1 0.7 reduce.1
  108.2 1.9 constant_dynamic-slice_fusion.4
  110.1 9.9 %project.3 = (bf16[1,2,400,1024]{3,2,1,0:T(8,128)(2,1)}, bf16[1,2,400,1024]{3,2,1,0:T(8,128)(2,1)}) custom-call(s32[1]{0:T(128)} %bitcast.shard, bf16[3,768,1024]{2,1,0:T(8,128)(2,1)} %get-tuple-element.195.active, bf16[3,192,1024]{2,1,0:T(8,128)(2,1)} %get-tuple-element.255.attended, bf16[3,768,1024]{2,1,0:T(8,128)(2,1)} %get-tuple-element.212.d_pre, ...), custom_call_target="tpu_custom_call" | custom-call | flops 8000 | bytes 16000 | tf_op jit(solution)/shard_map/project/pallas_call | solution.py:435
  120.1 0.7 all-to-all-done
  120.8 1.1 reduce_sum.75
  121.9 1.8 collective-permute-start.10
  123.7 2.3 %collective-permute-start.9 = (bf16[192,768]{1,0:T(8,128)(2,1)}, bf16[192,768]{1,0:T(8,128)(2,1)}, u32[]{:S(2)}, u32[]{:S(2)}) collective-permute-start(bf16[192,768]{1,0:T(8,128)(2,1)} %reduce_sum.75), channel_id=1, source_target_pairs={{0,16},{4,20},{8,24},{12,28},{16,0},{20,4},{24,8},{28,12},{1,17},{... | collective-permute-start | bytes 884744 | tf_op jit(solution)/shard_map/ppermute | solution.py:494
  126.0 0.8 collective-permute-start.7
  126.8 1.0 reduce_sum.78
  127.9 1.2 reduce_sum.77
  129.1 10.0 %project.4 = (bf16[1,2,400,1024]{3,2,1,0:T(8,128)(2,1)}, bf16[1,2,400,1024]{3,2,1,0:T(8,128)(2,1)}) custom-call(s32[1]{0:T(128)} %bitcast.shard, bf16[3,768,1024]{2,1,0:T(8,128)(2,1)} %get-tuple-element.195.active, bf16[3,192,1024]{2,1,0:T(8,128)(2,1)} %get-tuple-element.255.attended, bf16[3,768,1024]{2,1,0:T(8,128)(2,1)} %get-tuple-element.212.d_pre, ...), custom_call_target="tpu_custom_call" | custom-call | flops 8000 | bytes 16000 | tf_op jit(solution)/shard_map/project/pallas_call | solution.py:435
  139.3 1.3 add_convert_fusion.2
  140.5 1.3 maximum_select_fusion.1
  141.8 2.2 %add_convert_fusion.3 = (bf16[192,768]{1,0:T(8,128)(2,1)S(1)}, bf16[192,768]{1,0:T(8,128)(2,1)}) fusion(bf16[384,768]{1,0:T(8,128)(2,1)} %collective-permute-done.10, s32[]{:T(128)S(6)} %mul.38, bf16[768,768]{1,0:T(8,128)(2,1)S(1)} %copy-done.10, s32[]{:T(128)S(6)} %dynamic_slice.55, s32[]{:T(128)S(6)} %select_n.103, s32[]{:T(128)S(6)} %dynamic_slice.47), kind=kLoop, calls=%fused_computation.12 | loop fusion | flops 1179648 | bytes 1769488 | tf_op jit(solution)/shard_map/convert_element_type | solution.py:550
  144.0 1.2 collective-permute-start.15
  145.3 1.8 collective-permute-start.13
  147.2 1.0 collective-permute-start.14
  148.1 9.9 %project.5 = (bf16[1,2,400,1024]{3,2,1,0:T(8,128)(2,1)}, bf16[1,2,400,1024]{3,2,1,0:T(8,128)(2,1)}) custom-call(s32[1]{0:T(128)} %bitcast.shard, bf16[3,768,1024]{2,1,0:T(8,128)(2,1)} %get-tuple-element.195.active, bf16[3,192,1024]{2,1,0:T(8,128)(2,1)} %get-tuple-element.255.attended, bf16[3,768,1024]{2,1,0:T(8,128)(2,1)} %get-tuple-element.212.d_pre, ...), custom_call_target="tpu_custom_call" | custom-call | flops 8000 | bytes 16000 | tf_op jit(solution)/shard_map/project/pallas_call | solution.py:435
  158.6 2.4 %add_convert_fusion.1 = bf16[1,1,400,1024]{3,2,1,0:T(8,128)(2,1)} fusion(bf16[1,2,400,1024]{3,2,1,0:T(8,128)(2,1)} %collective-permute-done.12.from_core, bf16[1,2,400,1024]{3,2,1,0:T(8,128)(2,1)S(1)} %copy-done), kind=kLoop, calls=%fused_computation.2 | loop fusion | flops 1638400 | bytes 2457600 | tf_op jit(solution)/shard_map/convert_element_type | solution.py:590
  161.5 1.7 maximum_select_fusion
  163.2 3.8 %collective-permute-done.14 = bf16[192,768]{1,0:T(8,128)(2,1)S(1)} collective-permute-done((bf16[192,768]{1,0:T(8,128)(2,1)}, bf16[192,768]{1,0:T(8,128)(2,1)S(1)}, u32[]{:S(2)}, u32[]{:S(2)}) %collective-permute-start.14) | collective-permute-done | bytes 294944 | tf_op jit(solution)/shard_map/ppermute | solution.py:494
  167.1 0.7 add_convert_fusion.7
  167.8 0.9 collective-permute-start.16
  168.7 1.7 collective-permute-start.18
  170.4 1.2 collective-permute-start.21
  172.2 3.1 %finish.3 = (bf16[192,3072]{1,0:T(8,128)(2,1)}, f32[192,3072]{1,0:T(8,128)}) custom-call(bf16[1,2,400,1024]{3,2,1,0:T(8,128)(2,1)} %get-tuple-element.241.keep, bf16[1,2,400,1024]{3,2,1,0:T(8,128)(2,1)} %copy-done.3, bf16[1,1,400,1024]{3,2,1,0:T(8,128)(2,1)} %collective-permute-done.15.from_y, bf16[192,3072]{1,0:T(8,128)(2,1)} %bitcast.19, ...), custom_call_target="tpu_custom_call" | custom-call | flops 3000 | bytes 5000 | tf_op jit(solution)/shard_map/finish/pallas_call | solution.py:471
  175.4 2.9 %collective-permute-done.16 = bf16[96,768]{1,0:T(8,128)(2,1)S(1)} collective-permute-done((bf16[96,768]{1,0:T(8,128)(2,1)}, bf16[96,768]{1,0:T(8,128)(2,1)S(1)}, u32[]{:S(2)}, u32[]{:S(2)}) %collective-permute-start.16) | collective-permute-done | bytes 147488 | tf_op jit(solution)/shard_map/ppermute | solution.py:494
  178.4 0.7 add.122
  179.1 2.4 %add_convert_fusion = bf16[1,1,400,1024]{3,2,1,0:T(8,128)(2,1)} fusion(bf16[1,2,400,1024]{3,2,1,0:T(8,128)(2,1)} %collective-permute-done.17.from_core, bf16[1,2,400,1024]{3,2,1,0:T(8,128)(2,1)S(1)} %copy-done.1), kind=kLoop, calls=%fused_computation.1 | loop fusion | flops 1638400 | bytes 2457600 | tf_op jit(solution)/shard_map/convert_element_type | solution.py:590
  181.5 2.9 %collective-permute-start.19 = (f32[1536]{0:T(1024)S(1)}, f32[1536]{0:T(1024)S(1)}, u32[]{:S(2)}, u32[]{:S(2)}) collective-permute-start(f32[1536]{0:T(1024)S(1)} %add.122), channel_id=1, source_target_pairs={{0,16},{4,20},{8,24},{12,28},{16,0},{20,4},{24,8},{28,12},{1,17},{... | collective-permute-start | bytes 18440 | tf_op jit(solution)/shard_map/ppermute | solution.py:494
  184.4 6.5 %collective-permute-done.19 = f32[1536]{0:T(1024)S(1)} collective-permute-done((f32[1536]{0:T(1024)S(1)}, f32[1536]{0:T(1024)S(1)}, u32[]{:S(2)}, u32[]{:S(2)}) %collective-permute-start.19) | collective-permute-done | bytes 6176 | tf_op jit(solution)/shard_map/ppermute | solution.py:494
  191.1 1.3 collective-permute-start.24
  192.4 0.7 slice.88
  193.1 0.7 slice.78
  193.8 6.2 %collective-permute-done.22 = bf16[192,768]{1,0:T(8,128)(2,1)S(1)} collective-permute-done((bf16[192,768]{1,0:T(8,128)(2,1)S(1)}, bf16[192,768]{1,0:T(8,128)(2,1)S(1)}, u32[]{:S(2)}, u32[]{:S(2)}) %collective-permute-start.22) | collective-permute-done | bytes 294944 | tf_op jit(solution)/shard_map/ppermute | solution.py:494
  200.2 0.6 collective-permute-start.25
  200.8 0.6 fusion.6
  201.4 3.1 %finish.4 = (bf16[192,3072]{1,0:T(8,128)(2,1)}, f32[192,3072]{1,0:T(8,128)}) custom-call(bf16[1,2,400,1024]{3,2,1,0:T(8,128)(2,1)} %get-tuple-element.264.keep, bf16[1,2,400,1024]{3,2,1,0:T(8,128)(2,1)} %collective-permute-done.12.from_core, bf16[1,1,400,1024]{3,2,1,0:T(8,128)(2,1)} %collective-permute-done.21.from_y, ...), custom_call_target="tpu_custom_call", output_to_operand_aliasing={{0}: (8, {}), {1}: (9, {})} | custom-call | flops 3000 | bytes 5000 | tf_op jit(solution)/shard_map/finish/pallas_call | solution.py:471
  204.6 3.8 %select_convert_fusion = (f32[768,768]{1,0:T(8,128)}, f32[768,768]{1,0:T(8,128)}) fusion(bf16[768,768]{1,0:T(8,128)(2,1)S(1)} %maximum_select_fusion, bf16[768,768]{1,0:T(8,128)(2,1)} %collective-permute-done.23, pred[]{:T(512)S(6)} %gt.7), kind=kLoop, calls=%fused_computation.5 | loop fusion | flops 2359296 | bytes 7077889 | tf_op jit(solution)/shard_map/convert_element_type | solution.py:796
  208.3 3.2 %collective-permute-done.24.from_y = bf16[1,1,400,1024]{3,2,1,0:T(8,128)(2,1)S(1)} collective-permute-done((bf16[1,1,400,1024]{3,2,1,0:T(8,128)(2,1)}, bf16[1,1,400,1024]{3,2,1,0:T(8,128)(2,1)S(1)}, u32[]{:S(2)}, u32[]{:S(2)}) %collective-permute-start.24) | collective-permute-done | bytes 819232 | tf_op jit(solution)/shard_map/ppermute | solution.py:494
  211.5 0.9 copy-done.12
  212.4 3.1 %finish.5 = (bf16[192,3072]{1,0:T(8,128)(2,1)}, f32[192,3072]{1,0:T(8,128)}) custom-call(bf16[1,2,400,1024]{3,2,1,0:T(8,128)(2,1)} %get-tuple-element.276.keep, bf16[1,2,400,1024]{3,2,1,0:T(8,128)(2,1)} %collective-permute-done.17.from_core, bf16[1,1,400,1024]{3,2,1,0:T(8,128)(2,1)} %copy-done.12, ...), custom_call_target="tpu_custom_call", output_to_operand_aliasing={{0}: (8, {}), {1}: (9, {})} | custom-call | flops 3000 | bytes 5000 | tf_op jit(solution)/shard_map/finish/pallas_call | solution.py:471
  215.5 0.9 fusion.2
  216.7 1.4 convert_bitcast_fusion
  (92 shorter events, 4.7 us)
Async XLA Ops:
  1.4 27.5 %copy-start.6 = (bf16[192,128]{1,0:T(8,128)(2,1)}, bf16[192,128]{1,0:T(8,128)(2,1)S(1)}, u32[]{:S(2)}) copy-start(bf16[192,128]{1,0:T(8,128)(2,1)S(1)} %broadcast_in_dim.53.gain_own.gain) | copy-start | bytes 147460
  1.4 11.9 %collective-permute-start = (bf16[192,128]{1,0:T(8,128)(2,1)S(1)}, bf16[192,128]{1,0:T(8,128)(2,1)S(1)}, u32[]{:S(2)}, u32[]{:S(2)}) collective-permute-start(bf16[192,128]{1,0:T(8,128)(2,1)S(1)} %broadcast_in_dim.53.gain_own.gain), channel_id=1, source_target_pairs={{0,2},{1,3},{2,0},{3,1},{4,6},{5,7},{6,4},{7,5},{8,10},{9,11},{10,... | collective-permute-start | bytes 147464 | tf_op jit(solution)/shard_map/ppermute | solution.py:494
  4.4 8.9 %collective-permute-start.1 = (bf16[192,128]{1,0:T(8,128)(2,1)S(1)}, bf16[192,128]{1,0:T(8,128)(2,1)S(1)}, u32[]{:S(2)}, u32[]{:S(2)}) collective-permute-start(bf16[192,128]{1,0:T(8,128)(2,1)S(1)} %broadcast_in_dim.53.gain_own.gain), channel_id=1, source_target_pairs={{0,1},{1,0},{2,3},{3,2},{4,5},{5,4},{6,7},{7,6},{8,9},{9,8},{10,11... | collective-permute-start | bytes 147464 | tf_op jit(solution)/shard_map/ppermute | solution.py:494
  4.4 28.6 %collective-permute-start.2 = (bf16[192,3072]{1,0:T(8,128)(2,1)}, bf16[192,3072]{1,0:T(8,128)(2,1)S(1)}, u32[]{:S(2)}, u32[]{:S(2)}) collective-permute-start(bf16[192,3072]{1,0:T(8,128)(2,1)} %bitcast.16), channel_id=1, source_target_pairs={{0,2},{1,3},{2,0},{3,1},{4,6},{5,7},{6,4},{7,5},{8,10},{9,11},{10,... | collective-permute-start | bytes 3538952 | tf_op jit(solution)/shard_map/ppermute | solution.py:494
  4.6 28.4 %collective-permute-start.4 = (bf16[192,3072]{1,0:T(8,128)(2,1)}, bf16[192,3072]{1,0:T(8,128)(2,1)S(1)}, u32[]{:S(2)}, u32[]{:S(2)}) collective-permute-start(bf16[192,3072]{1,0:T(8,128)(2,1)} %bitcast.17), channel_id=1, source_target_pairs={{0,1},{1,0},{2,3},{3,2},{4,5},{5,4},{6,7},{7,6},{8,9},{9,8},{10,11... | collective-permute-start | bytes 3538952 | tf_op jit(solution)/shard_map/ppermute | solution.py:494
  13.3 15.6 %copy-start.15 = (bf16[192,128]{1,0:T(8,128)(2,1)}, bf16[192,128]{1,0:T(8,128)(2,1)S(1)}, u32[]{:S(2)}) copy-start(bf16[192,128]{1,0:T(8,128)(2,1)S(1)} %collective-permute-done.gain_y) | copy-start | bytes 147460
  13.3 15.6 %copy-start.16 = (bf16[192,128]{1,0:T(8,128)(2,1)}, bf16[192,128]{1,0:T(8,128)(2,1)S(1)}, u32[]{:S(2)}) copy-start(bf16[192,128]{1,0:T(8,128)(2,1)S(1)} %collective-permute-done.1.gain_c) | copy-start | bytes 147460
  17.0 11.9 %collective-permute-start.3 = (bf16[192,128]{1,0:T(8,128)(2,1)S(1)}, bf16[192,128]{1,0:T(8,128)(2,1)S(1)}, u32[]{:S(2)}, u32[]{:S(2)}) collective-permute-start(bf16[192,128]{1,0:T(8,128)(2,1)S(1)} %collective-permute-done.gain_y), channel_id=1, source_target_pairs={{0,1},{1,0},{2,3},{3,2},{4,5},{5,4},{6,7},{7,6},{8,9},{9,8},{10,11... | collective-permute-start | bytes 147464 | tf_op jit(solution)/shard_map/ppermute | solution.py:494
  28.9 4.1 %copy-start.17 = (bf16[192,128]{1,0:T(8,128)(2,1)}, bf16[192,128]{1,0:T(8,128)(2,1)S(1)}, u32[]{:S(2)}) copy-start(bf16[192,128]{1,0:T(8,128)(2,1)S(1)} %collective-permute-done.3.gain_cy) | copy-start | bytes 147460
  33.0 2.9 %copy-start.7 = (bf16[192,3072]{1,0:T(8,128)(2,1)}, bf16[192,3072]{1,0:T(8,128)(2,1)S(1)}, u32[]{:S(2)}) copy-start(bf16[192,3072]{1,0:T(8,128)(2,1)S(1)} %collective-permute-done.2.flip_y) | copy-start | bytes 3538948
  33.0 2.8 %collective-permute-start.5 = (bf16[192,3072]{1,0:T(8,128)(2,1)S(1)}, bf16[192,3072]{1,0:T(8,128)(2,1)S(1)}, u32[]{:S(2)}, u32[]{:S(2)}) collective-permute-start(bf16[192,3072]{1,0:T(8,128)(2,1)S(1)} %collective-permute-done.2.flip_y), channel_id=1, source_target_pairs={{0,1},{1,0},{2,3},{3,2},{4,5},{5,4},{6,7},{7,6},{8,9},{9,8},{10,11... | collective-permute-start | bytes 3538952 | tf_op jit(solution)/shard_map/ppermute | solution.py:494
  33.1 2.8 %copy-start.8 = (bf16[192,3072]{1,0:T(8,128)(2,1)}, bf16[192,3072]{1,0:T(8,128)(2,1)S(1)}, u32[]{:S(2)}) copy-start(bf16[192,3072]{1,0:T(8,128)(2,1)S(1)} %collective-permute-done.4.flip_c) | copy-start | bytes 3538948
  35.9 1.0 copy-start.9
  60.8 60.0 %all-to-all-start = ((bf16[8,192,768]{2,1,0:T(8,128)(2,1)}), bf16[8,192,768]{2,1,0:T(8,128)(2,1)S(1)}, u32[]{:S(2)}, u32[]{:S(2)}) async-start(bf16[8,192,768]{2,1,0:T(8,128)(2,1)} %bitcast.29), calls=%async_computation | async-start | bytes 4718592 | tf_op jit(solution)/shard_map/all_to_all | solution.py:523
  66.6 41.2 %copy-start.13 = (f32[768,128]{1,0:T(8,128)S(1)}, f32[768,128]{1,0:T(8,128)}, u32[]{:S(2)}) copy-start(f32[768,128]{1,0:T(8,128)} %get-tuple-element.210) | copy-start | bytes 1179652
  110.1 10.0 %collective-permute-start.6 = (f32[2,192]{1,0:T(2,128)S(1)}, f32[2,192]{1,0:T(2,128)S(1)}, u32[]{:S(2)}, u32[]{:S(2)}) collective-permute-start(f32[2,192]{1,0:T(2,128)S(1)} %pad_maximum_fusion.2), channel_id=1, source_target_pairs={{0,1},{1,0},{2,3},{3,2},{4,5},{5,4},{6,7},{7,6},{8,9},{9,8},{10,11... | collective-permute-start | bytes 4616 | tf_op jit(solution)/shard_map/ppermute | solution.py:494
  120.1 7.7 %copy-start.14 = (f32[384,128]{1,0:T(8,128)S(1)}, f32[384,128]{1,0:T(8,128)}, u32[]{:S(2)}) copy-start(f32[384,128]{1,0:T(8,128)} %get-tuple-element.238) | copy-start | bytes 589828
  121.9 17.3 %collective-permute-start.8 = (bf16[1,2,400,1024]{3,2,1,0:T(8,128)(2,1)}, bf16[1,2,400,1024]{3,2,1,0:T(8,128)(2,1)S(1)}, u32[]{:S(2)}, u32[]{:S(2)}) collective-permute-start(bf16[1,2,400,1024]{3,2,1,0:T(8,128)(2,1)} %get-tuple-element.234), channel_id=1, source_target_pairs={{0,1},{1,0},{2,3},{3,2},{4,5},{5,4},{6,7},{7,6},{8,9},{9,8},{10,11... | collective-permute-start | bytes 4915208 | tf_op jit(solution)/shard_map/ppermute | solution.py:494
  121.9 19.9 %collective-permute-start.10 = (bf16[384,768]{1,0:T(8,128)(2,1)}, bf16[384,768]{1,0:T(8,128)(2,1)}, u32[]{:S(2)}, u32[]{:S(2)}) collective-permute-start(bf16[384,768]{1,0:T(8,128)(2,1)} %constant_dynamic-slice_fusion.4), channel_id=1, source_target_pairs={{0,4},{4,0},{8,12},{12,8},{16,20},{20,16},{24,28},{28,24},{1,5},{5... | collective-permute-start | bytes 1769480 | tf_op jit(solution)/shard_map/ppermute | solution.py:494
  123.7 16.8 %collective-permute-start.9 = (bf16[192,768]{1,0:T(8,128)(2,1)}, bf16[192,768]{1,0:T(8,128)(2,1)}, u32[]{:S(2)}, u32[]{:S(2)}) collective-permute-start(bf16[192,768]{1,0:T(8,128)(2,1)} %reduce_sum.75), channel_id=1, source_target_pairs={{0,16},{4,20},{8,24},{12,28},{16,0},{20,4},{24,8},{28,12},{1,17},{... | collective-permute-start | bytes 884744 | tf_op jit(solution)/shard_map/ppermute | solution.py:494
  126.0 13.1 %collective-permute-start.7 = (f32[192]{0:T(256)S(1)}, f32[192]{0:T(256)S(1)}, u32[]{:S(2)}, u32[]{:S(2)}) collective-permute-start(f32[192]{0:T(256)S(1)} %bitcast.31), channel_id=1, source_target_pairs={{0,2},{1,3},{2,0},{3,1},{4,6},{5,7},{6,4},{7,5},{8,10},{9,11},{10,... | collective-permute-start | bytes 2312 | tf_op jit(solution)/shard_map/ppermute | solution.py:494
  129.1 10.1 %copy-start.2 = (bf16[1,2,400,1024]{3,2,1,0:T(8,128)(2,1)S(1)}, bf16[1,2,400,1024]{3,2,1,0:T(8,128)(2,1)}, u32[]{:S(2)}) copy-start(bf16[1,2,400,1024]{3,2,1,0:T(8,128)(2,1)} %get-tuple-element.241.keep) | copy-start | bytes 4915204
  139.2 2.6 %copy-start.3 = (bf16[1,2,400,1024]{3,2,1,0:T(8,128)(2,1)}, bf16[1,2,400,1024]{3,2,1,0:T(8,128)(2,1)S(1)}, u32[]{:S(2)}) copy-start(bf16[1,2,400,1024]{3,2,1,0:T(8,128)(2,1)S(1)} %collective-permute-done.8.from_core) | copy-start | bytes 4915204
  139.3 1.3 copy-start.11
  139.3 2.6 %copy-start.10 = (bf16[768,768]{1,0:T(8,128)(2,1)S(1)}, bf16[768,768]{1,0:T(8,128)(2,1)}, u32[]{:S(2)}) copy-start(bf16[768,768]{1,0:T(8,128)(2,1)} %get-tuple-element.208) | copy-start | bytes 3538948
  141.8 16.2 %copy-start.4 = (bf16[384,768]{1,0:T(8,128)(2,1)}, bf16[384,768]{1,0:T(8,128)(2,1)S(1)}, u32[]{:S(2)}) copy-start(bf16[384,768]{1,0:T(8,128)(2,1)S(1)} %maximum_select_fusion.1) | copy-start | bytes 1769476
  144.0 14.6 %copy-start = (bf16[1,2,400,1024]{3,2,1,0:T(8,128)(2,1)S(1)}, bf16[1,2,400,1024]{3,2,1,0:T(8,128)(2,1)}, u32[]{:S(2)}) copy-start(bf16[1,2,400,1024]{3,2,1,0:T(8,128)(2,1)} %get-tuple-element.264.keep) | copy-start | bytes 4915204
  144.0 14.0 %collective-permute-start.12 = (bf16[1,2,400,1024]{3,2,1,0:T(8,128)(2,1)}, bf16[1,2,400,1024]{3,2,1,0:T(8,128)(2,1)}, u32[]{:S(2)}, u32[]{:S(2)}) collective-permute-start(bf16[1,2,400,1024]{3,2,1,0:T(8,128)(2,1)} %get-tuple-element.260), channel_id=1, source_target_pairs={{0,1},{1,0},{2,3},{3,2},{4,5},{5,4},{6,7},{7,6},{8,9},{9,8},{10,11... | collective-permute-start | bytes 4915208 | tf_op jit(solution)/shard_map/ppermute | solution.py:494
  144.0 23.0 %collective-permute-start.15 = (bf16[1,1,400,1024]{3,2,1,0:T(8,128)(2,1)}, bf16[1,1,400,1024]{3,2,1,0:T(8,128)(2,1)}, u32[]{:S(2)}, u32[]{:S(2)}) collective-permute-start(bf16[1,1,400,1024]{3,2,1,0:T(8,128)(2,1)} %add_convert_fusion.2), channel_id=1, source_target_pairs={{0,2},{1,3},{2,0},{3,1},{4,6},{5,7},{6,4},{7,5},{8,10},{9,11},{10,... | collective-permute-start | bytes 2457608 | tf_op jit(solution)/shard_map/ppermute | solution.py:494
  145.3 16.3 %collective-permute-start.13 = (bf16[384,768]{1,0:T(8,128)(2,1)S(1)}, bf16[384,768]{1,0:T(8,128)(2,1)}, u32[]{:S(2)}, u32[]{:S(2)}) collective-permute-start(bf16[384,768]{1,0:T(8,128)(2,1)S(1)} %maximum_select_fusion.1), channel_id=1, source_target_pairs={{0,8},{4,12},{8,0},{12,4},{16,24},{20,28},{24,16},{28,20},{1,9},{5... | collective-permute-start | bytes 1769480 | tf_op jit(solution)/shard_map/ppermute | solution.py:494
  147.0 11.0 %collective-permute-start.11 = (f32[1536]{0:T(1024)S(1)}, f32[1536]{0:T(1024)S(1)}, u32[]{:S(2)}, u32[]{:S(2)}) collective-permute-start(f32[1536]{0:T(1024)S(1)} %concatenate.35), channel_id=1, source_target_pairs={{0,4},{4,0},{8,12},{12,8},{16,20},{20,16},{24,28},{28,24},{1,5},{5... | collective-permute-start | bytes 18440 | tf_op jit(solution)/shard_map/ppermute | solution.py:494
  147.2 19.9 %collective-permute-start.14 = (bf16[192,768]{1,0:T(8,128)(2,1)}, bf16[192,768]{1,0:T(8,128)(2,1)S(1)}, u32[]{:S(2)}, u32[]{:S(2)}) collective-permute-start(bf16[192,768]{1,0:T(8,128)(2,1)} %get-tuple-element.272), channel_id=1, source_target_pairs={{0,8},{4,12},{8,0},{12,4},{16,24},{20,28},{24,16},{28,20},{1,9},{5... | collective-permute-start | bytes 884744 | tf_op jit(solution)/shard_map/ppermute | solution.py:494
  158.0 3.5 %copy-start.5 = (bf16[384,768]{1,0:T(8,128)(2,1)S(1)}, bf16[384,768]{1,0:T(8,128)(2,1)}, u32[]{:S(2)}) copy-start(bf16[384,768]{1,0:T(8,128)(2,1)} %copy-done.4) | copy-start | bytes 1769476
  167.1 11.3 %collective-permute-start.17 = (bf16[1,2,400,1024]{3,2,1,0:T(8,128)(2,1)}, bf16[1,2,400,1024]{3,2,1,0:T(8,128)(2,1)}, u32[]{:S(2)}, u32[]{:S(2)}) collective-permute-start(bf16[1,2,400,1024]{3,2,1,0:T(8,128)(2,1)} %get-tuple-element.291), channel_id=1, source_target_pairs={{0,1},{1,0},{2,3},{3,2},{4,5},{5,4},{6,7},{7,6},{8,9},{9,8},{10,11... | collective-permute-start | bytes 4915208 | tf_op jit(solution)/shard_map/ppermute | solution.py:494
  167.8 10.5 %collective-permute-start.16 = (bf16[96,768]{1,0:T(8,128)(2,1)}, bf16[96,768]{1,0:T(8,128)(2,1)S(1)}, u32[]{:S(2)}, u32[]{:S(2)}) collective-permute-start(bf16[96,768]{1,0:T(8,128)(2,1)} %add_convert_fusion.7), channel_id=1, source_target_pairs={{0,16},{4,20},{8,24},{12,28},{16,0},{20,4},{24,8},{28,12},{1,17},{... | collective-permute-start | bytes 442376 | tf_op jit(solution)/shard_map/ppermute | solution.py:494
  168.7 9.7 %collective-permute-start.18 = (f32[1536]{0:T(1024)}, f32[1536]{0:T(1024)}, u32[]{:S(2)}, u32[]{:S(2)}) collective-permute-start(f32[1536]{0:T(1024)} %add.114), channel_id=1, source_target_pairs={{0,8},{4,12},{8,0},{12,4},{16,24},{20,28},{24,16},{28,20},{1,9},{5... | collective-permute-start | bytes 18440 | tf_op jit(solution)/shard_map/ppermute | solution.py:494
  170.4 23.3 %collective-permute-start.21 = (bf16[1,1,400,1024]{3,2,1,0:T(8,128)(2,1)}, bf16[1,1,400,1024]{3,2,1,0:T(8,128)(2,1)}, u32[]{:S(2)}, u32[]{:S(2)}) collective-permute-start(bf16[1,1,400,1024]{3,2,1,0:T(8,128)(2,1)} %add_convert_fusion.1), channel_id=1, source_target_pairs={{0,2},{1,3},{2,0},{3,1},{4,6},{5,7},{6,4},{7,5},{8,10},{9,11},{10,... | collective-permute-start | bytes 2457608 | tf_op jit(solution)/shard_map/ppermute | solution.py:494
  171.7 32.9 %collective-permute-start.23 = (bf16[768,768]{1,0:T(8,128)(2,1)S(1)}, bf16[768,768]{1,0:T(8,128)(2,1)}, u32[]{:S(2)}, u32[]{:S(2)}) collective-permute-start(bf16[768,768]{1,0:T(8,128)(2,1)S(1)} %maximum_select_fusion), channel_id=1, source_target_pairs={{0,4},{4,0},{8,12},{12,8},{16,20},{20,16},{24,28},{28,24},{1,5},{5... | collective-permute-start | bytes 3538952 | tf_op jit(solution)/shard_map/ppermute | solution.py:494
  172.2 6.9 %copy-start.1 = (bf16[1,2,400,1024]{3,2,1,0:T(8,128)(2,1)S(1)}, bf16[1,2,400,1024]{3,2,1,0:T(8,128)(2,1)}, u32[]{:S(2)}) copy-start(bf16[1,2,400,1024]{3,2,1,0:T(8,128)(2,1)} %get-tuple-element.276.keep) | copy-start | bytes 4915204
  179.1 21.7 %copy-start.18 = (bf16[192]{0:T(256)(128)(2,1)S(1)}, bf16[192]{0:T(256)(128)(2,1)}, u32[]{:S(2)}) copy-start(bf16[192]{0:T(256)(128)(2,1)} %param.14) | copy-start | bytes 1156
  181.5 9.4 %collective-permute-start.20 = (bf16[96,768]{1,0:T(8,128)(2,1)S(1)}, bf16[96,768]{1,0:T(8,128)(2,1)S(1)}, u32[]{:S(2)}, u32[]{:S(2)}) collective-permute-start(bf16[96,768]{1,0:T(8,128)(2,1)S(1)} %add_convert_fusion.5), channel_id=1, source_target_pairs={{0,16},{4,20},{8,24},{12,28},{16,0},{20,4},{24,8},{28,12},{1,17},{... | collective-permute-start | bytes 442376 | tf_op jit(solution)/shard_map/ppermute | solution.py:494
  181.5 9.4 %collective-permute-start.19 = (f32[1536]{0:T(1024)S(1)}, f32[1536]{0:T(1024)S(1)}, u32[]{:S(2)}, u32[]{:S(2)}) collective-permute-start(f32[1536]{0:T(1024)S(1)} %add.122), channel_id=1, source_target_pairs={{0,16},{4,20},{8,24},{12,28},{16,0},{20,4},{24,8},{28,12},{1,17},{... | collective-permute-start | bytes 18440 | tf_op jit(solution)/shard_map/ppermute | solution.py:494
  191.0 9.0 %collective-permute-start.22 = (bf16[192,768]{1,0:T(8,128)(2,1)S(1)}, bf16[192,768]{1,0:T(8,128)(2,1)S(1)}, u32[]{:S(2)}, u32[]{:S(2)}) collective-permute-start(bf16[192,768]{1,0:T(8,128)(2,1)S(1)} %maximum_select_fusion.3), channel_id=1, source_target_pairs={{0,8},{4,12},{8,0},{12,4},{16,24},{20,28},{24,16},{28,20},{1,9},{5... | collective-permute-start | bytes 884744 | tf_op jit(solution)/shard_map/ppermute | solution.py:494
  191.1 20.4 %collective-permute-start.24 = (bf16[1,1,400,1024]{3,2,1,0:T(8,128)(2,1)}, bf16[1,1,400,1024]{3,2,1,0:T(8,128)(2,1)S(1)}, u32[]{:S(2)}, u32[]{:S(2)}) collective-permute-start(bf16[1,1,400,1024]{3,2,1,0:T(8,128)(2,1)} %add_convert_fusion), channel_id=1, source_target_pairs={{0,2},{1,3},{2,0},{3,1},{4,6},{5,7},{6,4},{7,5},{8,10},{9,11},{10,... | collective-permute-start | bytes 2457608 | tf_op jit(solution)/shard_map/ppermute | solution.py:494
  200.2 15.4 %collective-permute-start.25 = (bf16[384,768]{1,0:T(8,128)(2,1)S(1)}, bf16[384,768]{1,0:T(8,128)(2,1)S(1)}, u32[]{:S(2)}, u32[]{:S(2)}) collective-permute-start(bf16[384,768]{1,0:T(8,128)(2,1)S(1)} %maximum_select_fusion.2), channel_id=1, source_target_pairs={{0,4},{4,0},{8,12},{12,8},{16,20},{20,16},{24,28},{28,24},{1,5},{5... | collective-permute-start | bytes 1769480 | tf_op jit(solution)/shard_map/ppermute | solution.py:494
  211.5 0.9 copy-start.12

commit v14 on v11

--- a/solution.py
+++ b/solution.py
@@ -784,7 +784,7 @@
         elif left == 1:
             now = wide + rest or across[:1] or chain
         else:
-            now = chain + rest or flying
+            now = chain or rest or flying
         final = [f for f in now if f[0] is mix_sum]
         finished, wide_grads = land_in_turn([[f for f in now if f not in final], final], (finished, wide_grads))
         flying = [f for f in flying if f not in now]

time: 216 us -> 216 us (level)
  waiting for transfers between devices: 32.5 us -> 25.6 us
  Pallas kernels: 110 us -> 115 us
    all_to_all x1, waiting for transfers between devices: 5.14 us -> 0.66 us  [move(): return lax.all_to_all(send, 'dp', 0, 0, tiled=True)]
    pallas_call x1, Pallas kernels: 36 us -> 40.5 us  [attention_call(): pl.pallas_call(attention_kernel, grid_spec=grid_spec, out_shape=[jax.Shap...]
    ppermute x26, waiting for transfers between devices: 27.3 us -> 24.9 us  [flip(): return lax.ppermute(value, axis, [(i, i ^ bit) for i in range(size)])]
    ppermute x26, starting transfers between devices: 20.3 us -> 22.4 us  [flip(): return lax.ppermute(value, axis, [(i, i ^ bit) for i in range(size)])]
  transfers between devices with their start and end apart: 27 -> 27, of which waited for: 11 -> 9; matrix products, arithmetic and copies ran while one was open for 17% -> 17% of each run, Pallas kernels for 40% -> 42%
where the time goes in v14:
time: 216 us; the launch traced here: 214 us
  Pallas kernels  115 us (53%)
  other arithmetic  31.8 us (15%)
  starting transfers between devices  28.2 us (13%)
  waiting for transfers between devices  25.6 us (12%)
  local copies, waits for them, and re-layouts  12.5 us (6%)
    pallas_call x1, Pallas kernels, attention_call(): pl.pallas_call(attention_kernel, grid_spec=grid_spec, out_shape=[jax.Shap...  40.5 us
    pallas_call x3, Pallas kernels, project_call(): pl.pallas_call(project_kernel, grid_spec=grid_spec, out_shape=[jax.ShapeD...  29.8 us
    ppermute x26, waiting for transfers between devices, flip(): return lax.ppermute(value, axis, [(i, i ^ bit) for i in range(size)])  24.9 us
    pallas_call x1, Pallas kernels, mlp_call(): pl.pallas_call(functools.partial(mlp_kernel, pieces_order), grid_spec=gri...  23.9 us
    ppermute x26, starting transfers between devices, flip(): return lax.ppermute(value, axis, [(i, i ^ bit) for i in range(size)])  22.4 us
    pallas_call x1, Pallas kernels, early_call(): pl.pallas_call(early_kernel, grid=(tokens // block,), in_specs=[pl.BlockS...  11.2 us
    pallas_call x3, Pallas kernels, finish_call(): pl.pallas_call(finish_kernel, grid=(size * steps,), in_specs=[packed, pac...  9.4 us
    convert_element_type x3, other arithmetic, take(): (self.keep[:, 1:].astype(F32) + arrived[:, 1:].astype(F32)).astype(BF16)  6.04 us
  transfers between devices with their start and end apart: 27, of which 9 were waited for; matrix products, arithmetic and copies ran while one was open for 17% of the time, Pallas kernels for 42%

profile of v14, /device:TPU:0, one launch (start us, length us, event | category | flops | bytes accessed | tf_op | source)
XLA Modules:
  0.0 214.0 jit_solution(14667080783726546369)
XLA Ops:
  0.6 0.7 broadcast_in_dim.53.gain_own.gain
  1.4 3.0 %collective-permute-start = (bf16[192,128]{1,0:T(8,128)(2,1)S(1)}, bf16[192,128]{1,0:T(8,128)(2,1)S(1)}, u32[]{:S(2)}, u32[]{:S(2)}) collective-permute-start(bf16[192,128]{1,0:T(8,128)(2,1)S(1)} %broadcast_in_dim.53.gain_own.gain), channel_id=1, source_target_pairs={{0,2},{1,3},{2,0},{3,1},{4,6},{5,7},{6,4},{7,5},{8,10},{9,11},{10,... | collective-permute-start | bytes 147464 | tf_op jit(solution)/shard_map/ppermute | solution.py:494
  4.9 0.8 slice.65
  5.8 0.8 slice.66
  6.6 1.0 convert_reduce_fusion
  7.6 1.4 fusion.4.mask_q
  8.9 1.5 select_convert_fusion.2.mask_k
  10.4 0.8 fusion.1.pick
  11.2 1.2 xor_multiply_fusion.place
  12.4 0.8 reshape.72
  13.3 0.8 broadcast_in_dim.27.gains
  14.1 1.5 broadcast_in_dim.24.up_bias
  15.7 1.4 broadcast_in_dim.52.bias
  17.8 11.2 %early.1 = (bf16[3,768,1024]{2,1,0:T(8,128)(2,1)}, bf16[3,192,1024]{2,1,0:T(8,128)(2,1)}, bf16[192,3072]{1,0:T(8,128)(2,1)}, f32[192,128]{1,0:T(8,128)}) custom-call(bf16[3072,768]{1,0:T(8,128)(2,1)} %cot.5, bf16[768,768]{1,0:T(8,128)(2,1)} %down.7, bf16[192,768]{1,0:T(8,128)(2,1)} %attn.7, bf16[192,768]{1,0:T(8,128)(2,1)} %fusion.1.pick), custom_call_target="tpu_custom_call" | custom-call | flops 10000 | bytes 12000 | tf_op jit(solution)/shard_map/early/pallas_call | solution.py:63
  29.0 4.0 %collective-permute-done.2.flip_y = bf16[192,3072]{1,0:T(8,128)(2,1)S(1)} collective-permute-done((bf16[192,3072]{1,0:T(8,128)(2,1)}, bf16[192,3072]{1,0:T(8,128)(2,1)S(1)}, u32[]{:S(2)}, u32[]{:S(2)}) %collective-permute-start.2) | collective-permute-done | bytes 1179680 | tf_op jit(solution)/shard_map/ppermute | solution.py:494
  33.1 2.8 %collective-permute-done.5.flip_cy = bf16[192,3072]{1,0:T(8,128)(2,1)S(1)} collective-permute-done((bf16[192,3072]{1,0:T(8,128)(2,1)S(1)}, bf16[192,3072]{1,0:T(8,128)(2,1)S(1)}, u32[]{:S(2)}, u32[]{:S(2)}) %collective-permute-start.5) | collective-permute-done | bytes 1179680 | tf_op jit(solution)/shard_map/ppermute | solution.py:494
  35.9 1.0 copy-done.9
  36.9 23.9 %mlp.1 = (bf16[3,768,1024]{2,1,0:T(8,128)(2,1)}, bf16[3,768,1024]{2,1,0:T(8,128)(2,1)}, bf16[3,768,1024]{2,1,0:T(8,128)(2,1)}, f32[8,3072]{1,0:T(8,128)}, f32[76...) custom-call(s32[4]{0:T(128)} %xor_multiply_fusion.place, ...), custom_call_target="tpu_custom_call" | custom-call | flops 20000 | bytes 30000 | tf_op jit(solution)/shard_map/mlp/pallas_call | solution.py:188
  60.8 5.8 %all-to-all-start = ((bf16[8,192,768]{2,1,0:T(8,128)(2,1)}), bf16[8,192,768]{2,1,0:T(8,128)(2,1)S(1)}, u32[]{:S(2)}, u32[]{:S(2)}) async-start(bf16[8,192,768]{2,1,0:T(8,128)(2,1)} %bitcast.29), calls=%async_computation | async-start | bytes 4718592 | tf_op jit(solution)/shard_map/all_to_all | solution.py:523
  66.6 40.5 %attention.1 = (bf16[3,192,1024]{2,1,0:T(8,128)(2,1)}, bf16[3,576,1024]{2,1,0:T(8,128)(2,1)}, f32[384,128]{1,0:T(8,128)}, f32[1,768]{1,0:T(1,128)}, bf16[768,768]{1,0:T(8,128)(2,1)}) custom-call(s32[12]{0:T(128)} %get-tuple-element.197.first, s32[12]{0:T(128)} %get-tuple-element.198.count, bf16[3,768,1024]{2,1,0:T(8,128)(2,1)} %get-tuple-element.201.normed, ...), custom_call_target="tpu_custom_call" | custom-call | flops 18000 | bytes 5000 | tf_op jit(solution)/shard_map/attention/pallas_call | solution.py:360
  107.1 0.7 reduce.1
  108.2 1.9 constant_dynamic-slice_fusion.4
  110.1 9.9 %project.3 = (bf16[1,2,400,1024]{3,2,1,0:T(8,128)(2,1)}, bf16[1,2,400,1024]{3,2,1,0:T(8,128)(2,1)}) custom-call(s32[1]{0:T(128)} %bitcast.shard, bf16[3,768,1024]{2,1,0:T(8,128)(2,1)} %get-tuple-element.196.active, bf16[3,192,1024]{2,1,0:T(8,128)(2,1)} %get-tuple-element.256.attended, bf16[3,768,1024]{2,1,0:T(8,128)(2,1)} %get-tuple-element.213.d_pre, ...), custom_call_target="tpu_custom_call" | custom-call | flops 8000 | bytes 16000 | tf_op jit(solution)/shard_map/project/pallas_call | solution.py:435
  120.8 1.1 reduce_sum.75
  121.9 1.5 collective-permute-start.10
  123.4 1.2 collective-permute-start.9
  124.6 0.8 collective-permute-start.7
  125.4 1.0 reduce_sum.78
  126.6 1.2 reduce_sum.77
  127.7 10.0 %project.4 = (bf16[1,2,400,1024]{3,2,1,0:T(8,128)(2,1)}, bf16[1,2,400,1024]{3,2,1,0:T(8,128)(2,1)}) custom-call(s32[1]{0:T(128)} %bitcast.shard, bf16[3,768,1024]{2,1,0:T(8,128)(2,1)} %get-tuple-element.196.active, bf16[3,192,1024]{2,1,0:T(8,128)(2,1)} %get-tuple-element.256.attended, bf16[3,768,1024]{2,1,0:T(8,128)(2,1)} %get-tuple-element.213.d_pre, ...), custom_call_target="tpu_custom_call" | custom-call | flops 8000 | bytes 16000 | tf_op jit(solution)/shard_map/project/pallas_call | solution.py:435
  137.9 1.3 add_convert_fusion.2
  139.1 0.9 collective-permute-done.9
  140.0 1.3 maximum_select_fusion.1
  141.3 2.2 %add_convert_fusion.3 = (bf16[192,768]{1,0:T(8,128)(2,1)S(1)}, bf16[192,768]{1,0:T(8,128)(2,1)}) fusion(bf16[384,768]{1,0:T(8,128)(2,1)} %collective-permute-done.10, s32[]{:T(128)S(6)} %mul.38, bf16[768,768]{1,0:T(8,128)(2,1)S(1)} %copy-done.10, s32[]{:T(128)S(6)} %dynamic_slice.55, s32[]{:T(128)S(6)} %select_n.103, s32[]{:T(128)S(6)} %dynamic_slice.47), kind=kLoop, calls=%fused_computation.12 | loop fusion | flops 1179648 | bytes 1769488 | tf_op jit(solution)/shard_map/convert_element_type | solution.py:550
  143.5 0.8 collective-permute-start.15
  144.7 1.4 collective-permute-start.11
  146.1 1.9 collective-permute-start.14
  147.9 9.9 %project.5 = (bf16[1,2,400,1024]{3,2,1,0:T(8,128)(2,1)}, bf16[1,2,400,1024]{3,2,1,0:T(8,128)(2,1)}) custom-call(s32[1]{0:T(128)} %bitcast.shard, bf16[3,768,1024]{2,1,0:T(8,128)(2,1)} %get-tuple-element.196.active, bf16[3,192,1024]{2,1,0:T(8,128)(2,1)} %get-tuple-element.256.attended, bf16[3,768,1024]{2,1,0:T(8,128)(2,1)} %get-tuple-element.213.d_pre, ...), custom_call_target="tpu_custom_call" | custom-call | flops 8000 | bytes 16000 | tf_op jit(solution)/shard_map/project/pallas_call | solution.py:435
  158.4 2.4 %add_convert_fusion.1 = bf16[1,1,400,1024]{3,2,1,0:T(8,128)(2,1)} fusion(bf16[1,2,400,1024]{3,2,1,0:T(8,128)(2,1)} %collective-permute-done.12.from_core, bf16[1,2,400,1024]{3,2,1,0:T(8,128)(2,1)S(1)} %copy-done), kind=kLoop, calls=%fused_computation.2 | loop fusion | flops 1638400 | bytes 2457600 | tf_op jit(solution)/shard_map/convert_element_type | solution.py:590
  160.8 1.8 maximum_select_fusion
  162.6 3.5 %collective-permute-done.14 = bf16[192,768]{1,0:T(8,128)(2,1)S(1)} collective-permute-done((bf16[192,768]{1,0:T(8,128)(2,1)}, bf16[192,768]{1,0:T(8,128)(2,1)S(1)}, u32[]{:S(2)}, u32[]{:S(2)}) %collective-permute-start.14) | collective-permute-done | bytes 294944 | tf_op jit(solution)/shard_map/ppermute | solution.py:494
  166.5 0.7 add_convert_fusion.7
  167.2 2.5 %collective-permute-start.18 = (bf16[96,768]{1,0:T(8,128)(2,1)}, bf16[96,768]{1,0:T(8,128)(2,1)S(1)}, u32[]{:S(2)}, u32[]{:S(2)}) collective-permute-start(bf16[96,768]{1,0:T(8,128)(2,1)} %add_convert_fusion.7), channel_id=1, source_target_pairs={{0,16},{4,20},{8,24},{12,28},{16,0},{20,4},{24,8},{28,12},{1,17},{... | collective-permute-start | bytes 442376 | tf_op jit(solution)/shard_map/ppermute | solution.py:494
  169.6 0.8 collective-permute-start.20
  170.4 1.0 collective-permute-start.23
  171.5 3.1 %finish.3 = (bf16[192,3072]{1,0:T(8,128)(2,1)}, f32[192,3072]{1,0:T(8,128)}) custom-call(bf16[1,2,400,1024]{3,2,1,0:T(8,128)(2,1)} %get-tuple-element.242.keep, bf16[1,2,400,1024]{3,2,1,0:T(8,128)(2,1)} %copy-done.3, bf16[1,1,400,1024]{3,2,1,0:T(8,128)(2,1)} %collective-permute-done.15.from_y, bf16[192,3072]{1,0:T(8,128)(2,1)} %bitcast.19, ...), custom_call_target="tpu_custom_call" | custom-call | flops 3000 | bytes 5000 | tf_op jit(solution)/shard_map/finish/pallas_call | solution.py:471
  174.6 2.4 %add_convert_fusion = bf16[1,1,400,1024]{3,2,1,0:T(8,128)(2,1)} fusion(bf16[1,2,400,1024]{3,2,1,0:T(8,128)(2,1)} %collective-permute-done.16.from_core, bf16[1,2,400,1024]{3,2,1,0:T(8,128)(2,1)S(1)} %copy-done.1), kind=kLoop, calls=%fused_computation.1 | loop fusion | flops 1638400 | bytes 2457600 | tf_op jit(solution)/shard_map/convert_element_type | solution.py:590
  177.0 0.7 add.117
  177.8 1.0 collective-permute-start.19
  178.8 8.0 %collective-permute-done.19 = bf16[96,768]{1,0:T(8,128)(2,1)S(1)} collective-permute-done((bf16[96,768]{1,0:T(8,128)(2,1)S(1)}, bf16[96,768]{1,0:T(8,128)(2,1)S(1)}, u32[]{:S(2)}, u32[]{:S(2)}) %collective-permute-start.19) | collective-permute-done | bytes 147488 | tf_op jit(solution)/shard_map/ppermute | solution.py:494
  186.9 1.1 collective-permute-start.24
  188.0 2.8 %collective-permute-start.21 = (f32[1536]{0:T(1024)S(1)}, f32[1536]{0:T(1024)S(1)}, u32[]{:S(2)}, u32[]{:S(2)}) collective-permute-start(f32[1536]{0:T(1024)S(1)} %add.117), channel_id=1, source_target_pairs={{0,16},{4,20},{8,24},{12,28},{16,0},{20,4},{24,8},{28,12},{1,17},{... | collective-permute-start | bytes 18440 | tf_op jit(solution)/shard_map/ppermute | solution.py:494
  190.8 3.0 %collective-permute-done.21 = f32[1536]{0:T(1024)S(1)} collective-permute-done((f32[1536]{0:T(1024)S(1)}, f32[1536]{0:T(1024)S(1)}, u32[]{:S(2)}, u32[]{:S(2)}) %collective-permute-start.21) | collective-permute-done | bytes 6176 | tf_op jit(solution)/shard_map/ppermute | solution.py:494
  193.9 0.7 slice.88
  195.2 0.8 collective-permute-done.22
  196.2 1.2 collective-permute-start.25
  197.4 1.3 fusion.6
  198.7 3.1 %finish.4 = (bf16[192,3072]{1,0:T(8,128)(2,1)}, f32[192,3072]{1,0:T(8,128)}) custom-call(bf16[1,2,400,1024]{3,2,1,0:T(8,128)(2,1)} %get-tuple-element.265.keep, bf16[1,2,400,1024]{3,2,1,0:T(8,128)(2,1)} %collective-permute-done.12.from_core, bf16[1,1,400,1024]{3,2,1,0:T(8,128)(2,1)} %collective-permute-done.20.from_y, ...), custom_call_target="tpu_custom_call", output_to_operand_aliasing={{0}: (8, {}), {1}: (9, {})} | custom-call | flops 3000 | bytes 5000 | tf_op jit(solution)/shard_map/finish/pallas_call | solution.py:471
  201.9 3.8 %select_convert_fusion = (f32[768,768]{1,0:T(8,128)}, f32[768,768]{1,0:T(8,128)}) fusion(bf16[768,768]{1,0:T(8,128)(2,1)S(1)} %maximum_select_fusion, bf16[768,768]{1,0:T(8,128)(2,1)} %collective-permute-done.23, pred[]{:T(512)S(6)} %gt.7), kind=kLoop, calls=%fused_computation.5 | loop fusion | flops 2359296 | bytes 7077889 | tf_op jit(solution)/shard_map/convert_element_type | solution.py:795
  205.6 1.9 collective-permute-done.24.from_y
  207.5 0.9 copy-done.12
  208.4 3.1 %finish.5 = (bf16[192,3072]{1,0:T(8,128)(2,1)}, f32[192,3072]{1,0:T(8,128)}) custom-call(bf16[1,2,400,1024]{3,2,1,0:T(8,128)(2,1)} %get-tuple-element.277.keep, bf16[1,2,400,1024]{3,2,1,0:T(8,128)(2,1)} %collective-permute-done.16.from_core, bf16[1,1,400,1024]{3,2,1,0:T(8,128)(2,1)} %copy-done.12, ...), custom_call_target="tpu_custom_call", output_to_operand_aliasing={{0}: (8, {}), {1}: (9, {})} | custom-call | flops 3000 | bytes 5000 | tf_op jit(solution)/shard_map/finish/pallas_call | solution.py:471
  211.5 0.9 fusion.2
  212.7 1.4 convert_bitcast_fusion
  (90 shorter events, 5.5 us)
Async XLA Ops:
  1.4 27.6 %copy-start.6 = (bf16[192,128]{1,0:T(8,128)(2,1)}, bf16[192,128]{1,0:T(8,128)(2,1)S(1)}, u32[]{:S(2)}) copy-start(bf16[192,128]{1,0:T(8,128)(2,1)S(1)} %broadcast_in_dim.53.gain_own.gain) | copy-start | bytes 147460
  1.4 11.9 %collective-permute-start = (bf16[192,128]{1,0:T(8,128)(2,1)S(1)}, bf16[192,128]{1,0:T(8,128)(2,1)S(1)}, u32[]{:S(2)}, u32[]{:S(2)}) collective-permute-start(bf16[192,128]{1,0:T(8,128)(2,1)S(1)} %broadcast_in_dim.53.gain_own.gain), channel_id=1, source_target_pairs={{0,2},{1,3},{2,0},{3,1},{4,6},{5,7},{6,4},{7,5},{8,10},{9,11},{10,... | collective-permute-start | bytes 147464 | tf_op jit(solution)/shard_map/ppermute | solution.py:494
  4.4 8.9 %collective-permute-start.1 = (bf16[192,128]{1,0:T(8,128)(2,1)S(1)}, bf16[192,128]{1,0:T(8,128)(2,1)S(1)}, u32[]{:S(2)}, u32[]{:S(2)}) collective-permute-start(bf16[192,128]{1,0:T(8,128)(2,1)S(1)} %broadcast_in_dim.53.gain_own.gain), channel_id=1, source_target_pairs={{0,1},{1,0},{2,3},{3,2},{4,5},{5,4},{6,7},{7,6},{8,9},{9,8},{10,11... | collective-permute-start | bytes 147464 | tf_op jit(solution)/shard_map/ppermute | solution.py:494
  4.4 28.6 %collective-permute-start.2 = (bf16[192,3072]{1,0:T(8,128)(2,1)}, bf16[192,3072]{1,0:T(8,128)(2,1)S(1)}, u32[]{:S(2)}, u32[]{:S(2)}) collective-permute-start(bf16[192,3072]{1,0:T(8,128)(2,1)} %bitcast.16), channel_id=1, source_target_pairs={{0,2},{1,3},{2,0},{3,1},{4,6},{5,7},{6,4},{7,5},{8,10},{9,11},{10,... | collective-permute-start | bytes 3538952 | tf_op jit(solution)/shard_map/ppermute | solution.py:494
  4.6 28.4 %collective-permute-start.4 = (bf16[192,3072]{1,0:T(8,128)(2,1)}, bf16[192,3072]{1,0:T(8,128)(2,1)S(1)}, u32[]{:S(2)}, u32[]{:S(2)}) collective-permute-start(bf16[192,3072]{1,0:T(8,128)(2,1)} %bitcast.17), channel_id=1, source_target_pairs={{0,1},{1,0},{2,3},{3,2},{4,5},{5,4},{6,7},{7,6},{8,9},{9,8},{10,11... | collective-permute-start | bytes 3538952 | tf_op jit(solution)/shard_map/ppermute | solution.py:494
  13.3 15.6 %copy-start.15 = (bf16[192,128]{1,0:T(8,128)(2,1)}, bf16[192,128]{1,0:T(8,128)(2,1)S(1)}, u32[]{:S(2)}) copy-start(bf16[192,128]{1,0:T(8,128)(2,1)S(1)} %collective-permute-done.gain_y) | copy-start | bytes 147460
  13.3 15.6 %copy-start.16 = (bf16[192,128]{1,0:T(8,128)(2,1)}, bf16[192,128]{1,0:T(8,128)(2,1)S(1)}, u32[]{:S(2)}) copy-start(bf16[192,128]{1,0:T(8,128)(2,1)S(1)} %collective-permute-done.1.gain_c) | copy-start | bytes 147460
  17.0 11.9 %collective-permute-start.3 = (bf16[192,128]{1,0:T(8,128)(2,1)S(1)}, bf16[192,128]{1,0:T(8,128)(2,1)S(1)}, u32[]{:S(2)}, u32[]{:S(2)}) collective-permute-start(bf16[192,128]{1,0:T(8,128)(2,1)S(1)} %collective-permute-done.gain_y), channel_id=1, source_target_pairs={{0,1},{1,0},{2,3},{3,2},{4,5},{5,4},{6,7},{7,6},{8,9},{9,8},{10,11... | collective-permute-start | bytes 147464 | tf_op jit(solution)/shard_map/ppermute | solution.py:494
  29.0 4.0 %copy-start.17 = (bf16[192,128]{1,0:T(8,128)(2,1)}, bf16[192,128]{1,0:T(8,128)(2,1)S(1)}, u32[]{:S(2)}) copy-start(bf16[192,128]{1,0:T(8,128)(2,1)S(1)} %collective-permute-done.3.gain_cy) | copy-start | bytes 147460
  33.0 2.9 %copy-start.7 = (bf16[192,3072]{1,0:T(8,128)(2,1)}, bf16[192,3072]{1,0:T(8,128)(2,1)S(1)}, u32[]{:S(2)}) copy-start(bf16[192,3072]{1,0:T(8,128)(2,1)S(1)} %collective-permute-done.2.flip_y) | copy-start | bytes 3538948
  33.0 2.8 %collective-permute-start.5 = (bf16[192,3072]{1,0:T(8,128)(2,1)S(1)}, bf16[192,3072]{1,0:T(8,128)(2,1)S(1)}, u32[]{:S(2)}, u32[]{:S(2)}) collective-permute-start(bf16[192,3072]{1,0:T(8,128)(2,1)S(1)} %collective-permute-done.2.flip_y), channel_id=1, source_target_pairs={{0,1},{1,0},{2,3},{3,2},{4,5},{5,4},{6,7},{7,6},{8,9},{9,8},{10,11... | collective-permute-start | bytes 3538952 | tf_op jit(solution)/shard_map/ppermute | solution.py:494
  33.1 2.8 %copy-start.8 = (bf16[192,3072]{1,0:T(8,128)(2,1)}, bf16[192,3072]{1,0:T(8,128)(2,1)S(1)}, u32[]{:S(2)}) copy-start(bf16[192,3072]{1,0:T(8,128)(2,1)S(1)} %collective-permute-done.4.flip_c) | copy-start | bytes 3538948
  35.9 1.0 copy-start.9
  60.8 60.0 %all-to-all-start = ((bf16[8,192,768]{2,1,0:T(8,128)(2,1)}), bf16[8,192,768]{2,1,0:T(8,128)(2,1)S(1)}, u32[]{:S(2)}, u32[]{:S(2)}) async-start(bf16[8,192,768]{2,1,0:T(8,128)(2,1)} %bitcast.29), calls=%async_computation | async-start | bytes 4718592 | tf_op jit(solution)/shard_map/all_to_all | solution.py:523
  66.6 41.3 %copy-start.13 = (f32[768,128]{1,0:T(8,128)S(1)}, f32[768,128]{1,0:T(8,128)}, u32[]{:S(2)}) copy-start(f32[768,128]{1,0:T(8,128)} %get-tuple-element.211) | copy-start | bytes 1179652
  110.1 10.0 %collective-permute-start.6 = (f32[2,192]{1,0:T(2,128)S(1)}, f32[2,192]{1,0:T(2,128)S(1)}, u32[]{:S(2)}, u32[]{:S(2)}) collective-permute-start(f32[2,192]{1,0:T(2,128)S(1)} %pad_maximum_fusion.2), channel_id=1, source_target_pairs={{0,1},{1,0},{2,3},{3,2},{4,5},{5,4},{6,7},{7,6},{8,9},{9,8},{10,11... | collective-permute-start | bytes 4616 | tf_op jit(solution)/shard_map/ppermute | solution.py:494
  120.1 6.3 %copy-start.14 = (f32[384,128]{1,0:T(8,128)S(1)}, f32[384,128]{1,0:T(8,128)}, u32[]{:S(2)}) copy-start(f32[384,128]{1,0:T(8,128)} %get-tuple-element.239) | copy-start | bytes 589828
  121.9 15.9 %collective-permute-start.8 = (bf16[1,2,400,1024]{3,2,1,0:T(8,128)(2,1)}, bf16[1,2,400,1024]{3,2,1,0:T(8,128)(2,1)S(1)}, u32[]{:S(2)}, u32[]{:S(2)}) collective-permute-start(bf16[1,2,400,1024]{3,2,1,0:T(8,128)(2,1)} %get-tuple-element.235), channel_id=1, source_target_pairs={{0,1},{1,0},{2,3},{3,2},{4,5},{5,4},{6,7},{7,6},{8,9},{9,8},{10,11... | collective-permute-start | bytes 4915208 | tf_op jit(solution)/shard_map/ppermute | solution.py:494
  121.9 19.4 %collective-permute-start.10 = (bf16[384,768]{1,0:T(8,128)(2,1)}, bf16[384,768]{1,0:T(8,128)(2,1)}, u32[]{:S(2)}, u32[]{:S(2)}) collective-permute-start(bf16[384,768]{1,0:T(8,128)(2,1)} %constant_dynamic-slice_fusion.4), channel_id=1, source_target_pairs={{0,4},{4,0},{8,12},{12,8},{16,20},{20,16},{24,28},{28,24},{1,5},{5... | collective-permute-start | bytes 1769480 | tf_op jit(solution)/shard_map/ppermute | solution.py:494
  123.4 16.7 %collective-permute-start.9 = (bf16[192,768]{1,0:T(8,128)(2,1)}, bf16[192,768]{1,0:T(8,128)(2,1)}, u32[]{:S(2)}, u32[]{:S(2)}) collective-permute-start(bf16[192,768]{1,0:T(8,128)(2,1)} %reduce_sum.75), channel_id=1, source_target_pairs={{0,16},{4,20},{8,24},{12,28},{16,0},{20,4},{24,8},{28,12},{1,17},{... | collective-permute-start | bytes 884744 | tf_op jit(solution)/shard_map/ppermute | solution.py:494
  124.6 13.1 %collective-permute-start.7 = (f32[192]{0:T(256)S(1)}, f32[192]{0:T(256)S(1)}, u32[]{:S(2)}, u32[]{:S(2)}) collective-permute-start(f32[192]{0:T(256)S(1)} %bitcast.31), channel_id=1, source_target_pairs={{0,2},{1,3},{2,0},{3,1},{4,6},{5,7},{6,4},{7,5},{8,10},{9,11},{10,... | collective-permute-start | bytes 2312 | tf_op jit(solution)/shard_map/ppermute | solution.py:494
  127.7 10.1 %copy-start.2 = (bf16[1,2,400,1024]{3,2,1,0:T(8,128)(2,1)S(1)}, bf16[1,2,400,1024]{3,2,1,0:T(8,128)(2,1)}, u32[]{:S(2)}) copy-start(bf16[1,2,400,1024]{3,2,1,0:T(8,128)(2,1)} %get-tuple-element.242.keep) | copy-start | bytes 4915204
  137.8 3.5 %copy-start.3 = (bf16[1,2,400,1024]{3,2,1,0:T(8,128)(2,1)}, bf16[1,2,400,1024]{3,2,1,0:T(8,128)(2,1)S(1)}, u32[]{:S(2)}) copy-start(bf16[1,2,400,1024]{3,2,1,0:T(8,128)(2,1)S(1)} %collective-permute-done.8.from_core) | copy-start | bytes 4915204
  137.9 2.2 %copy-start.11 = (bf16[192,768]{1,0:T(8,128)(2,1)S(1)}, bf16[192,768]{1,0:T(8,128)(2,1)}, u32[]{:S(2)}) copy-start(bf16[192,768]{1,0:T(8,128)(2,1)} %reduce_sum.75) | copy-start | bytes 884740
  137.9 3.5 %copy-start.10 = (bf16[768,768]{1,0:T(8,128)(2,1)S(1)}, bf16[768,768]{1,0:T(8,128)(2,1)}, u32[]{:S(2)}) copy-start(bf16[768,768]{1,0:T(8,128)(2,1)} %get-tuple-element.209) | copy-start | bytes 3538948
  141.3 16.5 %copy-start.4 = (bf16[384,768]{1,0:T(8,128)(2,1)}, bf16[384,768]{1,0:T(8,128)(2,1)S(1)}, u32[]{:S(2)}) copy-start(bf16[384,768]{1,0:T(8,128)(2,1)S(1)} %maximum_select_fusion.1) | copy-start | bytes 1769476
  143.5 14.9 %copy-start = (bf16[1,2,400,1024]{3,2,1,0:T(8,128)(2,1)S(1)}, bf16[1,2,400,1024]{3,2,1,0:T(8,128)(2,1)}, u32[]{:S(2)}) copy-start(bf16[1,2,400,1024]{3,2,1,0:T(8,128)(2,1)} %get-tuple-element.265.keep) | copy-start | bytes 4915204
  143.5 14.3 %collective-permute-start.12 = (bf16[1,2,400,1024]{3,2,1,0:T(8,128)(2,1)}, bf16[1,2,400,1024]{3,2,1,0:T(8,128)(2,1)}, u32[]{:S(2)}, u32[]{:S(2)}) collective-permute-start(bf16[1,2,400,1024]{3,2,1,0:T(8,128)(2,1)} %get-tuple-element.261), channel_id=1, source_target_pairs={{0,1},{1,0},{2,3},{3,2},{4,5},{5,4},{6,7},{7,6},{8,9},{9,8},{10,11... | collective-permute-start | bytes 4915208 | tf_op jit(solution)/shard_map/ppermute | solution.py:494
  143.5 22.6 %collective-permute-start.15 = (bf16[1,1,400,1024]{3,2,1,0:T(8,128)(2,1)}, bf16[1,1,400,1024]{3,2,1,0:T(8,128)(2,1)}, u32[]{:S(2)}, u32[]{:S(2)}) collective-permute-start(bf16[1,1,400,1024]{3,2,1,0:T(8,128)(2,1)} %add_convert_fusion.2), channel_id=1, source_target_pairs={{0,2},{1,3},{2,0},{3,1},{4,6},{5,7},{6,4},{7,5},{8,10},{9,11},{10,... | collective-permute-start | bytes 2457608 | tf_op jit(solution)/shard_map/ppermute | solution.py:494
  144.3 16.5 %collective-permute-start.13 = (bf16[384,768]{1,0:T(8,128)(2,1)S(1)}, bf16[384,768]{1,0:T(8,128)(2,1)}, u32[]{:S(2)}, u32[]{:S(2)}) collective-permute-start(bf16[384,768]{1,0:T(8,128)(2,1)S(1)} %maximum_select_fusion.1), channel_id=1, source_target_pairs={{0,8},{4,12},{8,0},{12,4},{16,24},{20,28},{24,16},{28,20},{1,9},{5... | collective-permute-start | bytes 1769480 | tf_op jit(solution)/shard_map/ppermute | solution.py:494
  144.7 13.1 %collective-permute-start.11 = (f32[1536]{0:T(1024)S(1)}, f32[1536]{0:T(1024)S(1)}, u32[]{:S(2)}, u32[]{:S(2)}) collective-permute-start(f32[1536]{0:T(1024)S(1)} %concatenate.35), channel_id=1, source_target_pairs={{0,4},{4,0},{8,12},{12,8},{16,20},{20,16},{24,28},{28,24},{1,5},{5... | collective-permute-start | bytes 18440 | tf_op jit(solution)/shard_map/ppermute | solution.py:494
  146.1 20.0 %collective-permute-start.14 = (bf16[192,768]{1,0:T(8,128)(2,1)}, bf16[192,768]{1,0:T(8,128)(2,1)S(1)}, u32[]{:S(2)}, u32[]{:S(2)}) collective-permute-start(bf16[192,768]{1,0:T(8,128)(2,1)} %get-tuple-element.273), channel_id=1, source_target_pairs={{0,8},{4,12},{8,0},{12,4},{16,24},{20,28},{24,16},{28,20},{1,9},{5... | collective-permute-start | bytes 884744 | tf_op jit(solution)/shard_map/ppermute | solution.py:494
  157.8 3.0 %copy-start.5 = (bf16[384,768]{1,0:T(8,128)(2,1)S(1)}, bf16[384,768]{1,0:T(8,128)(2,1)}, u32[]{:S(2)}) copy-start(bf16[384,768]{1,0:T(8,128)(2,1)} %copy-done.4) | copy-start | bytes 1769476
  166.1 8.5 %collective-permute-start.16 = (bf16[1,2,400,1024]{3,2,1,0:T(8,128)(2,1)}, bf16[1,2,400,1024]{3,2,1,0:T(8,128)(2,1)}, u32[]{:S(2)}, u32[]{:S(2)}) collective-permute-start(bf16[1,2,400,1024]{3,2,1,0:T(8,128)(2,1)} %get-tuple-element.288), channel_id=1, source_target_pairs={{0,1},{1,0},{2,3},{3,2},{4,5},{5,4},{6,7},{7,6},{8,9},{9,8},{10,11... | collective-permute-start | bytes 4915208 | tf_op jit(solution)/shard_map/ppermute | solution.py:494
  166.1 8.5 %collective-permute-start.17 = (f32[1536]{0:T(1024)}, f32[1536]{0:T(1024)}, u32[]{:S(2)}, u32[]{:S(2)}) collective-permute-start(f32[1536]{0:T(1024)} %add.114), channel_id=1, source_target_pairs={{0,8},{4,12},{8,0},{12,4},{16,24},{20,28},{24,16},{28,20},{1,9},{5... | collective-permute-start | bytes 18440 | tf_op jit(solution)/shard_map/ppermute | solution.py:494
  167.2 10.6 %collective-permute-start.18 = (bf16[96,768]{1,0:T(8,128)(2,1)}, bf16[96,768]{1,0:T(8,128)(2,1)S(1)}, u32[]{:S(2)}, u32[]{:S(2)}) collective-permute-start(bf16[96,768]{1,0:T(8,128)(2,1)} %add_convert_fusion.7), channel_id=1, source_target_pairs={{0,16},{4,20},{8,24},{12,28},{16,0},{20,4},{24,8},{28,12},{1,17},{... | collective-permute-start | bytes 442376 | tf_op jit(solution)/shard_map/ppermute | solution.py:494
  169.6 21.2 %collective-permute-start.20 = (bf16[1,1,400,1024]{3,2,1,0:T(8,128)(2,1)}, bf16[1,1,400,1024]{3,2,1,0:T(8,128)(2,1)}, u32[]{:S(2)}, u32[]{:S(2)}) collective-permute-start(bf16[1,1,400,1024]{3,2,1,0:T(8,128)(2,1)} %add_convert_fusion.1), channel_id=1, source_target_pairs={{0,2},{1,3},{2,0},{3,1},{4,6},{5,7},{6,4},{7,5},{8,10},{9,11},{10,... | collective-permute-start | bytes 2457608 | tf_op jit(solution)/shard_map/ppermute | solution.py:494
  170.4 31.4 %collective-permute-start.23 = (bf16[768,768]{1,0:T(8,128)(2,1)S(1)}, bf16[768,768]{1,0:T(8,128)(2,1)}, u32[]{:S(2)}, u32[]{:S(2)}) collective-permute-start(bf16[768,768]{1,0:T(8,128)(2,1)S(1)} %maximum_select_fusion), channel_id=1, source_target_pairs={{0,4},{4,0},{8,12},{12,8},{16,20},{20,16},{24,28},{28,24},{1,5},{5... | collective-permute-start | bytes 3538952 | tf_op jit(solution)/shard_map/ppermute | solution.py:494
  171.5 3.2 %copy-start.1 = (bf16[1,2,400,1024]{3,2,1,0:T(8,128)(2,1)S(1)}, bf16[1,2,400,1024]{3,2,1,0:T(8,128)(2,1)}, u32[]{:S(2)}) copy-start(bf16[1,2,400,1024]{3,2,1,0:T(8,128)(2,1)} %get-tuple-element.277.keep) | copy-start | bytes 4915204
  177.8 9.0 %collective-permute-start.19 = (bf16[96,768]{1,0:T(8,128)(2,1)S(1)}, bf16[96,768]{1,0:T(8,128)(2,1)S(1)}, u32[]{:S(2)}, u32[]{:S(2)}) collective-permute-start(bf16[96,768]{1,0:T(8,128)(2,1)S(1)} %add_convert_fusion.5), channel_id=1, source_target_pairs={{0,16},{4,20},{8,24},{12,28},{16,0},{20,4},{24,8},{28,12},{1,17},{... | collective-permute-start | bytes 442376 | tf_op jit(solution)/shard_map/ppermute | solution.py:494
  186.9 9.2 %collective-permute-start.22 = (bf16[192,768]{1,0:T(8,128)(2,1)S(1)}, bf16[192,768]{1,0:T(8,128)(2,1)S(1)}, u32[]{:S(2)}, u32[]{:S(2)}) collective-permute-start(bf16[192,768]{1,0:T(8,128)(2,1)S(1)} %maximum_select_fusion.3), channel_id=1, source_target_pairs={{0,8},{4,12},{8,0},{12,4},{16,24},{20,28},{24,16},{28,20},{1,9},{5... | collective-permute-start | bytes 884744 | tf_op jit(solution)/shard_map/ppermute | solution.py:494
  186.9 20.6 %collective-permute-start.24 = (bf16[1,1,400,1024]{3,2,1,0:T(8,128)(2,1)}, bf16[1,1,400,1024]{3,2,1,0:T(8,128)(2,1)S(1)}, u32[]{:S(2)}, u32[]{:S(2)}) collective-permute-start(bf16[1,1,400,1024]{3,2,1,0:T(8,128)(2,1)} %add_convert_fusion), channel_id=1, source_target_pairs={{0,2},{1,3},{2,0},{3,1},{4,6},{5,7},{6,4},{7,5},{8,10},{9,11},{10,... | collective-permute-start | bytes 2457608 | tf_op jit(solution)/shard_map/ppermute | solution.py:494
  188.0 5.8 %collective-permute-start.21 = (f32[1536]{0:T(1024)S(1)}, f32[1536]{0:T(1024)S(1)}, u32[]{:S(2)}, u32[]{:S(2)}) collective-permute-start(f32[1536]{0:T(1024)S(1)} %add.117), channel_id=1, source_target_pairs={{0,16},{4,20},{8,24},{12,28},{16,0},{20,4},{24,8},{28,12},{1,17},{... | collective-permute-start | bytes 18440 | tf_op jit(solution)/shard_map/ppermute | solution.py:494
  196.2 15.3 %collective-permute-start.25 = (bf16[384,768]{1,0:T(8,128)(2,1)S(1)}, bf16[384,768]{1,0:T(8,128)(2,1)S(1)}, u32[]{:S(2)}, u32[]{:S(2)}) collective-permute-start(bf16[384,768]{1,0:T(8,128)(2,1)S(1)} %maximum_select_fusion.2), channel_id=1, source_target_pairs={{0,4},{4,0},{8,12},{12,8},{16,20},{20,16},{24,28},{28,24},{1,5},{5... | collective-permute-start | bytes 1769480 | tf_op jit(solution)/shard_map/ppermute | solution.py:494
  207.5 0.9 copy-start.12

commit v15 on v11

--- a/solution.py
+++ b/solution.py
@@ -741,7 +741,7 @@
         wide = [f for f in flying if f[0] is mlp_sum]
         chain = [f for f in flying if f[0] is mix_sum and f not in late]
         quick = [f for f in flying if f not in late + wide + chain]
-        keep, send = land_in_turn([quick, wide, chain], sent)
+        keep, send = land_in_turn([quick, chain, wide] if begin == 1 else [quick, wide, chain], sent)
         if begin == final and begin > 0:
             _, ahead = launch([mix_sum], ())
             (keep, send), *_ = (land(late, (keep, send)),)

time: 216 us -> 217 us (level)
  transfers between devices with their start and end apart: 27 -> 27, of which waited for: 11 -> 9; matrix products, arithmetic and copies ran while one was open for 17% -> 17% of each run, Pallas kernels for 40% -> 40%
where the time goes in v15:
time: 217 us; the launch traced here: 216 us
  Pallas kernels  111 us (51%)
  waiting for transfers between devices  32.3 us (15%)
  other arithmetic  30.7 us (14%)
  starting transfers between devices  27.6 us (13%)
  local copies, waits for them, and re-layouts  13.3 us (6%)
    pallas_call x1, Pallas kernels, attention_call(): pl.pallas_call(attention_kernel, grid_spec=grid_spec, out_shape=[jax.Shap...  36.7 us
    pallas_call x3, Pallas kernels, project_call(): pl.pallas_call(project_kernel, grid_spec=grid_spec, out_shape=[jax.ShapeD...  29.7 us
    ppermute x26, waiting for transfers between devices, flip(): return lax.ppermute(value, axis, [(i, i ^ bit) for i in range(size)])  27.8 us
    pallas_call x1, Pallas kernels, mlp_call(): pl.pallas_call(functools.partial(mlp_kernel, pieces_order), grid_spec=gri...  23.9 us
    ppermute x26, starting transfers between devices, flip(): return lax.ppermute(value, axis, [(i, i ^ bit) for i in range(size)])  21.8 us
    pallas_call x1, Pallas kernels, early_call(): pl.pallas_call(early_kernel, grid=(tokens // block,), in_specs=[pl.BlockS...  11.2 us
    pallas_call x3, Pallas kernels, finish_call(): pl.pallas_call(finish_kernel, grid=(size * steps,), in_specs=[packed, pac...  9.4 us
    convert_element_type x3, other arithmetic, take(): (self.keep[:, 1:].astype(F32) + arrived[:, 1:].astype(F32)).astype(BF16)  6.02 us
  transfers between devices with their start and end apart: 27, of which 9 were waited for; matrix products, arithmetic and copies ran while one was open for 17% of the time, Pallas kernels for 40%

profile of v15, /device:TPU:0, one launch (start us, length us, event | category | flops | bytes accessed | tf_op | source)
XLA Modules:
  0.0 215.7 jit_solution(11290454147179697305)
XLA Ops:
  0.6 0.7 broadcast_in_dim.53.gain_own.gain
  1.4 3.0 %collective-permute-start = (bf16[192,128]{1,0:T(8,128)(2,1)S(1)}, bf16[192,128]{1,0:T(8,128)(2,1)S(1)}, u32[]{:S(2)}, u32[]{:S(2)}) collective-permute-start(bf16[192,128]{1,0:T(8,128)(2,1)S(1)} %broadcast_in_dim.53.gain_own.gain), channel_id=1, source_target_pairs={{0,2},{1,3},{2,0},{3,1},{4,6},{5,7},{6,4},{7,5},{8,10},{9,11},{10,... | collective-permute-start | bytes 147464 | tf_op jit(solution)/shard_map/ppermute | solution.py:494
  4.9 0.8 slice.65
  5.8 0.8 slice.66
  6.6 1.0 convert_reduce_fusion
  7.6 1.4 fusion.4.mask_q
  8.9 1.4 select_convert_fusion.2.mask_k
  10.4 0.8 fusion.1.pick
  11.2 1.2 xor_multiply_fusion.place
  12.4 0.8 reshape.72
  13.3 0.8 broadcast_in_dim.27.gains
  14.1 1.5 broadcast_in_dim.24.up_bias
  15.6 1.4 broadcast_in_dim.52.bias
  17.7 11.2 %early.1 = (bf16[3,768,1024]{2,1,0:T(8,128)(2,1)}, bf16[3,192,1024]{2,1,0:T(8,128)(2,1)}, bf16[192,3072]{1,0:T(8,128)(2,1)}, f32[192,128]{1,0:T(8,128)}) custom-call(bf16[3072,768]{1,0:T(8,128)(2,1)} %cot.5, bf16[768,768]{1,0:T(8,128)(2,1)} %down.7, bf16[192,768]{1,0:T(8,128)(2,1)} %attn.7, bf16[192,768]{1,0:T(8,128)(2,1)} %fusion.1.pick), custom_call_target="tpu_custom_call" | custom-call | flops 10000 | bytes 12000 | tf_op jit(solution)/shard_map/early/pallas_call | solution.py:63
  28.9 4.1 %collective-permute-done.2.flip_y = bf16[192,3072]{1,0:T(8,128)(2,1)S(1)} collective-permute-done((bf16[192,3072]{1,0:T(8,128)(2,1)}, bf16[192,3072]{1,0:T(8,128)(2,1)S(1)}, u32[]{:S(2)}, u32[]{:S(2)}) %collective-permute-start.2) | collective-permute-done | bytes 1179680 | tf_op jit(solution)/shard_map/ppermute | solution.py:494
  33.1 2.8 %collective-permute-done.5.flip_cy = bf16[192,3072]{1,0:T(8,128)(2,1)S(1)} collective-permute-done((bf16[192,3072]{1,0:T(8,128)(2,1)S(1)}, bf16[192,3072]{1,0:T(8,128)(2,1)S(1)}, u32[]{:S(2)}, u32[]{:S(2)}) %collective-permute-start.5) | collective-permute-done | bytes 1179680 | tf_op jit(solution)/shard_map/ppermute | solution.py:494
  35.9 1.0 copy-done.7
  36.9 23.9 %mlp.1 = (bf16[3,768,1024]{2,1,0:T(8,128)(2,1)}, bf16[3,768,1024]{2,1,0:T(8,128)(2,1)}, bf16[3,768,1024]{2,1,0:T(8,128)(2,1)}, f32[8,3072]{1,0:T(8,128)}, f32[76...) custom-call(s32[4]{0:T(128)} %xor_multiply_fusion.place, ...), custom_call_target="tpu_custom_call" | custom-call | flops 20000 | bytes 30000 | tf_op jit(solution)/shard_map/mlp/pallas_call | solution.py:188
  60.8 5.8 %all-to-all-start = ((bf16[8,192,768]{2,1,0:T(8,128)(2,1)}), bf16[8,192,768]{2,1,0:T(8,128)(2,1)S(1)}, u32[]{:S(2)}, u32[]{:S(2)}) async-start(bf16[8,192,768]{2,1,0:T(8,128)(2,1)} %bitcast.29), calls=%async_computation | async-start | bytes 4718592 | tf_op jit(solution)/shard_map/all_to_all | solution.py:523
  66.6 36.7 %attention.1 = (bf16[3,192,1024]{2,1,0:T(8,128)(2,1)}, bf16[3,576,1024]{2,1,0:T(8,128)(2,1)}, f32[384,128]{1,0:T(8,128)}, f32[1,768]{1,0:T(1,128)}, bf16[768,768]{1,0:T(8,128)(2,1)}) custom-call(s32[12]{0:T(128)} %get-tuple-element.197.first, s32[12]{0:T(128)} %get-tuple-element.198.count, bf16[3,768,1024]{2,1,0:T(8,128)(2,1)} %get-tuple-element.201.normed, ...), custom_call_target="tpu_custom_call" | custom-call | flops 18000 | bytes 5000 | tf_op jit(solution)/shard_map/attention/pallas_call | solution.py:360
  103.4 0.7 reduce.1
  104.5 1.9 constant_dynamic-slice_fusion.4
  106.4 9.9 %project.3 = (bf16[1,2,400,1024]{3,2,1,0:T(8,128)(2,1)}, bf16[1,2,400,1024]{3,2,1,0:T(8,128)(2,1)}) custom-call(s32[1]{0:T(128)} %bitcast.shard, bf16[3,768,1024]{2,1,0:T(8,128)(2,1)} %get-tuple-element.196.active, bf16[3,192,1024]{2,1,0:T(8,128)(2,1)} %get-tuple-element.256.attended, bf16[3,768,1024]{2,1,0:T(8,128)(2,1)} %get-tuple-element.213.d_pre, ...), custom_call_target="tpu_custom_call" | custom-call | flops 8000 | bytes 16000 | tf_op jit(solution)/shard_map/project/pallas_call | solution.py:435
  116.4 4.4 %all-to-all-done = bf16[8,192,768]{2,1,0:T(8,128)(2,1)S(1)} async-done(((bf16[8,192,768]{2,1,0:T(8,128)(2,1)}), bf16[8,192,768]{2,1,0:T(8,128)(2,1)S(1)}, u32[]{:S(2)}, u32[]{:S(2)}) %all-to-all-start) | async-done | bytes 2359328 | tf_op jit(solution)/shard_map/all_to_all | solution.py:523
  120.8 1.1 reduce_sum.75
  121.9 1.5 collective-permute-start.9
  123.4 0.8 collective-permute-start.7
  124.1 1.0 reduce_sum.78
  125.3 1.2 reduce_sum.77
  126.5 2.4 %collective-permute-start.10 = (bf16[192,768]{1,0:T(8,128)(2,1)}, bf16[192,768]{1,0:T(8,128)(2,1)}, u32[]{:S(2)}, u32[]{:S(2)}) collective-permute-start(bf16[192,768]{1,0:T(8,128)(2,1)} %reduce_sum.75), channel_id=1, source_target_pairs={{0,16},{4,20},{8,24},{12,28},{16,0},{20,4},{24,8},{28,12},{1,17},{... | collective-permute-start | bytes 884744 | tf_op jit(solution)/shard_map/ppermute | solution.py:494
  128.9 9.9 %project.4 = (bf16[1,2,400,1024]{3,2,1,0:T(8,128)(2,1)}, bf16[1,2,400,1024]{3,2,1,0:T(8,128)(2,1)}) custom-call(s32[1]{0:T(128)} %bitcast.shard, bf16[3,768,1024]{2,1,0:T(8,128)(2,1)} %get-tuple-element.196.active, bf16[3,192,1024]{2,1,0:T(8,128)(2,1)} %get-tuple-element.256.attended, bf16[3,768,1024]{2,1,0:T(8,128)(2,1)} %get-tuple-element.213.d_pre, ...), custom_call_target="tpu_custom_call" | custom-call | flops 8000 | bytes 16000 | tf_op jit(solution)/shard_map/project/pallas_call | solution.py:435
  138.9 1.3 add_convert_fusion.2
  140.1 0.8 copy-done.8
  140.9 2.1 add_convert_fusion.3
  143.1 1.3 maximum_select_fusion.1
  144.4 1.3 collective-permute-start.15
  145.7 1.1 collective-permute-start.11
  146.8 1.4 collective-permute-start.14
  148.2 9.9 %project.5 = (bf16[1,2,400,1024]{3,2,1,0:T(8,128)(2,1)}, bf16[1,2,400,1024]{3,2,1,0:T(8,128)(2,1)}) custom-call(s32[1]{0:T(128)} %bitcast.shard, bf16[3,768,1024]{2,1,0:T(8,128)(2,1)} %get-tuple-element.196.active, bf16[3,192,1024]{2,1,0:T(8,128)(2,1)} %get-tuple-element.256.attended, bf16[3,768,1024]{2,1,0:T(8,128)(2,1)} %get-tuple-element.213.d_pre, ...), custom_call_target="tpu_custom_call" | custom-call | flops 8000 | bytes 16000 | tf_op jit(solution)/shard_map/project/pallas_call | solution.py:435
  158.1 2.4 %add_convert_fusion.1 = bf16[1,1,400,1024]{3,2,1,0:T(8,128)(2,1)} fusion(bf16[1,2,400,1024]{3,2,1,0:T(8,128)(2,1)} %collective-permute-done.12.from_core, bf16[1,2,400,1024]{3,2,1,0:T(8,128)(2,1)S(1)} %copy-done), kind=kLoop, calls=%fused_computation.2 | loop fusion | flops 1638400 | bytes 2457600 | tf_op jit(solution)/shard_map/convert_element_type | solution.py:590
  160.5 1.5 collective-permute-done.13
  162.0 1.6 maximum_select_fusion
  163.6 3.9 %collective-permute-done.14 = bf16[192,768]{1,0:T(8,128)(2,1)} collective-permute-done((bf16[192,768]{1,0:T(8,128)(2,1)}, bf16[192,768]{1,0:T(8,128)(2,1)}, u32[]{:S(2)}, u32[]{:S(2)}) %collective-permute-start.14) | collective-permute-done | bytes 294944 | tf_op jit(solution)/shard_map/ppermute | solution.py:494
  167.8 0.9 add_convert_fusion.7
  168.8 1.7 collective-permute-start.18
  170.5 0.8 collective-permute-start.21
  171.3 1.4 collective-permute-start.23
  172.7 3.1 %finish.3 = (bf16[192,3072]{1,0:T(8,128)(2,1)}, f32[192,3072]{1,0:T(8,128)}) custom-call(bf16[1,2,400,1024]{3,2,1,0:T(8,128)(2,1)} %get-tuple-element.242.keep, bf16[1,2,400,1024]{3,2,1,0:T(8,128)(2,1)} %copy-done.3, bf16[1,1,400,1024]{3,2,1,0:T(8,128)(2,1)} %collective-permute-done.15.from_y, bf16[192,3072]{1,0:T(8,128)(2,1)} %bitcast.19, ...), custom_call_target="tpu_custom_call" | custom-call | flops 3000 | bytes 5000 | tf_op jit(solution)/shard_map/finish/pallas_call | solution.py:471
  175.8 2.4 %add_convert_fusion = bf16[1,1,400,1024]{3,2,1,0:T(8,128)(2,1)} fusion(bf16[1,2,400,1024]{3,2,1,0:T(8,128)(2,1)} %collective-permute-done.16.from_core, bf16[1,2,400,1024]{3,2,1,0:T(8,128)(2,1)S(1)} %copy-done.1), kind=kLoop, calls=%fused_computation.1 | loop fusion | flops 1638400 | bytes 2457600 | tf_op jit(solution)/shard_map/convert_element_type | solution.py:590
  178.9 1.0 add_convert_fusion.5
  180.0 2.8 %collective-permute-start.19 = (f32[1536]{0:T(1024)S(1)}, f32[1536]{0:T(1024)S(1)}, u32[]{:S(2)}, u32[]{:S(2)}) collective-permute-start(f32[1536]{0:T(1024)S(1)} %add.117), channel_id=1, source_target_pairs={{0,16},{4,20},{8,24},{12,28},{16,0},{20,4},{24,8},{28,12},{1,17},{... | collective-permute-start | bytes 18440 | tf_op jit(solution)/shard_map/ppermute | solution.py:494
  182.8 5.8 %collective-permute-done.19 = f32[1536]{0:T(1024)S(1)} collective-permute-done((f32[1536]{0:T(1024)S(1)}, f32[1536]{0:T(1024)S(1)}, u32[]{:S(2)}, u32[]{:S(2)}) %collective-permute-start.19) | collective-permute-done | bytes 6176 | tf_op jit(solution)/shard_map/ppermute | solution.py:494
  188.8 1.3 collective-permute-start.24
  190.1 0.7 slice.88
  190.8 0.7 slice.78
  191.4 6.3 %collective-permute-done.22 = bf16[192,768]{1,0:T(8,128)(2,1)S(1)} collective-permute-done((bf16[192,768]{1,0:T(8,128)(2,1)S(1)}, bf16[192,768]{1,0:T(8,128)(2,1)S(1)}, u32[]{:S(2)}, u32[]{:S(2)}) %collective-permute-start.22) | collective-permute-done | bytes 294944 | tf_op jit(solution)/shard_map/ppermute | solution.py:494
  197.9 1.1 collective-permute-start.25
  199.6 3.1 %finish.4 = (bf16[192,3072]{1,0:T(8,128)(2,1)}, f32[192,3072]{1,0:T(8,128)}) custom-call(bf16[1,2,400,1024]{3,2,1,0:T(8,128)(2,1)} %get-tuple-element.265.keep, bf16[1,2,400,1024]{3,2,1,0:T(8,128)(2,1)} %collective-permute-done.12.from_core, bf16[1,1,400,1024]{3,2,1,0:T(8,128)(2,1)} %collective-permute-done.21.from_y, ...), custom_call_target="tpu_custom_call", output_to_operand_aliasing={{0}: (8, {}), {1}: (9, {})} | custom-call | flops 3000 | bytes 5000 | tf_op jit(solution)/shard_map/finish/pallas_call | solution.py:471
  202.7 3.8 %select_convert_fusion = (f32[768,768]{1,0:T(8,128)}, f32[768,768]{1,0:T(8,128)}) fusion(bf16[768,768]{1,0:T(8,128)(2,1)S(1)} %maximum_select_fusion, bf16[768,768]{1,0:T(8,128)(2,1)} %collective-permute-done.23, pred[]{:T(512)S(6)} %gt.6), kind=kLoop, calls=%fused_computation.5 | loop fusion | flops 2359296 | bytes 7077889 | tf_op jit(solution)/shard_map/convert_element_type | solution.py:795
  206.5 2.7 %collective-permute-done.24.from_y = bf16[1,1,400,1024]{3,2,1,0:T(8,128)(2,1)S(1)} collective-permute-done((bf16[1,1,400,1024]{3,2,1,0:T(8,128)(2,1)}, bf16[1,1,400,1024]{3,2,1,0:T(8,128)(2,1)S(1)}, u32[]{:S(2)}, u32[]{:S(2)}) %collective-permute-start.24) | collective-permute-done | bytes 819232 | tf_op jit(solution)/shard_map/ppermute | solution.py:494
  209.2 0.9 copy-done.12
  210.1 3.1 %finish.5 = (bf16[192,3072]{1,0:T(8,128)(2,1)}, f32[192,3072]{1,0:T(8,128)}) custom-call(bf16[1,2,400,1024]{3,2,1,0:T(8,128)(2,1)} %get-tuple-element.277.keep, bf16[1,2,400,1024]{3,2,1,0:T(8,128)(2,1)} %collective-permute-done.16.from_core, bf16[1,1,400,1024]{3,2,1,0:T(8,128)(2,1)} %copy-done.12, ...), custom_call_target="tpu_custom_call", output_to_operand_aliasing={{0}: (8, {}), {1}: (9, {})} | custom-call | flops 3000 | bytes 5000 | tf_op jit(solution)/shard_map/finish/pallas_call | solution.py:471
  213.2 0.9 fusion.2
  214.4 1.4 convert_bitcast_fusion
  (92 shorter events, 4.6 us)
Async XLA Ops:
  1.4 27.5 %copy-start.4 = (bf16[192,128]{1,0:T(8,128)(2,1)}, bf16[192,128]{1,0:T(8,128)(2,1)S(1)}, u32[]{:S(2)}) copy-start(bf16[192,128]{1,0:T(8,128)(2,1)S(1)} %broadcast_in_dim.53.gain_own.gain) | copy-start | bytes 147460
  1.4 11.9 %collective-permute-start = (bf16[192,128]{1,0:T(8,128)(2,1)S(1)}, bf16[192,128]{1,0:T(8,128)(2,1)S(1)}, u32[]{:S(2)}, u32[]{:S(2)}) collective-permute-start(bf16[192,128]{1,0:T(8,128)(2,1)S(1)} %broadcast_in_dim.53.gain_own.gain), channel_id=1, source_target_pairs={{0,2},{1,3},{2,0},{3,1},{4,6},{5,7},{6,4},{7,5},{8,10},{9,11},{10,... | collective-permute-start | bytes 147464 | tf_op jit(solution)/shard_map/ppermute | solution.py:494
  4.4 8.9 %collective-permute-start.1 = (bf16[192,128]{1,0:T(8,128)(2,1)S(1)}, bf16[192,128]{1,0:T(8,128)(2,1)S(1)}, u32[]{:S(2)}, u32[]{:S(2)}) collective-permute-start(bf16[192,128]{1,0:T(8,128)(2,1)S(1)} %broadcast_in_dim.53.gain_own.gain), channel_id=1, source_target_pairs={{0,1},{1,0},{2,3},{3,2},{4,5},{5,4},{6,7},{7,6},{8,9},{9,8},{10,11... | collective-permute-start | bytes 147464 | tf_op jit(solution)/shard_map/ppermute | solution.py:494
  4.4 28.6 %collective-permute-start.2 = (bf16[192,3072]{1,0:T(8,128)(2,1)}, bf16[192,3072]{1,0:T(8,128)(2,1)S(1)}, u32[]{:S(2)}, u32[]{:S(2)}) collective-permute-start(bf16[192,3072]{1,0:T(8,128)(2,1)} %bitcast.16), channel_id=1, source_target_pairs={{0,2},{1,3},{2,0},{3,1},{4,6},{5,7},{6,4},{7,5},{8,10},{9,11},{10,... | collective-permute-start | bytes 3538952 | tf_op jit(solution)/shard_map/ppermute | solution.py:494
  4.6 28.4 %collective-permute-start.4 = (bf16[192,3072]{1,0:T(8,128)(2,1)}, bf16[192,3072]{1,0:T(8,128)(2,1)S(1)}, u32[]{:S(2)}, u32[]{:S(2)}) collective-permute-start(bf16[192,3072]{1,0:T(8,128)(2,1)} %bitcast.17), channel_id=1, source_target_pairs={{0,1},{1,0},{2,3},{3,2},{4,5},{5,4},{6,7},{7,6},{8,9},{9,8},{10,11... | collective-permute-start | bytes 3538952 | tf_op jit(solution)/shard_map/ppermute | solution.py:494
  13.3 15.6 %copy-start.15 = (bf16[192,128]{1,0:T(8,128)(2,1)}, bf16[192,128]{1,0:T(8,128)(2,1)S(1)}, u32[]{:S(2)}) copy-start(bf16[192,128]{1,0:T(8,128)(2,1)S(1)} %collective-permute-done.gain_y) | copy-start | bytes 147460
  13.3 15.6 %copy-start.16 = (bf16[192,128]{1,0:T(8,128)(2,1)}, bf16[192,128]{1,0:T(8,128)(2,1)S(1)}, u32[]{:S(2)}) copy-start(bf16[192,128]{1,0:T(8,128)(2,1)S(1)} %collective-permute-done.1.gain_c) | copy-start | bytes 147460
  17.0 11.9 %collective-permute-start.3 = (bf16[192,128]{1,0:T(8,128)(2,1)S(1)}, bf16[192,128]{1,0:T(8,128)(2,1)S(1)}, u32[]{:S(2)}, u32[]{:S(2)}) collective-permute-start(bf16[192,128]{1,0:T(8,128)(2,1)S(1)} %collective-permute-done.gain_y), channel_id=1, source_target_pairs={{0,1},{1,0},{2,3},{3,2},{4,5},{5,4},{6,7},{7,6},{8,9},{9,8},{10,11... | collective-permute-start | bytes 147464 | tf_op jit(solution)/shard_map/ppermute | solution.py:494
  28.9 4.1 %copy-start.17 = (bf16[192,128]{1,0:T(8,128)(2,1)}, bf16[192,128]{1,0:T(8,128)(2,1)S(1)}, u32[]{:S(2)}) copy-start(bf16[192,128]{1,0:T(8,128)(2,1)S(1)} %collective-permute-done.3.gain_cy) | copy-start | bytes 147460
  33.0 2.9 %copy-start.5 = (bf16[192,3072]{1,0:T(8,128)(2,1)}, bf16[192,3072]{1,0:T(8,128)(2,1)S(1)}, u32[]{:S(2)}) copy-start(bf16[192,3072]{1,0:T(8,128)(2,1)S(1)} %collective-permute-done.2.flip_y) | copy-start | bytes 3538948
  33.0 2.8 %collective-permute-start.5 = (bf16[192,3072]{1,0:T(8,128)(2,1)S(1)}, bf16[192,3072]{1,0:T(8,128)(2,1)S(1)}, u32[]{:S(2)}, u32[]{:S(2)}) collective-permute-start(bf16[192,3072]{1,0:T(8,128)(2,1)S(1)} %collective-permute-done.2.flip_y), channel_id=1, source_target_pairs={{0,1},{1,0},{2,3},{3,2},{4,5},{5,4},{6,7},{7,6},{8,9},{9,8},{10,11... | collective-permute-start | bytes 3538952 | tf_op jit(solution)/shard_map/ppermute | solution.py:494
  33.1 2.8 %copy-start.6 = (bf16[192,3072]{1,0:T(8,128)(2,1)}, bf16[192,3072]{1,0:T(8,128)(2,1)S(1)}, u32[]{:S(2)}) copy-start(bf16[192,3072]{1,0:T(8,128)(2,1)S(1)} %collective-permute-done.4.flip_c) | copy-start | bytes 3538948
  35.9 1.0 copy-start.7
  60.8 60.0 %all-to-all-start = ((bf16[8,192,768]{2,1,0:T(8,128)(2,1)}), bf16[8,192,768]{2,1,0:T(8,128)(2,1)S(1)}, u32[]{:S(2)}, u32[]{:S(2)}) async-start(bf16[8,192,768]{2,1,0:T(8,128)(2,1)} %bitcast.29), calls=%async_computation | async-start | bytes 4718592 | tf_op jit(solution)/shard_map/all_to_all | solution.py:523
  66.6 37.5 %copy-start.13 = (f32[768,128]{1,0:T(8,128)S(1)}, f32[768,128]{1,0:T(8,128)}, u32[]{:S(2)}) copy-start(f32[768,128]{1,0:T(8,128)} %get-tuple-element.211) | copy-start | bytes 1179652
  106.4 10.0 %collective-permute-start.6 = (f32[2,192]{1,0:T(2,128)S(1)}, f32[2,192]{1,0:T(2,128)S(1)}, u32[]{:S(2)}, u32[]{:S(2)}) collective-permute-start(f32[2,192]{1,0:T(2,128)S(1)} %pad_maximum_fusion.2), channel_id=1, source_target_pairs={{0,1},{1,0},{2,3},{3,2},{4,5},{5,4},{6,7},{7,6},{8,9},{9,8},{10,11... | collective-permute-start | bytes 4616 | tf_op jit(solution)/shard_map/ppermute | solution.py:494
  116.3 8.8 %copy-start.14 = (f32[384,128]{1,0:T(8,128)S(1)}, f32[384,128]{1,0:T(8,128)}, u32[]{:S(2)}) copy-start(f32[384,128]{1,0:T(8,128)} %get-tuple-element.239) | copy-start | bytes 589828
  121.9 16.9 %collective-permute-start.8 = (bf16[1,2,400,1024]{3,2,1,0:T(8,128)(2,1)}, bf16[1,2,400,1024]{3,2,1,0:T(8,128)(2,1)S(1)}, u32[]{:S(2)}, u32[]{:S(2)}) collective-permute-start(bf16[1,2,400,1024]{3,2,1,0:T(8,128)(2,1)} %get-tuple-element.235), channel_id=1, source_target_pairs={{0,1},{1,0},{2,3},{3,2},{4,5},{5,4},{6,7},{7,6},{8,9},{9,8},{10,11... | collective-permute-start | bytes 4915208 | tf_op jit(solution)/shard_map/ppermute | solution.py:494
  121.9 18.2 %collective-permute-start.9 = (bf16[384,768]{1,0:T(8,128)(2,1)}, bf16[384,768]{1,0:T(8,128)(2,1)}, u32[]{:S(2)}, u32[]{:S(2)}) collective-permute-start(bf16[384,768]{1,0:T(8,128)(2,1)} %constant_dynamic-slice_fusion.4), channel_id=1, source_target_pairs={{0,4},{4,0},{8,12},{12,8},{16,20},{20,16},{24,28},{28,24},{1,5},{5... | collective-permute-start | bytes 1769480 | tf_op jit(solution)/shard_map/ppermute | solution.py:494
  123.4 15.4 %collective-permute-start.7 = (f32[192]{0:T(256)S(1)}, f32[192]{0:T(256)S(1)}, u32[]{:S(2)}, u32[]{:S(2)}) collective-permute-start(f32[192]{0:T(256)S(1)} %bitcast.31), channel_id=1, source_target_pairs={{0,2},{1,3},{2,0},{3,1},{4,6},{5,7},{6,4},{7,5},{8,10},{9,11},{10,... | collective-permute-start | bytes 2312 | tf_op jit(solution)/shard_map/ppermute | solution.py:494
  126.5 12.4 %copy-start.2 = (bf16[1,2,400,1024]{3,2,1,0:T(8,128)(2,1)S(1)}, bf16[1,2,400,1024]{3,2,1,0:T(8,128)(2,1)}, u32[]{:S(2)}) copy-start(bf16[1,2,400,1024]{3,2,1,0:T(8,128)(2,1)} %get-tuple-element.242.keep) | copy-start | bytes 4915204
  126.5 16.6 %collective-permute-start.10 = (bf16[192,768]{1,0:T(8,128)(2,1)}, bf16[192,768]{1,0:T(8,128)(2,1)}, u32[]{:S(2)}, u32[]{:S(2)}) collective-permute-start(bf16[192,768]{1,0:T(8,128)(2,1)} %reduce_sum.75), channel_id=1, source_target_pairs={{0,16},{4,20},{8,24},{12,28},{16,0},{20,4},{24,8},{28,12},{1,17},{... | collective-permute-start | bytes 884744 | tf_op jit(solution)/shard_map/ppermute | solution.py:494
  138.8 4.3 %copy-start.3 = (bf16[1,2,400,1024]{3,2,1,0:T(8,128)(2,1)}, bf16[1,2,400,1024]{3,2,1,0:T(8,128)(2,1)S(1)}, u32[]{:S(2)}) copy-start(bf16[1,2,400,1024]{3,2,1,0:T(8,128)(2,1)S(1)} %collective-permute-done.8.from_core) | copy-start | bytes 4915204
  138.9 2.1 copy-start.8
  138.9 4.2 %copy-start.11 = (bf16[192,768]{1,0:T(8,128)(2,1)S(1)}, bf16[192,768]{1,0:T(8,128)(2,1)}, u32[]{:S(2)}) copy-start(bf16[192,768]{1,0:T(8,128)(2,1)} %reduce_sum.75) | copy-start | bytes 884740
  144.3 13.8 %copy-start = (bf16[1,2,400,1024]{3,2,1,0:T(8,128)(2,1)S(1)}, bf16[1,2,400,1024]{3,2,1,0:T(8,128)(2,1)}, u32[]{:S(2)}) copy-start(bf16[1,2,400,1024]{3,2,1,0:T(8,128)(2,1)} %get-tuple-element.265.keep) | copy-start | bytes 4915204
  144.3 13.8 %collective-permute-start.12 = (bf16[1,2,400,1024]{3,2,1,0:T(8,128)(2,1)}, bf16[1,2,400,1024]{3,2,1,0:T(8,128)(2,1)}, u32[]{:S(2)}, u32[]{:S(2)}) collective-permute-start(bf16[1,2,400,1024]{3,2,1,0:T(8,128)(2,1)} %get-tuple-element.261), channel_id=1, source_target_pairs={{0,1},{1,0},{2,3},{3,2},{4,5},{5,4},{6,7},{7,6},{8,9},{9,8},{10,11... | collective-permute-start | bytes 4915208 | tf_op jit(solution)/shard_map/ppermute | solution.py:494
  144.4 23.1 %collective-permute-start.15 = (bf16[1,1,400,1024]{3,2,1,0:T(8,128)(2,1)}, bf16[1,1,400,1024]{3,2,1,0:T(8,128)(2,1)}, u32[]{:S(2)}, u32[]{:S(2)}) collective-permute-start(bf16[1,1,400,1024]{3,2,1,0:T(8,128)(2,1)} %add_convert_fusion.2), channel_id=1, source_target_pairs={{0,2},{1,3},{2,0},{3,1},{4,6},{5,7},{6,4},{7,5},{8,10},{9,11},{10,... | collective-permute-start | bytes 2457608 | tf_op jit(solution)/shard_map/ppermute | solution.py:494
  145.7 16.3 %collective-permute-start.13 = (bf16[384,768]{1,0:T(8,128)(2,1)S(1)}, bf16[384,768]{1,0:T(8,128)(2,1)}, u32[]{:S(2)}, u32[]{:S(2)}) collective-permute-start(bf16[384,768]{1,0:T(8,128)(2,1)S(1)} %maximum_select_fusion.1), channel_id=1, source_target_pairs={{0,8},{4,12},{8,0},{12,4},{16,24},{20,28},{24,16},{28,20},{1,9},{5... | collective-permute-start | bytes 1769480 | tf_op jit(solution)/shard_map/ppermute | solution.py:494
  145.7 12.4 %collective-permute-start.11 = (f32[1536]{0:T(1024)S(1)}, f32[1536]{0:T(1024)S(1)}, u32[]{:S(2)}, u32[]{:S(2)}) collective-permute-start(f32[1536]{0:T(1024)S(1)} %concatenate.35), channel_id=1, source_target_pairs={{0,4},{4,0},{8,12},{12,8},{16,20},{20,16},{24,28},{28,24},{1,5},{5... | collective-permute-start | bytes 18440 | tf_op jit(solution)/shard_map/ppermute | solution.py:494
  146.8 20.7 %collective-permute-start.14 = (bf16[192,768]{1,0:T(8,128)(2,1)}, bf16[192,768]{1,0:T(8,128)(2,1)}, u32[]{:S(2)}, u32[]{:S(2)}) collective-permute-start(bf16[192,768]{1,0:T(8,128)(2,1)} %get-tuple-element.273), channel_id=1, source_target_pairs={{0,8},{4,12},{8,0},{12,4},{16,24},{20,28},{24,16},{28,20},{1,9},{5... | collective-permute-start | bytes 884744 | tf_op jit(solution)/shard_map/ppermute | solution.py:494
  160.5 7.3 %copy-start.9 = (bf16[192,768]{1,0:T(8,128)(2,1)S(1)}, bf16[192,768]{1,0:T(8,128)(2,1)}, u32[]{:S(2)}) copy-start(bf16[192,768]{1,0:T(8,128)(2,1)} %get-tuple-element.362) | copy-start | bytes 884740
  167.5 8.3 %collective-permute-start.16 = (bf16[1,2,400,1024]{3,2,1,0:T(8,128)(2,1)}, bf16[1,2,400,1024]{3,2,1,0:T(8,128)(2,1)}, u32[]{:S(2)}, u32[]{:S(2)}) collective-permute-start(bf16[1,2,400,1024]{3,2,1,0:T(8,128)(2,1)} %get-tuple-element.288), channel_id=1, source_target_pairs={{0,1},{1,0},{2,3},{3,2},{4,5},{5,4},{6,7},{7,6},{8,9},{9,8},{10,11... | collective-permute-start | bytes 4915208 | tf_op jit(solution)/shard_map/ppermute | solution.py:494
  167.5 8.3 %collective-permute-start.17 = (f32[1536]{0:T(1024)S(1)}, f32[1536]{0:T(1024)S(1)}, u32[]{:S(2)}, u32[]{:S(2)}) collective-permute-start(f32[1536]{0:T(1024)S(1)} %add.114), channel_id=1, source_target_pairs={{0,8},{4,12},{8,0},{12,4},{16,24},{20,28},{24,16},{28,20},{1,9},{5... | collective-permute-start | bytes 18440 | tf_op jit(solution)/shard_map/ppermute | solution.py:494
  168.8 10.1 %collective-permute-start.18 = (bf16[96,768]{1,0:T(8,128)(2,1)S(1)}, bf16[96,768]{1,0:T(8,128)(2,1)S(1)}, u32[]{:S(2)}, u32[]{:S(2)}) collective-permute-start(bf16[96,768]{1,0:T(8,128)(2,1)S(1)} %add_convert_fusion.7), channel_id=1, source_target_pairs={{0,16},{4,20},{8,24},{12,28},{16,0},{20,4},{24,8},{28,12},{1,17},{... | collective-permute-start | bytes 442376 | tf_op jit(solution)/shard_map/ppermute | solution.py:494
  170.5 20.9 %collective-permute-start.21 = (bf16[1,1,400,1024]{3,2,1,0:T(8,128)(2,1)}, bf16[1,1,400,1024]{3,2,1,0:T(8,128)(2,1)}, u32[]{:S(2)}, u32[]{:S(2)}) collective-permute-start(bf16[1,1,400,1024]{3,2,1,0:T(8,128)(2,1)} %add_convert_fusion.1), channel_id=1, source_target_pairs={{0,2},{1,3},{2,0},{3,1},{4,6},{5,7},{6,4},{7,5},{8,10},{9,11},{10,... | collective-permute-start | bytes 2457608 | tf_op jit(solution)/shard_map/ppermute | solution.py:494
  171.3 31.4 %collective-permute-start.23 = (bf16[768,768]{1,0:T(8,128)(2,1)S(1)}, bf16[768,768]{1,0:T(8,128)(2,1)}, u32[]{:S(2)}, u32[]{:S(2)}) collective-permute-start(bf16[768,768]{1,0:T(8,128)(2,1)S(1)} %maximum_select_fusion), channel_id=1, source_target_pairs={{0,4},{4,0},{8,12},{12,8},{16,20},{20,16},{24,28},{28,24},{1,5},{5... | collective-permute-start | bytes 3538952 | tf_op jit(solution)/shard_map/ppermute | solution.py:494
  172.6 3.2 %copy-start.1 = (bf16[1,2,400,1024]{3,2,1,0:T(8,128)(2,1)S(1)}, bf16[1,2,400,1024]{3,2,1,0:T(8,128)(2,1)}, u32[]{:S(2)}) copy-start(bf16[1,2,400,1024]{3,2,1,0:T(8,128)(2,1)} %get-tuple-element.277.keep) | copy-start | bytes 4915204
  175.8 3.1 %copy-start.10 = (bf16[192,768]{1,0:T(8,128)(2,1)S(1)}, bf16[192,768]{1,0:T(8,128)(2,1)}, u32[]{:S(2)}) copy-start(bf16[192,768]{1,0:T(8,128)(2,1)} %get-tuple-element.362) | copy-start | bytes 884740
  178.2 20.7 %copy-start.18 = (bf16[192]{0:T(256)(128)(2,1)S(1)}, bf16[192]{0:T(256)(128)(2,1)}, u32[]{:S(2)}) copy-start(bf16[192]{0:T(256)(128)(2,1)} %param.14) | copy-start | bytes 1156
  179.9 8.8 %collective-permute-start.20 = (bf16[96,768]{1,0:T(8,128)(2,1)S(1)}, bf16[96,768]{1,0:T(8,128)(2,1)S(1)}, u32[]{:S(2)}, u32[]{:S(2)}) collective-permute-start(bf16[96,768]{1,0:T(8,128)(2,1)S(1)} %add_convert_fusion.5), channel_id=1, source_target_pairs={{0,16},{4,20},{8,24},{12,28},{16,0},{20,4},{24,8},{28,12},{1,17},{... | collective-permute-start | bytes 442376 | tf_op jit(solution)/shard_map/ppermute | solution.py:494
  180.0 8.6 %collective-permute-start.19 = (f32[1536]{0:T(1024)S(1)}, f32[1536]{0:T(1024)S(1)}, u32[]{:S(2)}, u32[]{:S(2)}) collective-permute-start(f32[1536]{0:T(1024)S(1)} %add.117), channel_id=1, source_target_pairs={{0,16},{4,20},{8,24},{12,28},{16,0},{20,4},{24,8},{28,12},{1,17},{... | collective-permute-start | bytes 18440 | tf_op jit(solution)/shard_map/ppermute | solution.py:494
  188.7 9.0 %collective-permute-start.22 = (bf16[192,768]{1,0:T(8,128)(2,1)S(1)}, bf16[192,768]{1,0:T(8,128)(2,1)S(1)}, u32[]{:S(2)}, u32[]{:S(2)}) collective-permute-start(bf16[192,768]{1,0:T(8,128)(2,1)S(1)} %maximum_select_fusion.3), channel_id=1, source_target_pairs={{0,8},{4,12},{8,0},{12,4},{16,24},{20,28},{24,16},{28,20},{1,9},{5... | collective-permute-start | bytes 884744 | tf_op jit(solution)/shard_map/ppermute | solution.py:494
  188.8 20.4 %collective-permute-start.24 = (bf16[1,1,400,1024]{3,2,1,0:T(8,128)(2,1)}, bf16[1,1,400,1024]{3,2,1,0:T(8,128)(2,1)S(1)}, u32[]{:S(2)}, u32[]{:S(2)}) collective-permute-start(bf16[1,1,400,1024]{3,2,1,0:T(8,128)(2,1)} %add_convert_fusion), channel_id=1, source_target_pairs={{0,2},{1,3},{2,0},{3,1},{4,6},{5,7},{6,4},{7,5},{8,10},{9,11},{10,... | collective-permute-start | bytes 2457608 | tf_op jit(solution)/shard_map/ppermute | solution.py:494
  197.9 15.4 %collective-permute-start.25 = (bf16[384,768]{1,0:T(8,128)(2,1)S(1)}, bf16[384,768]{1,0:T(8,128)(2,1)S(1)}, u32[]{:S(2)}, u32[]{:S(2)}) collective-permute-start(bf16[384,768]{1,0:T(8,128)(2,1)S(1)} %maximum_select_fusion.2), channel_id=1, source_target_pairs={{0,4},{4,0},{8,12},{12,8},{16,20},{20,16},{24,28},{28,24},{1,5},{5... | collective-permute-start | bytes 1769480 | tf_op jit(solution)/shard_map/ppermute | solution.py:494
  209.2 0.9 copy-start.12
